TPU v7x, 32 devices: a whole 2x2x4 slice. The times are simulated.
32 devices in a mesh: grp: 4 (over y, x), sub: 8 (over z, core).
Axes of the slice: x: 2, y: 2, z: 4, core: 2. Of those that a mesh axis runs over, the one named last changes fastest.
Arguments:
- right_side: float32 [24576, 160], P(('grp', 'sub')), may hold values from -6 to 6
- iterate_in: float32 [24576, 160], P(('grp', 'sub')), may hold values from -6 to 6
- diagonal: float32 [24576], P(('grp', 'sub')), may hold values from 1.5 to 4
- block_values: bfloat16 [32, 6, 3, 128, 128], P(('grp', 'sub')), may hold values from -0.125 to 0.125
- block_cols: int32 [32, 6, 3], P(('grp', 'sub')), may hold values from 0 to 5, as said below
- couple_left: bfloat16 [24576, 128], P(('grp', 'sub')), may hold values from -0.125 to 0.125
- couple_right: bfloat16 [24576, 128], P(('grp', 'sub')), may hold values from -0.125 to 0.125
- send_rows: int32 [32, 2, 128], P(('grp', 'sub')), may hold values from 0 to 767, as said below
- local_inverse: bfloat16 [32, 1024, 1024], P(('grp', 'sub')), may hold values from -0.3 to 2.3, as said below
- coarse_basis: bfloat16 [32, 1024, 32], P(('grp', 'sub')), may hold values from -0.1875 to 0.1875
- coarse_diag: float32 [32, 32, 32], P(('grp', 'sub')), may hold values from -54 to 59.5, as said below
- coarse_up: float32 [32, 32, 32], P(('grp', 'sub')), may hold values from -29.7 to 27
Outputs:
- iterate: float32 [24576, 160], P(('grp', 'sub'))
- residual: float32 [24576, 160], P(('grp', 'sub'))
Inputs may be any that keep to these rules, and one draw needn't show every extreme that they name: `block_cols`: the 3 column blocks of one row block are distinct. `send_rows`: the 256 rows listed for one subdomain are distinct. `local_inverse`: each block is symmetric positive definite. `coarse_diag`: each block is symmetric; with coarse_up the coarse operator is symmetric positive definite.
All inputs are finite; a program needn't handle non-finite values.
Results may differ from a plain program's by a relative error of at most 0.0032.
Values may be sent and summed in bfloat16 or wider, within the bound.
No kernel may reach another device: no remote copies, remote signals or barrier semaphores. Data moves between devices by JAX's collectives and lax.ppermute only.
A program may use at most 64 MiB of HBM per device.

v0:
```python
import jax
import jax.numpy as jnp
from jax import lax
from jax.sharding import PartitionSpec as P


def with_halo(cells, sides, width):
    for axis, dim in sides:
        count = lax.axis_size(axis)
        ends = count - 1
        head = lax.slice_in_dim(cells, 0, width, axis=dim)
        tail = lax.slice_in_dim(cells, cells.shape[dim] - width, cells.shape[dim], axis=dim)
        cells = jnp.concatenate(
            [
                lax.ppermute(tail, axis, [(i, (i + 1) % count) for i in range(ends)]),
                cells,
                lax.ppermute(head, axis, [((i + 1) % count, i) for i in range(ends)]),
            ],
            axis=dim,
        )
    return cells


def chol_solve(factor, values):
    halfway = lax.linalg.triangular_solve(factor, values, left_side=True, lower=True)
    return lax.linalg.triangular_solve(
        factor, halfway, left_side=True, lower=True, transpose_a=True
    )


def solve_chain(diagonal_blocks, upper, values):
    highest = lax.Precision.HIGHEST
    blocks_total = diagonal_blocks.shape[0]
    padded_total = 1
    while padded_total < blocks_total:
        padded_total = padded_total * 2
    extra = padded_total - blocks_total
    block_width = diagonal_blocks.shape[1]
    identity = jnp.eye(block_width, dtype=jnp.float32)
    diag_now = jnp.concatenate(
        [diagonal_blocks, jnp.broadcast_to(identity, (extra, block_width, block_width))], axis=0
    )
    upper_now = jnp.concatenate(
        [upper[:-1], jnp.zeros((extra + 1, block_width, block_width), jnp.float32)], axis=0
    )
    rhs_now = jnp.concatenate([values, jnp.zeros((extra,) + values.shape[1:], jnp.float32)], axis=0)
    levels = []
    while diag_now.shape[0] > 1:
        diag_even = diag_now[0::2]
        diag_odd = diag_now[1::2]
        upper_even = upper_now[0::2]
        upper_odd = upper_now[1::2]
        rhs_even = rhs_now[0::2]
        rhs_odd = rhs_now[1::2]
        factor = jnp.linalg.cholesky(diag_odd)
        stacked = jnp.concatenate([jnp.swapaxes(upper_even, 1, 2), upper_odd, rhs_odd], axis=2)
        through = chol_solve(factor, stacked)
        toward_left = through[:, :, :block_width]
        toward_right = through[:, :, block_width : 2 * block_width]
        odd_loads = through[:, :, 2 * block_width :]
        new_diag = diag_even - jnp.einsum(
            "mab,mbc->mac", upper_even, toward_left, precision=highest
        )
        new_upper = -jnp.einsum("mab,mbc->mac", upper_even, toward_right, precision=highest)
        new_rhs = rhs_even - jnp.einsum("mab,mbn->man", upper_even, odd_loads, precision=highest)
        from_diag = jnp.einsum("mba,mbc->mac", upper_odd, toward_right, precision=highest)
        from_rhs = jnp.einsum("mba,mbn->man", upper_odd, odd_loads, precision=highest)
        new_diag = new_diag - jnp.concatenate(
            [jnp.zeros_like(from_diag[:1]), from_diag[:-1]], axis=0
        )
        new_rhs = new_rhs - jnp.concatenate([jnp.zeros_like(from_rhs[:1]), from_rhs[:-1]], axis=0)
        levels.append((toward_left, toward_right, odd_loads))
        diag_now, upper_now, rhs_now = (new_diag, new_upper, new_rhs)
    solution = chol_solve(jnp.linalg.cholesky(diag_now[0]), rhs_now[0])[None]
    for toward_left, toward_right, odd_loads in reversed(levels):
        next_sol = jnp.concatenate([solution[1:], jnp.zeros_like(solution[:1])], axis=0)
        odd_part = (
            odd_loads
            - jnp.einsum("mab,mbn->man", toward_left, solution, precision=highest)
            - jnp.einsum("mab,mbn->man", toward_right, next_sol, precision=highest)
        )
        solution = jnp.stack([solution, odd_part], axis=1).reshape((-1,) + solution.shape[1:])
    return solution[:blocks_total]


def shards(
    right_side,
    iterate_in,
    diagonal,
    block_values,
    block_cols,
    couple_left,
    couple_right,
    send_rows,
    local_inverse,
    coarse_basis,
    coarse_diag,
    coarse_up,
):
    bf16 = jnp.bfloat16
    f32 = jnp.float32
    highest = lax.Precision.HIGHEST
    intersection = send_rows.shape[2]
    rows_own = right_side.shape[0]
    cases = right_side.shape[1]
    row_blocks = block_cols.shape[1]
    modes = coarse_basis.shape[2]
    column_blocks = block_cols[0]
    sent_left_rows = send_rows[0, 0]
    sent_right_rows = send_rows[0, 1]

    def neighbour_rows(source):
        boundary = jnp.stack([source[sent_left_rows], source[sent_right_rows]])
        padded = with_halo(boundary, ((("grp", "sub"), 0),), 1)
        return (padded[0], padded[3])

    def apply_operator(vector):
        rounded = vector.astype(bf16)
        from_left, from_right = neighbour_rows(rounded)
        blocks = rounded.reshape(row_blocks, -1, cases)
        picked = blocks[column_blocks]
        sparse = jnp.einsum(
            "itab,itbn->ian", block_values[0], picked, preferred_element_type=f32
        ).reshape(rows_own, cases)
        coupled = jnp.dot(couple_left, from_left, preferred_element_type=f32) + jnp.dot(
            couple_right, from_right, preferred_element_type=f32
        )
        return diagonal[:, None] * vector + (sparse + coupled)

    residual_start = right_side - apply_operator(iterate_in)
    rounded = residual_start.astype(bf16)
    from_left, from_right = neighbour_rows(rounded)
    extended = jnp.concatenate([from_left, rounded, from_right], axis=0)
    local_part = jnp.dot(local_inverse[0], extended, preferred_element_type=f32)
    coarse_in = jnp.dot(coarse_basis[0].T, extended, preferred_element_type=f32)
    blocks_diag = lax.all_gather(coarse_diag, "sub", axis=0, tiled=True)
    blocks_up = lax.all_gather(coarse_up, "sub", axis=0, tiled=True)
    group = lax.axis_index("grp")
    groups = lax.axis_size("grp")
    member = lax.axis_index("sub")
    members = lax.axis_size("sub")
    keep = (group < groups - 1).astype(f32)
    first_up = blocks_up[0]
    last_up = blocks_up[members - 1] * keep
    columns = lax.all_gather(coarse_in[None], "sub", axis=0, tiled=True)
    width = columns.shape[2]
    inner_count = members - 1
    empty_cols = jnp.zeros((inner_count, modes, modes), f32)
    left_cols = empty_cols.at[0].set(first_up.T)
    right_cols = empty_cols.at[inner_count - 1].set(last_up)
    stacked = jnp.concatenate([columns[1:], left_cols, right_cols], axis=2)
    solved = solve_chain(blocks_diag[1:], blocks_up[1:], stacked)
    sol_loads = solved[:, :, :width]
    sol_left = solved[:, :, width : width + modes]
    sol_right = solved[:, :, width + modes :]
    self_left = jnp.dot(first_up, sol_left[0], precision=highest)
    cross_term = jnp.dot(first_up, sol_right[0], precision=highest)
    rhs_first = jnp.dot(first_up, sol_loads[0], precision=highest)
    self_right = jnp.dot(last_up.T, sol_right[-1], precision=highest)
    rhs_last = jnp.dot(last_up.T, sol_loads[-1], precision=highest)
    sep_diag = lax.all_gather(blocks_diag[0][None], "grp", axis=0, tiled=True)
    sep_rhs = lax.all_gather(columns[0][None], "grp", axis=0, tiled=True)
    all_left = lax.all_gather(self_left[None], "grp", axis=0, tiled=True)
    all_right = lax.all_gather(self_right[None], "grp", axis=0, tiled=True)
    all_cross = lax.all_gather(cross_term[None], "grp", axis=0, tiled=True)
    all_first = lax.all_gather(rhs_first[None], "grp", axis=0, tiled=True)
    all_last = lax.all_gather(rhs_last[None], "grp", axis=0, tiled=True)
    prev_right = jnp.concatenate([jnp.zeros_like(all_right[:1]), all_right[:-1]], axis=0)
    prev_last = jnp.concatenate([jnp.zeros_like(all_last[:1]), all_last[:-1]], axis=0)
    reduced_diag = sep_diag - all_left - prev_right
    reduced_rhs = sep_rhs - all_first - prev_last
    sep_sol = solve_chain(reduced_diag, -all_cross, reduced_rhs)
    padded_sol = jnp.concatenate([sep_sol, jnp.zeros_like(sep_sol[:1])], axis=0)
    mine = lax.dynamic_index_in_dim(padded_sol, group, 0, keepdims=False)
    after = lax.dynamic_index_in_dim(padded_sol, group + 1, 0, keepdims=False)
    inner_sol = (
        sol_loads
        - jnp.einsum("ivw,wn->ivn", sol_left, mine, precision=highest)
        - jnp.einsum("ivw,wn->ivn", sol_right, after, precision=highest)
    )
    group_sol = jnp.concatenate([mine[None], inner_sol], axis=0)
    coarse_sol = lax.dynamic_index_in_dim(group_sol, member, 0, keepdims=False)
    correction = local_part + jnp.dot(
        coarse_basis[0], coarse_sol.astype(bf16), preferred_element_type=f32
    )
    tails = jnp.stack([correction[:intersection], correction[intersection + rows_own :]])
    returned = with_halo(tails.astype(jnp.bfloat16), ((("grp", "sub"), 0),), 1).astype(tails.dtype)
    owned = correction[intersection : intersection + rows_own]
    owned = owned.at[sent_right_rows].add(returned[3])
    owned = owned.at[sent_left_rows].add(returned[0])
    inner = lax.psum(jnp.sum(residual_start * owned, axis=0), ("grp", "sub"))
    image = apply_operator(owned)
    curvature = lax.psum(jnp.sum(owned * image, axis=0), ("grp", "sub"))
    step_size = inner / curvature
    return (iterate_in + step_size * owned, residual_start - step_size * image)


def solution(mesh):
    in_specs = (
        P(("grp", "sub"), None),
        P(("grp", "sub"), None),
        P(("grp", "sub")),
        P(("grp", "sub"), None, None, None, None),
        P(("grp", "sub"), None, None),
        P(("grp", "sub"), None),
        P(("grp", "sub"), None),
        P(("grp", "sub"), None, None),
        P(("grp", "sub"), None, None),
        P(("grp", "sub"), None, None),
        P(("grp", "sub"), None, None),
        P(("grp", "sub"), None, None),
    )
    out_specs = (P(("grp", "sub"), None), P(("grp", "sub"), None))
    return jax.shard_map(shards, mesh=mesh, in_specs=in_specs, out_specs=out_specs, check_vma=False)
```

profile of v0, /device:TPU:0, one launch (start us, length us, event | category | flops | bytes accessed | tf_op | source)
XLA Modules:
  0.0 288.2 jit_solution(11546375033526299166)
XLA Ops:
  0.7 1.3 copy.175
  2.0 0.8 fusion.182
  2.8 1.5 gather_fusion.2
  4.3 1.3 collective-permute-start.1
  5.6 1.5 gather_fusion.1
  7.0 3.6 %collective-permute-start = (bf16[1,128,160]{2,1,0:T(8,128)(2,1)}, bf16[1,128,160]{2,1,0:T(8,128)(2,1)}, u32[]{:S(2)}, u32[]{:S(2)}) collective-permute-start(bf16[1,128,160]{2,1,0:T(8,128)(2,1)} %bitcast.9), channel_id=1, source_target_pairs={{0,1},{1,2},{2,3},{3,4},{4,5},{5,6},{6,7},{7,8},{8,9},{9,10},{10,1... | collective-permute-start | bytes 122888 | tf_op jit(solution)/shard_map/ppermute | solution.py:15
  11.0 18.4 %all_gather.32 = f32[8,32,32]{2,1,0:T(8,128)S(1)} all-gather(f32[1,32,32]{2,1,0:T(8,128)S(1)} %copy-done.34), channel_id=1, replica_groups=mesh['grp'=4,'sub'=8] {'sub'}, dimensions={0}, use_global_device_ids=true | all-gather | bytes 36864 | tf_op jit(solution)/shard_map/all_gather | solution.py:137
  29.4 14.0 %all_gather.30 = f32[8,32,32]{2,1,0:T(8,128)S(1)} all-gather(f32[1,32,32]{2,1,0:T(8,128)S(1)} %copy-done.35), channel_id=1, replica_groups=mesh['grp'=4,'sub'=8] {'sub'}, dimensions={0}, use_global_device_ids=true | all-gather | bytes 36864 | tf_op jit(solution)/shard_map/all_gather | solution.py:136
  43.7 11.7 %custom-call.47 = f32[4,32,32]{2,1,0:T(8,128)S(1)} custom-call(f32[4,32,32]{2,1,0:T(8,128)S(1)} %copy.185), custom_call_target="Cholesky" | custom-call | tf_op jit(solution)/shard_map/jit(cholesky)/cholesky | solution.py:55
  55.5 0.6 compare_reduce_fusion.6
  56.1 1.7 gather_fusion
  57.9 1.9 convolution_bitcast_fusion.1
  59.8 0.7 select_bitcast_fusion
  60.6 1.1 fusion.73
  61.7 1.9 fusion.211
  63.8 1.1 gather_fusion.4
  64.9 1.0 gather_fusion.3
  66.0 1.3 collective-permute-start.3
  67.4 3.0 %collective-permute-start.2 = (bf16[1,128,160]{1,2,0:T(8,128)(2,1)S(1)}, bf16[1,128,160]{1,2,0:T(8,128)(2,1)S(1)}, u32[]{:S(2)}, u32[]{:S(2)}) collective-permute-start(bf16[1,128,160]{1,2,0:T(8,128)(2,1)S(1)} %bitcast.413), channel_id=1, source_target_pairs={{0,1},{1,2},{2,3},{3,4},{4,5},{5,6},{6,7},{7,8},{8,9},{9,10},{10,1... | collective-permute-start | bytes 122888 | tf_op jit(solution)/shard_map/ppermute | solution.py:15
  70.5 0.7 copy.187
  71.3 11.2 %custom-call.48 = f32[4,1,32,32]{2,3,1,0:T(8,128)} custom-call(f32[4,1,32,32]{3,2,1,0:T(8,128)} %select_bitcast_fusion), custom_call_target="InvertDiagBlocksLowerTriangular" | custom-call | tf_op jit(solution)/shard_map/triangular_solve | solution.py:26
  82.4 10.3 %all_gather.31 = f32[4,32,32]{2,1,0:T(8,128)S(1)} all-gather(f32[1,32,32]{2,1,0:T(8,128)S(1)} %slice-done.1), channel_id=1, replica_groups=mesh['grp'=4,'sub'=8] {'grp'}, dimensions={0}, use_global_device_ids=true | all-gather | bytes 20480 | tf_op jit(solution)/shard_map/all_gather | solution.py:161
  92.7 0.7 copy.210
  93.4 0.6 copy-done.26
  94.2 14.4 %all-gather = f32[256,160]{1,0:T(8,128)S(1)} all-gather(f32[32,160]{1,0:T(8,128)S(1)} %convolution_bitcast_fusion.11), channel_id=2, replica_groups=mesh['grp'=4,'sub'=8] {'sub'}, dimensions={0}, use_global_device_ids=true | all-gather | bytes 184320 | tf_op jit(solution)/shard_map/all_gather | solution.py:145
  111.3 5.9 %custom-call.57 = f32[2,32,32]{2,1,0:T(8,128)S(1)} custom-call(f32[2,32,32]{2,1,0:T(8,128)S(1)} %fusion.117), custom_call_target="Cholesky" | custom-call | tf_op jit(solution)/shard_map/jit(cholesky)/cholesky | solution.py:55
  117.5 4.9 %custom-call.49 = f32[2,1,32,32]{2,3,1,0:T(8,128)S(1)} custom-call(f32[2,1,32,32]{3,2,1,0:T(8,128)S(1)} %fusion.119), custom_call_target="InvertDiagBlocksLowerTriangular" | custom-call | tf_op jit(solution)/shard_map/triangular_solve | solution.py:26
  124.5 2.9 %custom-call.58 = f32[1,32,32]{2,1,0:T(8,128)S(1)} custom-call(f32[1,32,32]{2,1,0:T(8,128)S(1)} %fusion.169), custom_call_target="Cholesky" | custom-call | tf_op jit(solution)/shard_map/jit(cholesky)/cholesky | solution.py:55
  127.4 0.6 compare_reduce_fusion.4
  128.6 2.4 custom-call.50
  132.3 2.9 %cholesky.184 = f32[32,32]{1,0:T(8,128)S(1)} custom-call(f32[32,32]{1,0:T(8,128)S(1)} %fusion.150), custom_call_target="Cholesky" | custom-call | tf_op jit(solution)/shard_map/jit(cholesky)/cholesky | solution.py:74
  135.2 0.6 compare_reduce_fusion.3
  136.4 2.4 custom-call.51
  141.8 7.0 %all-gather.6 = f32[128,160]{1,0:T(8,128)S(1)} all-gather(f32[32,160]{1,0:T(8,128)S(1)} %slice-done), channel_id=8, replica_groups=mesh['grp'=4,'sub'=8] {'grp'}, dimensions={0}, use_global_device_ids=true | all-gather | bytes 102400 | tf_op jit(solution)/shard_map/all_gather | solution.py:162
  148.9 8.9 %all-gather.4 = f32[128,160]{1,0:T(8,128)S(1)} all-gather(f32[32,160]{1,0:T(8,128)S(1)} %convolution_bitcast_fusion.7), channel_id=6, replica_groups=mesh['grp'=4,'sub'=8] {'grp'}, dimensions={0}, use_global_device_ids=true | all-gather | bytes 102400 | tf_op jit(solution)/shard_map/all_gather | solution.py:166
  157.8 7.1 %all-gather.5 = f32[128,160]{1,0:T(8,128)S(1)} all-gather(f32[32,160]{1,0:T(8,128)S(1)} %fusion.101), channel_id=7, replica_groups=mesh['grp'=4,'sub'=8] {'grp'}, dimensions={0}, use_global_device_ids=true | all-gather | bytes 102400 | tf_op jit(solution)/shard_map/all_gather | solution.py:167
  165.1 8.7 %all-gather.3 = f32[128,32]{1,0:T(8,128)S(1)} all-gather(f32[32,32]{1,0:T(8,128)S(1)} %copy.214), channel_id=5, replica_groups=mesh['grp'=4,'sub'=8] {'grp'}, dimensions={0}, use_global_device_ids=true | all-gather | bytes 20480 | tf_op jit(solution)/shard_map/all_gather | solution.py:165
  173.9 6.8 %all-gather.2 = f32[128,32]{1,0:T(8,128)S(1)} all-gather(f32[32,32]{1,0:T(8,128)S(1)} %fusion.145), channel_id=4, replica_groups=mesh['grp'=4,'sub'=8] {'grp'}, dimensions={0}, use_global_device_ids=true | all-gather | bytes 20480 | tf_op jit(solution)/shard_map/all_gather | solution.py:164
  180.9 8.9 %all-gather.1 = f32[128,32]{1,0:T(8,128)S(1)} all-gather(f32[32,32]{1,0:T(8,128)S(1)} %copy.208), channel_id=3, replica_groups=mesh['grp'=4,'sub'=8] {'grp'}, dimensions={0}, use_global_device_ids=true | all-gather | bytes 20480 | tf_op jit(solution)/shard_map/all_gather | solution.py:163
  190.0 5.9 %custom-call.59 = f32[2,32,32]{2,1,0:T(8,128)S(1)} custom-call(f32[2,32,32]{2,1,0:T(8,128)S(1)} %fusion.112), custom_call_target="Cholesky" | custom-call | tf_op jit(solution)/shard_map/jit(cholesky)/cholesky | solution.py:55
  196.1 4.9 %custom-call.52 = f32[2,1,32,32]{2,3,1,0:T(8,128)S(1)} custom-call(f32[2,1,32,32]{3,2,1,0:T(8,128)S(1)} %fusion.118), custom_call_target="InvertDiagBlocksLowerTriangular" | custom-call | tf_op jit(solution)/shard_map/triangular_solve | solution.py:26
  203.0 2.9 %custom-call.60 = f32[1,32,32]{2,1,0:T(8,128)S(1)} custom-call(f32[1,32,32]{2,1,0:T(8,128)S(1)} %fusion.158), custom_call_target="Cholesky" | custom-call | tf_op jit(solution)/shard_map/jit(cholesky)/cholesky | solution.py:55
  206.0 0.6 compare_reduce_fusion.1
  206.6 0.7 fusion.143
  207.3 2.4 custom-call.53
  210.9 2.9 %cholesky.216 = f32[32,32]{1,0:T(8,128)S(1)} custom-call(f32[32,32]{1,0:T(8,128)S(1)} %fusion.149), custom_call_target="Cholesky" | custom-call | tf_op jit(solution)/shard_map/jit(cholesky)/cholesky | solution.py:74
  213.9 0.6 compare_reduce_fusion
  214.5 0.7 fusion.144
  215.2 2.4 custom-call.54
  219.9 0.9 fusion.212
  220.8 1.3 collective-permute-start.5
  222.1 3.0 %collective-permute-start.4 = (bf16[1,128,160]{1,2,0:T(8,128)(2,1)S(1)}, bf16[1,128,160]{1,2,0:T(8,128)(2,1)S(1)}, u32[]{:S(2)}, u32[]{:S(2)}) collective-permute-start(bf16[1,128,160]{1,2,0:T(8,128)(2,1)S(1)} %get-tuple-element.33), channel_id=1, source_target_pairs={{0,1},{1,2},{2,3},{3,4},{4,5},{5,6},{6,7},{7,8},{8,9},{9,10},{10,1... | collective-permute-start | bytes 122888 | tf_op jit(solution)/shard_map/ppermute | solution.py:15
  226.2 1.6 scatter_fusion
  227.8 1.6 scatter_fusion.1
  229.4 1.0 copy.230
  230.5 1.6 gather_fusion.7
  232.1 1.0 gather_fusion.6
  233.0 1.3 collective-permute-start.7
  234.3 3.0 %collective-permute-start.6 = (bf16[1,128,160]{2,1,0:T(8,128)(2,1)S(1)}, bf16[1,128,160]{2,1,0:T(8,128)(2,1)S(1)}, u32[]{:S(2)}, u32[]{:S(2)}) collective-permute-start(bf16[1,128,160]{2,1,0:T(8,128)(2,1)S(1)} %bitcast.407), channel_id=1, source_target_pairs={{0,1},{1,2},{2,3},{3,4},{4,5},{5,6},{6,7},{7,8},{8,9},{9,10},{10,1... | collective-permute-start | bytes 122888 | tf_op jit(solution)/shard_map/ppermute | solution.py:15
  237.6 0.7 gather_fusion.5
  238.4 1.6 convolution_bitcast_fusion
  240.2 1.1 multiply_reduce_fusion
  241.4 44.6 %all-reduce.16 = (f32[160]{0:T(256)S(1)}, f32[160]{0:T(256)S(1)}) all-reduce(f32[160]{0:T(256)S(1)} %get-tuple-element.30, f32[160]{0:T(256)S(1)} %get-tuple-element.29), channel_id=1, replica_groups=mesh['grp'=4,'sub'=8] {'grp','sub'}, use_global_device_ids=true, to_apply=%region_11.15 | all-reduce | flops 320 | bytes 2560 | tf_op jit(solution)/shard_map/psum | solution.py:191
  285.9 2.3 multiply_subtract_fusion
  (250 shorter events, 19.2 us)
Async XLA Ops:
  0.6 219.2 %copy-start = (bf16[1,1024,1024]{2,1,0:T(8,128)(2,1)S(1)}, bf16[1,1024,1024]{2,1,0:T(8,128)(2,1)}, u32[]{:S(2)}) copy-start(bf16[1,1024,1024]{2,1,0:T(8,128)(2,1)} %param.27) | copy-start | bytes 6291460
  0.6 10.1 %copy-start.43 = (s32[1,6,3]{1,0,2:T(1,128)S(1)}, s32[1,6,3]{1,0,2:T(1,128)}, u32[]{:S(2)}) copy-start(s32[1,6,3]{1,0,2:T(1,128)} %param.23) | copy-start | bytes 220
  0.7 10.3 %copy-start.34 = (f32[1,32,32]{2,1,0:T(8,128)S(1)}, f32[1,32,32]{2,1,0:T(8,128)}, u32[]{:S(2)}) copy-start(f32[1,32,32]{2,1,0:T(8,128)} %param.30) | copy-start | bytes 12292
  0.7 28.7 %copy-start.35 = (f32[1,32,32]{2,1,0:T(8,128)S(1)}, f32[1,32,32]{2,1,0:T(8,128)}, u32[]{:S(2)}) copy-start(f32[1,32,32]{2,1,0:T(8,128)} %param.29) | copy-start | bytes 12292
  2.8 7.9 %copy-start.38 = (s32[128]{0:T(128)}, s32[128]{0:T(128)S(1)}, u32[]{:S(2)}) copy-start(s32[128]{0:T(128)S(1)} %get-tuple-element.52) | copy-start | bytes 1540
  2.8 26.6 %copy-start.40 = (s32[128]{0:T(128)}, s32[128]{0:T(128)S(1)}, u32[]{:S(2)}) copy-start(s32[128]{0:T(128)S(1)} %get-tuple-element.51) | copy-start | bytes 1540
  2.8 26.6 %copy-start.36 = (s32[1024]{0:T(1024)}, s32[1024]{0:T(1024)S(1)}, u32[]{:S(2)}) copy-start(s32[1024]{0:T(1024)S(1)} %get-tuple-element.59) | copy-start | bytes 12292
  2.8 26.6 %copy-start.37 = (s32[1024]{0:T(1024)}, s32[1024]{0:T(1024)S(1)}, u32[]{:S(2)}) copy-start(s32[1024]{0:T(1024)S(1)} %get-tuple-element.58) | copy-start | bytes 12292
  4.3 56.2 %collective-permute-start.1 = (bf16[1,128,160]{2,1,0:T(8,128)(2,1)}, bf16[1,128,160]{2,1,0:T(8,128)(2,1)}, u32[]{:S(2)}, u32[]{:S(2)}) collective-permute-start(bf16[1,128,160]{2,1,0:T(8,128)(2,1)} %bitcast.13), channel_id=1, source_target_pairs={{1,0},{2,1},{3,2},{4,3},{5,4},{6,5},{7,6},{8,7},{9,8},{10,9},{11,1... | collective-permute-start | bytes 122888 | tf_op jit(solution)/shard_map/ppermute | solution.py:17
  7.0 54.6 %collective-permute-start = (bf16[1,128,160]{2,1,0:T(8,128)(2,1)}, bf16[1,128,160]{2,1,0:T(8,128)(2,1)}, u32[]{:S(2)}, u32[]{:S(2)}) collective-permute-start(bf16[1,128,160]{2,1,0:T(8,128)(2,1)} %bitcast.9), channel_id=1, source_target_pairs={{0,1},{1,2},{2,3},{3,4},{4,5},{5,6},{6,7},{7,8},{8,9},{9,10},{10,1... | collective-permute-start | bytes 122888 | tf_op jit(solution)/shard_map/ppermute | solution.py:15
  10.7 47.1 %copy-start.24 = (pred[32,32]{1,0:T(8,128)(4,1)}, pred[32,32]{1,0:T(8,128)(4,1)S(1)}, u32[]{:S(2)}) copy-start(pred[32,32]{1,0:T(8,128)(4,1)S(1)} %iota_compare_fusion.3) | copy-start | bytes 3076
  10.7 49.1 %copy-start.22 = (pred[32,32]{1,0:T(8,128)(4,1)}, pred[32,32]{1,0:T(8,128)(4,1)S(1)}, u32[]{:S(2)}) copy-start(pred[32,32]{1,0:T(8,128)(4,1)S(1)} %iota_compare_fusion.7) | copy-start | bytes 3076
  11.0 46.9 %copy-start.30 = (s32[1024]{0:T(1024)}, s32[1024]{0:T(1024)S(1)}, u32[]{:S(2)}) copy-start(s32[1024]{0:T(1024)S(1)} %pad_clamp_fusion.2) | copy-start | bytes 12292
  43.3 12.7 %copy-start.11 = (f32[8,32,32]{2,1,0:T(8,128)}, f32[8,32,32]{2,1,0:T(8,128)S(1)}, u32[]{:S(2)}) copy-start(f32[8,32,32]{2,1,0:T(8,128)S(1)} %all_gather.30) | copy-start | bytes 98308
  55.4 0.7 copy-start.15
  56.1 1.8 copy-start.5
  57.9 2.0 copy-start.16
  57.9 2.0 copy-start.42
  57.9 2.7 copy-start.9
  57.9 3.8 %copy-start.1 = (f32[768,160]{0,1:T(8,128)S(1)}, f32[768,160]{0,1:T(8,128)}, u32[]{:S(2)}) copy-start(f32[768,160]{0,1:T(8,128)} %param.20) | copy-start | bytes 1474564
  57.9 3.8 %copy-start.7 = (bf16[768,128]{1,0:T(8,128)(2,1)S(1)}, bf16[768,128]{1,0:T(8,128)(2,1)}, u32[]{:S(2)}) copy-start(bf16[768,128]{1,0:T(8,128)(2,1)} %param.24) | copy-start | bytes 589828
  57.9 3.8 %copy-start.12 = (f32[768,160]{0,1:T(8,128)S(1)}, f32[768,160]{0,1:T(8,128)}, u32[]{:S(2)}) copy-start(f32[768,160]{0,1:T(8,128)} %param.19) | copy-start | bytes 1474564
  57.9 3.8 %copy-start.32 = (f32[768]{0:T(1024)S(1)}, f32[768]{0:T(1024)}, u32[]{:S(2)}) copy-start(f32[768]{0:T(1024)} %param.21) | copy-start | bytes 9220
  60.5 48.1 %copy-start.13 = (f32[1,32,32]{2,1,0:T(8,128)}, f32[1,32,32]{2,1,0:T(8,128)S(1)}, u32[]{:S(2)}) copy-start(f32[1,32,32]{2,1,0:T(8,128)S(1)} %get-tuple-element.38) | copy-start | bytes 12292
  63.6 18.8 %slice-start.1 = ((f32[8,32,32]{2,1,0:T(8,128)}), f32[1,32,32]{2,1,0:T(8,128)S(1)}, s32[]{:S(2)}) async-start(f32[8,32,32]{2,1,0:T(8,128)} %copy-done.11), calls=%async_computation.1 | async-start | bytes 32768 | tf_op jit(solution)/shard_map/slice | solution.py:161
  63.8 30.2 %copy-start.20 = (bf16[1,1024,32]{1,2,0:T(8,128)(2,1)S(1)}, bf16[1,1024,32]{1,2,0:T(8,128)(2,1)}, u32[]{:S(2)}) copy-start(bf16[1,1024,32]{1,2,0:T(8,128)(2,1)} %param.28) | copy-start | bytes 196612
  66.0 27.4 %collective-permute-start.3 = (bf16[1,128,160]{1,2,0:T(8,128)(2,1)S(1)}, bf16[1,128,160]{1,2,0:T(8,128)(2,1)S(1)}, u32[]{:S(2)}, u32[]{:S(2)}) collective-permute-start(bf16[1,128,160]{1,2,0:T(8,128)(2,1)S(1)} %bitcast.412), channel_id=1, source_target_pairs={{1,0},{2,1},{3,2},{4,3},{5,4},{6,5},{7,6},{8,7},{9,8},{10,9},{11,1... | collective-permute-start | bytes 122888 | tf_op jit(solution)/shard_map/ppermute | solution.py:17
  67.4 26.0 %collective-permute-start.2 = (bf16[1,128,160]{1,2,0:T(8,128)(2,1)S(1)}, bf16[1,128,160]{1,2,0:T(8,128)(2,1)S(1)}, u32[]{:S(2)}, u32[]{:S(2)}) collective-permute-start(bf16[1,128,160]{1,2,0:T(8,128)(2,1)S(1)} %bitcast.413), channel_id=1, source_target_pairs={{0,1},{1,2},{2,3},{3,4},{4,5},{5,6},{6,7},{7,8},{8,9},{9,10},{10,1... | collective-permute-start | bytes 122888 | tf_op jit(solution)/shard_map/ppermute | solution.py:15
  93.4 0.6 copy-start.26
  93.4 0.6 copy-start.28
  94.0 14.7 %copy-start.18 = (f32[4,1,32,32]{2,3,1,0:T(8,128)S(1)}, f32[4,1,32,32]{2,3,1,0:T(8,128)}, u32[]{:S(2)}) copy-start(f32[4,1,32,32]{2,3,1,0:T(8,128)} %custom-call.48) | copy-start | bytes 49156
  94.0 14.7 %copy-start.19 = (f32[4,32,32]{2,1,0:T(8,128)S(1)}, f32[4,32,32]{2,1,0:T(8,128)}, u32[]{:S(2)}) copy-start(f32[4,32,32]{2,1,0:T(8,128)} %copy.187) | copy-start | bytes 49156
  108.6 1.0 copy-start.6
  109.9 7.3 %copy-start.25 = (pred[32,32]{1,0:T(8,128)(4,1)S(1)}, pred[32,32]{1,0:T(8,128)(4,1)}, u32[]{:S(2)}) copy-start(pred[32,32]{1,0:T(8,128)(4,1)} %copy-done.24) | copy-start | bytes 3076
  109.9 7.5 %copy-start.23 = (pred[32,32]{1,0:T(8,128)(4,1)S(1)}, pred[32,32]{1,0:T(8,128)(4,1)}, u32[]{:S(2)}) copy-start(pred[32,32]{1,0:T(8,128)(4,1)} %copy-done.22) | copy-start | bytes 3076
  139.9 0.9 copy-start.14
  140.0 1.9 slice-start
  140.6 33.1 %copy-start.44 = (pred[4]{0:T(512)(128)(4,1)S(1)}, pred[4]{0:T(512)(128)(4,1)}, u32[]{:S(2)}) copy-start(pred[4]{0:T(512)(128)(4,1)} %constant.263.clone.1) | copy-start | bytes 16
  157.8 32.1 %copy-start.17 = (f32[4,32,32]{1,2,0:T(8,128)S(1)}, f32[4,32,32]{1,2,0:T(8,128)}, u32[]{:S(2)}) copy-start(f32[4,32,32]{1,2,0:T(8,128)} %copy.210) | copy-start | bytes 49156
  217.9 1.7 copy-start.21
  218.7 1.2 copy-start.27
  218.7 1.2 copy-start.29
  220.8 4.7 %collective-permute-start.5 = (bf16[1,128,160]{1,2,0:T(8,128)(2,1)S(1)}, bf16[1,128,160]{1,2,0:T(8,128)(2,1)S(1)}, u32[]{:S(2)}, u32[]{:S(2)}) collective-permute-start(bf16[1,128,160]{1,2,0:T(8,128)(2,1)S(1)} %get-tuple-element.34), channel_id=1, source_target_pairs={{1,0},{2,1},{3,2},{4,3},{5,4},{6,5},{7,6},{8,7},{9,8},{10,9},{11,1... | collective-permute-start | bytes 122888 | tf_op jit(solution)/shard_map/ppermute | solution.py:17
  222.1 3.9 %collective-permute-start.4 = (bf16[1,128,160]{1,2,0:T(8,128)(2,1)S(1)}, bf16[1,128,160]{1,2,0:T(8,128)(2,1)S(1)}, u32[]{:S(2)}, u32[]{:S(2)}) collective-permute-start(bf16[1,128,160]{1,2,0:T(8,128)(2,1)S(1)} %get-tuple-element.33), channel_id=1, source_target_pairs={{0,1},{1,2},{2,3},{3,4},{4,5},{5,6},{6,7},{7,8},{8,9},{9,10},{10,1... | collective-permute-start | bytes 122888 | tf_op jit(solution)/shard_map/ppermute | solution.py:15
  225.2 1.0 copy-start.41
  226.1 1.7 copy-start.39
  230.5 7.1 %copy-start.31 = (s32[1024]{0:T(1024)S(1)}, s32[1024]{0:T(1024)}, u32[]{:S(2)}) copy-start(s32[1024]{0:T(1024)} %copy-done.30) | copy-start | bytes 12292
  233.0 6.9 %collective-permute-start.7 = (bf16[1,128,160]{2,1,0:T(8,128)(2,1)}, bf16[1,128,160]{2,1,0:T(8,128)(2,1)S(1)}, u32[]{:S(2)}, u32[]{:S(2)}) collective-permute-start(bf16[1,128,160]{2,1,0:T(8,128)(2,1)} %bitcast.124), channel_id=1, source_target_pairs={{1,0},{2,1},{3,2},{4,3},{5,4},{6,5},{7,6},{8,7},{9,8},{10,9},{11,1... | collective-permute-start | bytes 122888 | tf_op jit(solution)/shard_map/ppermute | solution.py:17
  234.3 5.9 %collective-permute-start.6 = (bf16[1,128,160]{2,1,0:T(8,128)(2,1)S(1)}, bf16[1,128,160]{2,1,0:T(8,128)(2,1)S(1)}, u32[]{:S(2)}, u32[]{:S(2)}) collective-permute-start(bf16[1,128,160]{2,1,0:T(8,128)(2,1)S(1)} %bitcast.407), channel_id=1, source_target_pairs={{0,1},{1,2},{2,3},{3,4},{4,5},{5,6},{6,7},{7,8},{8,9},{9,10},{10,1... | collective-permute-start | bytes 122888 | tf_op jit(solution)/shard_map/ppermute | solution.py:15
  238.3 1.6 copy-start.10
  238.3 1.9 copy-start.3
  238.3 1.9 copy-start.4
  238.3 1.9 copy-start.8
  238.3 1.9 copy-start.33
  240.2 45.7 %copy-start.2 = (f32[768,160]{0,1:T(8,128)S(1)}, f32[768,160]{0,1:T(8,128)}, u32[]{:S(2)}) copy-start(f32[768,160]{0,1:T(8,128)} %param.20) | copy-start | bytes 1474564
where the time goes:
time: 290 us; the launch traced here: 288 us
  blocking collectives  149 us (51%)
  other arithmetic  79.4 us (27%)
  matrix products  21.8 us (8%)
  starting transfers between devices  17.9 us (6%)
  local copies, waits for them, and re-layouts  17.4 us (6%)
    psum x1, blocking collectives, shards(): inner = lax.psum(jnp.sum(residual_start * owned, axis=0), ('grp', 'sub'))  44.6 us
    another operation x15, other arithmetic, chol_solve(): lax.linalg.triangular_solve(factor, halfway, left_side=True, lower=True,...  34 us
    another operation x15, other arithmetic, solve_chain(): factor = jnp.linalg.cholesky(diag_odd)  31.6 us
    all_gather x1, blocking collectives, shards(): blocks_up = lax.all_gather(coarse_up, 'sub', axis=0, tiled=True)  18.4 us
    all_gather x1, blocking collectives, shards(): columns = lax.all_gather(coarse_in[None], 'sub', axis=0, tiled=True)  14.4 us
    all_gather x1, blocking collectives, shards(): blocks_diag = lax.all_gather(coarse_diag, 'sub', axis=0, tiled=True)  14 us
    ppermute x4, starting transfers between devices, with_halo(): lax.ppermute(tail, axis, [(i, (i + 1) % count) for i in range(ends)])  12.7 us
    all_gather x1, blocking collectives, shards(): sep_diag = lax.all_gather(blocks_diag[0][None], 'grp', axis=0, tiled=True)  10.3 us
  transfers between devices with their start and end apart: 8, of which 1 were waited for; matrix products, arithmetic and copies ran while one was open for 12% of the time, Pallas kernels for 0%

commit v1 on v0

v1 whole, which is shorter than its diff:
```python
import functools

import jax
import jax.numpy as jnp
from jax import lax
from jax.experimental import pallas as pl
from jax.experimental.pallas import tpu as pltpu
from jax.sharding import PartitionSpec as P

AXES = ("grp", "sub")
BF16 = jnp.bfloat16
F32 = jnp.float32
VMEM = pl.BlockSpec(memory_space=pltpu.VMEM)
SMEM = pl.BlockSpec(memory_space=pltpu.SMEM)


def mm(a, b):
    return jnp.dot(a, b, preferred_element_type=F32)


def mm_t(a, b, **kw):
    return lax.dot_general(a, b, (((0,), (0,)), ((), ())), preferred_element_type=F32, **kw)


def position():
    return lax.axis_index("grp") * lax.axis_size("sub") + lax.axis_index("sub")


def is_even():
    return position() % 2 == 0


def column_index(row):
    return jnp.transpose(jnp.broadcast_to(row, (row.shape[1], row.shape[1])))


def pick_matrix(row, total):
    column = column_index(row)
    width = column.shape[1]
    lane = lax.broadcasted_iota(jnp.int32, column.shape, 1)
    parts = [(column == lane + c * width).astype(F32).astype(BF16) for c in range(total // width)]
    return jnp.concatenate(parts, axis=1)


def place_matrix(row, total):
    place = lax.broadcasted_iota(jnp.int32, (total, row.shape[1]), 0)
    return (place == row).astype(F32).astype(BF16)


def gather_kernel(x_ref, rows_ref, to_pair_ref, to_other_ref):
    values = x_ref[...].astype(BF16)
    left, right = rows_ref[0, 0:1, :], rows_ref[0, 1:2, :]
    even = is_even()
    pair_rows = jnp.where(even, right, left)
    other_rows = jnp.where(even, left, right)
    to_pair_ref[...] = mm(pick_matrix(pair_rows, values.shape[0]), values).astype(BF16)
    to_other_ref[...] = mm(pick_matrix(other_rows, values.shape[0]), values).astype(BF16)


def times_operator(x, rounded_ref, left, right, diag_ref, values_ref, cols_ref, cl_ref, cr_ref, finish):
    blocks, nonzeros, size = values_ref.shape[1], values_ref.shape[2], values_ref.shape[3]
    for i in range(blocks):
        span = slice(i * size, (i + 1) * size)
        total = mm(cl_ref[span, :], left) + mm(cr_ref[span, :], right)
        for t in range(nonzeros):
            start = pl.multiple_of(cols_ref[0, i, t] * size, size)
            total = total + mm(values_ref[0, i, t], rounded_ref[pl.ds(start, size), :])
        column = jnp.transpose(jnp.broadcast_to(diag_ref[0:1, span], (size, size)))
        cases = x.shape[1]
        wide = jnp.concatenate([column] * pl.cdiv(cases, size), axis=1)[:, :cases]
        finish(span, wide * x[span, :] + total)


def residual_kernel(b_ref, x_ref, diag_ref, values_ref, cols_ref, cl_ref, cr_ref, rows_ref, pair_ref, other_ref,
                    r_ref, rb_ref, to_pair_ref, to_other_ref, xb_ref):
    x = x_ref[...]
    xb_ref[...] = x.astype(BF16)
    even = is_even()
    left = jnp.where(even, other_ref[...], pair_ref[...])
    right = jnp.where(even, pair_ref[...], other_ref[...])

    def finish(span, image):
        r = b_ref[span, :] - image
        r_ref[span, :] = r
        rb_ref[span, :] = r.astype(BF16)

    times_operator(x, xb_ref, left, right, diag_ref, values_ref, cols_ref, cl_ref, cr_ref, finish)
    values = rb_ref[...]
    row_left, row_right = rows_ref[0, 0:1, :], rows_ref[0, 1:2, :]
    pair_rows = jnp.where(even, row_right, row_left)
    other_rows = jnp.where(even, row_left, row_right)
    to_pair_ref[...] = mm(pick_matrix(pair_rows, values.shape[0]), values).astype(BF16)
    to_other_ref[...] = mm(pick_matrix(other_rows, values.shape[0]), values).astype(BF16)


def local_kernel(inverse_ref, basis_ref, diag_ref, up_ref, rb_ref, pair_ref, other_ref, local_ref, message_ref):
    even = is_even()
    left = jnp.where(even, other_ref[...], pair_ref[...])
    right = jnp.where(even, pair_ref[...], other_ref[...])
    extended = jnp.concatenate([left, rb_ref[...], right], axis=0)
    local_ref[...] = mm(inverse_ref[0], extended)
    coarse_in = mm_t(basis_ref[0], extended)
    last = position() == lax.axis_size("grp") * lax.axis_size("sub") - 1
    up = jnp.where(last, 0.0, up_ref[0])
    message = jnp.concatenate([diag_ref[0], jnp.transpose(up), up, coarse_in], axis=1)
    for slot in range(message_ref.shape[0]):
        message_ref[slot] = message


def reduce_rows(blocks):
    size = blocks[0].shape[0]
    here = lax.broadcasted_iota(jnp.int32, (size, 1), 0)
    for p in range(size):
        done = []
        for block in blocks:
            row = block[p:p + 1, :] / block[p:p + 1, p:p + 1]
            done.append(jnp.where(here == p, row, block - block[:, p:p + 1] * row))
        blocks = done
    return blocks


def schur(block, solved, size):
    width = solved.shape[1]
    product = -mm_t(block[:, :4 * size], solved, precision=lax.Precision.HIGHEST)
    top, bottom = product[size:2 * size], product[2 * size:3 * size]
    zero = jnp.zeros((size, size), F32)
    to_left = jnp.concatenate([top[:, size:2 * size], zero, top[:, 2 * size:]], axis=1)
    to_right = jnp.concatenate([bottom[:, 2 * size:3 * size], bottom[:, size:2 * size], zero, bottom[:, 3 * size:]], axis=1)
    return to_left, to_right


def own_part(block, size):
    lane = lax.broadcasted_iota(jnp.int32, block.shape, 1)
    return jnp.where((lane >= size) & (lane < 3 * size), 0.0, block)


def eliminate(chain, size, keep):
    count = len(chain) - 1
    step = 1
    while step < count:
        inner = list(range(step, count, 2 * step))
        solved = dict(zip(inner, reduce_rows([chain[j] for j in inner])))
        parts = {j: schur(chain[j], solved[j], size) for j in inner}
        for j in inner:
            keep(j, solved[j])
        for i in range(0, count + 1, 2 * step):
            total = own_part(chain[i], size)
            if i + step in parts:
                total = total + parts[i + step][0]
            if i - step in parts:
                total = total + parts[i - step][1]
            chain[i] = total
        step = 2 * step
    return chain[0], chain[count]


def back(solved, left, right, size):
    zero = jnp.zeros_like(left)
    stacked = jnp.concatenate([zero, left, right, zero], axis=0)
    return solved[:, 3 * size:] - jnp.dot(
        solved[:, :4 * size], stacked, precision=lax.Precision.HIGHEST, preferred_element_type=F32)


def padded(count):
    total = 1
    while total < count:
        total = 2 * total
    return total


def chain_of(blocks, size):
    width = blocks[0].shape[1]
    lane = lax.broadcasted_iota(jnp.int32, (size, width), 1)
    row = lax.broadcasted_iota(jnp.int32, (size, width), 0)
    from_previous = (lane >= size) & (lane < 2 * size)
    own = [jnp.where(from_previous, 0.0, block) for block in blocks]
    chain = [own[0]]
    for j in range(1, len(blocks)):
        chain.append(jnp.where(from_previous, blocks[j - 1], blocks[j]))
    return chain, from_previous, (lane == row).astype(F32)


def group_kernel(gathered_ref, solved_ref, message_ref):
    members, size, width = gathered_ref.shape
    blocks = [gathered_ref[j] for j in range(members)]
    chain, from_previous, identity = chain_of(blocks, size)
    tail = jnp.where(from_previous, blocks[members - 1], 0.0)
    total = padded(members)
    if total > members:
        raise NotImplementedError("members")
    chain.append(tail)

    def keep(j, solved):
        solved_ref[j] = solved

    head, tail = eliminate(chain, size, keep)
    message_ref[:size, :] = head
    message_ref[size:, :] = tail


def solve_kernel(reduced_ref, solved_ref, local_ref, basis_ref, rows_ref,
                 corr_ref, to_pair_ref, to_other_ref, sep_ref, x_ref, own_ref):
    groups, two_size, width = reduced_ref.shape
    size = two_size // 2
    members = solved_ref.shape[0]
    chain = []
    for g in range(groups):
        total = reduced_ref[g, :size, :]
        if g:
            total = total + reduced_ref[g - 1, size:, :]
        chain.append(total)
    count = padded(groups)
    row = lax.broadcasted_iota(jnp.int32, (size, width), 0)
    lane = lax.broadcasted_iota(jnp.int32, (size, width), 1)
    while len(chain) < count:
        chain.append((row == lane).astype(F32))
    chain.append(jnp.zeros((size, width), F32))
    factors = {}
    head, _ = eliminate(chain, size, factors.__setitem__)
    solution = {count: jnp.zeros((size, width - 3 * size), F32)}
    solution[0] = reduce_rows([head])[0][:, 3 * size:]
    step = count // 2
    while step >= 1:
        for j in range(step, count, 2 * step):
            solution[j] = back(factors[j], solution[j - step], solution[j + step], size)
        step = step // 2
    for g in range(groups):
        sep_ref[g] = solution[g]
    sep_ref[groups] = jnp.zeros((size, width - 3 * size), F32)
    group, member = lax.axis_index("grp"), lax.axis_index("sub")
    x_ref[0] = sep_ref[group]
    x_ref[members] = sep_ref[group + 1]
    step = members // 2
    while step >= 2:
        for j in range(step, members, 2 * step):
            x_ref[j] = back(solved_ref[j], x_ref[j - step], x_ref[j + step], size)
        step = step // 2
    odd = member // 2 * 2 + 1
    x_ref[odd] = back(solved_ref[odd], x_ref[odd - 1], x_ref[odd + 1], size)
    coarse = x_ref[member].astype(BF16)
    correction = local_ref[...] + mm(basis_ref[0], coarse)
    corr_ref[...] = correction
    margin = rows_ref.shape[2]
    owned = correction.shape[0] - 2 * margin
    rounded = correction.astype(BF16)
    even = is_even()
    head, tail = rounded[:margin], rounded[margin + owned:]
    values = rounded[margin:margin + owned]
    row_left, row_right = rows_ref[0, 0:1, :], rows_ref[0, 1:2, :]
    pair_rows = jnp.where(even, row_right, row_left)
    other_rows = jnp.where(even, row_left, row_right)
    to_pair_ref[:margin, :] = jnp.where(even, tail, head)
    to_other_ref[:margin, :] = jnp.where(even, head, tail)
    to_pair_ref[margin:, :] = mm(pick_matrix(pair_rows, owned), values).astype(BF16)
    to_other_ref[margin:, :] = mm(pick_matrix(other_rows, owned), values).astype(BF16)


def image_kernel(corr_ref, r_ref, diag_ref, values_ref, cols_ref, cl_ref, cr_ref, rows_ref, pair_ref, other_ref,
                 p_ref, image_ref, sums_ref, pb_ref):
    margin = rows_ref.shape[2]
    owned = p_ref.shape[0]
    even = is_even()
    from_left = jnp.where(even, other_ref[...], pair_ref[...])
    from_right = jnp.where(even, pair_ref[...], other_ref[...])
    place = jnp.concatenate(
        [place_matrix(rows_ref[0, 0:1, :], owned), place_matrix(rows_ref[0, 1:2, :], owned)], axis=1)
    tails = jnp.concatenate([from_left[:margin], from_right[:margin]], axis=0)
    p = corr_ref[margin:margin + owned, :] + mm(place, tails)
    p_ref[...] = p
    pb_ref[...] = p.astype(BF16)
    me = position()
    last = lax.axis_size("grp") * lax.axis_size("sub") - 1
    left = from_left[margin:].astype(F32) + corr_ref[:margin, :]
    right = from_right[margin:].astype(F32) + corr_ref[margin + owned:, :]
    left = jnp.where(me == 0, 0.0, left).astype(BF16)
    right = jnp.where(me == last, 0.0, right).astype(BF16)

    def finish(span, image):
        image_ref[span, :] = image

    times_operator(p, pb_ref, left, right, diag_ref, values_ref, cols_ref, cl_ref, cr_ref, finish)
    inner = jnp.sum(r_ref[...] * p, axis=0, keepdims=True)
    curvature = jnp.sum(p * image_ref[...], axis=0, keepdims=True)
    sums = jnp.concatenate([inner, curvature], axis=0)
    for slot in range(sums_ref.shape[0]):
        sums_ref[slot] = sums


def finish_kernel(x_ref, p_ref, r_ref, image_ref, sums_ref, out_x_ref, out_r_ref):
    sums = jnp.sum(sums_ref[...], axis=0)
    step = sums[0:1, :] / sums[1:2, :]
    out_x_ref[...] = x_ref[...] + step * p_ref[...]
    out_r_ref[...] = r_ref[...] - step * image_ref[...]


def call(kernel, out, in_specs, scratch=()):
    many = isinstance(out, (list, tuple))
    return pl.pallas_call(
        kernel,
        out_shape=out,
        in_specs=in_specs,
        out_specs=[VMEM] * len(out) if many else VMEM,
        scratch_shapes=list(scratch),
        name=kernel.__name__,
    )


def struct(shape, dtype):
    return jax.ShapeDtypeStruct(shape, dtype)


def shards(right_side, iterate_in, diagonal, block_values, block_cols, couple_left, couple_right, send_rows,
           local_inverse, coarse_basis, coarse_diag, coarse_up):
    groups, members = lax.axis_size("grp"), lax.axis_size("sub")
    total = groups * members
    rows, cases = right_side.shape
    margin = send_rows.shape[2]
    extended = local_inverse.shape[1]
    modes = coarse_basis.shape[2]
    width = 3 * modes + cases
    pairs = [(i, i ^ 1) for i in range(total)]
    others = [(i, i + 1 if i % 2 else i - 1) for i in range(1, total - 1)]
    diag = diagonal.reshape(1, rows)

    def swap(to_pair, to_other):
        return lax.ppermute(to_pair, AXES, pairs), lax.ppermute(to_other, AXES, others)

    halo = struct((margin, cases), BF16)
    full = struct((rows, cases), F32)
    operator = (diag, block_values, block_cols, couple_left, couple_right, send_rows)
    operator_specs = [VMEM, VMEM, SMEM, VMEM, VMEM, VMEM]
    sent = call(gather_kernel, [halo, halo], [VMEM] * 2)(iterate_in, send_rows)
    got = swap(*sent)
    residual, rounded, *sent = call(
        residual_kernel,
        [full, struct((rows, cases), BF16), halo, halo],
        [VMEM, VMEM] + operator_specs + [VMEM, VMEM],
        [pltpu.VMEM((rows, cases), BF16)],
    )(right_side, iterate_in, *operator, *got)
    got = swap(*sent)
    local, message = call(
        local_kernel, [struct((extended, cases), F32), struct((members, modes, width), F32)], [VMEM] * 7
    )(local_inverse, coarse_basis, coarse_diag, coarse_up, rounded, *got)
    gathered = lax.all_to_all(message, "sub", 0, 0, tiled=True)
    solved, reduced = call(
        group_kernel, [struct((members, modes, width), F32), struct((2 * modes, width), F32)], [VMEM]
    )(gathered)
    reduced = lax.all_gather(reduced, "grp", axis=0)
    correction, *sent = call(
        solve_kernel,
        [struct((extended, cases), F32)] + [struct((2 * margin, cases), BF16)] * 2,
        [VMEM] * 5,
        [
            pltpu.VMEM((groups + 1, modes, cases), F32),
            pltpu.VMEM((members + 1, modes, cases), F32),
            pltpu.VMEM((8, 128), F32),
        ],
    )(reduced, solved, local, coarse_basis, send_rows)
    got = swap(*sent)
    direction, image, sums = call(
        image_kernel,
        [full, full, struct((total, 2, cases), F32)],
        [VMEM, VMEM] + operator_specs + [VMEM, VMEM],
        [pltpu.VMEM((rows, cases), BF16)],
    )(correction, residual, *operator, *got)
    sums = lax.all_to_all(sums, AXES, 0, 0, tiled=True)
    return tuple(
        call(finish_kernel, [full, full], [VMEM] * 5)(iterate_in, direction, residual, image, sums)
    )


def solution(mesh):
    whole = P(AXES)

    def spec(rank):
        return P(AXES, *([None] * (rank - 1)))

    return jax.shard_map(
        shards,
        mesh=mesh,
        in_specs=tuple(spec(rank) for rank in (2, 2, 1, 5, 3, 2, 2, 3, 3, 3, 3, 3)),
        out_specs=(spec(2), spec(2)),
        check_vma=False,
    )
```

time: 290 us -> 117 us (0.40)
  blocking collectives: 149 us -> 52.6 us
  other arithmetic: 79.4 us -> 0 us
  Pallas kernels: 0 us -> 41.4 us
  matrix products: 21.8 us -> 0 us
  starting transfers between devices: 17.9 us -> 6.51 us
  local copies, waits for them, and re-layouts: 17.4 us -> 13.7 us
    all_gather x10 -> x1, blocking collectives: 104 us -> 11.9 us  [shards(): reduced = lax.all_gather(reduced, 'grp', axis=0)]
    another operation x42 -> x0, other arithmetic: 72.8 us -> none  [the longest x15 34 us: chol_solve(): lax.linalg.triangular_solve(factor, halfway, left_side=True, lower=True,...]
    psum x1 -> x0, blocking collectives: 44.6 us -> none  [shards(): inner = lax.psum(jnp.sum(residual_start * owned, axis=0), ('grp', 'sub'))]
    pallas_call x0 -> x7, Pallas kernels: none -> 41.4 us  [the longest x1 13.6 us: shards(): call(solve_kernel, [struct((extended, cases), F32)] + [struct((2 * margin...]
    all_to_all x0 -> x2, blocking collectives: none -> 40.7 us  [the longest x1 22.1 us: shards(): gathered = lax.all_to_all(message, 'sub', 0, 0, tiled=True)]
    dot_general x39 -> x0, matrix products: 16.5 us -> none  [the longest x2 3.42 us: apply_operator(): jnp.einsum('itab,itbn->ian', block_values[0], picked, preferred_element_t...]
    ppermute x8 -> x6, starting transfers between devices: 17.9 us -> 6.51 us  [the longest x3 4.55 us: swap(): lax.ppermute(to_pair, AXES, pairs)]
    gather x10 -> x0, local copies, waits for them, and re-layouts: 10.2 us -> none  [the longest x8 7.77 us: neighbour_rows(): boundary = jnp.stack([source[sent_left_rows], source[sent_right_rows]])]
  transfers between devices with their start and end apart: 8 -> 6, of which waited for: 1 -> 1; matrix products, arithmetic and copies ran while one was open for 12% -> 4% of each run, Pallas kernels for 0% -> 0%
where the time goes in v1:
time: 117 us; the launch traced here: 116 us
  blocking collectives  52.6 us (45%)
  Pallas kernels  41.4 us (35%)
  local copies, waits for them, and re-layouts  13.7 us (12%)
  starting transfers between devices  6.51 us (6%)
    all_to_all x1, blocking collectives, shards(): gathered = lax.all_to_all(message, 'sub', 0, 0, tiled=True)  22.1 us
    all_to_all x1, blocking collectives, shards(): sums = lax.all_to_all(sums, AXES, 0, 0, tiled=True)  18.6 us
    pallas_call x1, Pallas kernels, shards(): call(solve_kernel, [struct((extended, cases), F32)] + [struct((2 * margin...  13.6 us
    all_gather x1, blocking collectives, shards(): reduced = lax.all_gather(reduced, 'grp', axis=0)  11.9 us
    pallas_call x1, Pallas kernels, shards(): call(group_kernel, [struct((members, modes, width), F32), struct((2 * mod...  11.5 us
    unnamed x20, local copies, waits for them, and re-layouts  8.17 us
    ppermute x3, starting transfers between devices, swap(): lax.ppermute(to_pair, AXES, pairs)  4.55 us
    pallas_call x2, local copies, waits for them, and re-layouts, shards(): call(finish_kernel, [full, full], [VMEM] * 5)  4.31 us
  transfers between devices with their start and end apart: 6, of which 1 were waited for; matrix products, arithmetic and copies ran while one was open for 4% of the time, Pallas kernels for 0%

profile of v1, /device:TPU:0, one launch (start us, length us, event | category | flops | bytes accessed | tf_op | source)
XLA Modules:
  0.0 115.8 jit_solution(4319703569463716248)
XLA Ops:
  0.6 0.0 copy-start
  0.6 2.2 %copy.21.x_ref = f32[768,160]{1,0:T(8,128)} copy(f32[768,160]{0,1:T(8,128)} %param.13) | data formatting | bytes 983040 | tf_op args[1]
  2.9 2.1 %gather_kernel.1 = (bf16[128,160]{1,0:T(8,128)(2,1)}, bf16[128,160]{1,0:T(8,128)(2,1)}) custom-call(f32[768,160]{1,0:T(8,128)} %copy.21.x_ref, s32[1,2,128]{2,1,0:T(2,128)} %rows_ref.7), custom_call_target="tpu_custom_call" | custom-call | tf_op jit(solution)/shard_map/gather_kernel/pallas_call | solution.py:332
  5.0 0.0 copy-start.3
  5.0 0.5 collective-permute-start
  5.5 0.7 collective-permute-start.1
  6.2 1.3 %reshape.7.diag_ref = f32[1,768]{1,0:T(1,128)} reshape(f32[768]{0:T(1024)} %param.14) | data formatting | bytes 6144 | tf_op jit(solution)/shard_map/reshape | solution.py:323
  7.4 1.3 %copy.17.cols_ref = s32[1,6,3]{2,1,0:T(8,128)} copy(s32[1,6,3]{1,0,2:T(1,128)} %param.16) | data formatting | bytes 144 | tf_op args[4]
  8.8 0.0 copy-done
  8.8 1.2 copy.15.b_ref
  9.9 0.0 collective-permute-done.pair_ref
  9.9 0.0 copy-start.6
  9.9 0.0 collective-permute-done.1.other_ref
  10.0 0.6 copy-done.6
  10.6 0.0 copy-start.7
  10.6 0.6 copy-done.7
  11.2 3.4 %residual_kernel.1 = (f32[768,160]{1,0:T(8,128)}, bf16[768,160]{1,0:T(8,128)(2,1)}, bf16[128,160]{1,0:T(8,128)(2,1)}, bf16[128,160]{1,0:T(8,128)(2,1)}) custom-call(f32[768,160]{1,0:T(8,128)} %copy.15.b_ref, f32[768,160]{1,0:T(8,128)} %copy.21.x_ref, f32[1,768]{1,0:T(1,128)} %reshape.7.diag_ref, bf16[1,6,3,128,128]{4,3,2,1,0:T(8,128)(2,1)} %values_ref.3, ...), custom_call_target="tpu_custom_call" | custom-call | tf_op jit(solution)/shard_map/residual_kernel/pallas_call | solution.py:334
  14.6 4.1 %collective-permute-start.2 = (bf16[128,160]{1,0:T(8,128)(2,1)}, bf16[128,160]{1,0:T(8,128)(2,1)S(1)}, u32[]{:S(2)}, u32[]{:S(2)}) collective-permute-start(bf16[128,160]{1,0:T(8,128)(2,1)} %get-tuple-element.21), channel_id=1, source_target_pairs={{0,1},{1,0},{2,3},{3,2},{4,5},{5,4},{6,7},{7,6},{8,9},{9,8},{10,11... | collective-permute-start | bytes 122888 | tf_op jit(solution)/shard_map/ppermute | solution.py:326
  18.7 0.7 collective-permute-start.3
  19.4 0.0 copy-done.3
  19.4 0.8 copy.18.basis_ref
  20.2 0.0 collective-permute-done.2.pair_ref
  20.2 0.0 copy-start.4
  20.2 0.0 collective-permute-done.3.other_ref
  20.2 0.0 copy-start.5
  20.2 0.6 copy-done.4
  20.8 0.0 copy-done.5
  20.9 3.6 %local_kernel.1 = (f32[1024,160]{1,0:T(8,128)}, f32[8,32,256]{2,1,0:T(8,128)}) custom-call(bf16[1,1024,1024]{2,1,0:T(8,128)(2,1)} %inverse_ref.1, bf16[1,1024,32]{2,1,0:T(8,128)(2,1)} %copy.18.basis_ref, f32[1,32,32]{2,1,0:T(8,128)} %diag_ref.1, f32[1,32,32]{2,1,0:T(8,128)} %up_ref.1, bf16[768,160]{1,0:T(8,128)(2,1)} %get-tuple-element.20.rb_ref, ...), custom_call_target="tpu_custom_call" | custom-call | tf_op jit(solution)/shard_map/local_kernel/pallas_call | solution.py:341
  24.5 22.1 %all_to_all.10.gathered_ref = f32[8,32,256]{2,1,0:T(8,128)} all-to-all(f32[8,32,256]{2,1,0:T(8,128)} %get-tuple-element.23), channel_id=1, replica_groups=mesh['grp'=4,'sub'=8] {'sub'}, dimensions={0} | all-to-all | bytes 524288 | tf_op jit(solution)/shard_map/all_to_all | solution.py:344
  46.6 11.5 %group_kernel.1 = (f32[8,32,256]{2,1,0:T(8,128)}, f32[64,256]{1,0:T(8,128)}) custom-call(f32[8,32,256]{2,1,0:T(8,128)} %all_to_all.10.gathered_ref), custom_call_target="tpu_custom_call" | custom-call | tf_op jit(solution)/shard_map/group_kernel/pallas_call | solution.py:345
  58.1 11.9 %all-gather = f32[256,256]{1,0:T(8,128)} all-gather(f32[64,256]{1,0:T(8,128)} %get-tuple-element.24), channel_id=2, replica_groups=mesh['grp'=4,'sub'=8] {'grp'}, dimensions={0}, use_global_device_ids=true | all-gather | bytes 327680 | tf_op jit(solution)/shard_map/all_gather | solution.py:348
  70.0 13.6 %solve_kernel.1 = (f32[1024,160]{1,0:T(8,128)}, bf16[256,160]{1,0:T(8,128)(2,1)}, bf16[256,160]{1,0:T(8,128)(2,1)}) custom-call(f32[4,64,256]{2,1,0:T(8,128)} %bitcast.1, f32[8,32,256]{2,1,0:T(8,128)} %get-tuple-element.25.solved_ref, f32[1024,160]{1,0:T(8,128)} %get-tuple-element.26.local_ref, bf16[1,1024,32]{2,1,0:T(8,128)(2,1)} %copy.18.basis_ref, ...), custom_call_target="tpu_custom_call" | custom-call | tf_op jit(solution)/shard_map/solve_kernel/pallas_call | solution.py:349
  83.6 0.0 collective-permute-start.4
  83.6 0.7 collective-permute-start.5
  84.3 0.9 collective-permute-done.4.pair_ref
  85.1 0.0 copy-start.1
  85.1 0.0 collective-permute-done.5.other_ref
  85.2 0.0 copy-start.2
  85.2 0.6 copy-done.1
  85.8 0.0 copy-done.2
  85.8 3.9 %image_kernel.1 = (f32[768,160]{1,0:T(8,128)}, f32[768,160]{1,0:T(8,128)}, f32[32,2,160]{2,1,0:T(2,128)}) custom-call(f32[1024,160]{1,0:T(8,128)} %get-tuple-element.27.corr_ref, f32[768,160]{1,0:T(8,128)} %get-tuple-element.28.r_ref, f32[1,768]{1,0:T(1,128)} %reshape.7.diag_ref, bf16[1,6,3,128,128]{4,3,2,1,0:T(8,128)(2,1)} %values_ref.3, ...), custom_call_target="tpu_custom_call" | custom-call | tf_op jit(solution)/shard_map/image_kernel/pallas_call | solution.py:360
  89.7 18.6 %all_to_all.11.sums_ref = f32[32,2,160]{2,1,0:T(2,128)} all-to-all(f32[32,2,160]{2,1,0:T(2,128)} %get-tuple-element.33), channel_id=1, replica_groups=mesh['grp'=4,'sub'=8] {'grp','sub'}, dimensions={0} | all-to-all | bytes 81920 | tf_op jit(solution)/shard_map/all_to_all | solution.py:366
  108.4 3.1 %finish_kernel.1 = (f32[768,160]{1,0:T(8,128)}, f32[768,160]{1,0:T(8,128)}) custom-call(f32[768,160]{1,0:T(8,128)} %copy.21.x_ref, f32[768,160]{1,0:T(8,128)} %get-tuple-element.31.p_ref, f32[768,160]{1,0:T(8,128)} %get-tuple-element.28.r_ref, f32[768,160]{1,0:T(8,128)} %get-tuple-element.32.image_ref, f32[32,2,160]{2,1,0:T(2,128)} %all_to_all.11.sums_ref), custom_call_target="tpu_custom_call" | custom-call | tf_op jit(solution)/shard_map/finish_kernel/pallas_call | solution.py:368
  111.5 2.2 %copy.22 = f32[768,160]{0,1:T(8,128)} copy(f32[768,160]{1,0:T(8,128)} %get-tuple-element.34) | data formatting | bytes 983040 | tf_op jit(solution)/shard_map/finish_kernel/pallas_call | solution.py:368
  113.7 2.2 %copy.23 = f32[768,160]{0,1:T(8,128)} copy(f32[768,160]{1,0:T(8,128)} %get-tuple-element.35) | data formatting | bytes 983040 | tf_op jit(solution)/shard_map/finish_kernel/pallas_call | solution.py:368
Async XLA Ops:
  0.6 8.2 %copy-start = (f32[768,160]{0,1:T(8,128)S(1)}, f32[768,160]{0,1:T(8,128)}, u32[]{:S(2)}) copy-start(f32[768,160]{0,1:T(8,128)} %param.12) | copy-start | bytes 1474564
  5.0 14.3 %copy-start.3 = (bf16[1,1024,32]{1,2,0:T(8,128)(2,1)S(1)}, bf16[1,1024,32]{1,2,0:T(8,128)(2,1)}, u32[]{:S(2)}) copy-start(bf16[1,1024,32]{1,2,0:T(8,128)(2,1)} %param.21) | copy-start | bytes 196612
  5.0 4.9 %collective-permute-start = (bf16[128,160]{1,0:T(8,128)(2,1)}, bf16[128,160]{1,0:T(8,128)(2,1)S(1)}, u32[]{:S(2)}, u32[]{:S(2)}) collective-permute-start(bf16[128,160]{1,0:T(8,128)(2,1)} %get-tuple-element.18), channel_id=1, source_target_pairs={{0,1},{1,0},{2,3},{3,2},{4,5},{5,4},{6,7},{7,6},{8,9},{9,8},{10,11... | collective-permute-start | bytes 122888 | tf_op jit(solution)/shard_map/ppermute | solution.py:326
  5.5 4.4 %collective-permute-start.1 = (bf16[128,160]{1,0:T(8,128)(2,1)}, bf16[128,160]{1,0:T(8,128)(2,1)S(1)}, u32[]{:S(2)}, u32[]{:S(2)}) collective-permute-start(bf16[128,160]{1,0:T(8,128)(2,1)} %get-tuple-element.19), channel_id=1, source_target_pairs={{1,2},{2,1},{3,4},{4,3},{5,6},{6,5},{7,8},{8,7},{9,10},{10,9},{11,... | collective-permute-start | bytes 122888 | tf_op jit(solution)/shard_map/ppermute | solution.py:326
  9.9 0.6 copy-start.6
  10.6 0.6 copy-start.7
  14.6 5.6 %collective-permute-start.2 = (bf16[128,160]{1,0:T(8,128)(2,1)}, bf16[128,160]{1,0:T(8,128)(2,1)S(1)}, u32[]{:S(2)}, u32[]{:S(2)}) collective-permute-start(bf16[128,160]{1,0:T(8,128)(2,1)} %get-tuple-element.21), channel_id=1, source_target_pairs={{0,1},{1,0},{2,3},{3,2},{4,5},{5,4},{6,7},{7,6},{8,9},{9,8},{10,11... | collective-permute-start | bytes 122888 | tf_op jit(solution)/shard_map/ppermute | solution.py:326
  18.7 1.5 %collective-permute-start.3 = (bf16[128,160]{1,0:T(8,128)(2,1)}, bf16[128,160]{1,0:T(8,128)(2,1)S(1)}, u32[]{:S(2)}, u32[]{:S(2)}) collective-permute-start(bf16[128,160]{1,0:T(8,128)(2,1)} %get-tuple-element.22), channel_id=1, source_target_pairs={{1,2},{2,1},{3,4},{4,3},{5,6},{6,5},{7,8},{8,7},{9,10},{10,9},{11,... | collective-permute-start | bytes 122888 | tf_op jit(solution)/shard_map/ppermute | solution.py:326
  20.2 0.6 copy-start.4
  20.2 0.6 copy-start.5
  83.6 1.6 %collective-permute-start.4 = (bf16[256,160]{1,0:T(8,128)(2,1)}, bf16[256,160]{1,0:T(8,128)(2,1)S(1)}, u32[]{:S(2)}, u32[]{:S(2)}) collective-permute-start(bf16[256,160]{1,0:T(8,128)(2,1)} %get-tuple-element.29), channel_id=1, source_target_pairs={{0,1},{1,0},{2,3},{3,2},{4,5},{5,4},{6,7},{7,6},{8,9},{9,8},{10,11... | collective-permute-start | bytes 245768 | tf_op jit(solution)/shard_map/ppermute | solution.py:326
  83.6 1.6 %collective-permute-start.5 = (bf16[256,160]{1,0:T(8,128)(2,1)}, bf16[256,160]{1,0:T(8,128)(2,1)S(1)}, u32[]{:S(2)}, u32[]{:S(2)}) collective-permute-start(bf16[256,160]{1,0:T(8,128)(2,1)} %get-tuple-element.30), channel_id=1, source_target_pairs={{1,2},{2,1},{3,4},{4,3},{5,6},{6,5},{7,8},{8,7},{9,10},{10,9},{11,... | collective-permute-start | bytes 245768 | tf_op jit(solution)/shard_map/ppermute | solution.py:326
  85.1 0.7 copy-start.1
  85.2 0.7 copy-start.2

commit v2 on v1

--- a/solution.py
+++ b/solution.py
@@ -22,24 +22,16 @@
     return lax.dot_general(a, b, (((0,), (0,)), ((), ())), preferred_element_type=F32, **kw)
 
 
+def mm_nt(a, b, **kw):
+    return lax.dot_general(a, b, (((1,), (1,)), ((), ())), preferred_element_type=F32, **kw)
+
+
 def position():
     return lax.axis_index("grp") * lax.axis_size("sub") + lax.axis_index("sub")
 
 
 def is_even():
     return position() % 2 == 0
-
-
-def column_index(row):
-    return jnp.transpose(jnp.broadcast_to(row, (row.shape[1], row.shape[1])))
-
-
-def pick_matrix(row, total):
-    column = column_index(row)
-    width = column.shape[1]
-    lane = lax.broadcasted_iota(jnp.int32, column.shape, 1)
-    parts = [(column == lane + c * width).astype(F32).astype(BF16) for c in range(total // width)]
-    return jnp.concatenate(parts, axis=1)
 
 
 def place_matrix(row, total):
@@ -47,59 +39,62 @@
     return (place == row).astype(F32).astype(BF16)
 
 
+def send_matrix(rows_ref, total):
+    left, right = rows_ref[0, 0:1, :], rows_ref[0, 1:2, :]
+    even = is_even()
+    rows = jnp.concatenate([jnp.where(even, right, left), jnp.where(even, left, right)], axis=1)
+    return place_matrix(rows, total)
+
+
+def from_sides(pair_ref, other_ref):
+    even = is_even()
+    pair, other = pair_ref[...], other_ref[...]
+    return jnp.where(even, other, pair), jnp.where(even, pair, other)
+
+
 def gather_kernel(x_ref, rows_ref, to_pair_ref, to_other_ref):
     values = x_ref[...].astype(BF16)
-    left, right = rows_ref[0, 0:1, :], rows_ref[0, 1:2, :]
-    even = is_even()
-    pair_rows = jnp.where(even, right, left)
-    other_rows = jnp.where(even, left, right)
-    to_pair_ref[...] = mm(pick_matrix(pair_rows, values.shape[0]), values).astype(BF16)
-    to_other_ref[...] = mm(pick_matrix(other_rows, values.shape[0]), values).astype(BF16)
+    margin = rows_ref.shape[2]
+    sent = mm(values, send_matrix(rows_ref, values.shape[1])).astype(BF16)
+    to_pair_ref[...] = sent[:, :margin]
+    to_other_ref[...] = sent[:, margin:]
 
 
 def times_operator(x, rounded_ref, left, right, diag_ref, values_ref, cols_ref, cl_ref, cr_ref, finish):
     blocks, nonzeros, size = values_ref.shape[1], values_ref.shape[2], values_ref.shape[3]
+    diag = diag_ref[...].reshape(1, x.shape[1])
     for i in range(blocks):
         span = slice(i * size, (i + 1) * size)
-        total = mm(cl_ref[span, :], left) + mm(cr_ref[span, :], right)
+        total = mm_nt(left, cl_ref[span, :]) + mm_nt(right, cr_ref[span, :])
         for t in range(nonzeros):
-            start = pl.multiple_of(cols_ref[0, i, t] * size, size)
-            total = total + mm(values_ref[0, i, t], rounded_ref[pl.ds(start, size), :])
-        column = jnp.transpose(jnp.broadcast_to(diag_ref[0:1, span], (size, size)))
-        cases = x.shape[1]
-        wide = jnp.concatenate([column] * pl.cdiv(cases, size), axis=1)[:, :cases]
-        finish(span, wide * x[span, :] + total)
+            start = pl.multiple_of(cols_ref[t, 0, i] * size, size)
+            total = total + mm_nt(rounded_ref[:, pl.ds(start, size)], values_ref[0, i, t])
+        finish(span, diag[:, span] * x[:, span] + total)
 
 
 def residual_kernel(b_ref, x_ref, diag_ref, values_ref, cols_ref, cl_ref, cr_ref, rows_ref, pair_ref, other_ref,
                     r_ref, rb_ref, to_pair_ref, to_other_ref, xb_ref):
     x = x_ref[...]
     xb_ref[...] = x.astype(BF16)
-    even = is_even()
-    left = jnp.where(even, other_ref[...], pair_ref[...])
-    right = jnp.where(even, pair_ref[...], other_ref[...])
+    left, right = from_sides(pair_ref, other_ref)
 
     def finish(span, image):
-        r = b_ref[span, :] - image
-        r_ref[span, :] = r
-        rb_ref[span, :] = r.astype(BF16)
+        r = b_ref[:, span] - image
+        r_ref[:, span] = r
+        rb_ref[:, span] = r.astype(BF16)
 
     times_operator(x, xb_ref, left, right, diag_ref, values_ref, cols_ref, cl_ref, cr_ref, finish)
-    values = rb_ref[...]
-    row_left, row_right = rows_ref[0, 0:1, :], rows_ref[0, 1:2, :]
-    pair_rows = jnp.where(even, row_right, row_left)
-    other_rows = jnp.where(even, row_left, row_right)
-    to_pair_ref[...] = mm(pick_matrix(pair_rows, values.shape[0]), values).astype(BF16)
-    to_other_ref[...] = mm(pick_matrix(other_rows, values.shape[0]), values).astype(BF16)
+    margin = rows_ref.shape[2]
+    sent = mm(rb_ref[...], send_matrix(rows_ref, x.shape[1])).astype(BF16)
+    to_pair_ref[...] = sent[:, :margin]
+    to_other_ref[...] = sent[:, margin:]
 
 
 def local_kernel(inverse_ref, basis_ref, diag_ref, up_ref, rb_ref, pair_ref, other_ref, local_ref, message_ref):
-    even = is_even()
-    left = jnp.where(even, other_ref[...], pair_ref[...])
-    right = jnp.where(even, pair_ref[...], other_ref[...])
-    extended = jnp.concatenate([left, rb_ref[...], right], axis=0)
-    local_ref[...] = mm(inverse_ref[0], extended)
-    coarse_in = mm_t(basis_ref[0], extended)
+    left, right = from_sides(pair_ref, other_ref)
+    extended = jnp.concatenate([left, rb_ref[...], right], axis=1)
+    local_ref[...] = mm(extended, inverse_ref[0])
+    coarse_in = mm_nt(basis_ref[0], extended)
     last = position() == lax.axis_size("grp") * lax.axis_size("sub") - 1
     up = jnp.where(last, 0.0, up_ref[0])
     message = jnp.concatenate([diag_ref[0], jnp.transpose(up), up, coarse_in], axis=1)
@@ -108,14 +103,30 @@
 
 
 def reduce_rows(blocks):
-    size = blocks[0].shape[0]
+    size, width = blocks[0].shape
+    panel = 8 if len(blocks) <= 2 else 4
+    lanes = 128
     here = lax.broadcasted_iota(jnp.int32, (size, 1), 0)
-    for p in range(size):
-        done = []
-        for block in blocks:
-            row = block[p:p + 1, :] / block[p:p + 1, p:p + 1]
-            done.append(jnp.where(here == p, row, block - block[:, p:p + 1] * row))
-        blocks = done
+
+    def wide(value):
+        return jnp.concatenate([value] * (width // lanes), axis=1)
+
+    for first in range(0, size, panel):
+        panels = [
+            [jnp.broadcast_to(block[:, q:q + 1], (size, lanes)) for q in range(first, first + panel)] for block in blocks
+        ]
+        for a in range(panel):
+            p = first + a
+            done = []
+            for block, columns in zip(blocks, panels):
+                column = columns[a]
+                inverse = 1.0 / column[p:p + 1, :]
+                for b in range(a + 1, panel):
+                    entry = columns[b][p:p + 1, :] * inverse
+                    columns[b] = jnp.where(here == p, entry, columns[b] - column * entry)
+                row = block[p:p + 1, :] * wide(inverse)
+                done.append(jnp.where(here == p, row, block - wide(column) * row))
+            blocks = done
     return blocks
 
 
@@ -238,70 +249,69 @@
     odd = member // 2 * 2 + 1
     x_ref[odd] = back(solved_ref[odd], x_ref[odd - 1], x_ref[odd + 1], size)
     coarse = x_ref[member].astype(BF16)
-    correction = local_ref[...] + mm(basis_ref[0], coarse)
+    correction = local_ref[...] + mm_t(coarse, basis_ref[0])
     corr_ref[...] = correction
     margin = rows_ref.shape[2]
-    owned = correction.shape[0] - 2 * margin
+    owned = correction.shape[1] - 2 * margin
     rounded = correction.astype(BF16)
     even = is_even()
-    head, tail = rounded[:margin], rounded[margin + owned:]
-    values = rounded[margin:margin + owned]
-    row_left, row_right = rows_ref[0, 0:1, :], rows_ref[0, 1:2, :]
-    pair_rows = jnp.where(even, row_right, row_left)
-    other_rows = jnp.where(even, row_left, row_right)
-    to_pair_ref[:margin, :] = jnp.where(even, tail, head)
-    to_other_ref[:margin, :] = jnp.where(even, head, tail)
-    to_pair_ref[margin:, :] = mm(pick_matrix(pair_rows, owned), values).astype(BF16)
-    to_other_ref[margin:, :] = mm(pick_matrix(other_rows, owned), values).astype(BF16)
+    head, tail = rounded[:, :margin], rounded[:, margin + owned:]
+    sent = mm(rounded[:, margin:margin + owned], send_matrix(rows_ref, owned)).astype(BF16)
+    to_pair_ref[:, :margin] = jnp.where(even, tail, head)
+    to_other_ref[:, :margin] = jnp.where(even, head, tail)
+    to_pair_ref[:, margin:] = sent[:, :margin]
+    to_other_ref[:, margin:] = sent[:, margin:]
 
 
 def image_kernel(corr_ref, r_ref, diag_ref, values_ref, cols_ref, cl_ref, cr_ref, rows_ref, pair_ref, other_ref,
                  p_ref, image_ref, sums_ref, pb_ref):
     margin = rows_ref.shape[2]
-    owned = p_ref.shape[0]
-    even = is_even()
-    from_left = jnp.where(even, other_ref[...], pair_ref[...])
-    from_right = jnp.where(even, pair_ref[...], other_ref[...])
-    place = jnp.concatenate(
-        [place_matrix(rows_ref[0, 0:1, :], owned), place_matrix(rows_ref[0, 1:2, :], owned)], axis=1)
-    tails = jnp.concatenate([from_left[:margin], from_right[:margin]], axis=0)
-    p = corr_ref[margin:margin + owned, :] + mm(place, tails)
+    owned = p_ref.shape[1]
+    from_left, from_right = from_sides(pair_ref, other_ref)
+    place = place_matrix(jnp.concatenate([rows_ref[0, 0:1, :], rows_ref[0, 1:2, :]], axis=1), owned)
+    tails = jnp.concatenate([from_left[:, :margin], from_right[:, :margin]], axis=1)
+    p = corr_ref[:, margin:margin + owned] + mm_nt(tails, place)
     p_ref[...] = p
     pb_ref[...] = p.astype(BF16)
     me = position()
     last = lax.axis_size("grp") * lax.axis_size("sub") - 1
-    left = from_left[margin:].astype(F32) + corr_ref[:margin, :]
-    right = from_right[margin:].astype(F32) + corr_ref[margin + owned:, :]
+    left = from_left[:, margin:].astype(F32) + corr_ref[:, :margin]
+    right = from_right[:, margin:].astype(F32) + corr_ref[:, margin + owned:]
     left = jnp.where(me == 0, 0.0, left).astype(BF16)
     right = jnp.where(me == last, 0.0, right).astype(BF16)
 
     def finish(span, image):
-        image_ref[span, :] = image
+        image_ref[:, span] = image
 
     times_operator(p, pb_ref, left, right, diag_ref, values_ref, cols_ref, cl_ref, cr_ref, finish)
-    inner = jnp.sum(r_ref[...] * p, axis=0, keepdims=True)
-    curvature = jnp.sum(p * image_ref[...], axis=0, keepdims=True)
-    sums = jnp.concatenate([inner, curvature], axis=0)
+    ones = jnp.ones((8, owned), F32)
+    inner = mm_nt(ones, r_ref[...] * p, precision=lax.Precision.HIGHEST)
+    curvature = mm_nt(ones, p * image_ref[...], precision=lax.Precision.HIGHEST)
+    sums = jnp.concatenate([inner[0:1], curvature[0:1]], axis=0)
     for slot in range(sums_ref.shape[0]):
         sums_ref[slot] = sums
 
 
 def finish_kernel(x_ref, p_ref, r_ref, image_ref, sums_ref, out_x_ref, out_r_ref):
     sums = jnp.sum(sums_ref[...], axis=0)
-    step = sums[0:1, :] / sums[1:2, :]
-    out_x_ref[...] = x_ref[...] + step * p_ref[...]
-    out_r_ref[...] = r_ref[...] - step * image_ref[...]
+    row = sums[0:1, :] / sums[1:2, :]
+    lanes = 128
+    step = jnp.transpose(jnp.broadcast_to(row, (lanes, row.shape[1])))
+    for start in range(0, x_ref.shape[1], lanes):
+        span = slice(start, start + lanes)
+        out_x_ref[:, span] = x_ref[:, span] + step * p_ref[:, span]
+        out_r_ref[:, span] = r_ref[:, span] - step * image_ref[:, span]
 
 
 def call(kernel, out, in_specs, scratch=()):
-    many = isinstance(out, (list, tuple))
     return pl.pallas_call(
         kernel,
         out_shape=out,
         in_specs=in_specs,
-        out_specs=[VMEM] * len(out) if many else VMEM,
+        out_specs=[VMEM] * len(out),
         scratch_shapes=list(scratch),
         name=kernel.__name__,
+        compiler_params=pltpu.CompilerParams(vmem_limit_bytes=16 * 2**20),
     )
 
 
@@ -320,27 +330,29 @@
     width = 3 * modes + cases
     pairs = [(i, i ^ 1) for i in range(total)]
     others = [(i, i + 1 if i % 2 else i - 1) for i in range(1, total - 1)]
-    diag = diagonal.reshape(1, rows)
+    right_side, iterate_in = right_side.T, iterate_in.T
+    basis = jnp.swapaxes(coarse_basis, 1, 2)
+    block_cols = jnp.transpose(block_cols, (2, 0, 1))
 
     def swap(to_pair, to_other):
         return lax.ppermute(to_pair, AXES, pairs), lax.ppermute(to_other, AXES, others)
 
-    halo = struct((margin, cases), BF16)
-    full = struct((rows, cases), F32)
-    operator = (diag, block_values, block_cols, couple_left, couple_right, send_rows)
+    halo = struct((cases, margin), BF16)
+    full = struct((cases, rows), F32)
+    operator = (diagonal, block_values, block_cols, couple_left, couple_right, send_rows)
     operator_specs = [VMEM, VMEM, SMEM, VMEM, VMEM, VMEM]
     sent = call(gather_kernel, [halo, halo], [VMEM] * 2)(iterate_in, send_rows)
     got = swap(*sent)
     residual, rounded, *sent = call(
         residual_kernel,
-        [full, struct((rows, cases), BF16), halo, halo],
+        [full, struct((cases, rows), BF16), halo, halo],
         [VMEM, VMEM] + operator_specs + [VMEM, VMEM],
-        [pltpu.VMEM((rows, cases), BF16)],
+        [pltpu.VMEM((cases, rows), BF16)],
     )(right_side, iterate_in, *operator, *got)
     got = swap(*sent)
     local, message = call(
-        local_kernel, [struct((extended, cases), F32), struct((members, modes, width), F32)], [VMEM] * 7
-    )(local_inverse, coarse_basis, coarse_diag, coarse_up, rounded, *got)
+        local_kernel, [struct((cases, extended), F32), struct((members, modes, width), F32)], [VMEM] * 7
+    )(local_inverse, basis, coarse_diag, coarse_up, rounded, *got)
     gathered = lax.all_to_all(message, "sub", 0, 0, tiled=True)
     solved, reduced = call(
         group_kernel, [struct((members, modes, width), F32), struct((2 * modes, width), F32)], [VMEM]
@@ -348,25 +360,24 @@
     reduced = lax.all_gather(reduced, "grp", axis=0)
     correction, *sent = call(
         solve_kernel,
-        [struct((extended, cases), F32)] + [struct((2 * margin, cases), BF16)] * 2,
+        [struct((cases, extended), F32)] + [struct((cases, 2 * margin), BF16)] * 2,
         [VMEM] * 5,
         [
             pltpu.VMEM((groups + 1, modes, cases), F32),
             pltpu.VMEM((members + 1, modes, cases), F32),
             pltpu.VMEM((8, 128), F32),
         ],
-    )(reduced, solved, local, coarse_basis, send_rows)
+    )(reduced, solved, local, basis, send_rows)
     got = swap(*sent)
     direction, image, sums = call(
         image_kernel,
         [full, full, struct((total, 2, cases), F32)],
         [VMEM, VMEM] + operator_specs + [VMEM, VMEM],
-        [pltpu.VMEM((rows, cases), BF16)],
+        [pltpu.VMEM((cases, rows), BF16)],
     )(correction, residual, *operator, *got)
     sums = lax.all_to_all(sums, AXES, 0, 0, tiled=True)
-    return tuple(
-        call(finish_kernel, [full, full], [VMEM] * 5)(iterate_in, direction, residual, image, sums)
-    )
+    iterate, residual = call(finish_kernel, [full, full], [VMEM] * 5)(iterate_in, direction, residual, image, sums)
+    return iterate.T, residual.T
 
 
 def solution(mesh):

time: 117 us -> 87.3 us (0.75)
  Pallas kernels: 41.4 us -> 16.6 us
  local copies, waits for them, and re-layouts: 13.7 us -> 8.65 us
  starting transfers between devices: 6.51 us -> 8.06 us
    pallas_call x3, Pallas kernels: 20.7 us -> 7.67 us  [the longest x1 5.51 us: shards(): call(solve_kernel, [struct((cases, extended), F32)] + [struct((cases, 2 *...]
    pallas_call x1, Pallas kernels: 11.5 us -> 5.16 us  [shards(): call(group_kernel, [struct((members, modes, width), F32), struct((2 * mod...]
    pallas_call x2 -> x0, local copies, waits for them, and re-layouts: 4.31 us -> none  [shards(): call(finish_kernel, [full, full], [VMEM] * 5)]
    all_to_all x1, blocking collectives: 18.6 us -> 16.2 us  [shards(): sums = lax.all_to_all(sums, AXES, 0, 0, tiled=True)]
    all_to_all x1, blocking collectives: 22.1 us -> 24.4 us  [shards(): gathered = lax.all_to_all(message, 'sub', 0, 0, tiled=True)]
    pallas_call x1, Pallas kernels: 3.14 us -> 1.14 us  [shards(): call(finish_kernel, [full, full], [VMEM] * 5)]
    pallas_call x1, Pallas kernels: 2.13 us -> 0.25 us  [shards(): sent = call(gather_kernel, [halo, halo], [VMEM] * 2)(iterate_in, send_rows)]
    ppermute x3, starting transfers between devices: 4.55 us -> 6.09 us  [swap(): lax.ppermute(to_pair, AXES, pairs)]
  transfers between devices with their start and end apart: 6 -> 6, of which waited for: 1 -> 3; matrix products, arithmetic and copies ran while one was open for 4% -> 0% of each run, Pallas kernels for 0% -> 0%
where the time goes in v2:
time: 87.3 us; the launch traced here: 86.7 us
  blocking collectives  51.6 us (59%)
  Pallas kernels  16.6 us (19%)
  local copies, waits for them, and re-layouts  8.65 us (10%)
  starting transfers between devices  8.06 us (9%)
  waiting for transfers between devices  1.02 us (1%)
    all_to_all x1, blocking collectives, shards(): gathered = lax.all_to_all(message, 'sub', 0, 0, tiled=True)  24.4 us
    all_to_all x1, blocking collectives, shards(): sums = lax.all_to_all(sums, AXES, 0, 0, tiled=True)  16.2 us
    all_gather x1, blocking collectives, shards(): reduced = lax.all_gather(reduced, 'grp', axis=0)  11.1 us
    unnamed x38, local copies, waits for them, and re-layouts  8.65 us
    ppermute x3, starting transfers between devices, swap(): lax.ppermute(to_pair, AXES, pairs)  6.09 us
    pallas_call x1, Pallas kernels, shards(): call(solve_kernel, [struct((cases, extended), F32)] + [struct((cases, 2 *...  5.51 us
    pallas_call x1, Pallas kernels, shards(): call(group_kernel, [struct((members, modes, width), F32), struct((2 * mod...  5.16 us
    pallas_call x1, Pallas kernels, shards(): call(image_kernel, [full, full, struct((total, 2, cases), F32)], [VMEM, V...  2.35 us
  transfers between devices with their start and end apart: 6, of which 3 were waited for; matrix products, arithmetic and copies ran while one was open for 0% of the time, Pallas kernels for 0%

profile of v2, /device:TPU:0, one launch (start us, length us, event | category | flops | bytes accessed | tf_op | source)
XLA Modules:
  0.0 86.7 jit_solution(1078164731852373451)
XLA Ops:
  0.6 0.0 copy-start
  0.6 1.0 %copy-done = f32[768,160]{0,1:T(8,128)S(1)} copy-done((f32[768,160]{0,1:T(8,128)S(1)}, f32[768,160]{0,1:T(8,128)}, u32[]{:S(2)}) %copy-start) | copy-done | bytes 491544
  1.7 0.0 copy-start.15
  1.7 0.7 copy-done.15
  2.3 0.0 copy-start.10
  2.3 0.0 copy-start.11
  2.3 0.0 copy-start.12
  2.3 0.2 gather_kernel.1
  2.6 0.6 collective-permute-start
  3.2 0.7 collective-permute-start.1
  3.8 0.2 collective-permute-done.pair_ref
  4.0 0.0 collective-permute-done.1.other_ref
  4.0 0.0 copy-start.2
  4.0 1.1 %copy-done.2 = bf16[1,6,3,128,128]{4,3,2,1,0:T(8,128)(2,1)S(1)} copy-done((bf16[1,6,3,128,128]{4,3,2,1,0:T(8,128)(2,1)S(1)}, bf16[1,6,3,128,128]{4,3,2,1,0:T(8,128)(2,1)}, u32[]{:S(2)}) %copy-start.2) | copy-done | bytes 589848
  5.1 0.0 copy-start.5
  5.1 0.9 %copy-done.5 = bf16[768,128]{1,0:T(8,128)(2,1)S(1)} copy-done((bf16[768,128]{1,0:T(8,128)(2,1)S(1)}, bf16[768,128]{1,0:T(8,128)(2,1)}, u32[]{:S(2)}) %copy-start.5) | copy-done | bytes 196632
  6.0 0.0 copy-start.7
  6.0 0.9 %copy-done.7 = bf16[768,128]{1,0:T(8,128)(2,1)S(1)} copy-done((bf16[768,128]{1,0:T(8,128)(2,1)S(1)}, bf16[768,128]{1,0:T(8,128)(2,1)}, u32[]{:S(2)}) %copy-start.7) | copy-done | bytes 196632
  7.0 0.0 copy-start.9
  7.0 1.0 %copy-done.9 = f32[768,160]{0,1:T(8,128)S(1)} copy-done((f32[768,160]{0,1:T(8,128)S(1)}, f32[768,160]{0,1:T(8,128)}, u32[]{:S(2)}) %copy-start.9) | copy-done | bytes 491544
  8.0 0.0 copy-start.13
  8.0 0.7 copy-done.13
  8.7 0.0 copy-start.17
  8.7 0.7 copy-done.17
  9.4 1.5 %residual_kernel.1 = (f32[160,768]{1,0:T(8,128)S(1)}, bf16[160,768]{1,0:T(8,128)(2,1)S(1)}, bf16[160,128]{1,0:T(8,128)(2,1)S(1)}, bf16[160,128]{1,0:T(8,128)(2,1)S(1)}) custom-call(f32[160,768]{1,0:T(8,128)S(1)} %bitcast.11, f32[160,768]{1,0:T(8,128)S(1)} %bitcast.8, f32[768]{0:T(1024)S(1)} %copy-done.13, bf16[1,6,3,128,128]{4,3,2,1,0:T(8,128)(2,1)S(1)} %copy-done.2, ...), custom_call_target="tpu_custom_call" | custom-call | tf_op jit(solution)/shard_map/residual_kernel/pallas_call | solution.py:346
  10.9 0.0 copy-start.16
  10.9 5.5 %collective-permute-start.2 = (bf16[160,128]{1,0:T(8,128)(2,1)S(1)}, bf16[160,128]{1,0:T(8,128)(2,1)S(1)}, u32[]{:S(2)}, u32[]{:S(2)}) collective-permute-start(bf16[160,128]{1,0:T(8,128)(2,1)S(1)} %get-tuple-element.23), channel_id=1, source_target_pairs={{0,1},{1,0},{2,3},{3,2},{4,5},{5,4},{6,7},{7,6},{8,9},{9,8},{10,11... | collective-permute-start | bytes 122888 | tf_op jit(solution)/shard_map/ppermute | solution.py:338
  16.4 0.7 collective-permute-start.3
  17.0 0.2 collective-permute-done.2.pair_ref
  17.2 0.0 collective-permute-done.3.other_ref
  17.2 0.0 copy-done.10
  17.2 0.0 copy-done.11
  17.2 0.0 copy-done.12
  17.2 0.0 copy-start.4
  17.2 1.6 %copy-done.4 = bf16[1,1024,1024]{2,1,0:T(8,128)(2,1)S(1)} copy-done((bf16[1,1024,1024]{2,1,0:T(8,128)(2,1)S(1)}, bf16[1,1024,1024]{2,1,0:T(8,128)(2,1)}, u32[]{:S(2)}) %copy-start.4) | copy-done | bytes 2097176
  18.8 0.0 copy-start.3
  18.8 0.0 copy-start.6
  18.8 0.0 copy-start.8
  18.8 0.0 copy-start.14
  18.8 0.0 copy-start.18
  18.9 0.6 local_kernel.1
  19.5 24.4 %all_to_all.10.gathered_ref = f32[8,32,256]{2,1,0:T(8,128)S(1)} all-to-all(f32[8,32,256]{2,1,0:T(8,128)S(1)} %get-tuple-element.25), channel_id=1, replica_groups=mesh['grp'=4,'sub'=8] {'sub'}, dimensions={0} | all-to-all | bytes 524288 | tf_op jit(solution)/shard_map/all_to_all | solution.py:356
  43.9 0.0 copy-start.1
  43.9 5.2 %group_kernel.1 = (f32[8,32,256]{2,1,0:T(8,128)S(1)}, f32[64,256]{1,0:T(8,128)S(1)}) custom-call(f32[8,32,256]{2,1,0:T(8,128)S(1)} %all_to_all.10.gathered_ref), custom_call_target="tpu_custom_call" | custom-call | tf_op jit(solution)/shard_map/group_kernel/pallas_call | solution.py:357
  49.0 11.1 %all-gather = f32[256,256]{1,0:T(8,128)S(1)} all-gather(f32[64,256]{1,0:T(8,128)S(1)} %get-tuple-element.26), channel_id=2, replica_groups=mesh['grp'=4,'sub'=8] {'grp'}, dimensions={0}, use_global_device_ids=true | all-gather | bytes 327680 | tf_op jit(solution)/shard_map/all_gather | solution.py:360
  60.1 0.0 copy-done.16
  60.1 5.5 %solve_kernel.1 = (f32[160,1024]{1,0:T(8,128)S(1)}, bf16[160,256]{1,0:T(8,128)(2,1)S(1)}, bf16[160,256]{1,0:T(8,128)(2,1)S(1)}) custom-call(f32[4,64,256]{2,1,0:T(8,128)S(1)} %bitcast.10, f32[8,32,256]{2,1,0:T(8,128)S(1)} %get-tuple-element.27.solved_ref, f32[160,1024]{1,0:T(8,128)S(1)} %get-tuple-element.28.local_ref, bf16[1,32,1024]{2,1,0:T(8,128)(2,1)S(1)} %bitcast.13, ...), custom_call_target="tpu_custom_call" | custom-call | tf_op jit(solution)/shard_map/solve_kernel/pallas_call | solution.py:361
  65.6 0.1 collective-permute-start.4
  65.7 0.7 collective-permute-start.5
  66.4 0.6 collective-permute-done.4.pair_ref
  67.0 0.0 collective-permute-done.5.other_ref
  67.0 0.0 copy-done.3
  67.0 0.0 copy-done.6
  67.0 0.0 copy-done.8
  67.0 0.0 copy-done.14
  67.0 0.0 copy-done.18
  67.0 2.4 %image_kernel.1 = (f32[160,768]{1,0:T(8,128)S(1)}, f32[160,768]{1,0:T(8,128)S(1)}, f32[32,2,160]{2,1,0:T(2,128)S(1)}) custom-call(f32[160,1024]{1,0:T(8,128)S(1)} %get-tuple-element.29.corr_ref, f32[160,768]{1,0:T(8,128)S(1)} %get-tuple-element.30.r_ref, f32[768]{0:T(1024)S(1)} %copy-done.14, bf16[1,6,3,128,128]{4,3,2,1,0:T(8,128)(2,1)S(1)} %copy-done.3, ...), custom_call_target="tpu_custom_call" | custom-call | tf_op jit(solution)/shard_map/image_kernel/pallas_call | solution.py:372
  69.4 16.2 %all_to_all.11.sums_ref = f32[32,2,160]{2,1,0:T(2,128)S(1)} all-to-all(f32[32,2,160]{2,1,0:T(2,128)S(1)} %get-tuple-element.35), channel_id=1, replica_groups=mesh['grp'=4,'sub'=8] {'grp','sub'}, dimensions={0} | all-to-all | bytes 81920 | tf_op jit(solution)/shard_map/all_to_all | solution.py:378
  85.6 0.0 copy-done.1
  85.6 1.1 %finish_kernel.1 = (f32[160,768]{1,0:T(8,128)}, f32[160,768]{1,0:T(8,128)}) custom-call(f32[160,768]{1,0:T(8,128)S(1)} %bitcast.9, f32[160,768]{1,0:T(8,128)S(1)} %get-tuple-element.33.p_ref, f32[160,768]{1,0:T(8,128)S(1)} %get-tuple-element.30.r_ref, f32[160,768]{1,0:T(8,128)S(1)} %get-tuple-element.34.image_ref, f32[32,2,160]{2,1,0:T(2,128)S(1)} %all_to_all.11.sums_ref), custom_call_target="tpu_custom_call" | custom-call | tf_op jit(solution)/shard_map/finish_kernel/pallas_call | solution.py:379
Async XLA Ops:
  0.6 1.0 %copy-start = (f32[768,160]{0,1:T(8,128)S(1)}, f32[768,160]{0,1:T(8,128)}, u32[]{:S(2)}) copy-start(f32[768,160]{0,1:T(8,128)} %param.13) | copy-start | bytes 1474564
  1.7 0.7 copy-start.15
  2.3 14.9 %copy-start.10 = (bf16[1,1024,32]{1,2,0:T(8,128)(2,1)S(1)}, bf16[1,1024,32]{1,2,0:T(8,128)(2,1)}, u32[]{:S(2)}) copy-start(bf16[1,1024,32]{1,2,0:T(8,128)(2,1)} %param.21) | copy-start | bytes 196612
  2.3 14.9 %copy-start.11 = (f32[1,32,32]{2,1,0:T(8,128)S(1)}, f32[1,32,32]{2,1,0:T(8,128)}, u32[]{:S(2)}) copy-start(f32[1,32,32]{2,1,0:T(8,128)} %diag_ref.4) | copy-start | bytes 12292
  2.3 14.9 %copy-start.12 = (f32[1,32,32]{2,1,0:T(8,128)S(1)}, f32[1,32,32]{2,1,0:T(8,128)}, u32[]{:S(2)}) copy-start(f32[1,32,32]{2,1,0:T(8,128)} %up_ref.1) | copy-start | bytes 12292
  2.6 1.4 %collective-permute-start = (bf16[160,128]{1,0:T(8,128)(2,1)S(1)}, bf16[160,128]{1,0:T(8,128)(2,1)S(1)}, u32[]{:S(2)}, u32[]{:S(2)}) collective-permute-start(bf16[160,128]{1,0:T(8,128)(2,1)S(1)} %get-tuple-element.20), channel_id=1, source_target_pairs={{0,1},{1,0},{2,3},{3,2},{4,5},{5,4},{6,7},{7,6},{8,9},{9,8},{10,11... | collective-permute-start | bytes 122888 | tf_op jit(solution)/shard_map/ppermute | solution.py:338
  3.2 0.9 %collective-permute-start.1 = (bf16[160,128]{1,0:T(8,128)(2,1)S(1)}, bf16[160,128]{1,0:T(8,128)(2,1)S(1)}, u32[]{:S(2)}, u32[]{:S(2)}) collective-permute-start(bf16[160,128]{1,0:T(8,128)(2,1)S(1)} %get-tuple-element.21), channel_id=1, source_target_pairs={{1,2},{2,1},{3,4},{4,3},{5,6},{6,5},{7,8},{8,7},{9,10},{10,9},{11,... | collective-permute-start | bytes 122888 | tf_op jit(solution)/shard_map/ppermute | solution.py:338
  4.0 1.1 %copy-start.2 = (bf16[1,6,3,128,128]{4,3,2,1,0:T(8,128)(2,1)S(1)}, bf16[1,6,3,128,128]{4,3,2,1,0:T(8,128)(2,1)}, u32[]{:S(2)}) copy-start(bf16[1,6,3,128,128]{4,3,2,1,0:T(8,128)(2,1)} %values_ref.3) | copy-start | bytes 1769476
  5.1 0.9 %copy-start.5 = (bf16[768,128]{1,0:T(8,128)(2,1)S(1)}, bf16[768,128]{1,0:T(8,128)(2,1)}, u32[]{:S(2)}) copy-start(bf16[768,128]{1,0:T(8,128)(2,1)} %cl_ref.3) | copy-start | bytes 589828
  6.0 0.9 %copy-start.7 = (bf16[768,128]{1,0:T(8,128)(2,1)S(1)}, bf16[768,128]{1,0:T(8,128)(2,1)}, u32[]{:S(2)}) copy-start(bf16[768,128]{1,0:T(8,128)(2,1)} %cr_ref.3) | copy-start | bytes 589828
  7.0 1.0 %copy-start.9 = (f32[768,160]{0,1:T(8,128)S(1)}, f32[768,160]{0,1:T(8,128)}, u32[]{:S(2)}) copy-start(f32[768,160]{0,1:T(8,128)} %param.12) | copy-start | bytes 1474564
  8.0 0.7 copy-start.13
  8.7 0.7 copy-start.17
  10.9 49.2 %copy-start.16 = (s32[1,2,128]{2,1,0:T(2,128)S(1)}, s32[1,2,128]{2,1,0:T(2,128)}, u32[]{:S(2)}) copy-start(s32[1,2,128]{2,1,0:T(2,128)} %rows_ref.7) | copy-start | bytes 3076
  10.9 6.3 %collective-permute-start.2 = (bf16[160,128]{1,0:T(8,128)(2,1)S(1)}, bf16[160,128]{1,0:T(8,128)(2,1)S(1)}, u32[]{:S(2)}, u32[]{:S(2)}) collective-permute-start(bf16[160,128]{1,0:T(8,128)(2,1)S(1)} %get-tuple-element.23), channel_id=1, source_target_pairs={{0,1},{1,0},{2,3},{3,2},{4,5},{5,4},{6,7},{7,6},{8,9},{9,8},{10,11... | collective-permute-start | bytes 122888 | tf_op jit(solution)/shard_map/ppermute | solution.py:338
  16.4 0.9 %collective-permute-start.3 = (bf16[160,128]{1,0:T(8,128)(2,1)S(1)}, bf16[160,128]{1,0:T(8,128)(2,1)S(1)}, u32[]{:S(2)}, u32[]{:S(2)}) collective-permute-start(bf16[160,128]{1,0:T(8,128)(2,1)S(1)} %get-tuple-element.24), channel_id=1, source_target_pairs={{1,2},{2,1},{3,4},{4,3},{5,6},{6,5},{7,8},{8,7},{9,10},{10,9},{11,... | collective-permute-start | bytes 122888 | tf_op jit(solution)/shard_map/ppermute | solution.py:338
  17.2 1.6 %copy-start.4 = (bf16[1,1024,1024]{2,1,0:T(8,128)(2,1)S(1)}, bf16[1,1024,1024]{2,1,0:T(8,128)(2,1)}, u32[]{:S(2)}) copy-start(bf16[1,1024,1024]{2,1,0:T(8,128)(2,1)} %inverse_ref.1) | copy-start | bytes 6291460
  18.8 48.2 %copy-start.3 = (bf16[1,6,3,128,128]{4,3,2,1,0:T(8,128)(2,1)S(1)}, bf16[1,6,3,128,128]{4,3,2,1,0:T(8,128)(2,1)}, u32[]{:S(2)}) copy-start(bf16[1,6,3,128,128]{4,3,2,1,0:T(8,128)(2,1)} %values_ref.3) | copy-start | bytes 1769476
  18.8 48.2 %copy-start.6 = (bf16[768,128]{1,0:T(8,128)(2,1)S(1)}, bf16[768,128]{1,0:T(8,128)(2,1)}, u32[]{:S(2)}) copy-start(bf16[768,128]{1,0:T(8,128)(2,1)} %cl_ref.3) | copy-start | bytes 589828
  18.8 48.2 %copy-start.8 = (bf16[768,128]{1,0:T(8,128)(2,1)S(1)}, bf16[768,128]{1,0:T(8,128)(2,1)}, u32[]{:S(2)}) copy-start(bf16[768,128]{1,0:T(8,128)(2,1)} %cr_ref.3) | copy-start | bytes 589828
  18.8 48.2 %copy-start.14 = (f32[768]{0:T(1024)S(1)}, f32[768]{0:T(1024)}, u32[]{:S(2)}) copy-start(f32[768]{0:T(1024)} %diag_ref.5) | copy-start | bytes 9220
  18.8 48.2 %copy-start.18 = (s32[1,6,3]{1,0,2:T(1,128)S(1)}, s32[1,6,3]{1,0,2:T(1,128)}, u32[]{:S(2)}) copy-start(s32[1,6,3]{1,0,2:T(1,128)} %param.16) | copy-start | bytes 220
  43.9 41.7 %copy-start.1 = (f32[768,160]{0,1:T(8,128)S(1)}, f32[768,160]{0,1:T(8,128)}, u32[]{:S(2)}) copy-start(f32[768,160]{0,1:T(8,128)} %param.13) | copy-start | bytes 1474564
  65.6 1.3 %collective-permute-start.4 = (bf16[160,256]{1,0:T(8,128)(2,1)S(1)}, bf16[160,256]{1,0:T(8,128)(2,1)S(1)}, u32[]{:S(2)}, u32[]{:S(2)}) collective-permute-start(bf16[160,256]{1,0:T(8,128)(2,1)S(1)} %get-tuple-element.31), channel_id=1, source_target_pairs={{0,1},{1,0},{2,3},{3,2},{4,5},{5,4},{6,7},{7,6},{8,9},{9,8},{10,11... | collective-permute-start | bytes 245768 | tf_op jit(solution)/shard_map/ppermute | solution.py:338
  65.7 1.3 %collective-permute-start.5 = (bf16[160,256]{1,0:T(8,128)(2,1)S(1)}, bf16[160,256]{1,0:T(8,128)(2,1)S(1)}, u32[]{:S(2)}, u32[]{:S(2)}) collective-permute-start(bf16[160,256]{1,0:T(8,128)(2,1)S(1)} %get-tuple-element.32), channel_id=1, source_target_pairs={{1,2},{2,1},{3,4},{4,3},{5,6},{6,5},{7,8},{8,7},{9,10},{10,9},{11,... | collective-permute-start | bytes 245768 | tf_op jit(solution)/shard_map/ppermute | solution.py:338

commit v3 on v2

--- a/solution.py
+++ b/solution.py
@@ -11,7 +11,7 @@
 BF16 = jnp.bfloat16
 F32 = jnp.float32
 VMEM = pl.BlockSpec(memory_space=pltpu.VMEM)
-SMEM = pl.BlockSpec(memory_space=pltpu.SMEM)
+HBM = pl.BlockSpec(memory_space=pltpu.HBM)
 
 
 def mm(a, b):
@@ -52,7 +52,16 @@
     return jnp.where(even, other, pair), jnp.where(even, pair, other)
 
 
-def gather_kernel(x_ref, rows_ref, to_pair_ref, to_other_ref):
+def copy_all(copies, sems):
+    started = [pltpu.make_async_copy(source, target, sems.at[n]) for n, (source, target) in enumerate(copies)]
+    for copy in started:
+        copy.start()
+    return started
+
+
+def gather_kernel(x_hbm, rows_hbm, to_pair_ref, to_other_ref, x_ref, rows_ref, sems):
+    for copy in copy_all([(rows_hbm, rows_ref), (x_hbm, x_ref)], sems):
+        copy.wait()
     values = x_ref[...].astype(BF16)
     margin = rows_ref.shape[2]
     sent = mm(values, send_matrix(rows_ref, values.shape[1])).astype(BF16)
@@ -60,46 +69,86 @@
     to_other_ref[...] = sent[:, margin:]
 
 
-def times_operator(x, rounded_ref, left, right, diag_ref, values_ref, cols_ref, cl_ref, cr_ref, finish):
-    blocks, nonzeros, size = values_ref.shape[1], values_ref.shape[2], values_ref.shape[3]
-    diag = diag_ref[...].reshape(1, x.shape[1])
+def own_kernel(x_ref, b_hbm, diag_hbm, values_hbm, cols_hbm, cl_hbm, cr_hbm,
+               partial_ref, operator_ref, diag_ref, cols_ref, b_ref, sems):
+    blocks, nonzeros, size = values_hbm.shape[1], values_hbm.shape[2], values_hbm.shape[3]
+    rows = x_ref.shape[1]
+    margin = cl_hbm.shape[1]
+    first = copy_all(
+        [
+            (cols_hbm, cols_ref),
+            (diag_hbm, diag_ref),
+            (b_hbm, b_ref),
+            (cl_hbm, operator_ref.at[:, rows:rows + margin]),
+            (cr_hbm, operator_ref.at[:, rows + margin:]),
+        ],
+        sems,
+    )
+    operator_ref[:, :rows] = jnp.zeros((rows, rows), BF16)
+    first[0].wait()
+    placed = []
     for i in range(blocks):
-        span = slice(i * size, (i + 1) * size)
-        total = mm_nt(left, cl_ref[span, :]) + mm_nt(right, cr_ref[span, :])
         for t in range(nonzeros):
             start = pl.multiple_of(cols_ref[t, 0, i] * size, size)
-            total = total + mm_nt(rounded_ref[:, pl.ds(start, size)], values_ref[0, i, t])
-        finish(span, diag[:, span] * x[:, span] + total)
-
-
-def residual_kernel(b_ref, x_ref, diag_ref, values_ref, cols_ref, cl_ref, cr_ref, rows_ref, pair_ref, other_ref,
-                    r_ref, rb_ref, to_pair_ref, to_other_ref, xb_ref):
+            target = operator_ref.at[i * size:(i + 1) * size, pl.ds(start, size)]
+            copy = pltpu.make_async_copy(values_hbm.at[0, i, t], target, sems.at[len(first) + i * nonzeros + t])
+            copy.start()
+            placed.append(copy)
+    for copy in first[1:] + placed:
+        copy.wait()
     x = x_ref[...]
-    xb_ref[...] = x.astype(BF16)
-    left, right = from_sides(pair_ref, other_ref)
-
-    def finish(span, image):
-        r = b_ref[:, span] - image
-        r_ref[:, span] = r
-        rb_ref[:, span] = r.astype(BF16)
-
-    times_operator(x, xb_ref, left, right, diag_ref, values_ref, cols_ref, cl_ref, cr_ref, finish)
+    diag = diag_ref[...].reshape(1, rows)
+    partial_ref[...] = b_ref[...] - diag * x - mm_nt(x.astype(BF16), operator_ref[:, :rows])
+
+
+def residual_kernel(partial_ref, operator_ref, rows_ref, pair_ref, other_ref, r_ref, rb_ref, to_pair_ref, to_other_ref):
+    rows = partial_ref.shape[1]
     margin = rows_ref.shape[2]
-    sent = mm(rb_ref[...], send_matrix(rows_ref, x.shape[1])).astype(BF16)
+    halo = jnp.concatenate(from_sides(pair_ref, other_ref), axis=1)
+    r = partial_ref[...] - mm_nt(halo, operator_ref[:, rows:])
+    r_ref[...] = r
+    rounded = r.astype(BF16)
+    rb_ref[...] = rounded
+    sent = mm(rounded, send_matrix(rows_ref, rows)).astype(BF16)
     to_pair_ref[...] = sent[:, :margin]
     to_other_ref[...] = sent[:, margin:]
 
 
-def local_kernel(inverse_ref, basis_ref, diag_ref, up_ref, rb_ref, pair_ref, other_ref, local_ref, message_ref):
-    left, right = from_sides(pair_ref, other_ref)
-    extended = jnp.concatenate([left, rb_ref[...], right], axis=1)
-    local_ref[...] = mm(extended, inverse_ref[0])
-    coarse_in = mm_nt(basis_ref[0], extended)
+def inverse_kernel(rb_ref, inverse_hbm, basis_hbm, diag_hbm, up_hbm, local_ref, coarse_ref, ends_ref, basis_ref, blocks_ref,
+                   own_ref, sems):
+    rows = rb_ref.shape[1]
+    total = inverse_hbm.shape[1]
+    margin = (total - rows) // 2
+    copies = copy_all(
+        [
+            (basis_hbm, basis_ref),
+            (diag_hbm, blocks_ref.at[0:1]),
+            (up_hbm, blocks_ref.at[1:2]),
+            (inverse_hbm.at[0, margin:margin + rows], own_ref),
+            (inverse_hbm.at[0, :margin], ends_ref.at[:margin]),
+            (inverse_hbm.at[0, margin + rows:], ends_ref.at[margin:]),
+        ],
+        sems,
+    )
+    for copy in copies:
+        copy.wait()
+    rounded = rb_ref[...]
+    local_ref[...] = mm(rounded, own_ref[...])
+    coarse_ref[...] = mm_nt(basis_ref[0, :, margin:margin + rows], rounded)
+
+
+def local_kernel(own_local_ref, own_coarse_ref, ends_ref, basis_ref, blocks_ref, pair_ref, other_ref,
+                 local_ref, message_ref):
+    margin = pair_ref.shape[1]
+    halo = jnp.concatenate(from_sides(pair_ref, other_ref), axis=1)
+    ends = jnp.concatenate([basis_ref[0, :, :margin], basis_ref[0, :, basis_ref.shape[2] - margin:]], axis=1)
+    coarse_in = own_coarse_ref[...] + mm_nt(ends, halo)
     last = position() == lax.axis_size("grp") * lax.axis_size("sub") - 1
-    up = jnp.where(last, 0.0, up_ref[0])
-    message = jnp.concatenate([diag_ref[0], jnp.transpose(up), up, coarse_in], axis=1)
+    up = jnp.where(last, 0.0, blocks_ref[1])
+    message = jnp.concatenate([blocks_ref[0], jnp.transpose(up), up, coarse_in], axis=1)
     for slot in range(message_ref.shape[0]):
         message_ref[slot] = message
+    local_ref[...] = own_local_ref[...] + mm(halo, ends_ref[...])
 
 
 def reduce_rows(blocks):
@@ -210,7 +259,7 @@
 
 
 def solve_kernel(reduced_ref, solved_ref, local_ref, basis_ref, rows_ref,
-                 corr_ref, to_pair_ref, to_other_ref, sep_ref, x_ref, own_ref):
+                 corr_ref, to_pair_ref, to_other_ref, sep_ref, x_ref):
     groups, two_size, width = reduced_ref.shape
     size = two_size // 2
     members = solved_ref.shape[0]
@@ -263,8 +312,7 @@
     to_other_ref[:, margin:] = sent[:, margin:]
 
 
-def image_kernel(corr_ref, r_ref, diag_ref, values_ref, cols_ref, cl_ref, cr_ref, rows_ref, pair_ref, other_ref,
-                 p_ref, image_ref, sums_ref, pb_ref):
+def image_kernel(corr_ref, r_ref, diag_ref, operator_ref, rows_ref, pair_ref, other_ref, p_ref, image_ref, sums_ref):
     margin = rows_ref.shape[2]
     owned = p_ref.shape[1]
     from_left, from_right = from_sides(pair_ref, other_ref)
@@ -272,21 +320,18 @@
     tails = jnp.concatenate([from_left[:, :margin], from_right[:, :margin]], axis=1)
     p = corr_ref[:, margin:margin + owned] + mm_nt(tails, place)
     p_ref[...] = p
-    pb_ref[...] = p.astype(BF16)
     me = position()
     last = lax.axis_size("grp") * lax.axis_size("sub") - 1
     left = from_left[:, margin:].astype(F32) + corr_ref[:, :margin]
     right = from_right[:, margin:].astype(F32) + corr_ref[:, margin + owned:]
     left = jnp.where(me == 0, 0.0, left).astype(BF16)
     right = jnp.where(me == last, 0.0, right).astype(BF16)
-
-    def finish(span, image):
-        image_ref[:, span] = image
-
-    times_operator(p, pb_ref, left, right, diag_ref, values_ref, cols_ref, cl_ref, cr_ref, finish)
+    values = jnp.concatenate([p.astype(BF16), left, right], axis=1)
+    image = diag_ref[...].reshape(1, owned) * p + mm_nt(values, operator_ref[...])
+    image_ref[...] = image
     ones = jnp.ones((8, owned), F32)
     inner = mm_nt(ones, r_ref[...] * p, precision=lax.Precision.HIGHEST)
-    curvature = mm_nt(ones, p * image_ref[...], precision=lax.Precision.HIGHEST)
+    curvature = mm_nt(ones, p * image, precision=lax.Precision.HIGHEST)
     sums = jnp.concatenate([inner[0:1], curvature[0:1]], axis=0)
     for slot in range(sums_ref.shape[0]):
         sums_ref[slot] = sums
@@ -313,6 +358,10 @@
         name=kernel.__name__,
         compiler_params=pltpu.CompilerParams(vmem_limit_bytes=16 * 2**20),
     )
+
+
+def far(*arrays):
+    return [pltpu.with_memory_space_constraint(array, pltpu.HBM) for array in arrays]
 
 
 def struct(shape, dtype):
@@ -339,20 +388,41 @@
 
     halo = struct((cases, margin), BF16)
     full = struct((cases, rows), F32)
-    operator = (diagonal, block_values, block_cols, couple_left, couple_right, send_rows)
-    operator_specs = [VMEM, VMEM, SMEM, VMEM, VMEM, VMEM]
-    sent = call(gather_kernel, [halo, halo], [VMEM] * 2)(iterate_in, send_rows)
+    semaphores = pltpu.SemaphoreType.DMA
+    to_pair, to_other, start, send_rows = call(
+        gather_kernel, [halo, halo, full, struct(send_rows.shape, send_rows.dtype)], [HBM] * 2, [semaphores((2,))]
+    )(*far(iterate_in, send_rows))
+    got = swap(to_pair, to_other)
+    nonzero_blocks = block_cols.size
+    partial, operator, diag = call(
+        own_kernel,
+        [full, struct((rows, rows + 2 * margin), BF16), struct(diagonal.shape, F32)],
+        [VMEM] + [HBM] * 6,
+        [
+            pltpu.SMEM(block_cols.shape, block_cols.dtype),
+            pltpu.VMEM((cases, rows), F32),
+            semaphores((5 + nonzero_blocks,)),
+        ],
+    )(start, *far(right_side, diagonal, block_values, block_cols, couple_left, couple_right))
+    residual, rounded, *sent = call(
+        residual_kernel, [full, struct((cases, rows), BF16), halo, halo], [VMEM] * 5
+    )(partial, operator, send_rows, *got)
     got = swap(*sent)
-    residual, rounded, *sent = call(
-        residual_kernel,
-        [full, struct((cases, rows), BF16), halo, halo],
-        [VMEM, VMEM] + operator_specs + [VMEM, VMEM],
-        [pltpu.VMEM((cases, rows), BF16)],
-    )(right_side, iterate_in, *operator, *got)
-    got = swap(*sent)
+    local, coarse, ends, basis, blocks = call(
+        inverse_kernel,
+        [
+            struct((cases, extended), F32),
+            struct((modes, cases), F32),
+            struct((2 * margin, extended), BF16),
+            struct(basis.shape, BF16),
+            struct((2, modes, modes), F32),
+        ],
+        [VMEM] + [HBM] * 4,
+        [pltpu.VMEM((rows, extended), BF16), semaphores((6,))],
+    )(rounded, *far(local_inverse, basis, coarse_diag, coarse_up))
     local, message = call(
         local_kernel, [struct((cases, extended), F32), struct((members, modes, width), F32)], [VMEM] * 7
-    )(local_inverse, basis, coarse_diag, coarse_up, rounded, *got)
+    )(local, coarse, ends, basis, blocks, *got)
     gathered = lax.all_to_all(message, "sub", 0, 0, tiled=True)
     solved, reduced = call(
         group_kernel, [struct((members, modes, width), F32), struct((2 * modes, width), F32)], [VMEM]
@@ -362,21 +432,14 @@
         solve_kernel,
         [struct((cases, extended), F32)] + [struct((cases, 2 * margin), BF16)] * 2,
         [VMEM] * 5,
-        [
-            pltpu.VMEM((groups + 1, modes, cases), F32),
-            pltpu.VMEM((members + 1, modes, cases), F32),
-            pltpu.VMEM((8, 128), F32),
-        ],
+        [pltpu.VMEM((groups + 1, modes, cases), F32), pltpu.VMEM((members + 1, modes, cases), F32)],
     )(reduced, solved, local, basis, send_rows)
     got = swap(*sent)
-    direction, image, sums = call(
-        image_kernel,
-        [full, full, struct((total, 2, cases), F32)],
-        [VMEM, VMEM] + operator_specs + [VMEM, VMEM],
-        [pltpu.VMEM((cases, rows), BF16)],
-    )(correction, residual, *operator, *got)
+    direction, image, sums = call(image_kernel, [full, full, struct((total, 2, cases), F32)], [VMEM] * 7)(
+        correction, residual, diag, operator, send_rows, *got
+    )
     sums = lax.all_to_all(sums, AXES, 0, 0, tiled=True)
-    iterate, residual = call(finish_kernel, [full, full], [VMEM] * 5)(iterate_in, direction, residual, image, sums)
+    iterate, residual = call(finish_kernel, [full, full], [VMEM] * 5)(start, direction, residual, image, sums)
     return iterate.T, residual.T
 
 

time: 87.3 us -> 77.2 us (0.88)
  local copies, waits for them, and re-layouts: 8.65 us -> 0 us
  Pallas kernels: 16.6 us -> 20.1 us
  blocking collectives: 51.6 us -> 48.8 us
  starting transfers between devices: 8.06 us -> 6.6 us
    unnamed x38 -> x0, local copies, waits for them, and re-layouts: 8.65 us -> none
    pallas_call x2 -> x4, Pallas kernels: 2.6 us -> 7.53 us  [the longest x1 2.52 us: shards(): call(own_kernel, [full, struct((rows, rows + 2 * margin), BF16), struct(d...]
    all_to_all x1, blocking collectives: 24.4 us -> 21.6 us  [shards(): gathered = lax.all_to_all(message, 'sub', 0, 0, tiled=True)]
    ppermute x3, starting transfers between devices: 6.09 us -> 4.63 us  [swap(): lax.ppermute(to_pair, AXES, pairs)]
    pallas_call x1, Pallas kernels: 1.51 us -> 0.44 us  [shards(): call(residual_kernel, [full, struct((cases, rows), BF16), halo, halo], [V...]
  transfers between devices with their start and end apart: 6 -> 6, of which waited for: 3 -> 1; matrix products, arithmetic and copies ran while one was open for 0% -> 0% of each run, Pallas kernels for 0% -> 6%
where the time goes in v3:
time: 77.2 us; the launch traced here: 76.9 us
  blocking collectives  48.8 us (63%)
  Pallas kernels  20.1 us (26%)
  starting transfers between devices  6.6 us (9%)
    all_to_all x1, blocking collectives, shards(): gathered = lax.all_to_all(message, 'sub', 0, 0, tiled=True)  21.6 us
    all_to_all x1, blocking collectives, shards(): sums = lax.all_to_all(sums, AXES, 0, 0, tiled=True)  16.2 us
    all_gather x1, blocking collectives, shards(): reduced = lax.all_gather(reduced, 'grp', axis=0)  11.1 us
    pallas_call x1, Pallas kernels, shards(): call(solve_kernel, [struct((cases, extended), F32)] + [struct((cases, 2 *...  5.52 us
    pallas_call x1, Pallas kernels, shards(): call(group_kernel, [struct((members, modes, width), F32), struct((2 * mod...  5.16 us
    ppermute x3, starting transfers between devices, swap(): lax.ppermute(to_pair, AXES, pairs)  4.63 us
    pallas_call x1, Pallas kernels, shards(): call(own_kernel, [full, struct((rows, rows + 2 * margin), BF16), struct(d...  2.52 us
    pallas_call x1, Pallas kernels, shards(): call(inverse_kernel, [struct((cases, extended), F32), struct((modes, case...  2.1 us
  transfers between devices with their start and end apart: 6, of which 1 were waited for; matrix products, arithmetic and copies ran while one was open for 0% of the time, Pallas kernels for 6%

profile of v3, /device:TPU:0, one launch (start us, length us, event | category | flops | bytes accessed | tf_op | source)
XLA Modules:
  0.0 76.9 jit_solution(7024082920104351986)
XLA Ops:
  0.6 1.3 %gather_kernel.1 = (bf16[160,128]{1,0:T(8,128)(2,1)S(1)}, bf16[160,128]{1,0:T(8,128)(2,1)S(1)}, f32[160,768]{1,0:T(8,128)S(1)}, s32[1,2,128]{2,1,0:T(2,128)S(1)}) custom-call(f32[160,768]{1,0:T(8,128)} %bitcast.8, s32[1,2,128]{2,1,0:T(2,128)} %rows_hbm.1), custom_call_target="tpu_custom_call" | custom-call | tf_op jit(solution)/shard_map/gather_kernel/pallas_call | solution.py:392
  1.9 0.6 collective-permute-start
  2.5 0.7 collective-permute-start.1
  3.2 2.5 %own_kernel.1 = (f32[160,768]{1,0:T(8,128)S(1)}, bf16[768,1024]{1,0:T(8,128)(2,1)S(1)}, f32[768]{0:T(1024)S(1)}) custom-call(f32[160,768]{1,0:T(8,128)S(1)} %get-tuple-element.30.x_ref, f32[160,768]{1,0:T(8,128)} %bitcast.9, f32[768]{0:T(1024)} %diag_hbm.2, bf16[1,6,3,128,128]{4,3,2,1,0:T(8,128)(2,1)} %values_hbm.1, s32[3,1,6]{2,1,0:T(1,128)} %bitcast.11, ...), custom_call_target="tpu_custom_call" | custom-call | tf_op jit(solution)/shard_map/own_kernel/pallas_call | solution.py:397
  5.7 0.0 collective-permute-done.pair_ref
  5.7 0.0 collective-permute-done.1.other_ref
  5.7 0.4 residual_kernel.1
  6.2 4.0 %collective-permute-start.2 = (bf16[160,128]{1,0:T(8,128)(2,1)S(1)}, bf16[160,128]{1,0:T(8,128)(2,1)S(1)}, u32[]{:S(2)}, u32[]{:S(2)}) collective-permute-start(bf16[160,128]{1,0:T(8,128)(2,1)S(1)} %get-tuple-element.42), channel_id=1, source_target_pairs={{0,1},{1,0},{2,3},{3,2},{4,5},{5,4},{6,7},{7,6},{8,9},{9,8},{10,11... | collective-permute-start | bytes 122888 | tf_op jit(solution)/shard_map/ppermute | solution.py:387
  10.2 0.7 collective-permute-start.3
  10.8 2.1 %inverse_kernel.1 = (f32[160,1024]{1,0:T(8,128)S(1)}, f32[32,160]{1,0:T(8,128)S(1)}, bf16[256,1024]{1,0:T(8,128)(2,1)S(1)}, bf16[1,32,1024]{2,1,0:T(8,128)(2,1)S(1)}, f32[2,32,32]{2,1,0:T(8,128)S(1)}) custom-call(bf16[160,768]{1,0:T(8,128)(2,1)S(1)} %get-tuple-element.36.rb_ref, bf16[1,1024,1024]{2,1,0:T(8,128)(2,1)} %inverse_hbm.1, ...), custom_call_target="tpu_custom_call" | custom-call | tf_op jit(solution)/shard_map/inverse_kernel/pallas_call | solution.py:411
  12.9 0.0 collective-permute-done.2.pair_ref
  12.9 0.0 collective-permute-done.3.other_ref
  13.0 0.3 local_kernel.1
  13.3 21.6 %all_to_all.10.gathered_ref = f32[8,32,256]{2,1,0:T(8,128)S(1)} all-to-all(f32[8,32,256]{2,1,0:T(8,128)S(1)} %get-tuple-element.44), channel_id=1, replica_groups=mesh['grp'=4,'sub'=8] {'sub'}, dimensions={0} | all-to-all | bytes 524288 | tf_op jit(solution)/shard_map/all_to_all | solution.py:426
  34.8 5.2 %group_kernel.1 = (f32[8,32,256]{2,1,0:T(8,128)S(1)}, f32[64,256]{1,0:T(8,128)S(1)}) custom-call(f32[8,32,256]{2,1,0:T(8,128)S(1)} %all_to_all.10.gathered_ref), custom_call_target="tpu_custom_call" | custom-call | tf_op jit(solution)/shard_map/group_kernel/pallas_call | solution.py:427
  40.0 11.1 %all-gather = f32[256,256]{1,0:T(8,128)S(1)} all-gather(f32[64,256]{1,0:T(8,128)S(1)} %get-tuple-element.45), channel_id=2, replica_groups=mesh['grp'=4,'sub'=8] {'grp'}, dimensions={0}, use_global_device_ids=true | all-gather | bytes 327680 | tf_op jit(solution)/shard_map/all_gather | solution.py:430
  51.1 5.5 %solve_kernel.1 = (f32[160,1024]{1,0:T(8,128)S(1)}, bf16[160,256]{1,0:T(8,128)(2,1)S(1)}, bf16[160,256]{1,0:T(8,128)(2,1)S(1)}) custom-call(f32[4,64,256]{2,1,0:T(8,128)S(1)} %bitcast.7, f32[8,32,256]{2,1,0:T(8,128)S(1)} %get-tuple-element.46.solved_ref, f32[160,1024]{1,0:T(8,128)S(1)} %get-tuple-element.47.local_ref, ...), custom_call_target="tpu_custom_call" | custom-call | tf_op jit(solution)/shard_map/solve_kernel/pallas_call | solution.py:431
  56.6 0.1 collective-permute-start.4
  56.7 0.7 collective-permute-start.5
  57.3 0.6 collective-permute-done.4.pair_ref
  57.9 0.0 collective-permute-done.5.other_ref
  57.9 1.6 %image_kernel.1 = (f32[160,768]{1,0:T(8,128)S(1)}, f32[160,768]{1,0:T(8,128)S(1)}, f32[32,2,160]{2,1,0:T(2,128)S(1)}) custom-call(f32[160,1024]{1,0:T(8,128)S(1)} %get-tuple-element.48.corr_ref, f32[160,768]{1,0:T(8,128)S(1)} %get-tuple-element.49.r_ref, f32[768]{0:T(1024)S(1)} %get-tuple-element.50.diag_ref, ...), custom_call_target="tpu_custom_call" | custom-call | tf_op jit(solution)/shard_map/image_kernel/pallas_call | solution.py:438
  59.5 16.2 %all_to_all.11.sums_ref = f32[32,2,160]{2,1,0:T(2,128)S(1)} all-to-all(f32[32,2,160]{2,1,0:T(2,128)S(1)} %get-tuple-element.55), channel_id=1, replica_groups=mesh['grp'=4,'sub'=8] {'grp','sub'}, dimensions={0} | all-to-all | bytes 81920 | tf_op jit(solution)/shard_map/all_to_all | solution.py:441
  75.7 1.1 %finish_kernel.1 = (f32[160,768]{1,0:T(8,128)}, f32[160,768]{1,0:T(8,128)}) custom-call(f32[160,768]{1,0:T(8,128)S(1)} %get-tuple-element.30.x_ref, f32[160,768]{1,0:T(8,128)S(1)} %get-tuple-element.53.p_ref, f32[160,768]{1,0:T(8,128)S(1)} %get-tuple-element.49.r_ref, f32[160,768]{1,0:T(8,128)S(1)} %get-tuple-element.54.image_ref, ...), custom_call_target="tpu_custom_call" | custom-call | tf_op jit(solution)/shard_map/finish_kernel/pallas_call | solution.py:442
Async XLA Ops:
  1.9 3.7 %collective-permute-start = (bf16[160,128]{1,0:T(8,128)(2,1)S(1)}, bf16[160,128]{1,0:T(8,128)(2,1)S(1)}, u32[]{:S(2)}, u32[]{:S(2)}) collective-permute-start(bf16[160,128]{1,0:T(8,128)(2,1)S(1)} %get-tuple-element.34), channel_id=1, source_target_pairs={{0,1},{1,0},{2,3},{3,2},{4,5},{5,4},{6,7},{7,6},{8,9},{9,8},{10,11... | collective-permute-start | bytes 122888 | tf_op jit(solution)/shard_map/ppermute | solution.py:387
  2.5 3.2 %collective-permute-start.1 = (bf16[160,128]{1,0:T(8,128)(2,1)S(1)}, bf16[160,128]{1,0:T(8,128)(2,1)S(1)}, u32[]{:S(2)}, u32[]{:S(2)}) collective-permute-start(bf16[160,128]{1,0:T(8,128)(2,1)S(1)} %get-tuple-element.35), channel_id=1, source_target_pairs={{1,2},{2,1},{3,4},{4,3},{5,6},{6,5},{7,8},{8,7},{9,10},{10,9},{11,... | collective-permute-start | bytes 122888 | tf_op jit(solution)/shard_map/ppermute | solution.py:387
  6.2 6.8 %collective-permute-start.2 = (bf16[160,128]{1,0:T(8,128)(2,1)S(1)}, bf16[160,128]{1,0:T(8,128)(2,1)S(1)}, u32[]{:S(2)}, u32[]{:S(2)}) collective-permute-start(bf16[160,128]{1,0:T(8,128)(2,1)S(1)} %get-tuple-element.42), channel_id=1, source_target_pairs={{0,1},{1,0},{2,3},{3,2},{4,5},{5,4},{6,7},{7,6},{8,9},{9,8},{10,11... | collective-permute-start | bytes 122888 | tf_op jit(solution)/shard_map/ppermute | solution.py:387
  10.2 2.8 %collective-permute-start.3 = (bf16[160,128]{1,0:T(8,128)(2,1)S(1)}, bf16[160,128]{1,0:T(8,128)(2,1)S(1)}, u32[]{:S(2)}, u32[]{:S(2)}) collective-permute-start(bf16[160,128]{1,0:T(8,128)(2,1)S(1)} %get-tuple-element.43), channel_id=1, source_target_pairs={{1,2},{2,1},{3,4},{4,3},{5,6},{6,5},{7,8},{8,7},{9,10},{10,9},{11,... | collective-permute-start | bytes 122888 | tf_op jit(solution)/shard_map/ppermute | solution.py:387
  56.6 1.3 %collective-permute-start.4 = (bf16[160,256]{1,0:T(8,128)(2,1)S(1)}, bf16[160,256]{1,0:T(8,128)(2,1)S(1)}, u32[]{:S(2)}, u32[]{:S(2)}) collective-permute-start(bf16[160,256]{1,0:T(8,128)(2,1)S(1)} %get-tuple-element.51), channel_id=1, source_target_pairs={{0,1},{1,0},{2,3},{3,2},{4,5},{5,4},{6,7},{7,6},{8,9},{9,8},{10,11... | collective-permute-start | bytes 245768 | tf_op jit(solution)/shard_map/ppermute | solution.py:387
  56.7 1.3 %collective-permute-start.5 = (bf16[160,256]{1,0:T(8,128)(2,1)S(1)}, bf16[160,256]{1,0:T(8,128)(2,1)S(1)}, u32[]{:S(2)}, u32[]{:S(2)}) collective-permute-start(bf16[160,256]{1,0:T(8,128)(2,1)S(1)} %get-tuple-element.52), channel_id=1, source_target_pairs={{1,2},{2,1},{3,4},{4,3},{5,6},{6,5},{7,8},{8,7},{9,10},{10,9},{11,... | collective-permute-start | bytes 245768 | tf_op jit(solution)/shard_map/ppermute | solution.py:387

commit v4 on v3

--- a/solution.py
+++ b/solution.py
@@ -48,7 +48,8 @@
 
 def from_sides(pair_ref, other_ref):
     even = is_even()
-    pair, other = pair_ref[...], other_ref[...]
+    other = other_ref[...]
+    pair = pair_ref[:other.shape[0], :]
     return jnp.where(even, other, pair), jnp.where(even, pair, other)
 
 
@@ -59,14 +60,26 @@
     return started
 
 
-def gather_kernel(x_hbm, rows_hbm, to_pair_ref, to_other_ref, x_ref, rows_ref, sems):
-    for copy in copy_all([(rows_hbm, rows_ref), (x_hbm, x_ref)], sems):
+def split_three(value):
+    high = value.astype(BF16)
+    rest = value - high.astype(F32)
+    middle = rest.astype(BF16)
+    return high, middle, (rest - middle.astype(F32)).astype(BF16)
+
+
+def gather_kernel(x_hbm, rows_hbm, up_hbm, to_pair_ref, to_other_ref, x_ref, rows_ref, up_ref, sems):
+    for copy in copy_all([(rows_hbm, rows_ref), (up_hbm, up_ref), (x_hbm, x_ref)], sems):
         copy.wait()
     values = x_ref[...].astype(BF16)
+    cases = values.shape[0]
     margin = rows_ref.shape[2]
     sent = mm(values, send_matrix(rows_ref, values.shape[1])).astype(BF16)
-    to_pair_ref[...] = sent[:, :margin]
+    to_pair_ref[:cases, :] = sent[:, :margin]
     to_other_ref[...] = sent[:, margin:]
+    parts = [part.astype(F32) for part in split_three(up_ref[0])]
+    size = up_ref.shape[1]
+    parts.append(jnp.zeros((size, margin - 3 * size), F32))
+    to_pair_ref[cases:, :] = jnp.concatenate(parts, axis=1).astype(BF16)
 
 
 def own_kernel(x_ref, b_hbm, diag_hbm, values_hbm, cols_hbm, cl_hbm, cr_hbm,
@@ -114,38 +127,58 @@
     to_other_ref[...] = sent[:, margin:]
 
 
-def inverse_kernel(rb_ref, inverse_hbm, basis_hbm, diag_hbm, up_hbm, local_ref, coarse_ref, ends_ref, basis_ref, blocks_ref,
-                   own_ref, sems):
-    rows = rb_ref.shape[1]
+def inverse_kernel(rb_ref, first_pair_ref, inverse_hbm, basis_hbm, diag_hbm, up_hbm,
+                   local_ref, coarse_ref, ends_ref, basis_ref, factor_ref, plain_ref, own_ref, blocks_ref, sems):
+    cases, rows = rb_ref.shape
     total = inverse_hbm.shape[1]
     margin = (total - rows) // 2
+    size = diag_hbm.shape[1]
     copies = copy_all(
         [
-            (basis_hbm, basis_ref),
             (diag_hbm, blocks_ref.at[0:1]),
             (up_hbm, blocks_ref.at[1:2]),
+            (basis_hbm, basis_ref),
             (inverse_hbm.at[0, margin:margin + rows], own_ref),
             (inverse_hbm.at[0, :margin], ends_ref.at[:margin]),
             (inverse_hbm.at[0, margin + rows:], ends_ref.at[margin:]),
         ],
         sems,
     )
-    for copy in copies:
+    parts = first_pair_ref[cases:, :].astype(F32)
+    up_left = parts[:, :size] + (parts[:, size:2 * size] + parts[:, 2 * size:3 * size])
+    for copy in copies[:2]:
+        copy.wait()
+    last = position() == lax.axis_size("grp") * lax.axis_size("sub") - 1
+    up = jnp.where(last, 0.0, blocks_ref[1])
+    diag = blocks_ref[0]
+    row = lax.broadcasted_iota(jnp.int32, (size, size), 0)
+    lane = lax.broadcasted_iota(jnp.int32, (size, size), 1)
+    identity = (row == lane).astype(F32)
+    factor = reduce_rows([jnp.concatenate([diag, jnp.transpose(up_left), up, identity], axis=1)])[0]
+    odd = jnp.concatenate([jnp.transpose(up), factor[:, size:3 * size], jnp.zeros((size, size), F32)], axis=1)
+    even = jnp.concatenate([diag, up, jnp.zeros((size, 2 * size), F32)], axis=1)
+    plain_ref[...] = jnp.where(is_even(), even, odd)
+    place = jnp.concatenate([jnp.zeros((size, 3 * size), F32), identity], axis=1)
+    lanes = lax.broadcasted_iota(jnp.int32, factor.shape, 1)
+    factor_ref[...] = jnp.where(is_even(), place, jnp.where(lanes >= 3 * size, factor, 0.0))
+    for copy in copies[2:]:
         copy.wait()
     rounded = rb_ref[...]
     local_ref[...] = mm(rounded, own_ref[...])
     coarse_ref[...] = mm_nt(basis_ref[0, :, margin:margin + rows], rounded)
 
 
-def local_kernel(own_local_ref, own_coarse_ref, ends_ref, basis_ref, blocks_ref, pair_ref, other_ref,
+def local_kernel(own_local_ref, own_coarse_ref, ends_ref, basis_ref, factor_ref, plain_ref, pair_ref, other_ref,
                  local_ref, message_ref):
     margin = pair_ref.shape[1]
     halo = jnp.concatenate(from_sides(pair_ref, other_ref), axis=1)
     ends = jnp.concatenate([basis_ref[0, :, :margin], basis_ref[0, :, basis_ref.shape[2] - margin:]], axis=1)
     coarse_in = own_coarse_ref[...] + mm_nt(ends, halo)
-    last = position() == lax.axis_size("grp") * lax.axis_size("sub") - 1
-    up = jnp.where(last, 0.0, blocks_ref[1])
-    message = jnp.concatenate([blocks_ref[0], jnp.transpose(up), up, coarse_in], axis=1)
+    size = coarse_in.shape[0]
+    stacked = jnp.concatenate([jnp.zeros((3 * size, coarse_in.shape[1]), F32), coarse_in], axis=0)
+    reduced = jnp.dot(factor_ref[...], stacked, precision=lax.Precision.HIGHEST, preferred_element_type=F32)
+    right_side = jnp.where(is_even(), coarse_in, reduced)
+    message = jnp.concatenate([plain_ref[:, :3 * size], right_side], axis=1)
     for slot in range(message_ref.shape[0]):
         message_ref[slot] = message
     local_ref[...] = own_local_ref[...] + mm(halo, ends_ref[...])
@@ -153,63 +186,85 @@
 
 def reduce_rows(blocks):
     size, width = blocks[0].shape
-    panel = 8 if len(blocks) <= 2 else 4
-    lanes = 128
-    here = lax.broadcasted_iota(jnp.int32, (size, 1), 0)
+    panel = 16 if len(blocks) == 1 else 8 if len(blocks) == 2 else 4
+    lanes, tile = 128, 8
+    here = lax.broadcasted_iota(jnp.int32, (tile, 1), 0)
+    tiles = range(size // tile)
+    blocks = [[block[t * tile:(t + 1) * tile, :] for t in tiles] for block in blocks]
 
     def wide(value):
         return jnp.concatenate([value] * (width // lanes), axis=1)
 
     for first in range(0, size, panel):
         panels = [
-            [jnp.broadcast_to(block[:, q:q + 1], (size, lanes)) for q in range(first, first + panel)] for block in blocks
+            [[jnp.broadcast_to(rows[:, q:q + 1], (tile, lanes)) for rows in block] for q in range(first, first + panel)]
+            for block in blocks
         ]
         for a in range(panel):
-            p = first + a
-            done = []
+            at, inside = divmod(first + a, tile)
             for block, columns in zip(blocks, panels):
                 column = columns[a]
-                inverse = 1.0 / column[p:p + 1, :]
+                inverse = 1.0 / column[at][inside:inside + 1, :]
                 for b in range(a + 1, panel):
-                    entry = columns[b][p:p + 1, :] * inverse
-                    columns[b] = jnp.where(here == p, entry, columns[b] - column * entry)
-                row = block[p:p + 1, :] * wide(inverse)
-                done.append(jnp.where(here == p, row, block - wide(column) * row))
-            blocks = done
-    return blocks
-
-
-def schur(block, solved, size):
-    width = solved.shape[1]
-    product = -mm_t(block[:, :4 * size], solved, precision=lax.Precision.HIGHEST)
-    top, bottom = product[size:2 * size], product[2 * size:3 * size]
+                    entry = columns[b][at][inside:inside + 1, :] * inverse
+                    columns[b] = [
+                        jnp.where(here == inside, entry, columns[b][t] - column[t] * entry)
+                        if t == at else columns[b][t] - column[t] * entry
+                        for t in tiles
+                    ]
+                row = block[at][inside:inside + 1, :] * wide(inverse)
+                for t in tiles:
+                    rest = block[t] - wide(column[t]) * row
+                    block[t] = jnp.where(here == inside, row, rest) if t == at else rest
+    return [jnp.concatenate(block, axis=0) for block in blocks]
+
+
+def shares(top, bottom, size):
     zero = jnp.zeros((size, size), F32)
     to_left = jnp.concatenate([top[:, size:2 * size], zero, top[:, 2 * size:]], axis=1)
     to_right = jnp.concatenate([bottom[:, 2 * size:3 * size], bottom[:, size:2 * size], zero, bottom[:, 3 * size:]], axis=1)
     return to_left, to_right
 
 
+def schur(block, solved, size):
+    product = -mm_t(block[:, :4 * size], solved, precision=lax.Precision.HIGHEST)
+    return shares(product[size:2 * size], product[2 * size:3 * size], size)
+
+
+def first_schur(previous, block, size):
+    highest = lax.Precision.HIGHEST
+    zero = jnp.zeros_like(block)
+    above = jnp.concatenate([zero, block, zero, zero], axis=0)
+    below = jnp.concatenate([block, zero, zero, zero], axis=0)
+    top = -jnp.dot(previous[:, :4 * size], above, precision=highest, preferred_element_type=F32)
+    bottom = -jnp.dot(block[:, :4 * size], below, precision=highest, preferred_element_type=F32)
+    return shares(top, bottom, size)
+
+
 def own_part(block, size):
     lane = lax.broadcasted_iota(jnp.int32, block.shape, 1)
     return jnp.where((lane >= size) & (lane < 3 * size), 0.0, block)
 
 
-def eliminate(chain, size, keep):
+def combine(chain, parts, step, size):
+    for i in range(0, len(chain), 2 * step):
+        total = own_part(chain[i], size)
+        if i + step in parts:
+            total = total + parts[i + step][0]
+        if i - step in parts:
+            total = total + parts[i - step][1]
+        chain[i] = total
+
+
+def eliminate(chain, size, keep, step=1):
     count = len(chain) - 1
-    step = 1
     while step < count:
         inner = list(range(step, count, 2 * step))
         solved = dict(zip(inner, reduce_rows([chain[j] for j in inner])))
         parts = {j: schur(chain[j], solved[j], size) for j in inner}
         for j in inner:
             keep(j, solved[j])
-        for i in range(0, count + 1, 2 * step):
-            total = own_part(chain[i], size)
-            if i + step in parts:
-                total = total + parts[i + step][0]
-            if i - step in parts:
-                total = total + parts[i - step][1]
-            chain[i] = total
+        combine(chain, parts, step, size)
         step = 2 * step
     return chain[0], chain[count]
 
@@ -228,32 +283,25 @@
     return total
 
 
-def chain_of(blocks, size):
-    width = blocks[0].shape[1]
-    lane = lax.broadcasted_iota(jnp.int32, (size, width), 1)
-    row = lax.broadcasted_iota(jnp.int32, (size, width), 0)
-    from_previous = (lane >= size) & (lane < 2 * size)
-    own = [jnp.where(from_previous, 0.0, block) for block in blocks]
-    chain = [own[0]]
-    for j in range(1, len(blocks)):
-        chain.append(jnp.where(from_previous, blocks[j - 1], blocks[j]))
-    return chain, from_previous, (lane == row).astype(F32)
-
-
-def group_kernel(gathered_ref, solved_ref, message_ref):
-    members, size, width = gathered_ref.shape
-    blocks = [gathered_ref[j] for j in range(members)]
-    chain, from_previous, identity = chain_of(blocks, size)
-    tail = jnp.where(from_previous, blocks[members - 1], 0.0)
-    total = padded(members)
-    if total > members:
-        raise NotImplementedError("members")
-    chain.append(tail)
+def group_kernel(same_ref, opposite_ref, solved_ref, message_ref):
+    half, size, width = same_ref.shape
+    members = 2 * half
+    even = is_even()
+    chain = []
+    for j in range(half):
+        same, opposite = same_ref[j], opposite_ref[j]
+        chain += [jnp.where(even, same, opposite), jnp.where(even, opposite, same)]
+    chain.append(jnp.zeros((size, width), F32))
 
     def keep(j, solved):
         solved_ref[j] = solved
 
-    head, tail = eliminate(chain, size, keep)
+    parts = {}
+    for j in range(1, members, 2):
+        keep(j, chain[j])
+        parts[j] = first_schur(chain[j - 1], chain[j], size)
+    combine(chain, parts, 1, size)
+    head, tail = eliminate(chain, size, keep, 2)
     message_ref[:size, :] = head
     message_ref[size:, :] = tail
 
@@ -390,9 +438,13 @@
     full = struct((cases, rows), F32)
     semaphores = pltpu.SemaphoreType.DMA
     to_pair, to_other, start, send_rows = call(
-        gather_kernel, [halo, halo, full, struct(send_rows.shape, send_rows.dtype)], [HBM] * 2, [semaphores((2,))]
-    )(*far(iterate_in, send_rows))
+        gather_kernel,
+        [struct((cases + modes, margin), BF16), halo, full, struct(send_rows.shape, send_rows.dtype)],
+        [HBM] * 3,
+        [pltpu.VMEM(coarse_up.shape, F32), semaphores((3,))],
+    )(*far(iterate_in, send_rows, coarse_up))
     got = swap(to_pair, to_other)
+    first_pair = got[0]
     nonzero_blocks = block_cols.size
     partial, operator, diag = call(
         own_kernel,
@@ -408,25 +460,29 @@
         residual_kernel, [full, struct((cases, rows), BF16), halo, halo], [VMEM] * 5
     )(partial, operator, send_rows, *got)
     got = swap(*sent)
-    local, coarse, ends, basis, blocks = call(
+    local, coarse, ends, basis, factor, plain = call(
         inverse_kernel,
         [
             struct((cases, extended), F32),
             struct((modes, cases), F32),
             struct((2 * margin, extended), BF16),
             struct(basis.shape, BF16),
-            struct((2, modes, modes), F32),
+            struct((modes, 4 * modes), F32),
+            struct((modes, 4 * modes), F32),
         ],
-        [VMEM] + [HBM] * 4,
-        [pltpu.VMEM((rows, extended), BF16), semaphores((6,))],
-    )(rounded, *far(local_inverse, basis, coarse_diag, coarse_up))
+        [VMEM] * 2 + [HBM] * 4,
+        [pltpu.VMEM((rows, extended), BF16), pltpu.VMEM((2, modes, modes), F32), semaphores((6,))],
+    )(rounded, first_pair, *far(local_inverse, basis, coarse_diag, coarse_up))
+    chips = members // 2
     local, message = call(
-        local_kernel, [struct((cases, extended), F32), struct((members, modes, width), F32)], [VMEM] * 7
-    )(local, coarse, ends, basis, blocks, *got)
-    gathered = lax.all_to_all(message, "sub", 0, 0, tiled=True)
+        local_kernel, [struct((cases, extended), F32), struct((chips, modes, width), F32)], [VMEM] * 8
+    )(local, coarse, ends, basis, factor, plain, *got)
+    cores = [[2 * chip + core for chip in range(chips)] for core in range(2)]
+    same = lax.all_to_all(message, "sub", 0, 0, tiled=True, axis_index_groups=cores)
+    opposite = lax.ppermute(same, AXES, pairs)
     solved, reduced = call(
-        group_kernel, [struct((members, modes, width), F32), struct((2 * modes, width), F32)], [VMEM]
-    )(gathered)
+        group_kernel, [struct((members, modes, width), F32), struct((2 * modes, width), F32)], [VMEM] * 2
+    )(same, opposite)
     reduced = lax.all_gather(reduced, "grp", axis=0)
     correction, *sent = call(
         solve_kernel,

time: 77.2 us -> 71.7 us (0.929)
  blocking collectives: 48.8 us -> 43 us
  Pallas kernels: 20.1 us -> 17.9 us
  starting transfers between devices: 6.6 us -> 8.06 us
  waiting for transfers between devices: 0.6 us -> 1.59 us
    all_to_all x1, blocking collectives: 21.6 us -> 15.4 us  [shards(): lax.all_to_all(message, 'sub', 0, 0, tiled=True, axis_index_groups=cores)]
    pallas_call x1, Pallas kernels: 5.16 us -> 2.92 us  [shards(): call(group_kernel, [struct((members, modes, width), F32), struct((2 * mod...]
    ppermute x0 -> x1, starting transfers between devices: none -> 1.45 us  [shards(): opposite = lax.ppermute(same, AXES, pairs)]
    ppermute x0 -> x1, waiting for transfers between devices: none -> 0.99 us  [shards(): opposite = lax.ppermute(same, AXES, pairs)]
  transfers between devices with their start and end apart: 6 -> 7, of which waited for: 1 -> 2; matrix products, arithmetic and copies ran while one was open for 0% -> 0% of each run, Pallas kernels for 6% -> 6%
where the time goes in v4:
time: 71.7 us; the launch traced here: 71.3 us
  blocking collectives  43 us (60%)
  Pallas kernels  17.9 us (25%)
  starting transfers between devices  8.06 us (11%)
  waiting for transfers between devices  1.59 us (2%)
  between operations  0.76 us (1%)
    all_to_all x1, blocking collectives, shards(): sums = lax.all_to_all(sums, AXES, 0, 0, tiled=True)  17 us
    all_to_all x1, blocking collectives, shards(): lax.all_to_all(message, 'sub', 0, 0, tiled=True, axis_index_groups=cores)  15.4 us
    all_gather x1, blocking collectives, shards(): reduced = lax.all_gather(reduced, 'grp', axis=0)  10.6 us
    pallas_call x1, Pallas kernels, shards(): call(solve_kernel, [struct((cases, extended), F32)] + [struct((cases, 2 *...  5.33 us
    ppermute x3, starting transfers between devices, swap(): lax.ppermute(to_pair, AXES, pairs)  4.64 us
    pallas_call x1, Pallas kernels, shards(): call(group_kernel, [struct((members, modes, width), F32), struct((2 * mod...  2.92 us
    pallas_call x1, Pallas kernels, shards(): call(own_kernel, [full, struct((rows, rows + 2 * margin), BF16), struct(d...  2.52 us
    pallas_call x1, Pallas kernels, shards(): call(inverse_kernel, [struct((cases, extended), F32), struct((modes, case...  2.11 us
  transfers between devices with their start and end apart: 7, of which 2 were waited for; matrix products, arithmetic and copies ran while one was open for 0% of the time, Pallas kernels for 6%

profile of v4, /device:TPU:0, one launch (start us, length us, event | category | flops | bytes accessed | tf_op | source)
XLA Modules:
  0.0 71.3 jit_solution(12752180781159968193)
XLA Ops:
  0.6 1.3 %gather_kernel.1 = (bf16[192,128]{1,0:T(8,128)(2,1)S(1)}, bf16[160,128]{1,0:T(8,128)(2,1)S(1)}, f32[160,768]{1,0:T(8,128)S(1)}, s32[1,2,128]{2,1,0:T(2,128)S(1)}) custom-call(f32[160,768]{1,0:T(8,128)} %bitcast.8, s32[1,2,128]{2,1,0:T(2,128)} %rows_hbm.1, f32[1,32,32]{2,1,0:T(8,128)} %up_hbm.3), custom_call_target="tpu_custom_call" | custom-call | tf_op jit(solution)/shard_map/gather_kernel/pallas_call | solution.py:440
  2.0 0.6 collective-permute-start
  2.5 0.7 collective-permute-start.1
  3.2 2.5 %own_kernel.1 = (f32[160,768]{1,0:T(8,128)S(1)}, bf16[768,1024]{1,0:T(8,128)(2,1)S(1)}, f32[768]{0:T(1024)S(1)}) custom-call(f32[160,768]{1,0:T(8,128)S(1)} %get-tuple-element.31.x_ref, f32[160,768]{1,0:T(8,128)} %bitcast.9, f32[768]{0:T(1024)} %diag_hbm.2, bf16[1,6,3,128,128]{4,3,2,1,0:T(8,128)(2,1)} %values_hbm.1, s32[3,1,6]{2,1,0:T(1,128)} %bitcast.11, ...), custom_call_target="tpu_custom_call" | custom-call | tf_op jit(solution)/shard_map/own_kernel/pallas_call | solution.py:449
  5.7 0.0 collective-permute-done.1.other_ref
  5.7 0.0 collective-permute-done.pair_ref.first_pair_ref
  5.7 0.4 residual_kernel.1
  6.2 4.0 %collective-permute-start.2 = (bf16[160,128]{1,0:T(8,128)(2,1)S(1)}, bf16[160,128]{1,0:T(8,128)(2,1)S(1)}, u32[]{:S(2)}, u32[]{:S(2)}) collective-permute-start(bf16[160,128]{1,0:T(8,128)(2,1)S(1)} %get-tuple-element.44), channel_id=1, source_target_pairs={{0,1},{1,0},{2,3},{3,2},{4,5},{5,4},{6,7},{7,6},{8,9},{9,8},{10,11... | collective-permute-start | bytes 122888 | tf_op jit(solution)/shard_map/ppermute | solution.py:435
  10.2 0.7 collective-permute-start.3
  10.9 2.1 %inverse_kernel.1 = (f32[160,1024]{1,0:T(8,128)S(1)}, f32[32,160]{1,0:T(8,128)S(1)}, bf16[256,1024]{1,0:T(8,128)(2,1)S(1)}, bf16[1,32,1024]{2,1,0:T(8,128)(2,1)S...) custom-call(bf16[160,768]{1,0:T(8,128)(2,1)S(1)} %get-tuple-element.37.rb_ref, ...), custom_call_target="tpu_custom_call" | custom-call | tf_op jit(solution)/shard_map/inverse_kernel/pallas_call | solution.py:463
  13.0 0.0 collective-permute-done.2.pair_ref
  13.0 0.0 collective-permute-done.3.other_ref
  13.0 0.5 local_kernel.1
  13.5 15.4 %all_to_all.10.same_ref = f32[4,32,256]{2,1,0:T(8,128)S(1)} all-to-all(f32[4,32,256]{2,1,0:T(8,128)S(1)} %get-tuple-element.46), channel_id=1, replica_groups={{0,2,4,6},{1,3,5,7},{8,10,12,14},{9,11,13,15},{16,18,20,22},{17,19,21,2..., dimensions={0} | all-to-all | bytes 262144 | tf_op jit(solution)/shard_map/all_to_all | solution.py:481
  28.9 1.4 %collective-permute-start.4 = (f32[4,32,256]{2,1,0:T(8,128)S(1)}, f32[4,32,256]{2,1,0:T(8,128)S(1)}, u32[]{:S(2)}, u32[]{:S(2)}) collective-permute-start(f32[4,32,256]{2,1,0:T(8,128)S(1)} %all_to_all.10.same_ref), channel_id=1, source_target_pairs={{0,1},{1,0},{2,3},{3,2},{4,5},{5,4},{6,7},{7,6},{8,9},{9,8},{10,11... | collective-permute-start | bytes 393224 | tf_op jit(solution)/shard_map/ppermute | solution.py:482
  30.4 1.0 %collective-permute-done.4.opposite_ref = f32[4,32,256]{2,1,0:T(8,128)S(1)} collective-permute-done((f32[4,32,256]{2,1,0:T(8,128)S(1)}, f32[4,32,256]{2,1,0:T(8,128)S(1)}, u32[]{:S(2)}, u32[]{:S(2)}) %collective-permute-start.4) | collective-permute-done | bytes 131104 | tf_op jit(solution)/shard_map/ppermute | solution.py:482
  31.4 2.9 %group_kernel.1 = (f32[8,32,256]{2,1,0:T(8,128)S(1)}, f32[64,256]{1,0:T(8,128)S(1)}) custom-call(f32[4,32,256]{2,1,0:T(8,128)S(1)} %all_to_all.10.same_ref, f32[4,32,256]{2,1,0:T(8,128)S(1)} %collective-permute-done.4.opposite_ref), custom_call_target="tpu_custom_call" | custom-call | tf_op jit(solution)/shard_map/group_kernel/pallas_call | solution.py:483
  34.3 10.6 %all-gather = f32[256,256]{1,0:T(8,128)S(1)} all-gather(f32[64,256]{1,0:T(8,128)S(1)} %get-tuple-element.47), channel_id=2, replica_groups=mesh['grp'=4,'sub'=8] {'grp'}, dimensions={0}, use_global_device_ids=true | all-gather | bytes 327680 | tf_op jit(solution)/shard_map/all_gather | solution.py:486
  44.9 5.3 %solve_kernel.1 = (f32[160,1024]{1,0:T(8,128)S(1)}, bf16[160,256]{1,0:T(8,128)(2,1)S(1)}, bf16[160,256]{1,0:T(8,128)(2,1)S(1)}) custom-call(f32[4,64,256]{2,1,0:T(8,128)S(1)} %bitcast.7, f32[8,32,256]{2,1,0:T(8,128)S(1)} %get-tuple-element.48.solved_ref, f32[160,1024]{1,0:T(8,128)S(1)} %get-tuple-element.49.local_ref, ...), custom_call_target="tpu_custom_call" | custom-call | tf_op jit(solution)/shard_map/solve_kernel/pallas_call | solution.py:487
  50.2 0.1 collective-permute-start.5
  50.3 0.7 collective-permute-start.6
  51.0 0.6 collective-permute-done.5.pair_ref
  51.6 0.0 collective-permute-done.6.other_ref
  51.6 1.6 %image_kernel.1 = (f32[160,768]{1,0:T(8,128)S(1)}, f32[160,768]{1,0:T(8,128)S(1)}, f32[32,2,160]{2,1,0:T(2,128)S(1)}) custom-call(f32[160,1024]{1,0:T(8,128)S(1)} %get-tuple-element.50.corr_ref, f32[160,768]{1,0:T(8,128)S(1)} %get-tuple-element.51.r_ref, f32[768]{0:T(1024)S(1)} %get-tuple-element.52.diag_ref, ...), custom_call_target="tpu_custom_call" | custom-call | tf_op jit(solution)/shard_map/image_kernel/pallas_call | solution.py:494
  53.2 17.0 %all_to_all.11.sums_ref = f32[32,2,160]{2,1,0:T(2,128)S(1)} all-to-all(f32[32,2,160]{2,1,0:T(2,128)S(1)} %get-tuple-element.57), channel_id=1, replica_groups=mesh['grp'=4,'sub'=8] {'grp','sub'}, dimensions={0} | all-to-all | bytes 81920 | tf_op jit(solution)/shard_map/all_to_all | solution.py:497
  70.2 1.1 %finish_kernel.1 = (f32[160,768]{1,0:T(8,128)}, f32[160,768]{1,0:T(8,128)}) custom-call(f32[160,768]{1,0:T(8,128)S(1)} %get-tuple-element.31.x_ref, f32[160,768]{1,0:T(8,128)S(1)} %get-tuple-element.55.p_ref, f32[160,768]{1,0:T(8,128)S(1)} %get-tuple-element.51.r_ref, f32[160,768]{1,0:T(8,128)S(1)} %get-tuple-element.56.image_ref, ...), custom_call_target="tpu_custom_call" | custom-call | tf_op jit(solution)/shard_map/finish_kernel/pallas_call | solution.py:498
Async XLA Ops:
  2.0 3.8 %collective-permute-start = (bf16[192,128]{1,0:T(8,128)(2,1)S(1)}, bf16[192,128]{1,0:T(8,128)(2,1)S(1)}, u32[]{:S(2)}, u32[]{:S(2)}) collective-permute-start(bf16[192,128]{1,0:T(8,128)(2,1)S(1)} %get-tuple-element.35), channel_id=1, source_target_pairs={{0,1},{1,0},{2,3},{3,2},{4,5},{5,4},{6,7},{7,6},{8,9},{9,8},{10,11... | collective-permute-start | bytes 147464 | tf_op jit(solution)/shard_map/ppermute | solution.py:435
  2.5 3.2 %collective-permute-start.1 = (bf16[160,128]{1,0:T(8,128)(2,1)S(1)}, bf16[160,128]{1,0:T(8,128)(2,1)S(1)}, u32[]{:S(2)}, u32[]{:S(2)}) collective-permute-start(bf16[160,128]{1,0:T(8,128)(2,1)S(1)} %get-tuple-element.36), channel_id=1, source_target_pairs={{1,2},{2,1},{3,4},{4,3},{5,6},{6,5},{7,8},{8,7},{9,10},{10,9},{11,... | collective-permute-start | bytes 122888 | tf_op jit(solution)/shard_map/ppermute | solution.py:435
  6.2 6.8 %collective-permute-start.2 = (bf16[160,128]{1,0:T(8,128)(2,1)S(1)}, bf16[160,128]{1,0:T(8,128)(2,1)S(1)}, u32[]{:S(2)}, u32[]{:S(2)}) collective-permute-start(bf16[160,128]{1,0:T(8,128)(2,1)S(1)} %get-tuple-element.44), channel_id=1, source_target_pairs={{0,1},{1,0},{2,3},{3,2},{4,5},{5,4},{6,7},{7,6},{8,9},{9,8},{10,11... | collective-permute-start | bytes 122888 | tf_op jit(solution)/shard_map/ppermute | solution.py:435
  10.2 2.8 %collective-permute-start.3 = (bf16[160,128]{1,0:T(8,128)(2,1)S(1)}, bf16[160,128]{1,0:T(8,128)(2,1)S(1)}, u32[]{:S(2)}, u32[]{:S(2)}) collective-permute-start(bf16[160,128]{1,0:T(8,128)(2,1)S(1)} %get-tuple-element.45), channel_id=1, source_target_pairs={{1,2},{2,1},{3,4},{4,3},{5,6},{6,5},{7,8},{8,7},{9,10},{10,9},{11,... | collective-permute-start | bytes 122888 | tf_op jit(solution)/shard_map/ppermute | solution.py:435
  28.9 2.4 %collective-permute-start.4 = (f32[4,32,256]{2,1,0:T(8,128)S(1)}, f32[4,32,256]{2,1,0:T(8,128)S(1)}, u32[]{:S(2)}, u32[]{:S(2)}) collective-permute-start(f32[4,32,256]{2,1,0:T(8,128)S(1)} %all_to_all.10.same_ref), channel_id=1, source_target_pairs={{0,1},{1,0},{2,3},{3,2},{4,5},{5,4},{6,7},{7,6},{8,9},{9,8},{10,11... | collective-permute-start | bytes 393224 | tf_op jit(solution)/shard_map/ppermute | solution.py:482
  50.2 1.3 %collective-permute-start.5 = (bf16[160,256]{1,0:T(8,128)(2,1)S(1)}, bf16[160,256]{1,0:T(8,128)(2,1)S(1)}, u32[]{:S(2)}, u32[]{:S(2)}) collective-permute-start(bf16[160,256]{1,0:T(8,128)(2,1)S(1)} %get-tuple-element.53), channel_id=1, source_target_pairs={{0,1},{1,0},{2,3},{3,2},{4,5},{5,4},{6,7},{7,6},{8,9},{9,8},{10,11... | collective-permute-start | bytes 245768 | tf_op jit(solution)/shard_map/ppermute | solution.py:435
  50.3 1.3 %collective-permute-start.6 = (bf16[160,256]{1,0:T(8,128)(2,1)S(1)}, bf16[160,256]{1,0:T(8,128)(2,1)S(1)}, u32[]{:S(2)}, u32[]{:S(2)}) collective-permute-start(bf16[160,256]{1,0:T(8,128)(2,1)S(1)} %get-tuple-element.54), channel_id=1, source_target_pairs={{1,2},{2,1},{3,4},{4,3},{5,6},{6,5},{7,8},{8,7},{9,10},{10,9},{11,... | collective-permute-start | bytes 245768 | tf_op jit(solution)/shard_map/ppermute | solution.py:435

commit v5 on v4

--- a/solution.py
+++ b/solution.py
@@ -83,64 +83,61 @@
 
 
 def own_kernel(x_ref, b_hbm, diag_hbm, values_hbm, cols_hbm, cl_hbm, cr_hbm,
-               partial_ref, operator_ref, diag_ref, cols_ref, b_ref, sems):
+               partial_ref, operator_ref, diag_ref, cols_ref, b_ref, values_ref, sems):
     blocks, nonzeros, size = values_hbm.shape[1], values_hbm.shape[2], values_hbm.shape[3]
     rows = x_ref.shape[1]
     margin = cl_hbm.shape[1]
-    first = copy_all(
+    copies = copy_all(
         [
             (cols_hbm, cols_ref),
+            (values_hbm, values_ref),
+            (b_hbm, b_ref),
             (diag_hbm, diag_ref),
-            (b_hbm, b_ref),
             (cl_hbm, operator_ref.at[:, rows:rows + margin]),
             (cr_hbm, operator_ref.at[:, rows + margin:]),
         ],
         sems,
     )
     operator_ref[:, :rows] = jnp.zeros((rows, rows), BF16)
-    first[0].wait()
-    placed = []
+    for copy in copies:
+        copy.wait()
     for i in range(blocks):
         for t in range(nonzeros):
             start = pl.multiple_of(cols_ref[t, 0, i] * size, size)
-            target = operator_ref.at[i * size:(i + 1) * size, pl.ds(start, size)]
-            copy = pltpu.make_async_copy(values_hbm.at[0, i, t], target, sems.at[len(first) + i * nonzeros + t])
-            copy.start()
-            placed.append(copy)
-    for copy in first[1:] + placed:
-        copy.wait()
+            operator_ref[i * size:(i + 1) * size, pl.ds(start, size)] = values_ref[0, i, t]
     x = x_ref[...]
     diag = diag_ref[...].reshape(1, rows)
     partial_ref[...] = b_ref[...] - diag * x - mm_nt(x.astype(BF16), operator_ref[:, :rows])
 
 
-def residual_kernel(partial_ref, operator_ref, rows_ref, pair_ref, other_ref, r_ref, rb_ref, to_pair_ref, to_other_ref):
-    rows = partial_ref.shape[1]
+def offer_kernel(partial_ref, operator_ref, rows_ref, pair_ref, to_other_ref, known_ref, message_ref):
+    cases, rows = partial_ref.shape
     margin = rows_ref.shape[2]
-    halo = jnp.concatenate(from_sides(pair_ref, other_ref), axis=1)
-    r = partial_ref[...] - mm_nt(halo, operator_ref[:, rows:])
-    r_ref[...] = r
-    rounded = r.astype(BF16)
-    rb_ref[...] = rounded
-    sent = mm(rounded, send_matrix(rows_ref, rows)).astype(BF16)
-    to_pair_ref[...] = sent[:, :margin]
-    to_other_ref[...] = sent[:, margin:]
-
-
-def inverse_kernel(rb_ref, first_pair_ref, inverse_hbm, basis_hbm, diag_hbm, up_hbm,
-                   local_ref, coarse_ref, ends_ref, basis_ref, factor_ref, plain_ref, own_ref, blocks_ref, sems):
-    cases, rows = rb_ref.shape
-    total = inverse_hbm.shape[1]
-    margin = (total - rows) // 2
+    even = is_even()
+    left, right = operator_ref[:, rows:rows + margin], operator_ref[:, rows + margin:]
+    from_pair = jnp.where(even, right, left)
+    from_other = jnp.where(even, left, right)
+    known = partial_ref[...] - mm_nt(pair_ref[:cases, :], from_pair)
+    known_ref[...] = known
+    high = known.astype(BF16)
+    low = (known - high.astype(F32)).astype(BF16)
+    place = place_matrix(jnp.where(even, rows_ref[0, 0:1, :], rows_ref[0, 1:2, :]), rows)
+    message_ref[:cases, :] = to_other_ref[...]
+    message_ref[cases:2 * cases, :] = mm(high, place).astype(BF16)
+    message_ref[2 * cases:3 * cases, :] = mm(low, place).astype(BF16)
+    message_ref[3 * cases:, :] = mm_t(place, from_other).astype(BF16)
+
+
+def inverse_kernel(first_pair_ref, inverse_hbm, basis_hbm, diag_hbm, up_hbm,
+                   inverse_ref, basis_ref, factor_ref, plain_ref, blocks_ref, sems):
     size = diag_hbm.shape[1]
+    cases = first_pair_ref.shape[0] - size
     copies = copy_all(
         [
             (diag_hbm, blocks_ref.at[0:1]),
             (up_hbm, blocks_ref.at[1:2]),
             (basis_hbm, basis_ref),
-            (inverse_hbm.at[0, margin:margin + rows], own_ref),
-            (inverse_hbm.at[0, :margin], ends_ref.at[:margin]),
-            (inverse_hbm.at[0, margin + rows:], ends_ref.at[margin:]),
+            (inverse_hbm, inverse_ref),
         ],
         sems,
     )
@@ -158,30 +155,57 @@
     odd = jnp.concatenate([jnp.transpose(up), factor[:, size:3 * size], jnp.zeros((size, size), F32)], axis=1)
     even = jnp.concatenate([diag, up, jnp.zeros((size, 2 * size), F32)], axis=1)
     plain_ref[...] = jnp.where(is_even(), even, odd)
-    place = jnp.concatenate([jnp.zeros((size, 3 * size), F32), identity], axis=1)
     lanes = lax.broadcasted_iota(jnp.int32, factor.shape, 1)
-    factor_ref[...] = jnp.where(is_even(), place, jnp.where(lanes >= 3 * size, factor, 0.0))
+    factor_ref[...] = jnp.where(lanes >= 3 * size, factor, 0.0)
     for copy in copies[2:]:
         copy.wait()
-    rounded = rb_ref[...]
-    local_ref[...] = mm(rounded, own_ref[...])
-    coarse_ref[...] = mm_nt(basis_ref[0, :, margin:margin + rows], rounded)
-
-
-def local_kernel(own_local_ref, own_coarse_ref, ends_ref, basis_ref, factor_ref, plain_ref, pair_ref, other_ref,
+
+
+def residual_kernel(known_ref, operator_ref, rows_ref, sent_ref, other_ref, loaded_ref, r_ref, rb_ref, to_pair_ref, halo_ref):
+    cases, rows = known_ref.shape
+    margin = rows_ref.shape[2]
+    even = is_even()
+    from_other = jnp.where(even, operator_ref[:, rows:rows + margin], operator_ref[:, rows + margin:])
+    r = known_ref[...] - mm_nt(other_ref[:cases, :], from_other)
+    r_ref[...] = r
+    rounded = r.astype(BF16)
+    rb_ref[...] = rounded
+    place = place_matrix(jnp.where(even, rows_ref[0, 1:2, :], rows_ref[0, 0:1, :]), rows)
+    to_pair_ref[...] = mm(rounded, place).astype(BF16)
+    offered = other_ref[cases:2 * cases, :].astype(F32) + other_ref[2 * cases:3 * cases, :].astype(F32)
+    halo_ref[...] = (offered - mm_nt(sent_ref[...], other_ref[3 * cases:, :])).astype(BF16)
+
+
+def own_local_kernel(rb_ref, inverse_ref, basis_ref, halo_ref, local_ref, coarse_ref):
+    rows = rb_ref.shape[1]
+    margin = (inverse_ref.shape[1] - rows) // 2
+    even = is_even()
+    me = position()
+    exists = (me > 0) & (me < lax.axis_size("grp") * lax.axis_size("sub") - 1)
+    halo = jnp.where(exists, halo_ref[...], jnp.zeros_like(halo_ref))
+    zero = jnp.zeros_like(halo)
+    extended = jnp.concatenate([jnp.where(even, halo, zero), rb_ref[...], jnp.where(even, zero, halo)], axis=1)
+    local_ref[...] = mm(extended, inverse_ref[0])
+    coarse_ref[...] = mm_nt(basis_ref[0], extended)
+
+
+def local_kernel(own_local_ref, own_coarse_ref, inverse_ref, basis_ref, factor_ref, plain_ref, pair_ref,
                  local_ref, message_ref):
     margin = pair_ref.shape[1]
-    halo = jnp.concatenate(from_sides(pair_ref, other_ref), axis=1)
-    ends = jnp.concatenate([basis_ref[0, :, :margin], basis_ref[0, :, basis_ref.shape[2] - margin:]], axis=1)
-    coarse_in = own_coarse_ref[...] + mm_nt(ends, halo)
+    even = is_even()
+    pair = pair_ref[...]
+    total = inverse_ref.shape[1]
+    ends = jnp.where(even, basis_ref[0, :, total - margin:], basis_ref[0, :, :margin])
+    coarse_in = own_coarse_ref[...] + mm_nt(ends, pair)
     size = coarse_in.shape[0]
     stacked = jnp.concatenate([jnp.zeros((3 * size, coarse_in.shape[1]), F32), coarse_in], axis=0)
     reduced = jnp.dot(factor_ref[...], stacked, precision=lax.Precision.HIGHEST, preferred_element_type=F32)
-    right_side = jnp.where(is_even(), coarse_in, reduced)
+    right_side = jnp.where(even, coarse_in, reduced)
     message = jnp.concatenate([plain_ref[:, :3 * size], right_side], axis=1)
     for slot in range(message_ref.shape[0]):
         message_ref[slot] = message
-    local_ref[...] = own_local_ref[...] + mm(halo, ends_ref[...])
+    rows = jnp.where(even, inverse_ref[0, total - margin:, :], inverse_ref[0, :margin, :])
+    local_ref[...] = own_local_ref[...] + mm(pair, rows)
 
 
 def reduce_rows(blocks):
@@ -431,9 +455,6 @@
     basis = jnp.swapaxes(coarse_basis, 1, 2)
     block_cols = jnp.transpose(block_cols, (2, 0, 1))
 
-    def swap(to_pair, to_other):
-        return lax.ppermute(to_pair, AXES, pairs), lax.ppermute(to_other, AXES, others)
-
     halo = struct((cases, margin), BF16)
     full = struct((cases, rows), F32)
     semaphores = pltpu.SemaphoreType.DMA
@@ -443,9 +464,7 @@
         [HBM] * 3,
         [pltpu.VMEM(coarse_up.shape, F32), semaphores((3,))],
     )(*far(iterate_in, send_rows, coarse_up))
-    got = swap(to_pair, to_other)
-    first_pair = got[0]
-    nonzero_blocks = block_cols.size
+    first_pair = lax.ppermute(to_pair, AXES, pairs)
     partial, operator, diag = call(
         own_kernel,
         [full, struct((rows, rows + 2 * margin), BF16), struct(diagonal.shape, F32)],
@@ -453,30 +472,36 @@
         [
             pltpu.SMEM(block_cols.shape, block_cols.dtype),
             pltpu.VMEM((cases, rows), F32),
-            semaphores((5 + nonzero_blocks,)),
+            pltpu.VMEM(block_values.shape, BF16),
+            semaphores((6,)),
         ],
     )(start, *far(right_side, diagonal, block_values, block_cols, couple_left, couple_right))
-    residual, rounded, *sent = call(
-        residual_kernel, [full, struct((cases, rows), BF16), halo, halo], [VMEM] * 5
-    )(partial, operator, send_rows, *got)
-    got = swap(*sent)
-    local, coarse, ends, basis, factor, plain = call(
+    known, message = call(offer_kernel, [full, struct((3 * cases + margin, margin), BF16)], [VMEM] * 5)(
+        partial, operator, send_rows, first_pair, to_other
+    )
+    first_other = lax.ppermute(message, AXES, others)
+    inverse, basis, factor, plain = call(
         inverse_kernel,
         [
-            struct((cases, extended), F32),
-            struct((modes, cases), F32),
-            struct((2 * margin, extended), BF16),
+            struct(local_inverse.shape, BF16),
             struct(basis.shape, BF16),
             struct((modes, 4 * modes), F32),
             struct((modes, 4 * modes), F32),
         ],
-        [VMEM] * 2 + [HBM] * 4,
-        [pltpu.VMEM((rows, extended), BF16), pltpu.VMEM((2, modes, modes), F32), semaphores((6,))],
-    )(rounded, first_pair, *far(local_inverse, basis, coarse_diag, coarse_up))
+        [VMEM] + [HBM] * 4,
+        [pltpu.VMEM((2, modes, modes), F32), semaphores((4,))],
+    )(first_pair, *far(local_inverse, basis, coarse_diag, coarse_up))
+    residual, rounded, to_pair, other_halo = call(
+        residual_kernel, [full, struct((cases, rows), BF16), halo, halo], [VMEM] * 6
+    )(known, operator, send_rows, to_other, first_other, plain)
+    pair_halo = lax.ppermute(to_pair, AXES, pairs)
+    local, coarse = call(own_local_kernel, [struct((cases, extended), F32), struct((modes, cases), F32)], [VMEM] * 4)(
+        rounded, inverse, basis, other_halo
+    )
     chips = members // 2
     local, message = call(
-        local_kernel, [struct((cases, extended), F32), struct((chips, modes, width), F32)], [VMEM] * 8
-    )(local, coarse, ends, basis, factor, plain, *got)
+        local_kernel, [struct((cases, extended), F32), struct((chips, modes, width), F32)], [VMEM] * 7
+    )(local, coarse, inverse, basis, factor, plain, pair_halo)
     cores = [[2 * chip + core for chip in range(chips)] for core in range(2)]
     same = lax.all_to_all(message, "sub", 0, 0, tiled=True, axis_index_groups=cores)
     opposite = lax.ppermute(same, AXES, pairs)
@@ -490,9 +515,11 @@
         [VMEM] * 5,
         [pltpu.VMEM((groups + 1, modes, cases), F32), pltpu.VMEM((members + 1, modes, cases), F32)],
     )(reduced, solved, local, basis, send_rows)
-    got = swap(*sent)
+    to_pair, to_other = sent
+    from_other = lax.ppermute(to_other, AXES, others)
+    from_pair = lax.ppermute(to_pair, AXES, pairs)
     direction, image, sums = call(image_kernel, [full, full, struct((total, 2, cases), F32)], [VMEM] * 7)(
-        correction, residual, diag, operator, send_rows, *got
+        correction, residual, diag, operator, send_rows, from_pair, from_other
     )
     sums = lax.all_to_all(sums, AXES, 0, 0, tiled=True)
     iterate, residual = call(finish_kernel, [full, full], [VMEM] * 5)(start, direction, residual, image, sums)

time: 71.7 us -> 69.5 us (0.969)
  blocking collectives: 43 us -> 41 us
  starting transfers between devices: 8.06 us -> 7.14 us
    ppermute x1, starting transfers between devices: 1.45 us -> 0.01 us  [shards(): opposite = lax.ppermute(same, AXES, pairs)]
    all_to_all x1, blocking collectives: 15.4 us -> 14.3 us  [shards(): lax.all_to_all(message, 'sub', 0, 0, tiled=True, axis_index_groups=cores)]
    all_gather x1, blocking collectives: 10.6 us -> 9.87 us  [shards(): reduced = lax.all_gather(reduced, 'grp', axis=0)]
    pallas_call x1 -> x3, Pallas kernels: 2.11 us -> 2.81 us  [the longest x1 1.7 us: shards(): call(inverse_kernel, [struct(local_inverse.shape, BF16), struct(basis.sha...]
    ppermute x6 -> x5, starting transfers between devices: 6.61 us -> 7.14 us  [the longest x1 5.17 us: shards(): pair_halo = lax.ppermute(to_pair, AXES, pairs)]
  transfers between devices with their start and end apart: 7 -> 6, of which waited for: 2 -> 3; matrix products, arithmetic and copies ran while one was open for 0% -> 0% of each run, Pallas kernels for 6% -> 6%
where the time goes in v5:
time: 69.5 us; the launch traced here: 69.2 us
  blocking collectives  41 us (59%)
  Pallas kernels  18.1 us (26%)
  starting transfers between devices  7.14 us (10%)
  waiting for transfers between devices  2.25 us (3%)
  between operations  0.75 us (1%)
    all_to_all x1, blocking collectives, shards(): sums = lax.all_to_all(sums, AXES, 0, 0, tiled=True)  16.8 us
    all_to_all x1, blocking collectives, shards(): lax.all_to_all(message, 'sub', 0, 0, tiled=True, axis_index_groups=cores)  14.3 us
    all_gather x1, blocking collectives, shards(): reduced = lax.all_gather(reduced, 'grp', axis=0)  9.87 us
    pallas_call x1, Pallas kernels, shards(): call(solve_kernel, [struct((cases, extended), F32)] + [struct((cases, 2 *...  5.33 us
    ppermute x1, starting transfers between devices, shards(): pair_halo = lax.ppermute(to_pair, AXES, pairs)  5.17 us
    pallas_call x1, Pallas kernels, shards(): call(group_kernel, [struct((members, modes, width), F32), struct((2 * mod...  2.92 us
    pallas_call x1, Pallas kernels, shards(): call(own_kernel, [full, struct((rows, rows + 2 * margin), BF16), struct(d...  2.09 us
    pallas_call x1, Pallas kernels, shards(): call(inverse_kernel, [struct(local_inverse.shape, BF16), struct(basis.sha...  1.7 us
  transfers between devices with their start and end apart: 6, of which 3 were waited for; matrix products, arithmetic and copies ran while one was open for 0% of the time, Pallas kernels for 6%

profile of v5, /device:TPU:0, one launch (start us, length us, event | category | flops | bytes accessed | tf_op | source)
XLA Modules:
  0.0 69.2 jit_solution(13658355120068830971)
XLA Ops:
  0.6 1.3 %gather_kernel.1 = (bf16[192,128]{1,0:T(8,128)(2,1)S(1)}, bf16[160,128]{1,0:T(8,128)(2,1)S(1)}, f32[160,768]{1,0:T(8,128)S(1)}, s32[1,2,128]{2,1,0:T(2,128)S(1)}) custom-call(f32[160,768]{1,0:T(8,128)} %bitcast.8, s32[1,2,128]{2,1,0:T(2,128)} %rows_hbm.1, f32[1,32,32]{2,1,0:T(8,128)} %up_hbm.3), custom_call_target="tpu_custom_call" | custom-call | tf_op jit(solution)/shard_map/gather_kernel/pallas_call | solution.py:461
  2.0 0.6 collective-permute-start
  2.5 2.1 %own_kernel.1 = (f32[160,768]{1,0:T(8,128)S(1)}, bf16[768,1024]{1,0:T(8,128)(2,1)S(1)}, f32[768]{0:T(1024)S(1)}) custom-call(f32[160,768]{1,0:T(8,128)S(1)} %get-tuple-element.33.x_ref, f32[160,768]{1,0:T(8,128)} %bitcast.9, f32[768]{0:T(1024)} %diag_hbm.2, bf16[1,6,3,128,128]{4,3,2,1,0:T(8,128)(2,1)} %values_hbm.1, s32[3,1,6]{2,1,0:T(1,128)} %bitcast.11, ...), custom_call_target="tpu_custom_call" | custom-call | tf_op jit(solution)/shard_map/own_kernel/pallas_call | solution.py:468
  4.6 0.0 collective-permute-done.pair_ref.first_pair_ref
  4.6 0.5 offer_kernel.1
  5.2 0.7 collective-permute-start.1
  5.9 1.7 %inverse_kernel.1 = (bf16[1,1024,1024]{2,1,0:T(8,128)(2,1)S(1)}, bf16[1,32,1024]{2,1,0:T(8,128)(2,1)S(1)}, f32[32,128]{1,0:T(8,128)S(1)}, f32[32,128]{1,0:T(8,128)S(1)}) custom-call(bf16[192,128]{1,0:T(8,128)(2,1)S(1)} %collective-permute-done.pair_ref.first_pair_ref, bf16[1,1024,1024]{2,1,0:T(8,128)(2,1)} %inverse_hbm.1, bf16[1,32,1024]{2,1,0:T(8,128)(2,1)} %bitcast.10, ...), custom_call_target="tpu_custom_call" | custom-call | tf_op jit(solution)/shard_map/inverse_kernel/pallas_call | solution.py:483
  7.6 0.0 collective-permute-done.1.other_ref
  7.6 0.4 residual_kernel.1
  8.0 5.2 %collective-permute-start.2 = (bf16[160,128]{1,0:T(8,128)(2,1)S(1)}, bf16[160,128]{1,0:T(8,128)(2,1)S(1)}, u32[]{:S(2)}, u32[]{:S(2)}) collective-permute-start(bf16[160,128]{1,0:T(8,128)(2,1)S(1)} %get-tuple-element.49), channel_id=1, source_target_pairs={{0,1},{1,0},{2,3},{3,2},{4,5},{5,4},{6,7},{7,6},{8,9},{9,8},{10,11... | collective-permute-start | bytes 122888 | tf_op jit(solution)/shard_map/ppermute | solution.py:497
  13.2 0.6 own_local_kernel.1
  13.7 0.3 collective-permute-done.2.pair_ref
  14.1 0.4 local_kernel.1
  14.5 14.3 %all_to_all.10.same_ref = f32[4,32,256]{2,1,0:T(8,128)S(1)} all-to-all(f32[4,32,256]{2,1,0:T(8,128)S(1)} %get-tuple-element.50), channel_id=1, replica_groups={{0,2,4,6},{1,3,5,7},{8,10,12,14},{9,11,13,15},{16,18,20,22},{17,19,21,2..., dimensions={0} | all-to-all | bytes 262144 | tf_op jit(solution)/shard_map/all_to_all | solution.py:506
  28.8 0.0 collective-permute-start.3
  28.8 1.3 %collective-permute-done.3.opposite_ref = f32[4,32,256]{2,1,0:T(8,128)S(1)} collective-permute-done((f32[4,32,256]{2,1,0:T(8,128)S(1)}, f32[4,32,256]{2,1,0:T(8,128)S(1)}, u32[]{:S(2)}, u32[]{:S(2)}) %collective-permute-start.3) | collective-permute-done | bytes 131104 | tf_op jit(solution)/shard_map/ppermute | solution.py:507
  30.2 2.9 %group_kernel.1 = (f32[8,32,256]{2,1,0:T(8,128)S(1)}, f32[64,256]{1,0:T(8,128)S(1)}) custom-call(f32[4,32,256]{2,1,0:T(8,128)S(1)} %all_to_all.10.same_ref, f32[4,32,256]{2,1,0:T(8,128)S(1)} %collective-permute-done.3.opposite_ref), custom_call_target="tpu_custom_call" | custom-call | tf_op jit(solution)/shard_map/group_kernel/pallas_call | solution.py:508
  33.1 9.9 %all-gather = f32[256,256]{1,0:T(8,128)S(1)} all-gather(f32[64,256]{1,0:T(8,128)S(1)} %get-tuple-element.51), channel_id=2, replica_groups=mesh['grp'=4,'sub'=8] {'grp'}, dimensions={0}, use_global_device_ids=true | all-gather | bytes 327680 | tf_op jit(solution)/shard_map/all_gather | solution.py:511
  43.0 5.3 %solve_kernel.1 = (f32[160,1024]{1,0:T(8,128)S(1)}, bf16[160,256]{1,0:T(8,128)(2,1)S(1)}, bf16[160,256]{1,0:T(8,128)(2,1)S(1)}) custom-call(f32[4,64,256]{2,1,0:T(8,128)S(1)} %bitcast.7, f32[8,32,256]{2,1,0:T(8,128)S(1)} %get-tuple-element.52.solved_ref, f32[160,1024]{1,0:T(8,128)S(1)} %get-tuple-element.53.local_ref, ...), custom_call_target="tpu_custom_call" | custom-call | tf_op jit(solution)/shard_map/solve_kernel/pallas_call | solution.py:512
  48.3 0.1 collective-permute-start.4
  48.4 0.7 collective-permute-start.5
  49.1 0.6 collective-permute-done.4.pair_ref
  49.7 0.0 collective-permute-done.5.other_ref
  49.7 1.6 %image_kernel.1 = (f32[160,768]{1,0:T(8,128)S(1)}, f32[160,768]{1,0:T(8,128)S(1)}, f32[32,2,160]{2,1,0:T(2,128)S(1)}) custom-call(f32[160,1024]{1,0:T(8,128)S(1)} %get-tuple-element.54.corr_ref, f32[160,768]{1,0:T(8,128)S(1)} %get-tuple-element.55.r_ref, f32[768]{0:T(1024)S(1)} %get-tuple-element.56.diag_ref, ...), custom_call_target="tpu_custom_call" | custom-call | tf_op jit(solution)/shard_map/image_kernel/pallas_call | solution.py:521
  51.3 16.8 %all_to_all.11.sums_ref = f32[32,2,160]{2,1,0:T(2,128)S(1)} all-to-all(f32[32,2,160]{2,1,0:T(2,128)S(1)} %get-tuple-element.61), channel_id=1, replica_groups=mesh['grp'=4,'sub'=8] {'grp','sub'}, dimensions={0} | all-to-all | bytes 81920 | tf_op jit(solution)/shard_map/all_to_all | solution.py:524
  68.1 1.1 %finish_kernel.1 = (f32[160,768]{1,0:T(8,128)}, f32[160,768]{1,0:T(8,128)}) custom-call(f32[160,768]{1,0:T(8,128)S(1)} %get-tuple-element.33.x_ref, f32[160,768]{1,0:T(8,128)S(1)} %get-tuple-element.59.p_ref, f32[160,768]{1,0:T(8,128)S(1)} %get-tuple-element.55.r_ref, f32[160,768]{1,0:T(8,128)S(1)} %get-tuple-element.60.image_ref, ...), custom_call_target="tpu_custom_call" | custom-call | tf_op jit(solution)/shard_map/finish_kernel/pallas_call | solution.py:525
Async XLA Ops:
  2.0 2.7 %collective-permute-start = (bf16[192,128]{1,0:T(8,128)(2,1)S(1)}, bf16[192,128]{1,0:T(8,128)(2,1)S(1)}, u32[]{:S(2)}, u32[]{:S(2)}) collective-permute-start(bf16[192,128]{1,0:T(8,128)(2,1)S(1)} %get-tuple-element.37), channel_id=1, source_target_pairs={{0,1},{1,0},{2,3},{3,2},{4,5},{5,4},{6,7},{7,6},{8,9},{9,8},{10,11... | collective-permute-start | bytes 147464 | tf_op jit(solution)/shard_map/ppermute | solution.py:467
  5.2 2.4 %collective-permute-start.1 = (bf16[608,128]{1,0:T(8,128)(2,1)S(1)}, bf16[608,128]{1,0:T(8,128)(2,1)S(1)}, u32[]{:S(2)}, u32[]{:S(2)}) collective-permute-start(bf16[608,128]{1,0:T(8,128)(2,1)S(1)} %get-tuple-element.40), channel_id=1, source_target_pairs={{1,2},{2,1},{3,4},{4,3},{5,6},{6,5},{7,8},{8,7},{9,10},{10,9},{11,... | collective-permute-start | bytes 466952 | tf_op jit(solution)/shard_map/ppermute | solution.py:482
  8.0 6.0 %collective-permute-start.2 = (bf16[160,128]{1,0:T(8,128)(2,1)S(1)}, bf16[160,128]{1,0:T(8,128)(2,1)S(1)}, u32[]{:S(2)}, u32[]{:S(2)}) collective-permute-start(bf16[160,128]{1,0:T(8,128)(2,1)S(1)} %get-tuple-element.49), channel_id=1, source_target_pairs={{0,1},{1,0},{2,3},{3,2},{4,5},{5,4},{6,7},{7,6},{8,9},{9,8},{10,11... | collective-permute-start | bytes 122888 | tf_op jit(solution)/shard_map/ppermute | solution.py:497
  28.8 1.3 %collective-permute-start.3 = (f32[4,32,256]{2,1,0:T(8,128)S(1)}, f32[4,32,256]{2,1,0:T(8,128)S(1)}, u32[]{:S(2)}, u32[]{:S(2)}) collective-permute-start(f32[4,32,256]{2,1,0:T(8,128)S(1)} %all_to_all.10.same_ref), channel_id=1, source_target_pairs={{0,1},{1,0},{2,3},{3,2},{4,5},{5,4},{6,7},{7,6},{8,9},{9,8},{10,11... | collective-permute-start | bytes 393224 | tf_op jit(solution)/shard_map/ppermute | solution.py:507
  48.3 1.3 %collective-permute-start.4 = (bf16[160,256]{1,0:T(8,128)(2,1)S(1)}, bf16[160,256]{1,0:T(8,128)(2,1)S(1)}, u32[]{:S(2)}, u32[]{:S(2)}) collective-permute-start(bf16[160,256]{1,0:T(8,128)(2,1)S(1)} %get-tuple-element.57), channel_id=1, source_target_pairs={{0,1},{1,0},{2,3},{3,2},{4,5},{5,4},{6,7},{7,6},{8,9},{9,8},{10,11... | collective-permute-start | bytes 245768 | tf_op jit(solution)/shard_map/ppermute | solution.py:520
  48.4 1.3 %collective-permute-start.5 = (bf16[160,256]{1,0:T(8,128)(2,1)S(1)}, bf16[160,256]{1,0:T(8,128)(2,1)S(1)}, u32[]{:S(2)}, u32[]{:S(2)}) collective-permute-start(bf16[160,256]{1,0:T(8,128)(2,1)S(1)} %get-tuple-element.58), channel_id=1, source_target_pairs={{1,2},{2,1},{3,4},{4,3},{5,6},{6,5},{7,8},{8,7},{9,10},{10,9},{11,... | collective-permute-start | bytes 245768 | tf_op jit(solution)/shard_map/ppermute | solution.py:519

commit v6 on v5

--- a/solution.py
+++ b/solution.py
@@ -1,11 +1,10 @@
-import functools
-
 import jax
 import jax.numpy as jnp
 from jax import lax
 from jax.experimental import pallas as pl
 from jax.experimental.pallas import tpu as pltpu
 from jax.sharding import PartitionSpec as P
+
 
 AXES = ("grp", "sub")
 BF16 = jnp.bfloat16
@@ -177,8 +176,6 @@
 
 
 def own_local_kernel(rb_ref, inverse_ref, basis_ref, halo_ref, local_ref, coarse_ref):
-    rows = rb_ref.shape[1]
-    margin = (inverse_ref.shape[1] - rows) // 2
     even = is_even()
     me = position()
     exists = (me > 0) & (me < lax.axis_size("grp") * lax.axis_size("sub") - 1)
@@ -244,15 +241,22 @@
 
 
 def shares(top, bottom, size):
-    zero = jnp.zeros((size, size), F32)
-    to_left = jnp.concatenate([top[:, size:2 * size], zero, top[:, 2 * size:]], axis=1)
-    to_right = jnp.concatenate([bottom[:, 2 * size:3 * size], bottom[:, size:2 * size], zero, bottom[:, 3 * size:]], axis=1)
-    return to_left, to_right
+    lanes = 4 * size
+    lane = lax.broadcasted_iota(jnp.int32, (size, lanes), 1)
+
+    def placed(product, slot, empty):
+        first = product[:, :lanes]
+        diag = pltpu.roll(first, lanes - slot * size, axis=1)
+        first = jnp.where(lane < size, diag, jnp.where((lane >= empty * size) & (lane < (empty + 1) * size), 0.0, first))
+        return jnp.concatenate([first, product[:, lanes:]], axis=1)
+
+    return placed(top, 1, 1), placed(bottom, 2, 2)
 
 
 def schur(block, solved, size):
-    product = -mm_t(block[:, :4 * size], solved, precision=lax.Precision.HIGHEST)
-    return shares(product[size:2 * size], product[2 * size:3 * size], size)
+    couplings = jnp.transpose(block[:, :4 * size])[size:3 * size]
+    product = -jnp.dot(couplings, solved, precision=lax.Precision.HIGHEST, preferred_element_type=F32)
+    return shares(product[:size], product[size:], size)
 
 
 def first_schur(previous, block, size):
@@ -296,7 +300,7 @@
 def back(solved, left, right, size):
     zero = jnp.zeros_like(left)
     stacked = jnp.concatenate([zero, left, right, zero], axis=0)
-    return solved[:, 3 * size:] - jnp.dot(
+    return solved - jnp.dot(
         solved[:, :4 * size], stacked, precision=lax.Precision.HIGHEST, preferred_element_type=F32)
 
 
@@ -331,7 +335,7 @@
 
 
 def solve_kernel(reduced_ref, solved_ref, local_ref, basis_ref, rows_ref,
-                 corr_ref, to_pair_ref, to_other_ref, sep_ref, x_ref):
+                 corr_ref, to_other_ref, sep_ref, x_ref):
     groups, two_size, width = reduced_ref.shape
     size = two_size // 2
     members = solved_ref.shape[0]
@@ -349,8 +353,8 @@
     chain.append(jnp.zeros((size, width), F32))
     factors = {}
     head, _ = eliminate(chain, size, factors.__setitem__)
-    solution = {count: jnp.zeros((size, width - 3 * size), F32)}
-    solution[0] = reduce_rows([head])[0][:, 3 * size:]
+    solution = {count: jnp.zeros((size, width), F32)}
+    solution[0] = reduce_rows([head])[0]
     step = count // 2
     while step >= 1:
         for j in range(step, count, 2 * step):
@@ -358,7 +362,7 @@
         step = step // 2
     for g in range(groups):
         sep_ref[g] = solution[g]
-    sep_ref[groups] = jnp.zeros((size, width - 3 * size), F32)
+    sep_ref[groups] = jnp.zeros((size, width), F32)
     group, member = lax.axis_index("grp"), lax.axis_index("sub")
     x_ref[0] = sep_ref[group]
     x_ref[members] = sep_ref[group + 1]
@@ -370,18 +374,32 @@
     odd = member // 2 * 2 + 1
     x_ref[odd] = back(solved_ref[odd], x_ref[odd - 1], x_ref[odd + 1], size)
     coarse = x_ref[member].astype(BF16)
-    correction = local_ref[...] + mm_t(coarse, basis_ref[0])
+    correction = local_ref[...] + mm_t(coarse, basis_ref[0])[3 * size:]
     corr_ref[...] = correction
-    margin = rows_ref.shape[2]
+    even = is_even()
+    to_other_ref[...] = return_rows(
+        correction, rows_ref.shape[2], jnp.where(even, rows_ref[0, 0:1, :], rows_ref[0, 1:2, :]), even)
+
+
+def return_rows(correction, margin, rows, head):
     owned = correction.shape[1] - 2 * margin
     rounded = correction.astype(BF16)
-    even = is_even()
-    head, tail = rounded[:, :margin], rounded[:, margin + owned:]
-    sent = mm(rounded[:, margin:margin + owned], send_matrix(rows_ref, owned)).astype(BF16)
-    to_pair_ref[:, :margin] = jnp.where(even, tail, head)
-    to_other_ref[:, :margin] = jnp.where(even, head, tail)
-    to_pair_ref[:, margin:] = sent[:, :margin]
-    to_other_ref[:, margin:] = sent[:, margin:]
+    tail = jnp.where(head, rounded[:, :margin], rounded[:, margin + owned:])
+    return jnp.concatenate([tail, mm(rounded[:, margin:margin + owned], place_matrix(rows, owned)).astype(BF16)], axis=1)
+
+
+def pair_kernel(corr_ref, rows_ref, to_pair_ref):
+    even = is_even()
+    to_pair_ref[...] = return_rows(
+        corr_ref[...], rows_ref.shape[2], jnp.where(even, rows_ref[0, 1:2, :], rows_ref[0, 0:1, :]), jnp.logical_not(even))
+
+
+def row_sum(values):
+    lanes = 128
+    total = values[:, :lanes]
+    for start in range(lanes, values.shape[1], lanes):
+        total = total + values[:, start:start + lanes]
+    return mm_nt(jnp.ones((8, lanes), F32), total, precision=lax.Precision.HIGHEST)
 
 
 def image_kernel(corr_ref, r_ref, diag_ref, operator_ref, rows_ref, pair_ref, other_ref, p_ref, image_ref, sums_ref):
@@ -401,9 +419,8 @@
     values = jnp.concatenate([p.astype(BF16), left, right], axis=1)
     image = diag_ref[...].reshape(1, owned) * p + mm_nt(values, operator_ref[...])
     image_ref[...] = image
-    ones = jnp.ones((8, owned), F32)
-    inner = mm_nt(ones, r_ref[...] * p, precision=lax.Precision.HIGHEST)
-    curvature = mm_nt(ones, p * image, precision=lax.Precision.HIGHEST)
+    inner = row_sum(r_ref[...] * p)
+    curvature = row_sum(p * image)
     sums = jnp.concatenate([inner[0:1], curvature[0:1]], axis=0)
     for slot in range(sums_ref.shape[0]):
         sums_ref[slot] = sums
@@ -427,7 +444,6 @@
         in_specs=in_specs,
         out_specs=[VMEM] * len(out),
         scratch_shapes=list(scratch),
-        name=kernel.__name__,
         compiler_params=pltpu.CompilerParams(vmem_limit_bytes=16 * 2**20),
     )
 
@@ -509,14 +525,15 @@
         group_kernel, [struct((members, modes, width), F32), struct((2 * modes, width), F32)], [VMEM] * 2
     )(same, opposite)
     reduced = lax.all_gather(reduced, "grp", axis=0)
-    correction, *sent = call(
+    returned = struct((cases, 2 * margin), BF16)
+    correction, to_other = call(
         solve_kernel,
-        [struct((cases, extended), F32)] + [struct((cases, 2 * margin), BF16)] * 2,
+        [struct((cases, extended), F32), returned],
         [VMEM] * 5,
-        [pltpu.VMEM((groups + 1, modes, cases), F32), pltpu.VMEM((members + 1, modes, cases), F32)],
+        [pltpu.VMEM((groups + 1, modes, width), F32), pltpu.VMEM((members + 1, modes, width), F32)],
     )(reduced, solved, local, basis, send_rows)
-    to_pair, to_other = sent
     from_other = lax.ppermute(to_other, AXES, others)
+    (to_pair,) = call(pair_kernel, [returned], [VMEM] * 2)(correction, send_rows)
     from_pair = lax.ppermute(to_pair, AXES, pairs)
     direction, image, sums = call(image_kernel, [full, full, struct((total, 2, cases), F32)], [VMEM] * 7)(
         correction, residual, diag, operator, send_rows, from_pair, from_other
@@ -527,8 +544,6 @@
 
 
 def solution(mesh):
-    whole = P(AXES)
-
     def spec(rank):
         return P(AXES, *([None] * (rank - 1)))
 

time: 69.5 us -> 67.9 us (0.977)
  Pallas kernels: 18.1 us -> 16.4 us
    pallas_call x1 -> x2, Pallas kernels: 5.33 us -> 4.4 us  [the longest x1 4.17 us: shards(): call(solve_kernel, [struct((cases, extended), F32), returned], [VMEM] * 5...]
where the time goes in v6:
time: 67.9 us; the launch traced here: 67.5 us
  blocking collectives  41 us (60%)
  Pallas kernels  16.4 us (24%)
  starting transfers between devices  7.15 us (11%)
  waiting for transfers between devices  2.22 us (3%)
  between operations  0.74 us (1%)
    all_to_all x1, blocking collectives, shards(): sums = lax.all_to_all(sums, AXES, 0, 0, tiled=True)  16.8 us
    all_to_all x1, blocking collectives, shards(): lax.all_to_all(message, 'sub', 0, 0, tiled=True, axis_index_groups=cores)  14.3 us
    all_gather x1, blocking collectives, shards(): reduced = lax.all_gather(reduced, 'grp', axis=0)  9.86 us
    ppermute x1, starting transfers between devices, shards(): pair_halo = lax.ppermute(to_pair, AXES, pairs)  5.18 us
    pallas_call x1, Pallas kernels, shards(): call(solve_kernel, [struct((cases, extended), F32), returned], [VMEM] * 5...  4.17 us
    pallas_call x1, Pallas kernels, shards(): call(group_kernel, [struct((members, modes, width), F32), struct((2 * mod...  2.6 us
    pallas_call x1, Pallas kernels, shards(): call(own_kernel, [full, struct((rows, rows + 2 * margin), BF16), struct(d...  2.09 us
    pallas_call x1, Pallas kernels, shards(): call(inverse_kernel, [struct(local_inverse.shape, BF16), struct(basis.sha...  1.7 us
  transfers between devices with their start and end apart: 6, of which 3 were waited for; matrix products, arithmetic and copies ran while one was open for 0% of the time, Pallas kernels for 6%

profile of v6, /device:TPU:0, one launch (start us, length us, event | category | flops | bytes accessed | tf_op | source)
XLA Modules:
  0.0 67.5 jit_solution(2238852579356199736)
XLA Ops:
  0.6 1.3 %shard_map.131 = (bf16[192,128]{1,0:T(8,128)(2,1)S(1)}, bf16[160,128]{1,0:T(8,128)(2,1)S(1)}, f32[160,768]{1,0:T(8,128)S(1)}, s32[1,2,128]{2,1,0:T(2,128)S(1)}) custom-call(f32[160,768]{1,0:T(8,128)} %bitcast.8, s32[1,2,128]{2,1,0:T(2,128)} %rows_hbm.1, f32[1,32,32]{2,1,0:T(8,128)} %up_hbm.3), custom_call_target="tpu_custom_call" | custom-call | tf_op jit(solution)/shard_map/pallas_call | solution.py:477
  2.0 0.6 collective-permute-start
  2.5 2.1 %shard_map.132 = (f32[160,768]{1,0:T(8,128)S(1)}, bf16[768,1024]{1,0:T(8,128)(2,1)S(1)}, f32[768]{0:T(1024)S(1)}) custom-call(f32[160,768]{1,0:T(8,128)S(1)} %get-tuple-element.32.x_ref, f32[160,768]{1,0:T(8,128)} %bitcast.9, f32[768]{0:T(1024)} %diag_hbm.2, bf16[1,6,3,128,128]{4,3,2,1,0:T(8,128)(2,1)} %values_hbm.1, s32[3,1,6]{2,1,0:T(1,128)} %bitcast.11, ...), custom_call_target="tpu_custom_call" | custom-call | tf_op jit(solution)/shard_map/pallas_call | solution.py:484
  4.6 0.0 collective-permute-done.pair_ref.first_pair_ref
  4.6 0.5 shard_map.133
  5.2 0.7 collective-permute-start.1
  5.9 1.7 %shard_map.134 = (bf16[1,1024,1024]{2,1,0:T(8,128)(2,1)S(1)}, bf16[1,32,1024]{2,1,0:T(8,128)(2,1)S(1)}, f32[32,128]{1,0:T(8,128)S(1)}, f32[32,128]{1,0:T(8,128)S(1)}) custom-call(bf16[192,128]{1,0:T(8,128)(2,1)S(1)} %collective-permute-done.pair_ref.first_pair_ref, bf16[1,1024,1024]{2,1,0:T(8,128)(2,1)} %inverse_hbm.1, bf16[1,32,1024]{2,1,0:T(8,128)(2,1)} %bitcast.10, ...), custom_call_target="tpu_custom_call" | custom-call | tf_op jit(solution)/shard_map/pallas_call | solution.py:499
  7.6 0.0 collective-permute-done.1.other_ref
  7.6 0.4 shard_map.135
  8.0 5.2 %collective-permute-start.2 = (bf16[160,128]{1,0:T(8,128)(2,1)S(1)}, bf16[160,128]{1,0:T(8,128)(2,1)S(1)}, u32[]{:S(2)}, u32[]{:S(2)}) collective-permute-start(bf16[160,128]{1,0:T(8,128)(2,1)S(1)} %get-tuple-element.48), channel_id=1, source_target_pairs={{0,1},{1,0},{2,3},{3,2},{4,5},{5,4},{6,7},{7,6},{8,9},{9,8},{10,11... | collective-permute-start | bytes 122888 | tf_op jit(solution)/shard_map/ppermute | solution.py:513
  13.2 0.6 shard_map.136
  13.8 0.3 collective-permute-done.2.pair_ref
  14.1 0.4 shard_map.137
  14.5 14.3 %all_to_all.10.same_ref = f32[4,32,256]{2,1,0:T(8,128)S(1)} all-to-all(f32[4,32,256]{2,1,0:T(8,128)S(1)} %get-tuple-element.49), channel_id=1, replica_groups={{0,2,4,6},{1,3,5,7},{8,10,12,14},{9,11,13,15},{16,18,20,22},{17,19,21,2..., dimensions={0} | all-to-all | bytes 262144 | tf_op jit(solution)/shard_map/all_to_all | solution.py:522
  28.8 0.0 collective-permute-start.3
  28.8 1.3 %collective-permute-done.3.opposite_ref = f32[4,32,256]{2,1,0:T(8,128)S(1)} collective-permute-done((f32[4,32,256]{2,1,0:T(8,128)S(1)}, f32[4,32,256]{2,1,0:T(8,128)S(1)}, u32[]{:S(2)}, u32[]{:S(2)}) %collective-permute-start.3) | collective-permute-done | bytes 131104 | tf_op jit(solution)/shard_map/ppermute | solution.py:523
  30.2 2.6 %shard_map.138 = (f32[8,32,256]{2,1,0:T(8,128)S(1)}, f32[64,256]{1,0:T(8,128)S(1)}) custom-call(f32[4,32,256]{2,1,0:T(8,128)S(1)} %all_to_all.10.same_ref, f32[4,32,256]{2,1,0:T(8,128)S(1)} %collective-permute-done.3.opposite_ref), custom_call_target="tpu_custom_call" | custom-call | tf_op jit(solution)/shard_map/pallas_call | solution.py:524
  32.8 9.9 %all-gather = f32[256,256]{1,0:T(8,128)S(1)} all-gather(f32[64,256]{1,0:T(8,128)S(1)} %get-tuple-element.50), channel_id=2, replica_groups=mesh['grp'=4,'sub'=8] {'grp'}, dimensions={0}, use_global_device_ids=true | all-gather | bytes 327680 | tf_op jit(solution)/shard_map/all_gather | solution.py:527
  42.6 4.2 %shard_map.139 = (f32[160,1024]{1,0:T(8,128)S(1)}, bf16[160,256]{1,0:T(8,128)(2,1)S(1)}) custom-call(f32[4,64,256]{2,1,0:T(8,128)S(1)} %bitcast.7, f32[8,32,256]{2,1,0:T(8,128)S(1)} %get-tuple-element.51.solved_ref, f32[160,1024]{1,0:T(8,128)S(1)} %get-tuple-element.52.local_ref, bf16[1,32,1024]{2,1,0:T(8,128)(2,1)S(1)} %get-tuple-element.43.basis_ref, ...), custom_call_target="tpu_custom_call" | custom-call | tf_op jit(solution)/shard_map/pallas_call | solution.py:529
  46.8 0.2 shard_map.140
  47.0 0.1 collective-permute-start.4
  47.1 0.7 collective-permute-start.5
  47.8 0.6 collective-permute-done.4.pair_ref
  48.4 0.0 collective-permute-done.5.other_ref
  48.4 1.2 %shard_map.141 = (f32[160,768]{1,0:T(8,128)S(1)}, f32[160,768]{1,0:T(8,128)S(1)}, f32[32,2,160]{2,1,0:T(2,128)S(1)}) custom-call(f32[160,1024]{1,0:T(8,128)S(1)} %get-tuple-element.53.corr_ref, f32[160,768]{1,0:T(8,128)S(1)} %get-tuple-element.54.r_ref, f32[768]{0:T(1024)S(1)} %get-tuple-element.55.diag_ref, ...), custom_call_target="tpu_custom_call" | custom-call | tf_op jit(solution)/shard_map/pallas_call | solution.py:538
  49.6 16.8 %all_to_all.11.sums_ref = f32[32,2,160]{2,1,0:T(2,128)S(1)} all-to-all(f32[32,2,160]{2,1,0:T(2,128)S(1)} %get-tuple-element.59), channel_id=1, replica_groups=mesh['grp'=4,'sub'=8] {'grp','sub'}, dimensions={0} | all-to-all | bytes 81920 | tf_op jit(solution)/shard_map/all_to_all | solution.py:541
  66.4 1.1 %shard_map.142 = (f32[160,768]{1,0:T(8,128)}, f32[160,768]{1,0:T(8,128)}) custom-call(f32[160,768]{1,0:T(8,128)S(1)} %get-tuple-element.32.x_ref, f32[160,768]{1,0:T(8,128)S(1)} %get-tuple-element.57.p_ref, f32[160,768]{1,0:T(8,128)S(1)} %get-tuple-element.54.r_ref, f32[160,768]{1,0:T(8,128)S(1)} %get-tuple-element.58.image_ref, ...), custom_call_target="tpu_custom_call" | custom-call | tf_op jit(solution)/shard_map/pallas_call | solution.py:542
Async XLA Ops:
  2.0 2.7 %collective-permute-start = (bf16[192,128]{1,0:T(8,128)(2,1)S(1)}, bf16[192,128]{1,0:T(8,128)(2,1)S(1)}, u32[]{:S(2)}, u32[]{:S(2)}) collective-permute-start(bf16[192,128]{1,0:T(8,128)(2,1)S(1)} %get-tuple-element.36), channel_id=1, source_target_pairs={{0,1},{1,0},{2,3},{3,2},{4,5},{5,4},{6,7},{7,6},{8,9},{9,8},{10,11... | collective-permute-start | bytes 147464 | tf_op jit(solution)/shard_map/ppermute | solution.py:483
  5.2 2.4 %collective-permute-start.1 = (bf16[608,128]{1,0:T(8,128)(2,1)S(1)}, bf16[608,128]{1,0:T(8,128)(2,1)S(1)}, u32[]{:S(2)}, u32[]{:S(2)}) collective-permute-start(bf16[608,128]{1,0:T(8,128)(2,1)S(1)} %get-tuple-element.39), channel_id=1, source_target_pairs={{1,2},{2,1},{3,4},{4,3},{5,6},{6,5},{7,8},{8,7},{9,10},{10,9},{11,... | collective-permute-start | bytes 466952 | tf_op jit(solution)/shard_map/ppermute | solution.py:498
  8.0 6.1 %collective-permute-start.2 = (bf16[160,128]{1,0:T(8,128)(2,1)S(1)}, bf16[160,128]{1,0:T(8,128)(2,1)S(1)}, u32[]{:S(2)}, u32[]{:S(2)}) collective-permute-start(bf16[160,128]{1,0:T(8,128)(2,1)S(1)} %get-tuple-element.48), channel_id=1, source_target_pairs={{0,1},{1,0},{2,3},{3,2},{4,5},{5,4},{6,7},{7,6},{8,9},{9,8},{10,11... | collective-permute-start | bytes 122888 | tf_op jit(solution)/shard_map/ppermute | solution.py:513
  28.8 1.3 %collective-permute-start.3 = (f32[4,32,256]{2,1,0:T(8,128)S(1)}, f32[4,32,256]{2,1,0:T(8,128)S(1)}, u32[]{:S(2)}, u32[]{:S(2)}) collective-permute-start(f32[4,32,256]{2,1,0:T(8,128)S(1)} %all_to_all.10.same_ref), channel_id=1, source_target_pairs={{0,1},{1,0},{2,3},{3,2},{4,5},{5,4},{6,7},{7,6},{8,9},{9,8},{10,11... | collective-permute-start | bytes 393224 | tf_op jit(solution)/shard_map/ppermute | solution.py:523
  47.0 1.3 %collective-permute-start.4 = (bf16[160,256]{1,0:T(8,128)(2,1)S(1)}, bf16[160,256]{1,0:T(8,128)(2,1)S(1)}, u32[]{:S(2)}, u32[]{:S(2)}) collective-permute-start(bf16[160,256]{1,0:T(8,128)(2,1)S(1)} %shard_map.140), channel_id=1, source_target_pairs={{0,1},{1,0},{2,3},{3,2},{4,5},{5,4},{6,7},{7,6},{8,9},{9,8},{10,11... | collective-permute-start | bytes 245768 | tf_op jit(solution)/shard_map/ppermute | solution.py:537
  47.1 1.3 %collective-permute-start.5 = (bf16[160,256]{1,0:T(8,128)(2,1)S(1)}, bf16[160,256]{1,0:T(8,128)(2,1)S(1)}, u32[]{:S(2)}, u32[]{:S(2)}) collective-permute-start(bf16[160,256]{1,0:T(8,128)(2,1)S(1)} %get-tuple-element.56), channel_id=1, source_target_pairs={{1,2},{2,1},{3,4},{4,3},{5,6},{6,5},{7,8},{8,7},{9,10},{10,9},{11,... | collective-permute-start | bytes 245768 | tf_op jit(solution)/shard_map/ppermute | solution.py:535

commit v7 on v6

--- a/solution.py
+++ b/solution.py
@@ -66,45 +66,47 @@
     return high, middle, (rest - middle.astype(F32)).astype(BF16)
 
 
-def gather_kernel(x_hbm, rows_hbm, up_hbm, to_pair_ref, to_other_ref, x_ref, rows_ref, up_ref, sems):
-    for copy in copy_all([(rows_hbm, rows_ref), (up_hbm, up_ref), (x_hbm, x_ref)], sems):
+def load_kernel(x_hbm, rows_hbm, up_hbm, b_hbm, diag_hbm, values_hbm, cols_hbm, cl_hbm, cr_hbm,
+                to_pair_ref, to_other_ref, x_ref, rows_ref, b_ref, diag_ref, operator_ref,
+                up_ref, cols_ref, values_ref, sems):
+    blocks, nonzeros, size = values_hbm.shape[1], values_hbm.shape[2], values_hbm.shape[3]
+    cases, rows = x_ref.shape
+    margin = rows_ref.shape[2]
+    copies = copy_all(
+        [
+            (rows_hbm, rows_ref),
+            (x_hbm, x_ref),
+            (up_hbm, up_ref),
+            (cols_hbm, cols_ref),
+            (values_hbm, values_ref),
+            (cl_hbm, operator_ref.at[:, rows:rows + margin]),
+            (cr_hbm, operator_ref.at[:, rows + margin:]),
+            (diag_hbm, diag_ref),
+            (b_hbm, b_ref),
+        ],
+        sems,
+    )
+    operator_ref[:, :rows] = jnp.zeros((rows, rows), BF16)
+    for copy in copies[:3]:
         copy.wait()
-    values = x_ref[...].astype(BF16)
-    cases = values.shape[0]
-    margin = rows_ref.shape[2]
-    sent = mm(values, send_matrix(rows_ref, values.shape[1])).astype(BF16)
+    sent = mm(x_ref[...].astype(BF16), send_matrix(rows_ref, rows)).astype(BF16)
     to_pair_ref[:cases, :] = sent[:, :margin]
     to_other_ref[...] = sent[:, margin:]
     parts = [part.astype(F32) for part in split_three(up_ref[0])]
-    size = up_ref.shape[1]
-    parts.append(jnp.zeros((size, margin - 3 * size), F32))
+    modes = up_ref.shape[1]
+    parts.append(jnp.zeros((modes, margin - 3 * modes), F32))
     to_pair_ref[cases:, :] = jnp.concatenate(parts, axis=1).astype(BF16)
-
-
-def own_kernel(x_ref, b_hbm, diag_hbm, values_hbm, cols_hbm, cl_hbm, cr_hbm,
-               partial_ref, operator_ref, diag_ref, cols_ref, b_ref, values_ref, sems):
-    blocks, nonzeros, size = values_hbm.shape[1], values_hbm.shape[2], values_hbm.shape[3]
-    rows = x_ref.shape[1]
-    margin = cl_hbm.shape[1]
-    copies = copy_all(
-        [
-            (cols_hbm, cols_ref),
-            (values_hbm, values_ref),
-            (b_hbm, b_ref),
-            (diag_hbm, diag_ref),
-            (cl_hbm, operator_ref.at[:, rows:rows + margin]),
-            (cr_hbm, operator_ref.at[:, rows + margin:]),
-        ],
-        sems,
-    )
-    operator_ref[:, :rows] = jnp.zeros((rows, rows), BF16)
-    for copy in copies:
+    for copy in copies[3:]:
         copy.wait()
     for i in range(blocks):
         for t in range(nonzeros):
             start = pl.multiple_of(cols_ref[t, 0, i] * size, size)
             operator_ref[i * size:(i + 1) * size, pl.ds(start, size)] = values_ref[0, i, t]
+
+
+def own_kernel(x_ref, b_ref, diag_ref, operator_ref, partial_ref):
     x = x_ref[...]
+    rows = x.shape[1]
     diag = diag_ref[...].reshape(1, rows)
     partial_ref[...] = b_ref[...] - diag * x - mm_nt(x.astype(BF16), operator_ref[:, :rows])
 
@@ -199,8 +201,7 @@
     reduced = jnp.dot(factor_ref[...], stacked, precision=lax.Precision.HIGHEST, preferred_element_type=F32)
     right_side = jnp.where(even, coarse_in, reduced)
     message = jnp.concatenate([plain_ref[:, :3 * size], right_side], axis=1)
-    for slot in range(message_ref.shape[0]):
-        message_ref[slot] = message
+    message_ref[...] = message
     rows = jnp.where(even, inverse_ref[0, total - margin:, :], inverse_ref[0, :margin, :])
     local_ref[...] = own_local_ref[...] + mm(pair, rows)
 
@@ -311,14 +312,16 @@
     return total
 
 
-def group_kernel(same_ref, opposite_ref, solved_ref, message_ref):
-    half, size, width = same_ref.shape
+def group_kernel(*refs):
+    *received, solved_ref, message_ref, blocks_ref = refs
+    half = len(received) // 2
+    size, width = received[0].shape
     members = 2 * half
-    even = is_even()
-    chain = []
-    for j in range(half):
-        same, opposite = same_ref[j], opposite_ref[j]
-        chain += [jnp.where(even, same, opposite), jnp.where(even, opposite, same)]
+    member = lax.axis_index("sub")
+    for d in range(half):
+        blocks_ref[member ^ (2 * d)] = received[d][...]
+        blocks_ref[member ^ (2 * d + 1)] = received[half + d][...]
+    chain = [blocks_ref[j] for j in range(members)]
     chain.append(jnp.zeros((size, width), F32))
 
     def keep(j, solved):
@@ -334,16 +337,19 @@
     message_ref[size:, :] = tail
 
 
-def solve_kernel(reduced_ref, solved_ref, local_ref, basis_ref, rows_ref,
-                 corr_ref, to_other_ref, sep_ref, x_ref):
-    groups, two_size, width = reduced_ref.shape
+def solve_kernel(*refs):
+    *received, solved_ref, local_ref, basis_ref, rows_ref, corr_ref, to_other_ref, messages_ref, sep_ref, x_ref = refs
+    groups = len(received)
+    two_size, width = received[0].shape
     size = two_size // 2
     members = solved_ref.shape[0]
+    for d in range(groups):
+        messages_ref[lax.axis_index("grp") ^ d] = received[d][...]
     chain = []
     for g in range(groups):
-        total = reduced_ref[g, :size, :]
+        total = messages_ref[g, :size, :]
         if g:
-            total = total + reduced_ref[g - 1, size:, :]
+            total = total + messages_ref[g - 1, size:, :]
         chain.append(total)
     count = padded(groups)
     row = lax.broadcasted_iota(jnp.int32, (size, width), 0)
@@ -474,24 +480,29 @@
     halo = struct((cases, margin), BF16)
     full = struct((cases, rows), F32)
     semaphores = pltpu.SemaphoreType.DMA
-    to_pair, to_other, start, send_rows = call(
-        gather_kernel,
-        [struct((cases + modes, margin), BF16), halo, full, struct(send_rows.shape, send_rows.dtype)],
-        [HBM] * 3,
-        [pltpu.VMEM(coarse_up.shape, F32), semaphores((3,))],
-    )(*far(iterate_in, send_rows, coarse_up))
+    to_pair, to_other, start, send_rows, loads, diag, operator = call(
+        load_kernel,
+        [
+            struct((cases + modes, margin), BF16),
+            halo,
+            full,
+            struct(send_rows.shape, send_rows.dtype),
+            full,
+            struct(diagonal.shape, F32),
+            struct((rows, rows + 2 * margin), BF16),
+        ],
+        [HBM] * 9,
+        [
+            pltpu.VMEM(coarse_up.shape, F32),
+            pltpu.SMEM(block_cols.shape, block_cols.dtype),
+            pltpu.VMEM(block_values.shape, BF16),
+            semaphores((9,)),
+        ],
+    )(*far(
+        iterate_in, send_rows, coarse_up, right_side, diagonal, block_values, block_cols, couple_left, couple_right
+    ))
     first_pair = lax.ppermute(to_pair, AXES, pairs)
-    partial, operator, diag = call(
-        own_kernel,
-        [full, struct((rows, rows + 2 * margin), BF16), struct(diagonal.shape, F32)],
-        [VMEM] + [HBM] * 6,
-        [
-            pltpu.SMEM(block_cols.shape, block_cols.dtype),
-            pltpu.VMEM((cases, rows), F32),
-            pltpu.VMEM(block_values.shape, BF16),
-            semaphores((6,)),
-        ],
-    )(start, *far(right_side, diagonal, block_values, block_cols, couple_left, couple_right))
+    (partial,) = call(own_kernel, [full], [VMEM] * 4)(start, loads, diag, operator)
     known, message = call(offer_kernel, [full, struct((3 * cases + margin, margin), BF16)], [VMEM] * 5)(
         partial, operator, send_rows, first_pair, to_other
     )
@@ -516,22 +527,34 @@
     )
     chips = members // 2
     local, message = call(
-        local_kernel, [struct((cases, extended), F32), struct((chips, modes, width), F32)], [VMEM] * 7
+        local_kernel, [struct((cases, extended), F32), struct((modes, width), F32)], [VMEM] * 7
     )(local, coarse, inverse, basis, factor, plain, pair_halo)
-    cores = [[2 * chip + core for chip in range(chips)] for core in range(2)]
-    same = lax.all_to_all(message, "sub", 0, 0, tiled=True, axis_index_groups=cores)
-    opposite = lax.ppermute(same, AXES, pairs)
+
+    def partners(value, stride, count):
+        swaps = [[(i, i ^ (stride * d)) for i in range(total)] for d in range(1, count)]
+        return [value] + [lax.ppermute(value, AXES, swap) for swap in swaps]
+
+    same = partners(message, 2, chips)
+    opposite = [lax.ppermute(value, AXES, pairs) for value in same]
+    block = pltpu.VMEM((members, modes, width), F32)
     solved, reduced = call(
-        group_kernel, [struct((members, modes, width), F32), struct((2 * modes, width), F32)], [VMEM] * 2
-    )(same, opposite)
-    reduced = lax.all_gather(reduced, "grp", axis=0)
+        group_kernel,
+        [struct((members, modes, width), F32), struct((2 * modes, width), F32)],
+        [VMEM] * members,
+        [block],
+    )(*same, *opposite)
+    reduced = partners(reduced, members, groups)
     returned = struct((cases, 2 * margin), BF16)
     correction, to_other = call(
         solve_kernel,
         [struct((cases, extended), F32), returned],
-        [VMEM] * 5,
-        [pltpu.VMEM((groups + 1, modes, width), F32), pltpu.VMEM((members + 1, modes, width), F32)],
-    )(reduced, solved, local, basis, send_rows)
+        [VMEM] * (groups + 4),
+        [
+            pltpu.VMEM((groups, 2 * modes, width), F32),
+            pltpu.VMEM((groups + 1, modes, width), F32),
+            pltpu.VMEM((members + 1, modes, width), F32),
+        ],
+    )(*reduced, solved, local, basis, send_rows)
     from_other = lax.ppermute(to_other, AXES, others)
     (to_pair,) = call(pair_kernel, [returned], [VMEM] * 2)(correction, send_rows)
     from_pair = lax.ppermute(to_pair, AXES, pairs)

time: 67.9 us -> 63.5 us (0.935)
  blocking collectives: 41 us -> 17.5 us
  starting transfers between devices: 7.15 us -> 19.1 us
  waiting for transfers between devices: 2.22 us -> 10.5 us
  Pallas kernels: 16.4 us -> 15.3 us
    all_to_all x1 -> x0, blocking collectives: 14.3 us -> none  [shards(): lax.all_to_all(message, 'sub', 0, 0, tiled=True, axis_index_groups=cores)]
    ppermute x1 -> x10, starting transfers between devices: 0.01 us -> 11.6 us  [the longest x6 11.1 us: partners(): return [value] + [lax.ppermute(value, AXES, swap) for swap in swaps]]
    all_gather x1 -> x0, blocking collectives: 9.86 us -> none  [shards(): reduced = lax.all_gather(reduced, 'grp', axis=0)]
    ppermute x1 -> x10, waiting for transfers between devices: 1.35 us -> 9.29 us  [the longest x6 8.43 us: partners(): return [value] + [lax.ppermute(value, AXES, swap) for swap in swaps]]
    pallas_call x4, Pallas kernels: 8.04 us -> 6.95 us  [the longest x1 4.19 us: shards(): call(solve_kernel, [struct((cases, extended), F32), returned], [VMEM] * (...]
    all_to_all x1, blocking collectives: 16.8 us -> 17.5 us  [shards(): sums = lax.all_to_all(sums, AXES, 0, 0, tiled=True)]
  transfers between devices with their start and end apart: 6 -> 15, of which waited for: 3 -> 10; matrix products, arithmetic and copies ran while one was open for 0% -> 0% of each run, Pallas kernels for 6% -> 4%
where the time goes in v7:
time: 63.5 us; the launch traced here: 63.2 us
  starting transfers between devices  19.1 us (30%)
  blocking collectives  17.5 us (28%)
  Pallas kernels  15.3 us (24%)
  waiting for transfers between devices  10.5 us (17%)
  between operations  0.74 us (1%)
    all_to_all x1, blocking collectives, shards(): sums = lax.all_to_all(sums, AXES, 0, 0, tiled=True)  17.5 us
    ppermute x6, starting transfers between devices, partners(): return [value] + [lax.ppermute(value, AXES, swap) for swap in swaps]  11.1 us
    ppermute x6, waiting for transfers between devices, partners(): return [value] + [lax.ppermute(value, AXES, swap) for swap in swaps]  8.43 us
    ppermute x1, starting transfers between devices, shards(): pair_halo = lax.ppermute(to_pair, AXES, pairs)  5.51 us
    pallas_call x1, Pallas kernels, shards(): call(solve_kernel, [struct((cases, extended), F32), returned], [VMEM] * (...  4.19 us
    pallas_call x1, Pallas kernels, shards(): call(group_kernel, [struct((members, modes, width), F32), struct((2 * mod...  2.62 us
    pallas_call x1, Pallas kernels, shards(): call(load_kernel, [struct((cases + modes, margin), BF16), halo, full, str...  1.76 us
    pallas_call x1, Pallas kernels, shards(): call(inverse_kernel, [struct(local_inverse.shape, BF16), struct(basis.sha...  1.7 us
  transfers between devices with their start and end apart: 15, of which 10 were waited for; matrix products, arithmetic and copies ran while one was open for 0% of the time, Pallas kernels for 4%

profile of v7, /device:TPU:0, one launch (start us, length us, event | category | flops | bytes accessed | tf_op | source)
XLA Modules:
  0.0 63.2 jit_solution(8419343853347892834)
XLA Ops:
  0.6 1.8 %shard_map.131 = (bf16[192,128]{1,0:T(8,128)(2,1)S(1)}, bf16[160,128]{1,0:T(8,128)(2,1)S(1)}, f32[160,768]{1,0:T(8,128)S(1)}, s32[1,2,128]{2,1,0:T(2,128)S(1)}, ...) custom-call(f32[160,768]{1,0:T(8,128)} %bitcast.6, s32[1,2,128]{2,1,0:T(2,128)} %rows_hbm.1, ...), custom_call_target="tpu_custom_call" | custom-call | tf_op jit(solution)/shard_map/pallas_call | solution.py:483
  2.4 0.6 collective-permute-start
  3.0 0.6 shard_map.132.partial_ref
  3.5 0.3 collective-permute-done.pair_ref.first_pair_ref
  3.8 0.5 shard_map.133
  4.4 0.7 %collective-permute-start.1 = (bf16[608,128]{1,0:T(8,128)(2,1)S(1)}, bf16[608,128]{1,0:T(8,128)(2,1)S(1)}, u32[]{:S(2)}, u32[]{:S(2)}) collective-permute-start(bf16[608,128]{1,0:T(8,128)(2,1)S(1)} %get-tuple-element.40), channel_id=1, source_target_pairs={{1,2},{2,1},{3,4},{4,3},{5,6},{6,5},{7,8},{8,7},{9,10},{10,9},{11,... | collective-permute-start | bytes 466952 | tf_op jit(solution)/shard_map/ppermute | solution.py:509
  5.1 1.7 %shard_map.134 = (bf16[1,1024,1024]{2,1,0:T(8,128)(2,1)S(1)}, bf16[1,32,1024]{2,1,0:T(8,128)(2,1)S(1)}, f32[32,128]{1,0:T(8,128)S(1)}, f32[32,128]{1,0:T(8,128)S(1)}) custom-call(bf16[192,128]{1,0:T(8,128)(2,1)S(1)} %collective-permute-done.pair_ref.first_pair_ref, bf16[1,1024,1024]{2,1,0:T(8,128)(2,1)} %inverse_hbm.1, bf16[1,32,1024]{2,1,0:T(8,128)(2,1)} %bitcast.8, ...), custom_call_target="tpu_custom_call" | custom-call | tf_op jit(solution)/shard_map/pallas_call | solution.py:510
  6.8 0.0 collective-permute-done.1.other_ref
  6.8 0.4 shard_map.135
  7.2 5.5 %collective-permute-start.2 = (bf16[160,128]{1,0:T(8,128)(2,1)S(1)}, bf16[160,128]{1,0:T(8,128)(2,1)S(1)}, u32[]{:S(2)}, u32[]{:S(2)}) collective-permute-start(bf16[160,128]{1,0:T(8,128)(2,1)S(1)} %get-tuple-element.49), channel_id=1, source_target_pairs={{0,1},{1,0},{2,3},{3,2},{4,5},{5,4},{6,7},{7,6},{8,9},{9,8},{10,11... | collective-permute-start | bytes 122888 | tf_op jit(solution)/shard_map/ppermute | solution.py:524
  12.7 0.6 shard_map.136
  13.3 0.3 collective-permute-done.2.pair_ref
  13.6 0.4 shard_map.137
  14.0 6.6 %collective-permute-start.5 = (f32[32,256]{1,0:T(8,128)S(1)}, f32[32,256]{1,0:T(8,128)S(1)}, u32[]{:S(2)}, u32[]{:S(2)}) collective-permute-start(f32[32,256]{1,0:T(8,128)S(1)} %get-tuple-element.50.refs_0_), channel_id=1, source_target_pairs={{0,6},{1,7},{2,4},{3,5},{4,2},{5,3},{6,0},{7,1},{8,14},{9,15},{10,... | collective-permute-start | bytes 98312 | tf_op jit(solution)/shard_map/ppermute | solution.py:535
  20.6 0.0 collective-permute-start.4
  20.6 0.6 %collective-permute-start.3 = (f32[32,256]{1,0:T(8,128)S(1)}, f32[32,256]{1,0:T(8,128)S(1)}, u32[]{:S(2)}, u32[]{:S(2)}) collective-permute-start(f32[32,256]{1,0:T(8,128)S(1)} %get-tuple-element.50.refs_0_), channel_id=1, source_target_pairs={{0,2},{1,3},{2,0},{3,1},{4,6},{5,7},{6,4},{7,5},{8,10},{9,11},{10,... | collective-permute-start | bytes 98312 | tf_op jit(solution)/shard_map/ppermute | solution.py:535
  21.2 0.0 collective-permute-start.6
  21.2 1.6 %collective-permute-done.5.refs_3_ = f32[32,256]{1,0:T(8,128)S(1)} collective-permute-done((f32[32,256]{1,0:T(8,128)S(1)}, f32[32,256]{1,0:T(8,128)S(1)}, u32[]{:S(2)}, u32[]{:S(2)}) %collective-permute-start.5) | collective-permute-done | bytes 32800 | tf_op jit(solution)/shard_map/ppermute | solution.py:535
  22.8 0.0 collective-permute-start.9
  22.8 2.6 %collective-permute-done.4.refs_2_ = f32[32,256]{1,0:T(8,128)S(1)} collective-permute-done((f32[32,256]{1,0:T(8,128)S(1)}, f32[32,256]{1,0:T(8,128)S(1)}, u32[]{:S(2)}, u32[]{:S(2)}) %collective-permute-start.4) | collective-permute-done | bytes 32800 | tf_op jit(solution)/shard_map/ppermute | solution.py:535
  25.4 0.0 collective-permute-start.8
  25.4 0.0 collective-permute-done.3.refs_1_
  25.4 0.5 collective-permute-start.7
  25.9 0.0 collective-permute-done.6.refs_4_
  25.9 0.0 collective-permute-done.9.refs_7_
  25.9 0.7 %collective-permute-done.8.refs_6_ = f32[32,256]{1,0:T(8,128)S(1)} collective-permute-done((f32[32,256]{1,0:T(8,128)S(1)}, f32[32,256]{1,0:T(8,128)S(1)}, u32[]{:S(2)}, u32[]{:S(2)}) %collective-permute-start.8) | collective-permute-done | bytes 32800 | tf_op jit(solution)/shard_map/ppermute | solution.py:538
  26.6 0.2 collective-permute-done.7.refs_5_
  26.8 2.6 %shard_map.138 = (f32[8,32,256]{2,1,0:T(8,128)S(1)}, f32[64,256]{1,0:T(8,128)S(1)}) custom-call(f32[32,256]{1,0:T(8,128)S(1)} %get-tuple-element.50.refs_0_, f32[32,256]{1,0:T(8,128)S(1)} %collective-permute-done.3.refs_1_, f32[32,256]{1,0:T(8,128)S(1)} %collective-permute-done.4.refs_2_, f32[32,256]{1,0:T(8,128)S(1)} %collective-permute-done.5.refs_3_, ...), custom_call_target="tpu_custom_call" | custom-call | tf_op jit(solution)/shard_map/pallas_call | solution.py:540
  29.4 1.9 %collective-permute-start.12 = (f32[64,256]{1,0:T(8,128)S(1)}, f32[64,256]{1,0:T(8,128)S(1)}, u32[]{:S(2)}, u32[]{:S(2)}) collective-permute-start(f32[64,256]{1,0:T(8,128)S(1)} %get-tuple-element.51.refs_0_), channel_id=1, source_target_pairs={{0,24},{1,25},{2,26},{3,27},{4,28},{5,29},{6,30},{7,31},{8,16},{9,... | collective-permute-start | bytes 196616 | tf_op jit(solution)/shard_map/ppermute | solution.py:535
  31.3 2.0 %collective-permute-start.11 = (f32[64,256]{1,0:T(8,128)S(1)}, f32[64,256]{1,0:T(8,128)S(1)}, u32[]{:S(2)}, u32[]{:S(2)}) collective-permute-start(f32[64,256]{1,0:T(8,128)S(1)} %get-tuple-element.51.refs_0_), channel_id=1, source_target_pairs={{0,16},{1,17},{2,18},{3,19},{4,20},{5,21},{6,22},{7,23},{8,24},{9,... | collective-permute-start | bytes 196616 | tf_op jit(solution)/shard_map/ppermute | solution.py:535
  33.3 0.0 collective-permute-start.10
  33.3 1.4 %collective-permute-done.12.refs_3_ = f32[64,256]{1,0:T(8,128)S(1)} collective-permute-done((f32[64,256]{1,0:T(8,128)S(1)}, f32[64,256]{1,0:T(8,128)S(1)}, u32[]{:S(2)}, u32[]{:S(2)}) %collective-permute-start.12) | collective-permute-done | bytes 65568 | tf_op jit(solution)/shard_map/ppermute | solution.py:535
  34.8 1.4 %collective-permute-done.11.refs_2_ = f32[64,256]{1,0:T(8,128)S(1)} collective-permute-done((f32[64,256]{1,0:T(8,128)S(1)}, f32[64,256]{1,0:T(8,128)S(1)}, u32[]{:S(2)}, u32[]{:S(2)}) %collective-permute-start.11) | collective-permute-done | bytes 65568 | tf_op jit(solution)/shard_map/ppermute | solution.py:535
  36.1 1.5 %collective-permute-done.10.refs_1_ = f32[64,256]{1,0:T(8,128)S(1)} collective-permute-done((f32[64,256]{1,0:T(8,128)S(1)}, f32[64,256]{1,0:T(8,128)S(1)}, u32[]{:S(2)}, u32[]{:S(2)}) %collective-permute-start.10) | collective-permute-done | bytes 65568 | tf_op jit(solution)/shard_map/ppermute | solution.py:535
  37.6 4.2 %shard_map.139 = (f32[160,1024]{1,0:T(8,128)S(1)}, bf16[160,256]{1,0:T(8,128)(2,1)S(1)}) custom-call(f32[64,256]{1,0:T(8,128)S(1)} %get-tuple-element.51.refs_0_, f32[64,256]{1,0:T(8,128)S(1)} %collective-permute-done.10.refs_1_, f32[64,256]{1,0:T(8,128)S(1)} %collective-permute-done.11.refs_2_, f32[64,256]{1,0:T(8,128)S(1)} %collective-permute-done.12.refs_3_, ...), custom_call_target="tpu_custom_call" | custom-call | tf_op jit(solution)/shard_map/pallas_call | solution.py:548
  41.8 0.2 shard_map.140
  42.0 0.1 collective-permute-start.13
  42.1 0.7 %collective-permute-start.14 = (bf16[160,256]{1,0:T(8,128)(2,1)S(1)}, bf16[160,256]{1,0:T(8,128)(2,1)S(1)}, u32[]{:S(2)}, u32[]{:S(2)}) collective-permute-start(bf16[160,256]{1,0:T(8,128)(2,1)S(1)} %get-tuple-element.56), channel_id=1, source_target_pairs={{1,2},{2,1},{3,4},{4,3},{5,6},{6,5},{7,8},{8,7},{9,10},{10,9},{11,... | collective-permute-start | bytes 245768 | tf_op jit(solution)/shard_map/ppermute | solution.py:558
  42.8 0.6 collective-permute-done.13.pair_ref
  43.4 0.0 collective-permute-done.14.other_ref
  43.4 1.2 %shard_map.141 = (f32[160,768]{1,0:T(8,128)S(1)}, f32[160,768]{1,0:T(8,128)S(1)}, f32[32,2,160]{2,1,0:T(2,128)S(1)}) custom-call(f32[160,1024]{1,0:T(8,128)S(1)} %get-tuple-element.54.corr_ref, f32[160,768]{1,0:T(8,128)S(1)} %get-tuple-element.55.r_ref, f32[768]{0:T(1024)S(1)} %get-tuple-element.34.diag_ref, ...), custom_call_target="tpu_custom_call" | custom-call | tf_op jit(solution)/shard_map/pallas_call | solution.py:561
  44.5 17.5 %all_to_all.5.sums_ref = f32[32,2,160]{2,1,0:T(2,128)S(1)} all-to-all(f32[32,2,160]{2,1,0:T(2,128)S(1)} %get-tuple-element.59), channel_id=1, replica_groups=mesh['grp'=4,'sub'=8] {'grp','sub'}, dimensions={0} | all-to-all | bytes 81920 | tf_op jit(solution)/shard_map/all_to_all | solution.py:564
  62.1 1.1 %shard_map.142 = (f32[160,768]{1,0:T(8,128)}, f32[160,768]{1,0:T(8,128)}) custom-call(f32[160,768]{1,0:T(8,128)S(1)} %get-tuple-element.32.x_ref, f32[160,768]{1,0:T(8,128)S(1)} %get-tuple-element.57.p_ref, f32[160,768]{1,0:T(8,128)S(1)} %get-tuple-element.55.r_ref, f32[160,768]{1,0:T(8,128)S(1)} %get-tuple-element.58.image_ref, ...), custom_call_target="tpu_custom_call" | custom-call | tf_op jit(solution)/shard_map/pallas_call | solution.py:565
Async XLA Ops:
  2.4 1.4 %collective-permute-start = (bf16[192,128]{1,0:T(8,128)(2,1)S(1)}, bf16[192,128]{1,0:T(8,128)(2,1)S(1)}, u32[]{:S(2)}, u32[]{:S(2)}) collective-permute-start(bf16[192,128]{1,0:T(8,128)(2,1)S(1)} %get-tuple-element.37), channel_id=1, source_target_pairs={{0,1},{1,0},{2,3},{3,2},{4,5},{5,4},{6,7},{7,6},{8,9},{9,8},{10,11... | collective-permute-start | bytes 147464 | tf_op jit(solution)/shard_map/ppermute | solution.py:504
  4.4 2.4 %collective-permute-start.1 = (bf16[608,128]{1,0:T(8,128)(2,1)S(1)}, bf16[608,128]{1,0:T(8,128)(2,1)S(1)}, u32[]{:S(2)}, u32[]{:S(2)}) collective-permute-start(bf16[608,128]{1,0:T(8,128)(2,1)S(1)} %get-tuple-element.40), channel_id=1, source_target_pairs={{1,2},{2,1},{3,4},{4,3},{5,6},{6,5},{7,8},{8,7},{9,10},{10,9},{11,... | collective-permute-start | bytes 466952 | tf_op jit(solution)/shard_map/ppermute | solution.py:509
  7.2 6.4 %collective-permute-start.2 = (bf16[160,128]{1,0:T(8,128)(2,1)S(1)}, bf16[160,128]{1,0:T(8,128)(2,1)S(1)}, u32[]{:S(2)}, u32[]{:S(2)}) collective-permute-start(bf16[160,128]{1,0:T(8,128)(2,1)S(1)} %get-tuple-element.49), channel_id=1, source_target_pairs={{0,1},{1,0},{2,3},{3,2},{4,5},{5,4},{6,7},{7,6},{8,9},{9,8},{10,11... | collective-permute-start | bytes 122888 | tf_op jit(solution)/shard_map/ppermute | solution.py:524
  14.0 8.8 %collective-permute-start.5 = (f32[32,256]{1,0:T(8,128)S(1)}, f32[32,256]{1,0:T(8,128)S(1)}, u32[]{:S(2)}, u32[]{:S(2)}) collective-permute-start(f32[32,256]{1,0:T(8,128)S(1)} %get-tuple-element.50.refs_0_), channel_id=1, source_target_pairs={{0,6},{1,7},{2,4},{3,5},{4,2},{5,3},{6,0},{7,1},{8,14},{9,15},{10,... | collective-permute-start | bytes 98312 | tf_op jit(solution)/shard_map/ppermute | solution.py:535
  20.6 4.8 %collective-permute-start.4 = (f32[32,256]{1,0:T(8,128)S(1)}, f32[32,256]{1,0:T(8,128)S(1)}, u32[]{:S(2)}, u32[]{:S(2)}) collective-permute-start(f32[32,256]{1,0:T(8,128)S(1)} %get-tuple-element.50.refs_0_), channel_id=1, source_target_pairs={{0,4},{1,5},{2,6},{3,7},{4,0},{5,1},{6,2},{7,3},{8,12},{9,13},{10,... | collective-permute-start | bytes 98312 | tf_op jit(solution)/shard_map/ppermute | solution.py:535
  20.6 4.8 %collective-permute-start.3 = (f32[32,256]{1,0:T(8,128)S(1)}, f32[32,256]{1,0:T(8,128)S(1)}, u32[]{:S(2)}, u32[]{:S(2)}) collective-permute-start(f32[32,256]{1,0:T(8,128)S(1)} %get-tuple-element.50.refs_0_), channel_id=1, source_target_pairs={{0,2},{1,3},{2,0},{3,1},{4,6},{5,7},{6,4},{7,5},{8,10},{9,11},{10,... | collective-permute-start | bytes 98312 | tf_op jit(solution)/shard_map/ppermute | solution.py:535
  21.2 4.7 %collective-permute-start.6 = (f32[32,256]{1,0:T(8,128)S(1)}, f32[32,256]{1,0:T(8,128)S(1)}, u32[]{:S(2)}, u32[]{:S(2)}) collective-permute-start(f32[32,256]{1,0:T(8,128)S(1)} %get-tuple-element.50.refs_0_), channel_id=1, source_target_pairs={{0,1},{1,0},{2,3},{3,2},{4,5},{5,4},{6,7},{7,6},{8,9},{9,8},{10,11... | collective-permute-start | bytes 98312 | tf_op jit(solution)/shard_map/ppermute | solution.py:538
  22.8 3.1 %collective-permute-start.9 = (f32[32,256]{1,0:T(8,128)S(1)}, f32[32,256]{1,0:T(8,128)S(1)}, u32[]{:S(2)}, u32[]{:S(2)}) collective-permute-start(f32[32,256]{1,0:T(8,128)S(1)} %collective-permute-done.5.refs_3_), channel_id=1, source_target_pairs={{0,1},{1,0},{2,3},{3,2},{4,5},{5,4},{6,7},{7,6},{8,9},{9,8},{10,11... | collective-permute-start | bytes 98312 | tf_op jit(solution)/shard_map/ppermute | solution.py:538
  25.4 1.2 %collective-permute-start.8 = (f32[32,256]{1,0:T(8,128)S(1)}, f32[32,256]{1,0:T(8,128)S(1)}, u32[]{:S(2)}, u32[]{:S(2)}) collective-permute-start(f32[32,256]{1,0:T(8,128)S(1)} %collective-permute-done.4.refs_2_), channel_id=1, source_target_pairs={{0,1},{1,0},{2,3},{3,2},{4,5},{5,4},{6,7},{7,6},{8,9},{9,8},{10,11... | collective-permute-start | bytes 98312 | tf_op jit(solution)/shard_map/ppermute | solution.py:538
  25.4 1.4 %collective-permute-start.7 = (f32[32,256]{1,0:T(8,128)S(1)}, f32[32,256]{1,0:T(8,128)S(1)}, u32[]{:S(2)}, u32[]{:S(2)}) collective-permute-start(f32[32,256]{1,0:T(8,128)S(1)} %collective-permute-done.3.refs_1_), channel_id=1, source_target_pairs={{0,1},{1,0},{2,3},{3,2},{4,5},{5,4},{6,7},{7,6},{8,9},{9,8},{10,11... | collective-permute-start | bytes 98312 | tf_op jit(solution)/shard_map/ppermute | solution.py:538
  29.4 5.4 %collective-permute-start.12 = (f32[64,256]{1,0:T(8,128)S(1)}, f32[64,256]{1,0:T(8,128)S(1)}, u32[]{:S(2)}, u32[]{:S(2)}) collective-permute-start(f32[64,256]{1,0:T(8,128)S(1)} %get-tuple-element.51.refs_0_), channel_id=1, source_target_pairs={{0,24},{1,25},{2,26},{3,27},{4,28},{5,29},{6,30},{7,31},{8,16},{9,... | collective-permute-start | bytes 196616 | tf_op jit(solution)/shard_map/ppermute | solution.py:535
  31.3 4.8 %collective-permute-start.11 = (f32[64,256]{1,0:T(8,128)S(1)}, f32[64,256]{1,0:T(8,128)S(1)}, u32[]{:S(2)}, u32[]{:S(2)}) collective-permute-start(f32[64,256]{1,0:T(8,128)S(1)} %get-tuple-element.51.refs_0_), channel_id=1, source_target_pairs={{0,16},{1,17},{2,18},{3,19},{4,20},{5,21},{6,22},{7,23},{8,24},{9,... | collective-permute-start | bytes 196616 | tf_op jit(solution)/shard_map/ppermute | solution.py:535
  33.3 4.3 %collective-permute-start.10 = (f32[64,256]{1,0:T(8,128)S(1)}, f32[64,256]{1,0:T(8,128)S(1)}, u32[]{:S(2)}, u32[]{:S(2)}) collective-permute-start(f32[64,256]{1,0:T(8,128)S(1)} %get-tuple-element.51.refs_0_), channel_id=1, source_target_pairs={{0,8},{1,9},{2,10},{3,11},{4,12},{5,13},{6,14},{7,15},{8,0},{9,1},... | collective-permute-start | bytes 196616 | tf_op jit(solution)/shard_map/ppermute | solution.py:535
  42.0 1.3 %collective-permute-start.13 = (bf16[160,256]{1,0:T(8,128)(2,1)S(1)}, bf16[160,256]{1,0:T(8,128)(2,1)S(1)}, u32[]{:S(2)}, u32[]{:S(2)}) collective-permute-start(bf16[160,256]{1,0:T(8,128)(2,1)S(1)} %shard_map.140), channel_id=1, source_target_pairs={{0,1},{1,0},{2,3},{3,2},{4,5},{5,4},{6,7},{7,6},{8,9},{9,8},{10,11... | collective-permute-start | bytes 245768 | tf_op jit(solution)/shard_map/ppermute | solution.py:560
  42.1 1.3 %collective-permute-start.14 = (bf16[160,256]{1,0:T(8,128)(2,1)S(1)}, bf16[160,256]{1,0:T(8,128)(2,1)S(1)}, u32[]{:S(2)}, u32[]{:S(2)}) collective-permute-start(bf16[160,256]{1,0:T(8,128)(2,1)S(1)} %get-tuple-element.56), channel_id=1, source_target_pairs={{1,2},{2,1},{3,4},{4,3},{5,6},{6,5},{7,8},{8,7},{9,10},{10,9},{11,... | collective-permute-start | bytes 245768 | tf_op jit(solution)/shard_map/ppermute | solution.py:558

commit v8 on v7

--- a/solution.py
+++ b/solution.py
@@ -45,13 +45,6 @@
     return place_matrix(rows, total)
 
 
-def from_sides(pair_ref, other_ref):
-    even = is_even()
-    other = other_ref[...]
-    pair = pair_ref[:other.shape[0], :]
-    return jnp.where(even, other, pair), jnp.where(even, pair, other)
-
-
 def copy_all(copies, sems):
     started = [pltpu.make_async_copy(source, target, sems.at[n]) for n, (source, target) in enumerate(copies)]
     for copy in started:
@@ -66,8 +59,8 @@
     return high, middle, (rest - middle.astype(F32)).astype(BF16)
 
 
-def load_kernel(x_hbm, rows_hbm, up_hbm, b_hbm, diag_hbm, values_hbm, cols_hbm, cl_hbm, cr_hbm,
-                to_pair_ref, to_other_ref, x_ref, rows_ref, b_ref, diag_ref, operator_ref,
+def load_kernel(x_hbm, rows_hbm, up_hbm, basis_hbm, b_hbm, diag_hbm, values_hbm, cols_hbm, cl_hbm, cr_hbm,
+                to_pair_ref, to_other_ref, basis_other_ref, x_ref, rows_ref, basis_ref, b_ref, diag_ref, operator_ref,
                 up_ref, cols_ref, values_ref, sems):
     blocks, nonzeros, size = values_hbm.shape[1], values_hbm.shape[2], values_hbm.shape[3]
     cases, rows = x_ref.shape
@@ -77,6 +70,7 @@
             (rows_hbm, rows_ref),
             (x_hbm, x_ref),
             (up_hbm, up_ref),
+            (basis_hbm, basis_ref),
             (cols_hbm, cols_ref),
             (values_hbm, values_ref),
             (cl_hbm, operator_ref.at[:, rows:rows + margin]),
@@ -87,16 +81,25 @@
         sems,
     )
     operator_ref[:, :rows] = jnp.zeros((rows, rows), BF16)
-    for copy in copies[:3]:
+    for copy in copies[:4]:
         copy.wait()
-    sent = mm(x_ref[...].astype(BF16), send_matrix(rows_ref, rows)).astype(BF16)
+    place = send_matrix(rows_ref, rows)
+    sent = mm(x_ref[...].astype(BF16), place).astype(BF16)
     to_pair_ref[:cases, :] = sent[:, :margin]
     to_other_ref[...] = sent[:, margin:]
     parts = [part.astype(F32) for part in split_three(up_ref[0])]
     modes = up_ref.shape[1]
     parts.append(jnp.zeros((modes, margin - 3 * modes), F32))
-    to_pair_ref[cases:, :] = jnp.concatenate(parts, axis=1).astype(BF16)
-    for copy in copies[3:]:
+    to_pair_ref[cases:cases + modes, :] = jnp.concatenate(parts, axis=1).astype(BF16)
+    basis = basis_ref[0]
+    even = is_even()
+    head, tail = basis[:, :margin], basis[:, margin + rows:]
+    picked = mm(basis[:, margin:margin + rows], place).astype(BF16)
+    to_pair_ref[cases + modes:cases + 2 * modes, :] = jnp.where(even, tail, head)
+    to_pair_ref[cases + 2 * modes:, :] = picked[:, :margin]
+    basis_other_ref[:modes, :] = jnp.where(even, head, tail)
+    basis_other_ref[modes:, :] = picked[:, margin:]
+    for copy in copies[4:]:
         copy.wait()
     for i in range(blocks):
         for t in range(nonzeros):
@@ -111,7 +114,7 @@
     partial_ref[...] = b_ref[...] - diag * x - mm_nt(x.astype(BF16), operator_ref[:, :rows])
 
 
-def offer_kernel(partial_ref, operator_ref, rows_ref, pair_ref, to_other_ref, known_ref, message_ref):
+def offer_kernel(partial_ref, operator_ref, rows_ref, pair_ref, to_other_ref, basis_other_ref, known_ref, message_ref):
     cases, rows = partial_ref.shape
     margin = rows_ref.shape[2]
     even = is_even()
@@ -126,23 +129,23 @@
     message_ref[:cases, :] = to_other_ref[...]
     message_ref[cases:2 * cases, :] = mm(high, place).astype(BF16)
     message_ref[2 * cases:3 * cases, :] = mm(low, place).astype(BF16)
-    message_ref[3 * cases:, :] = mm_t(place, from_other).astype(BF16)
-
-
-def inverse_kernel(first_pair_ref, inverse_hbm, basis_hbm, diag_hbm, up_hbm,
-                   inverse_ref, basis_ref, factor_ref, plain_ref, blocks_ref, sems):
+    message_ref[3 * cases:3 * cases + margin, :] = mm_t(place, from_other).astype(BF16)
+    message_ref[3 * cases + margin:, :] = basis_other_ref[...]
+
+
+def inverse_kernel(first_pair_ref, inverse_hbm, diag_hbm, up_hbm,
+                   inverse_ref, factor_ref, plain_ref, blocks_ref, sems):
     size = diag_hbm.shape[1]
-    cases = first_pair_ref.shape[0] - size
+    cases = first_pair_ref.shape[0] - 3 * size
     copies = copy_all(
         [
             (diag_hbm, blocks_ref.at[0:1]),
             (up_hbm, blocks_ref.at[1:2]),
-            (basis_hbm, basis_ref),
             (inverse_hbm, inverse_ref),
         ],
         sems,
     )
-    parts = first_pair_ref[cases:, :].astype(F32)
+    parts = first_pair_ref[cases:cases + size, :].astype(F32)
     up_left = parts[:, :size] + (parts[:, size:2 * size] + parts[:, 2 * size:3 * size])
     for copy in copies[:2]:
         copy.wait()
@@ -174,7 +177,7 @@
     place = place_matrix(jnp.where(even, rows_ref[0, 1:2, :], rows_ref[0, 0:1, :]), rows)
     to_pair_ref[...] = mm(rounded, place).astype(BF16)
     offered = other_ref[cases:2 * cases, :].astype(F32) + other_ref[2 * cases:3 * cases, :].astype(F32)
-    halo_ref[...] = (offered - mm_nt(sent_ref[...], other_ref[3 * cases:, :])).astype(BF16)
+    halo_ref[...] = (offered - mm_nt(sent_ref[...], other_ref[3 * cases:3 * cases + margin, :])).astype(BF16)
 
 
 def own_local_kernel(rb_ref, inverse_ref, basis_ref, halo_ref, local_ref, coarse_ref):
@@ -188,8 +191,8 @@
     coarse_ref[...] = mm_nt(basis_ref[0], extended)
 
 
-def local_kernel(own_local_ref, own_coarse_ref, inverse_ref, basis_ref, factor_ref, plain_ref, pair_ref,
-                 local_ref, message_ref):
+def local_kernel(own_local_ref, own_coarse_ref, inverse_ref, basis_ref, factor_ref, plain_ref, pair_ref, rows_ref,
+                 local_ref, message_ref, to_pair_ref, to_other_ref):
     margin = pair_ref.shape[1]
     even = is_even()
     pair = pair_ref[...]
@@ -203,7 +206,18 @@
     message = jnp.concatenate([plain_ref[:, :3 * size], right_side], axis=1)
     message_ref[...] = message
     rows = jnp.where(even, inverse_ref[0, total - margin:, :], inverse_ref[0, :margin, :])
-    local_ref[...] = own_local_ref[...] + mm(pair, rows)
+    local = own_local_ref[...] + mm(pair, rows)
+    local_ref[...] = local
+    left, right = rows_ref[0, 0:1, :], rows_ref[0, 1:2, :]
+    to_pair_ref[...] = return_rows(local, margin, jnp.where(even, right, left), jnp.logical_not(even))
+    to_other_ref[...] = return_rows(local, margin, jnp.where(even, left, right), even)
+
+
+def return_rows(local, margin, rows, head):
+    owned = local.shape[1] - 2 * margin
+    rounded = local.astype(BF16)
+    tail = jnp.where(head, rounded[:, :margin], rounded[:, margin + owned:])
+    return jnp.concatenate([tail, mm(rounded[:, margin:margin + owned], place_matrix(rows, owned)).astype(BF16)], axis=1)
 
 
 def reduce_rows(blocks):
@@ -334,14 +348,29 @@
     combine(chain, parts, 1, size)
     head, tail = eliminate(chain, size, keep, 2)
     message_ref[:size, :] = head
-    message_ref[size:, :] = tail
+    message_ref[size:2 * size, :] = tail
+    lane = lax.broadcasted_iota(jnp.int32, (size, width), 1)
+    step = members // 2
+    at = step
+    whole = solved_ref[at]
+    zero = jnp.zeros((size, width), F32)
+    while at < members - 1:
+        step = step // 2
+        at = at + step
+        block = solved_ref[at]
+        stacked = jnp.concatenate([zero, whole, zero, zero], axis=0)
+        through = jnp.dot(
+            block[:, :4 * size], stacked, precision=lax.Precision.HIGHEST, preferred_element_type=F32)
+        whole = jnp.where((lane >= size) & (lane < 2 * size), 0.0, block) - through
+    message_ref[2 * size:, :] = whole
 
 
 def solve_kernel(*refs):
-    *received, solved_ref, local_ref, basis_ref, rows_ref, corr_ref, to_other_ref, messages_ref, sep_ref, x_ref = refs
+    (*received, solved_ref, local_ref, basis_ref, rows_ref, first_pair_ref, first_other_ref, pair_ref, other_ref,
+     r_ref, diag_ref, operator_ref, p_ref, image_ref, sums_ref, messages_ref, sep_ref, x_ref) = refs
     groups = len(received)
-    two_size, width = received[0].shape
-    size = two_size // 2
+    size, width = received[0].shape
+    size = size // 3
     members = solved_ref.shape[0]
     for d in range(groups):
         messages_ref[lax.axis_index("grp") ^ d] = received[d][...]
@@ -349,7 +378,7 @@
     for g in range(groups):
         total = messages_ref[g, :size, :]
         if g:
-            total = total + messages_ref[g - 1, size:, :]
+            total = total + messages_ref[g - 1, size:2 * size, :]
         chain.append(total)
     count = padded(groups)
     row = lax.broadcasted_iota(jnp.int32, (size, width), 0)
@@ -377,51 +406,39 @@
         for j in range(step, members, 2 * step):
             x_ref[j] = back(solved_ref[j], x_ref[j - step], x_ref[j + step], size)
         step = step // 2
-    odd = member // 2 * 2 + 1
-    x_ref[odd] = back(solved_ref[odd], x_ref[odd - 1], x_ref[odd + 1], size)
-    coarse = x_ref[member].astype(BF16)
-    correction = local_ref[...] + mm_t(coarse, basis_ref[0])[3 * size:]
-    corr_ref[...] = correction
-    even = is_even()
-    to_other_ref[...] = return_rows(
-        correction, rows_ref.shape[2], jnp.where(even, rows_ref[0, 0:1, :], rows_ref[0, 1:2, :]), even)
-
-
-def return_rows(correction, margin, rows, head):
-    owned = correction.shape[1] - 2 * margin
-    rounded = correction.astype(BF16)
-    tail = jnp.where(head, rounded[:, :margin], rounded[:, margin + owned:])
-    return jnp.concatenate([tail, mm(rounded[:, margin:margin + owned], place_matrix(rows, owned)).astype(BF16)], axis=1)
-
-
-def pair_kernel(corr_ref, rows_ref, to_pair_ref):
-    even = is_even()
-    to_pair_ref[...] = return_rows(
-        corr_ref[...], rows_ref.shape[2], jnp.where(even, rows_ref[0, 1:2, :], rows_ref[0, 0:1, :]), jnp.logical_not(even))
-
-
-def row_sum(values):
-    lanes = 128
-    total = values[:, :lanes]
-    for start in range(lanes, values.shape[1], lanes):
-        total = total + values[:, start:start + lanes]
-    return mm_nt(jnp.ones((8, lanes), F32), total, precision=lax.Precision.HIGHEST)
-
-
-def image_kernel(corr_ref, r_ref, diag_ref, operator_ref, rows_ref, pair_ref, other_ref, p_ref, image_ref, sums_ref):
+    before = jnp.maximum(group - 1, 0)
+    earlier = back(messages_ref[before, 2 * size:, :], sep_ref[before], sep_ref[group], size)
+    lower = jnp.maximum(member - 1, 0)
+    for odd in (member // 2 * 2 + 1, lower // 2 * 2 + 1):
+        x_ref[odd] = back(solved_ref[odd], x_ref[odd - 1], x_ref[odd + 1], size)
+    left_solution = jnp.where(member == 0, earlier, x_ref[lower])
+    right_solution = x_ref[member + 1]
+
+    def lifted(solution, basis):
+        return mm_t(solution.astype(BF16), basis)[3 * size:]
+
+    cases = pair_ref.shape[0]
     margin = rows_ref.shape[2]
     owned = p_ref.shape[1]
-    from_left, from_right = from_sides(pair_ref, other_ref)
+    even = is_even()
+
+    def columns(ref, start):
+        return jnp.concatenate([ref[start:start + size, :], ref[start + size:start + 2 * size, :]], axis=1)
+
+    pair_basis = columns(first_pair_ref, cases + size)
+    other_basis = columns(first_other_ref, 3 * cases + margin)
+    pair, other = pair_ref[...].astype(F32), other_ref[...].astype(F32)
+    left = jnp.where(even, other, pair) + lifted(left_solution, jnp.where(even, other_basis, pair_basis))
+    right = jnp.where(even, pair, other) + lifted(right_solution, jnp.where(even, pair_basis, other_basis))
+    correction = local_ref[...] + lifted(x_ref[member], basis_ref[0])
     place = place_matrix(jnp.concatenate([rows_ref[0, 0:1, :], rows_ref[0, 1:2, :]], axis=1), owned)
-    tails = jnp.concatenate([from_left[:, :margin], from_right[:, :margin]], axis=1)
-    p = corr_ref[:, margin:margin + owned] + mm_nt(tails, place)
+    tails = jnp.concatenate([left[:, :margin], right[:, :margin]], axis=1).astype(BF16)
+    p = correction[:, margin:margin + owned] + mm_nt(tails, place)
     p_ref[...] = p
     me = position()
     last = lax.axis_size("grp") * lax.axis_size("sub") - 1
-    left = from_left[:, margin:].astype(F32) + corr_ref[:, :margin]
-    right = from_right[:, margin:].astype(F32) + corr_ref[:, margin + owned:]
-    left = jnp.where(me == 0, 0.0, left).astype(BF16)
-    right = jnp.where(me == last, 0.0, right).astype(BF16)
+    left = jnp.where(me == 0, 0.0, left[:, margin:] + correction[:, :margin]).astype(BF16)
+    right = jnp.where(me == last, 0.0, right[:, margin:] + correction[:, margin + owned:]).astype(BF16)
     values = jnp.concatenate([p.astype(BF16), left, right], axis=1)
     image = diag_ref[...].reshape(1, owned) * p + mm_nt(values, operator_ref[...])
     image_ref[...] = image
@@ -430,6 +447,14 @@
     sums = jnp.concatenate([inner[0:1], curvature[0:1]], axis=0)
     for slot in range(sums_ref.shape[0]):
         sums_ref[slot] = sums
+
+
+def row_sum(values):
+    lanes = 128
+    total = values[:, :lanes]
+    for start in range(lanes, values.shape[1], lanes):
+        total = total + values[:, start:start + lanes]
+    return mm_nt(jnp.ones((8, lanes), F32), total, precision=lax.Precision.HIGHEST)
 
 
 def finish_kernel(x_ref, p_ref, r_ref, image_ref, sums_ref, out_x_ref, out_r_ref):
@@ -480,44 +505,41 @@
     halo = struct((cases, margin), BF16)
     full = struct((cases, rows), F32)
     semaphores = pltpu.SemaphoreType.DMA
-    to_pair, to_other, start, send_rows, loads, diag, operator = call(
+    to_pair, to_other, basis_other, start, send_rows, basis, loads, diag, operator = call(
         load_kernel,
         [
-            struct((cases + modes, margin), BF16),
+            struct((cases + 3 * modes, margin), BF16),
             halo,
+            struct((2 * modes, margin), BF16),
             full,
             struct(send_rows.shape, send_rows.dtype),
+            struct(basis.shape, BF16),
             full,
             struct(diagonal.shape, F32),
             struct((rows, rows + 2 * margin), BF16),
         ],
-        [HBM] * 9,
+        [HBM] * 10,
         [
             pltpu.VMEM(coarse_up.shape, F32),
             pltpu.SMEM(block_cols.shape, block_cols.dtype),
             pltpu.VMEM(block_values.shape, BF16),
-            semaphores((9,)),
+            semaphores((10,)),
         ],
     )(*far(
-        iterate_in, send_rows, coarse_up, right_side, diagonal, block_values, block_cols, couple_left, couple_right
+        iterate_in, send_rows, coarse_up, basis, right_side, diagonal, block_values, block_cols, couple_left, couple_right
     ))
     first_pair = lax.ppermute(to_pair, AXES, pairs)
     (partial,) = call(own_kernel, [full], [VMEM] * 4)(start, loads, diag, operator)
-    known, message = call(offer_kernel, [full, struct((3 * cases + margin, margin), BF16)], [VMEM] * 5)(
-        partial, operator, send_rows, first_pair, to_other
-    )
+    known, message = call(
+        offer_kernel, [full, struct((3 * cases + margin + 2 * modes, margin), BF16)], [VMEM] * 6
+    )(partial, operator, send_rows, first_pair, to_other, basis_other)
     first_other = lax.ppermute(message, AXES, others)
-    inverse, basis, factor, plain = call(
+    inverse, factor, plain = call(
         inverse_kernel,
-        [
-            struct(local_inverse.shape, BF16),
-            struct(basis.shape, BF16),
-            struct((modes, 4 * modes), F32),
-            struct((modes, 4 * modes), F32),
-        ],
-        [VMEM] + [HBM] * 4,
-        [pltpu.VMEM((2, modes, modes), F32), semaphores((4,))],
-    )(first_pair, *far(local_inverse, basis, coarse_diag, coarse_up))
+        [struct(local_inverse.shape, BF16), struct((modes, 4 * modes), F32), struct((modes, 4 * modes), F32)],
+        [VMEM] + [HBM] * 3,
+        [pltpu.VMEM((2, modes, modes), F32), semaphores((3,))],
+    )(first_pair, *far(local_inverse, coarse_diag, coarse_up))
     residual, rounded, to_pair, other_halo = call(
         residual_kernel, [full, struct((cases, rows), BF16), halo, halo], [VMEM] * 6
     )(known, operator, send_rows, to_other, first_other, plain)
@@ -526,9 +548,12 @@
         rounded, inverse, basis, other_halo
     )
     chips = members // 2
-    local, message = call(
-        local_kernel, [struct((cases, extended), F32), struct((modes, width), F32)], [VMEM] * 7
-    )(local, coarse, inverse, basis, factor, plain, pair_halo)
+    returned = struct((cases, 2 * margin), BF16)
+    local, message, to_pair, to_other = call(
+        local_kernel, [struct((cases, extended), F32), struct((modes, width), F32), returned, returned], [VMEM] * 8
+    )(local, coarse, inverse, basis, factor, plain, pair_halo, send_rows)
+    from_other = lax.ppermute(to_other, AXES, others)
+    from_pair = lax.ppermute(to_pair, AXES, pairs)
 
     def partners(value, stride, count):
         swaps = [[(i, i ^ (stride * d)) for i in range(total)] for d in range(1, count)]
@@ -539,27 +564,23 @@
     block = pltpu.VMEM((members, modes, width), F32)
     solved, reduced = call(
         group_kernel,
-        [struct((members, modes, width), F32), struct((2 * modes, width), F32)],
+        [struct((members, modes, width), F32), struct((3 * modes, width), F32)],
         [VMEM] * members,
         [block],
     )(*same, *opposite)
     reduced = partners(reduced, members, groups)
-    returned = struct((cases, 2 * margin), BF16)
-    correction, to_other = call(
+    direction, image, sums = call(
         solve_kernel,
-        [struct((cases, extended), F32), returned],
-        [VMEM] * (groups + 4),
+        [full, full, struct((total, 2, cases), F32)],
+        [VMEM] * (groups + 11),
         [
-            pltpu.VMEM((groups, 2 * modes, width), F32),
+            pltpu.VMEM((groups, 3 * modes, width), F32),
             pltpu.VMEM((groups + 1, modes, width), F32),
             pltpu.VMEM((members + 1, modes, width), F32),
         ],
-    )(*reduced, solved, local, basis, send_rows)
-    from_other = lax.ppermute(to_other, AXES, others)
-    (to_pair,) = call(pair_kernel, [returned], [VMEM] * 2)(correction, send_rows)
-    from_pair = lax.ppermute(to_pair, AXES, pairs)
-    direction, image, sums = call(image_kernel, [full, full, struct((total, 2, cases), F32)], [VMEM] * 7)(
-        correction, residual, diag, operator, send_rows, from_pair, from_other
+    )(
+        *reduced, solved, local, basis, send_rows, first_pair, first_other, from_pair, from_other,
+        residual, diag, operator
     )
     sums = lax.all_to_all(sums, AXES, 0, 0, tiled=True)
     iterate, residual = call(finish_kernel, [full, full], [VMEM] * 5)(start, direction, residual, image, sums)

time: 63.5 us -> 60.9 us (0.959)
  blocking collectives: 17.5 us -> 15 us
    all_to_all x1, blocking collectives: 17.5 us -> 15 us  [shards(): sums = lax.all_to_all(sums, AXES, 0, 0, tiled=True)]
    pallas_call x7 -> x5, Pallas kernels: 12.2 us -> 12.2 us  [the longest x1 5.52 us: shards(): call(solve_kernel, [full, full, struct((total, 2, cases), F32)], [VMEM] *...]
  transfers between devices with their start and end apart: 15 -> 15, of which waited for: 10 -> 10; matrix products, arithmetic and copies ran while one was open for 0% -> 0% of each run, Pallas kernels for 4% -> 5%
where the time goes in v8:
time: 60.9 us; the launch traced here: 60.6 us
  starting transfers between devices  19.2 us (32%)
  Pallas kernels  15.6 us (26%)
  blocking collectives  15 us (25%)
  waiting for transfers between devices  10.1 us (17%)
  between operations  0.72 us (1%)
    all_to_all x1, blocking collectives, shards(): sums = lax.all_to_all(sums, AXES, 0, 0, tiled=True)  15 us
    ppermute x6, starting transfers between devices, partners(): return [value] + [lax.ppermute(value, AXES, swap) for swap in swaps]  11.1 us
    ppermute x6, waiting for transfers between devices, partners(): return [value] + [lax.ppermute(value, AXES, swap) for swap in swaps]  7.95 us
    ppermute x1, starting transfers between devices, shards(): pair_halo = lax.ppermute(to_pair, AXES, pairs)  5.73 us
    pallas_call x1, Pallas kernels, shards(): call(solve_kernel, [full, full, struct((total, 2, cases), F32)], [VMEM] *...  5.52 us
    pallas_call x1, Pallas kernels, shards(): call(group_kernel, [struct((members, modes, width), F32), struct((3 * mod...  2.74 us
    pallas_call x1, Pallas kernels, shards(): call(load_kernel, [struct((cases + 3 * modes, margin), BF16), halo, struc...  1.8 us
    pallas_call x1, Pallas kernels, shards(): call(inverse_kernel, [struct(local_inverse.shape, BF16), struct((modes, 4...  1.66 us
  transfers between devices with their start and end apart: 15, of which 10 were waited for; matrix products, arithmetic and copies ran while one was open for 0% of the time, Pallas kernels for 5%

profile of v8, /device:TPU:0, one launch (start us, length us, event | category | flops | bytes accessed | tf_op | source)
XLA Modules:
  0.0 60.6 jit_solution(16896715365286976880)
XLA Ops:
  0.6 1.8 %shard_map.131 = (bf16[256,128]{1,0:T(8,128)(2,1)S(1)}, bf16[160,128]{1,0:T(8,128)(2,1)S(1)}, bf16[64,128]{1,0:T(8,128)(2,1)S(1)}, f32[160,768]{1,0:T(8,128)S(1)...) custom-call(f32[160,768]{1,0:T(8,128)} %bitcast.6, ...), custom_call_target="tpu_custom_call" | custom-call | tf_op jit(solution)/shard_map/pallas_call | solution.py:508
  2.4 0.6 collective-permute-start
  3.0 0.6 shard_map.132.partial_ref
  3.6 0.3 collective-permute-done.pair_ref.first_pair_ref.refs_8_
  3.9 0.5 shard_map.133
  4.4 0.7 %collective-permute-start.1 = (bf16[672,128]{1,0:T(8,128)(2,1)S(1)}, bf16[672,128]{1,0:T(8,128)(2,1)S(1)}, u32[]{:S(2)}, u32[]{:S(2)}) collective-permute-start(bf16[672,128]{1,0:T(8,128)(2,1)S(1)} %get-tuple-element.42), channel_id=1, source_target_pairs={{1,2},{2,1},{3,4},{4,3},{5,6},{6,5},{7,8},{8,7},{9,10},{10,9},{11,... | collective-permute-start | bytes 516104 | tf_op jit(solution)/shard_map/ppermute | solution.py:536
  5.1 1.7 %shard_map.134 = (bf16[1,1024,1024]{2,1,0:T(8,128)(2,1)S(1)}, f32[32,128]{1,0:T(8,128)S(1)}, f32[32,128]{1,0:T(8,128)S(1)}) custom-call(bf16[256,128]{1,0:T(8,128)(2,1)S(1)} %collective-permute-done.pair_ref.first_pair_ref.refs_8_, bf16[1,1024,1024]{2,1,0:T(8,128)(2,1)} %inverse_hbm.1, f32[1,32,32]{2,1,0:T(8,128)} %diag_hbm.3, f32[1,32,32]{2,1,0:T(8,128)} %up_hbm.3), custom_call_target="tpu_custom_call" | custom-call | tf_op jit(solution)/shard_map/pallas_call | solution.py:537
  6.8 0.0 collective-permute-done.1.other_ref.refs_9_
  6.8 0.4 shard_map.135
  7.2 5.7 %collective-permute-start.2 = (bf16[160,128]{1,0:T(8,128)(2,1)S(1)}, bf16[160,128]{1,0:T(8,128)(2,1)S(1)}, u32[]{:S(2)}, u32[]{:S(2)}) collective-permute-start(bf16[160,128]{1,0:T(8,128)(2,1)S(1)} %get-tuple-element.51), channel_id=1, source_target_pairs={{0,1},{1,0},{2,3},{3,2},{4,5},{5,4},{6,7},{7,6},{8,9},{9,8},{10,11... | collective-permute-start | bytes 122888 | tf_op jit(solution)/shard_map/ppermute | solution.py:546
  12.9 0.6 shard_map.136
  13.5 0.3 collective-permute-done.2.pair_ref
  13.8 0.6 %shard_map.137 = (f32[160,1024]{1,0:T(8,128)S(1)}, f32[32,256]{1,0:T(8,128)S(1)}, bf16[160,256]{1,0:T(8,128)(2,1)S(1)}, bf16[160,256]{1,0:T(8,128)(2,1)S(1)}) custom-call(f32[160,1024]{1,0:T(8,128)S(1)} %get-tuple-element.48.own_local_ref, f32[32,160]{1,0:T(8,128)S(1)} %get-tuple-element.49.own_coarse_ref, ...), custom_call_target="tpu_custom_call" | custom-call | tf_op jit(solution)/shard_map/pallas_call | solution.py:552
  14.5 6.6 %collective-permute-start.5 = (f32[32,256]{1,0:T(8,128)S(1)}, f32[32,256]{1,0:T(8,128)S(1)}, u32[]{:S(2)}, u32[]{:S(2)}) collective-permute-start(f32[32,256]{1,0:T(8,128)S(1)} %get-tuple-element.52.refs_0_), channel_id=1, source_target_pairs={{0,6},{1,7},{2,4},{3,5},{4,2},{5,3},{6,0},{7,1},{8,14},{9,15},{10,... | collective-permute-start | bytes 98312 | tf_op jit(solution)/shard_map/ppermute | solution.py:560
  21.0 0.0 collective-permute-start.4
  21.0 0.6 %collective-permute-start.3 = (f32[32,256]{1,0:T(8,128)S(1)}, f32[32,256]{1,0:T(8,128)S(1)}, u32[]{:S(2)}, u32[]{:S(2)}) collective-permute-start(f32[32,256]{1,0:T(8,128)S(1)} %get-tuple-element.52.refs_0_), channel_id=1, source_target_pairs={{0,2},{1,3},{2,0},{3,1},{4,6},{5,7},{6,4},{7,5},{8,10},{9,11},{10,... | collective-permute-start | bytes 98312 | tf_op jit(solution)/shard_map/ppermute | solution.py:560
  21.7 0.0 collective-permute-start.6
  21.7 1.6 %collective-permute-done.5.refs_3_ = f32[32,256]{1,0:T(8,128)S(1)} collective-permute-done((f32[32,256]{1,0:T(8,128)S(1)}, f32[32,256]{1,0:T(8,128)S(1)}, u32[]{:S(2)}, u32[]{:S(2)}) %collective-permute-start.5) | collective-permute-done | bytes 32800 | tf_op jit(solution)/shard_map/ppermute | solution.py:560
  23.3 0.0 collective-permute-start.9
  23.3 2.6 %collective-permute-done.4.refs_2_ = f32[32,256]{1,0:T(8,128)S(1)} collective-permute-done((f32[32,256]{1,0:T(8,128)S(1)}, f32[32,256]{1,0:T(8,128)S(1)}, u32[]{:S(2)}, u32[]{:S(2)}) %collective-permute-start.4) | collective-permute-done | bytes 32800 | tf_op jit(solution)/shard_map/ppermute | solution.py:560
  25.8 0.0 collective-permute-start.8
  25.8 0.0 collective-permute-done.3.refs_1_
  25.8 0.5 collective-permute-start.7
  26.3 0.0 collective-permute-done.6.refs_4_
  26.3 0.0 collective-permute-done.9.refs_7_
  26.4 0.7 %collective-permute-done.8.refs_6_ = f32[32,256]{1,0:T(8,128)S(1)} collective-permute-done((f32[32,256]{1,0:T(8,128)S(1)}, f32[32,256]{1,0:T(8,128)S(1)}, u32[]{:S(2)}, u32[]{:S(2)}) %collective-permute-start.8) | collective-permute-done | bytes 32800 | tf_op jit(solution)/shard_map/ppermute | solution.py:563
  27.0 0.2 collective-permute-done.7.refs_5_
  27.2 2.7 %shard_map.138 = (f32[8,32,256]{2,1,0:T(8,128)S(1)}, f32[96,256]{1,0:T(8,128)S(1)}) custom-call(f32[32,256]{1,0:T(8,128)S(1)} %get-tuple-element.52.refs_0_, f32[32,256]{1,0:T(8,128)S(1)} %collective-permute-done.3.refs_1_, f32[32,256]{1,0:T(8,128)S(1)} %collective-permute-done.4.refs_2_, f32[32,256]{1,0:T(8,128)S(1)} %collective-permute-done.5.refs_3_, ...), custom_call_target="tpu_custom_call" | custom-call | tf_op jit(solution)/shard_map/pallas_call | solution.py:565
  29.9 2.1 %collective-permute-start.12 = (f32[96,256]{1,0:T(8,128)S(1)}, f32[96,256]{1,0:T(8,128)S(1)}, u32[]{:S(2)}, u32[]{:S(2)}) collective-permute-start(f32[96,256]{1,0:T(8,128)S(1)} %get-tuple-element.53.refs_0_), channel_id=1, source_target_pairs={{0,24},{1,25},{2,26},{3,27},{4,28},{5,29},{6,30},{7,31},{8,16},{9,... | collective-permute-start | bytes 294920 | tf_op jit(solution)/shard_map/ppermute | solution.py:560
  32.0 1.8 %collective-permute-start.11 = (f32[96,256]{1,0:T(8,128)S(1)}, f32[96,256]{1,0:T(8,128)S(1)}, u32[]{:S(2)}, u32[]{:S(2)}) collective-permute-start(f32[96,256]{1,0:T(8,128)S(1)} %get-tuple-element.53.refs_0_), channel_id=1, source_target_pairs={{0,16},{1,17},{2,18},{3,19},{4,20},{5,21},{6,22},{7,23},{8,24},{9,... | collective-permute-start | bytes 294920 | tf_op jit(solution)/shard_map/ppermute | solution.py:560
  33.9 0.0 collective-permute-start.10
  33.9 0.0 collective-permute-start.13
  33.9 0.7 %collective-permute-start.14 = (bf16[160,256]{1,0:T(8,128)(2,1)S(1)}, bf16[160,256]{1,0:T(8,128)(2,1)S(1)}, u32[]{:S(2)}, u32[]{:S(2)}) collective-permute-start(bf16[160,256]{1,0:T(8,128)(2,1)S(1)} %get-tuple-element.57), channel_id=1, source_target_pairs={{1,2},{2,1},{3,4},{4,3},{5,6},{6,5},{7,8},{8,7},{9,10},{10,9},{11,... | collective-permute-start | bytes 245768 | tf_op jit(solution)/shard_map/ppermute | solution.py:555
  34.5 0.6 %collective-permute-done.13.refs_10_ = bf16[160,256]{1,0:T(8,128)(2,1)S(1)} collective-permute-done((bf16[160,256]{1,0:T(8,128)(2,1)S(1)}, bf16[160,256]{1,0:T(8,128)(2,1)S(1)}, u32[]{:S(2)}, u32[]{:S(2)}) %collective-permute-start.13) | collective-permute-done | bytes 81952 | tf_op jit(solution)/shard_map/ppermute | solution.py:556
  35.1 0.0 collective-permute-done.14.refs_11_
  35.1 0.9 %collective-permute-done.12.refs_3_ = f32[96,256]{1,0:T(8,128)S(1)} collective-permute-done((f32[96,256]{1,0:T(8,128)S(1)}, f32[96,256]{1,0:T(8,128)S(1)}, u32[]{:S(2)}, u32[]{:S(2)}) %collective-permute-start.12) | collective-permute-done | bytes 98336 | tf_op jit(solution)/shard_map/ppermute | solution.py:560
  36.0 2.0 %collective-permute-done.11.refs_2_ = f32[96,256]{1,0:T(8,128)S(1)} collective-permute-done((f32[96,256]{1,0:T(8,128)S(1)}, f32[96,256]{1,0:T(8,128)S(1)}, u32[]{:S(2)}, u32[]{:S(2)}) %collective-permute-start.11) | collective-permute-done | bytes 98336 | tf_op jit(solution)/shard_map/ppermute | solution.py:560
  38.1 0.9 %collective-permute-done.10.refs_1_ = f32[96,256]{1,0:T(8,128)S(1)} collective-permute-done((f32[96,256]{1,0:T(8,128)S(1)}, f32[96,256]{1,0:T(8,128)S(1)}, u32[]{:S(2)}, u32[]{:S(2)}) %collective-permute-start.10) | collective-permute-done | bytes 98336 | tf_op jit(solution)/shard_map/ppermute | solution.py:560
  38.9 5.5 %shard_map.139 = (f32[160,768]{1,0:T(8,128)S(1)}, f32[160,768]{1,0:T(8,128)S(1)}, f32[32,2,160]{2,1,0:T(2,128)S(1)}) custom-call(f32[96,256]{1,0:T(8,128)S(1)} %get-tuple-element.53.refs_0_, f32[96,256]{1,0:T(8,128)S(1)} %collective-permute-done.10.refs_1_, f32[96,256]{1,0:T(8,128)S(1)} %collective-permute-done.11.refs_2_, ...), custom_call_target="tpu_custom_call" | custom-call | tf_op jit(solution)/shard_map/pallas_call | solution.py:572
  44.5 15.0 %all_to_all.5.sums_ref = f32[32,2,160]{2,1,0:T(2,128)S(1)} all-to-all(f32[32,2,160]{2,1,0:T(2,128)S(1)} %get-tuple-element.61), channel_id=1, replica_groups=mesh['grp'=4,'sub'=8] {'grp','sub'}, dimensions={0} | all-to-all | bytes 81920 | tf_op jit(solution)/shard_map/all_to_all | solution.py:585
  59.5 1.1 %shard_map.140 = (f32[160,768]{1,0:T(8,128)}, f32[160,768]{1,0:T(8,128)}) custom-call(f32[160,768]{1,0:T(8,128)S(1)} %get-tuple-element.33.x_ref, f32[160,768]{1,0:T(8,128)S(1)} %get-tuple-element.59.p_ref, f32[160,768]{1,0:T(8,128)S(1)} %get-tuple-element.58.refs_12_.r_ref, f32[160,768]{1,0:T(8,128)S(1)} %get-tuple-element.60.image_ref, ...), custom_call_target="tpu_custom_call" | custom-call | tf_op jit(solution)/shard_map/pallas_call | solution.py:586
Async XLA Ops:
  2.4 1.5 %collective-permute-start = (bf16[256,128]{1,0:T(8,128)(2,1)S(1)}, bf16[256,128]{1,0:T(8,128)(2,1)S(1)}, u32[]{:S(2)}, u32[]{:S(2)}) collective-permute-start(bf16[256,128]{1,0:T(8,128)(2,1)S(1)} %get-tuple-element.38), channel_id=1, source_target_pairs={{0,1},{1,0},{2,3},{3,2},{4,5},{5,4},{6,7},{7,6},{8,9},{9,8},{10,11... | collective-permute-start | bytes 196616 | tf_op jit(solution)/shard_map/ppermute | solution.py:531
  4.4 2.3 %collective-permute-start.1 = (bf16[672,128]{1,0:T(8,128)(2,1)S(1)}, bf16[672,128]{1,0:T(8,128)(2,1)S(1)}, u32[]{:S(2)}, u32[]{:S(2)}) collective-permute-start(bf16[672,128]{1,0:T(8,128)(2,1)S(1)} %get-tuple-element.42), channel_id=1, source_target_pairs={{1,2},{2,1},{3,4},{4,3},{5,6},{6,5},{7,8},{8,7},{9,10},{10,9},{11,... | collective-permute-start | bytes 516104 | tf_op jit(solution)/shard_map/ppermute | solution.py:536
  7.2 6.6 %collective-permute-start.2 = (bf16[160,128]{1,0:T(8,128)(2,1)S(1)}, bf16[160,128]{1,0:T(8,128)(2,1)S(1)}, u32[]{:S(2)}, u32[]{:S(2)}) collective-permute-start(bf16[160,128]{1,0:T(8,128)(2,1)S(1)} %get-tuple-element.51), channel_id=1, source_target_pairs={{0,1},{1,0},{2,3},{3,2},{4,5},{5,4},{6,7},{7,6},{8,9},{9,8},{10,11... | collective-permute-start | bytes 122888 | tf_op jit(solution)/shard_map/ppermute | solution.py:546
  14.5 8.8 %collective-permute-start.5 = (f32[32,256]{1,0:T(8,128)S(1)}, f32[32,256]{1,0:T(8,128)S(1)}, u32[]{:S(2)}, u32[]{:S(2)}) collective-permute-start(f32[32,256]{1,0:T(8,128)S(1)} %get-tuple-element.52.refs_0_), channel_id=1, source_target_pairs={{0,6},{1,7},{2,4},{3,5},{4,2},{5,3},{6,0},{7,1},{8,14},{9,15},{10,... | collective-permute-start | bytes 98312 | tf_op jit(solution)/shard_map/ppermute | solution.py:560
  21.0 4.8 %collective-permute-start.4 = (f32[32,256]{1,0:T(8,128)S(1)}, f32[32,256]{1,0:T(8,128)S(1)}, u32[]{:S(2)}, u32[]{:S(2)}) collective-permute-start(f32[32,256]{1,0:T(8,128)S(1)} %get-tuple-element.52.refs_0_), channel_id=1, source_target_pairs={{0,4},{1,5},{2,6},{3,7},{4,0},{5,1},{6,2},{7,3},{8,12},{9,13},{10,... | collective-permute-start | bytes 98312 | tf_op jit(solution)/shard_map/ppermute | solution.py:560
  21.0 4.8 %collective-permute-start.3 = (f32[32,256]{1,0:T(8,128)S(1)}, f32[32,256]{1,0:T(8,128)S(1)}, u32[]{:S(2)}, u32[]{:S(2)}) collective-permute-start(f32[32,256]{1,0:T(8,128)S(1)} %get-tuple-element.52.refs_0_), channel_id=1, source_target_pairs={{0,2},{1,3},{2,0},{3,1},{4,6},{5,7},{6,4},{7,5},{8,10},{9,11},{10,... | collective-permute-start | bytes 98312 | tf_op jit(solution)/shard_map/ppermute | solution.py:560
  21.7 4.7 %collective-permute-start.6 = (f32[32,256]{1,0:T(8,128)S(1)}, f32[32,256]{1,0:T(8,128)S(1)}, u32[]{:S(2)}, u32[]{:S(2)}) collective-permute-start(f32[32,256]{1,0:T(8,128)S(1)} %get-tuple-element.52.refs_0_), channel_id=1, source_target_pairs={{0,1},{1,0},{2,3},{3,2},{4,5},{5,4},{6,7},{7,6},{8,9},{9,8},{10,11... | collective-permute-start | bytes 98312 | tf_op jit(solution)/shard_map/ppermute | solution.py:563
  23.3 3.1 %collective-permute-start.9 = (f32[32,256]{1,0:T(8,128)S(1)}, f32[32,256]{1,0:T(8,128)S(1)}, u32[]{:S(2)}, u32[]{:S(2)}) collective-permute-start(f32[32,256]{1,0:T(8,128)S(1)} %collective-permute-done.5.refs_3_), channel_id=1, source_target_pairs={{0,1},{1,0},{2,3},{3,2},{4,5},{5,4},{6,7},{7,6},{8,9},{9,8},{10,11... | collective-permute-start | bytes 98312 | tf_op jit(solution)/shard_map/ppermute | solution.py:563
  25.8 1.2 %collective-permute-start.8 = (f32[32,256]{1,0:T(8,128)S(1)}, f32[32,256]{1,0:T(8,128)S(1)}, u32[]{:S(2)}, u32[]{:S(2)}) collective-permute-start(f32[32,256]{1,0:T(8,128)S(1)} %collective-permute-done.4.refs_2_), channel_id=1, source_target_pairs={{0,1},{1,0},{2,3},{3,2},{4,5},{5,4},{6,7},{7,6},{8,9},{9,8},{10,11... | collective-permute-start | bytes 98312 | tf_op jit(solution)/shard_map/ppermute | solution.py:563
  25.8 1.4 %collective-permute-start.7 = (f32[32,256]{1,0:T(8,128)S(1)}, f32[32,256]{1,0:T(8,128)S(1)}, u32[]{:S(2)}, u32[]{:S(2)}) collective-permute-start(f32[32,256]{1,0:T(8,128)S(1)} %collective-permute-done.3.refs_1_), channel_id=1, source_target_pairs={{0,1},{1,0},{2,3},{3,2},{4,5},{5,4},{6,7},{7,6},{8,9},{9,8},{10,11... | collective-permute-start | bytes 98312 | tf_op jit(solution)/shard_map/ppermute | solution.py:563
  29.9 6.1 %collective-permute-start.12 = (f32[96,256]{1,0:T(8,128)S(1)}, f32[96,256]{1,0:T(8,128)S(1)}, u32[]{:S(2)}, u32[]{:S(2)}) collective-permute-start(f32[96,256]{1,0:T(8,128)S(1)} %get-tuple-element.53.refs_0_), channel_id=1, source_target_pairs={{0,24},{1,25},{2,26},{3,27},{4,28},{5,29},{6,30},{7,31},{8,16},{9,... | collective-permute-start | bytes 294920 | tf_op jit(solution)/shard_map/ppermute | solution.py:560
  32.0 6.0 %collective-permute-start.11 = (f32[96,256]{1,0:T(8,128)S(1)}, f32[96,256]{1,0:T(8,128)S(1)}, u32[]{:S(2)}, u32[]{:S(2)}) collective-permute-start(f32[96,256]{1,0:T(8,128)S(1)} %get-tuple-element.53.refs_0_), channel_id=1, source_target_pairs={{0,16},{1,17},{2,18},{3,19},{4,20},{5,21},{6,22},{7,23},{8,24},{9,... | collective-permute-start | bytes 294920 | tf_op jit(solution)/shard_map/ppermute | solution.py:560
  33.9 5.1 %collective-permute-start.10 = (f32[96,256]{1,0:T(8,128)S(1)}, f32[96,256]{1,0:T(8,128)S(1)}, u32[]{:S(2)}, u32[]{:S(2)}) collective-permute-start(f32[96,256]{1,0:T(8,128)S(1)} %get-tuple-element.53.refs_0_), channel_id=1, source_target_pairs={{0,8},{1,9},{2,10},{3,11},{4,12},{5,13},{6,14},{7,15},{8,0},{9,1},... | collective-permute-start | bytes 294920 | tf_op jit(solution)/shard_map/ppermute | solution.py:560
  33.9 1.3 %collective-permute-start.13 = (bf16[160,256]{1,0:T(8,128)(2,1)S(1)}, bf16[160,256]{1,0:T(8,128)(2,1)S(1)}, u32[]{:S(2)}, u32[]{:S(2)}) collective-permute-start(bf16[160,256]{1,0:T(8,128)(2,1)S(1)} %get-tuple-element.56), channel_id=1, source_target_pairs={{0,1},{1,0},{2,3},{3,2},{4,5},{5,4},{6,7},{7,6},{8,9},{9,8},{10,11... | collective-permute-start | bytes 245768 | tf_op jit(solution)/shard_map/ppermute | solution.py:556
  33.9 1.3 %collective-permute-start.14 = (bf16[160,256]{1,0:T(8,128)(2,1)S(1)}, bf16[160,256]{1,0:T(8,128)(2,1)S(1)}, u32[]{:S(2)}, u32[]{:S(2)}) collective-permute-start(bf16[160,256]{1,0:T(8,128)(2,1)S(1)} %get-tuple-element.57), channel_id=1, source_target_pairs={{1,2},{2,1},{3,4},{4,3},{5,6},{6,5},{7,8},{8,7},{9,10},{10,9},{11,... | collective-permute-start | bytes 245768 | tf_op jit(solution)/shard_map/ppermute | solution.py:555

commit v9 on v8

--- a/solution.py
+++ b/solution.py
@@ -60,7 +60,7 @@
 
 
 def load_kernel(x_hbm, rows_hbm, up_hbm, basis_hbm, b_hbm, diag_hbm, values_hbm, cols_hbm, cl_hbm, cr_hbm,
-                to_pair_ref, to_other_ref, basis_other_ref, x_ref, rows_ref, basis_ref, b_ref, diag_ref, operator_ref,
+                to_pair_ref, to_other_ref, basis_pair_ref, basis_other_ref, x_ref, rows_ref, basis_ref, b_ref, diag_ref, operator_ref,
                 up_ref, cols_ref, values_ref, sems):
     blocks, nonzeros, size = values_hbm.shape[1], values_hbm.shape[2], values_hbm.shape[3]
     cases, rows = x_ref.shape
@@ -90,21 +90,23 @@
     parts = [part.astype(F32) for part in split_three(up_ref[0])]
     modes = up_ref.shape[1]
     parts.append(jnp.zeros((modes, margin - 3 * modes), F32))
-    to_pair_ref[cases:cases + modes, :] = jnp.concatenate(parts, axis=1).astype(BF16)
+    to_pair_ref[cases:, :] = jnp.concatenate(parts, axis=1).astype(BF16)
     basis = basis_ref[0]
     even = is_even()
     head, tail = basis[:, :margin], basis[:, margin + rows:]
     picked = mm(basis[:, margin:margin + rows], place).astype(BF16)
-    to_pair_ref[cases + modes:cases + 2 * modes, :] = jnp.where(even, tail, head)
-    to_pair_ref[cases + 2 * modes:, :] = picked[:, :margin]
-    basis_other_ref[:modes, :] = jnp.where(even, head, tail)
-    basis_other_ref[modes:, :] = picked[:, margin:]
-    for copy in copies[4:]:
+    basis_pair_ref[:, :margin] = jnp.where(even, tail, head)
+    basis_pair_ref[:, margin:] = picked[:, :margin]
+    basis_other_ref[:, :margin] = jnp.where(even, head, tail)
+    basis_other_ref[:, margin:] = picked[:, margin:]
+    for copy in copies[4:6]:
         copy.wait()
     for i in range(blocks):
         for t in range(nonzeros):
             start = pl.multiple_of(cols_ref[t, 0, i] * size, size)
             operator_ref[i * size:(i + 1) * size, pl.ds(start, size)] = values_ref[0, i, t]
+    for copy in copies[6:]:
+        copy.wait()
 
 
 def own_kernel(x_ref, b_ref, diag_ref, operator_ref, partial_ref):
@@ -114,7 +116,7 @@
     partial_ref[...] = b_ref[...] - diag * x - mm_nt(x.astype(BF16), operator_ref[:, :rows])
 
 
-def offer_kernel(partial_ref, operator_ref, rows_ref, pair_ref, to_other_ref, basis_other_ref, known_ref, message_ref):
+def offer_kernel(partial_ref, operator_ref, rows_ref, pair_ref, to_other_ref, known_ref, message_ref):
     cases, rows = partial_ref.shape
     margin = rows_ref.shape[2]
     even = is_even()
@@ -129,14 +131,13 @@
     message_ref[:cases, :] = to_other_ref[...]
     message_ref[cases:2 * cases, :] = mm(high, place).astype(BF16)
     message_ref[2 * cases:3 * cases, :] = mm(low, place).astype(BF16)
-    message_ref[3 * cases:3 * cases + margin, :] = mm_t(place, from_other).astype(BF16)
-    message_ref[3 * cases + margin:, :] = basis_other_ref[...]
+    message_ref[3 * cases:, :] = mm_t(place, from_other).astype(BF16)
 
 
 def inverse_kernel(first_pair_ref, inverse_hbm, diag_hbm, up_hbm,
                    inverse_ref, factor_ref, plain_ref, blocks_ref, sems):
     size = diag_hbm.shape[1]
-    cases = first_pair_ref.shape[0] - 3 * size
+    cases = first_pair_ref.shape[0] - size
     copies = copy_all(
         [
             (diag_hbm, blocks_ref.at[0:1]),
@@ -145,7 +146,7 @@
         ],
         sems,
     )
-    parts = first_pair_ref[cases:cases + size, :].astype(F32)
+    parts = first_pair_ref[cases:, :].astype(F32)
     up_left = parts[:, :size] + (parts[:, size:2 * size] + parts[:, 2 * size:3 * size])
     for copy in copies[:2]:
         copy.wait()
@@ -177,7 +178,7 @@
     place = place_matrix(jnp.where(even, rows_ref[0, 1:2, :], rows_ref[0, 0:1, :]), rows)
     to_pair_ref[...] = mm(rounded, place).astype(BF16)
     offered = other_ref[cases:2 * cases, :].astype(F32) + other_ref[2 * cases:3 * cases, :].astype(F32)
-    halo_ref[...] = (offered - mm_nt(sent_ref[...], other_ref[3 * cases:3 * cases + margin, :])).astype(BF16)
+    halo_ref[...] = (offered - mm_nt(sent_ref[...], other_ref[3 * cases:, :])).astype(BF16)
 
 
 def own_local_kernel(rb_ref, inverse_ref, basis_ref, halo_ref, local_ref, coarse_ref):
@@ -191,8 +192,8 @@
     coarse_ref[...] = mm_nt(basis_ref[0], extended)
 
 
-def local_kernel(own_local_ref, own_coarse_ref, inverse_ref, basis_ref, factor_ref, plain_ref, pair_ref, rows_ref,
-                 local_ref, message_ref, to_pair_ref, to_other_ref):
+def local_kernel(own_local_ref, own_coarse_ref, inverse_ref, basis_ref, factor_ref, plain_ref, pair_ref,
+                 local_ref, message_ref):
     margin = pair_ref.shape[1]
     even = is_even()
     pair = pair_ref[...]
@@ -206,11 +207,19 @@
     message = jnp.concatenate([plain_ref[:, :3 * size], right_side], axis=1)
     message_ref[...] = message
     rows = jnp.where(even, inverse_ref[0, total - margin:, :], inverse_ref[0, :margin, :])
-    local = own_local_ref[...] + mm(pair, rows)
-    local_ref[...] = local
+    local_ref[...] = own_local_ref[...] + mm(pair, rows)
+
+
+def return_kernel(local_ref, basis_pair_ref, basis_other_ref, rows_ref, to_pair_ref, to_other_ref):
+    cases = local_ref.shape[0]
+    margin = rows_ref.shape[2]
+    even = is_even()
+    local = local_ref[...]
     left, right = rows_ref[0, 0:1, :], rows_ref[0, 1:2, :]
-    to_pair_ref[...] = return_rows(local, margin, jnp.where(even, right, left), jnp.logical_not(even))
-    to_other_ref[...] = return_rows(local, margin, jnp.where(even, left, right), even)
+    to_pair_ref[:cases, :] = return_rows(local, margin, jnp.where(even, right, left), jnp.logical_not(even))
+    to_pair_ref[cases:, :] = basis_pair_ref[...]
+    to_other_ref[:cases, :] = return_rows(local, margin, jnp.where(even, left, right), even)
+    to_other_ref[cases:, :] = basis_other_ref[...]
 
 
 def return_rows(local, margin, rows, head):
@@ -268,20 +277,22 @@
     return placed(top, 1, 1), placed(bottom, 2, 2)
 
 
+def exact_product(left, right):
+    a, b, c = split_three(left)
+    x, y, z = split_three(right)
+    return mm(jnp.concatenate([a, a, b, a, b, c], axis=1), jnp.concatenate([x, y, x, z, y, x], axis=0))
+
+
 def schur(block, solved, size):
     couplings = jnp.transpose(block[:, :4 * size])[size:3 * size]
-    product = -jnp.dot(couplings, solved, precision=lax.Precision.HIGHEST, preferred_element_type=F32)
+    product = -exact_product(couplings, solved)
     return shares(product[:size], product[size:], size)
 
 
 def first_schur(previous, block, size):
-    highest = lax.Precision.HIGHEST
-    zero = jnp.zeros_like(block)
-    above = jnp.concatenate([zero, block, zero, zero], axis=0)
-    below = jnp.concatenate([block, zero, zero, zero], axis=0)
-    top = -jnp.dot(previous[:, :4 * size], above, precision=highest, preferred_element_type=F32)
-    bottom = -jnp.dot(block[:, :4 * size], below, precision=highest, preferred_element_type=F32)
-    return shares(top, bottom, size)
+    couplings = jnp.concatenate([previous[:, size:2 * size], block[:, :size]], axis=0)
+    product = -exact_product(couplings, block)
+    return shares(product[:size], product[size:], size)
 
 
 def own_part(block, size):
@@ -312,10 +323,11 @@
     return chain[0], chain[count]
 
 
-def back(solved, left, right, size):
+def back(solved, left, right, size, alone=None):
     zero = jnp.zeros_like(left)
     stacked = jnp.concatenate([zero, left, right, zero], axis=0)
-    return solved - jnp.dot(
+    alone = solved if alone is None else alone
+    return alone - jnp.dot(
         solved[:, :4 * size], stacked, precision=lax.Precision.HIGHEST, preferred_element_type=F32)
 
 
@@ -365,13 +377,31 @@
     message_ref[2 * size:, :] = whole
 
 
+def compose_kernel(solved_ref, maps_ref, all_ref):
+    members, size, width = solved_ref.shape
+    lane = lax.broadcasted_iota(jnp.int32, (size, width), 1)
+    row = lax.broadcasted_iota(jnp.int32, (size, width), 0)
+    maps = {0: -(lane == row + size).astype(F32), members: -(lane == row + 2 * size).astype(F32)}
+    step = members // 2
+    while step >= 1:
+        for j in range(step, members, 2 * step):
+            block = solved_ref[j]
+            maps[j] = back(block, maps[j - step], maps[j + step], size, own_part(block, size))
+        step = step // 2
+    for j in range(members + 1):
+        all_ref[j] = maps[j]
+    member = lax.axis_index("sub")
+    maps_ref[0] = all_ref[jnp.maximum(member - 1, 0)]
+    maps_ref[1] = all_ref[member]
+    maps_ref[2] = all_ref[member + 1]
+
+
 def solve_kernel(*refs):
-    (*received, solved_ref, local_ref, basis_ref, rows_ref, first_pair_ref, first_other_ref, pair_ref, other_ref,
-     r_ref, diag_ref, operator_ref, p_ref, image_ref, sums_ref, messages_ref, sep_ref, x_ref) = refs
+    (*received, maps_ref, local_ref, basis_ref, rows_ref, pair_ref, other_ref, r_ref, diag_ref, operator_ref,
+     p_ref, image_ref, sums_ref, messages_ref, sep_ref) = refs
     groups = len(received)
     size, width = received[0].shape
     size = size // 3
-    members = solved_ref.shape[0]
     for d in range(groups):
         messages_ref[lax.axis_index("grp") ^ d] = received[d][...]
     chain = []
@@ -399,38 +429,27 @@
         sep_ref[g] = solution[g]
     sep_ref[groups] = jnp.zeros((size, width), F32)
     group, member = lax.axis_index("grp"), lax.axis_index("sub")
-    x_ref[0] = sep_ref[group]
-    x_ref[members] = sep_ref[group + 1]
-    step = members // 2
-    while step >= 2:
-        for j in range(step, members, 2 * step):
-            x_ref[j] = back(solved_ref[j], x_ref[j - step], x_ref[j + step], size)
-        step = step // 2
+    first, after = sep_ref[group], sep_ref[group + 1]
     before = jnp.maximum(group - 1, 0)
-    earlier = back(messages_ref[before, 2 * size:, :], sep_ref[before], sep_ref[group], size)
-    lower = jnp.maximum(member - 1, 0)
-    for odd in (member // 2 * 2 + 1, lower // 2 * 2 + 1):
-        x_ref[odd] = back(solved_ref[odd], x_ref[odd - 1], x_ref[odd + 1], size)
-    left_solution = jnp.where(member == 0, earlier, x_ref[lower])
-    right_solution = x_ref[member + 1]
+    is_first = member == 0
+    left_map = jnp.where(is_first, messages_ref[before, 2 * size:, :], maps_ref[0])
+    left_solution = back(
+        left_map, jnp.where(is_first, sep_ref[before], first), jnp.where(is_first, first, after), size)
+    own_solution = back(maps_ref[1], first, after, size)
+    right_solution = back(maps_ref[2], first, after, size)
 
     def lifted(solution, basis):
         return mm_t(solution.astype(BF16), basis)[3 * size:]
 
-    cases = pair_ref.shape[0]
+    cases = local_ref.shape[0]
     margin = rows_ref.shape[2]
     owned = p_ref.shape[1]
     even = is_even()
-
-    def columns(ref, start):
-        return jnp.concatenate([ref[start:start + size, :], ref[start + size:start + 2 * size, :]], axis=1)
-
-    pair_basis = columns(first_pair_ref, cases + size)
-    other_basis = columns(first_other_ref, 3 * cases + margin)
-    pair, other = pair_ref[...].astype(F32), other_ref[...].astype(F32)
-    left = jnp.where(even, other, pair) + lifted(left_solution, jnp.where(even, other_basis, pair_basis))
-    right = jnp.where(even, pair, other) + lifted(right_solution, jnp.where(even, pair_basis, other_basis))
-    correction = local_ref[...] + lifted(x_ref[member], basis_ref[0])
+    pair, other = pair_ref[...], other_ref[...]
+    left, right = jnp.where(even, other, pair), jnp.where(even, pair, other)
+    left = left[:cases].astype(F32) + lifted(left_solution, left[cases:])
+    right = right[:cases].astype(F32) + lifted(right_solution, right[cases:])
+    correction = local_ref[...] + lifted(own_solution, basis_ref[0])
     place = place_matrix(jnp.concatenate([rows_ref[0, 0:1, :], rows_ref[0, 1:2, :]], axis=1), owned)
     tails = jnp.concatenate([left[:, :margin], right[:, :margin]], axis=1).astype(BF16)
     p = correction[:, margin:margin + owned] + mm_nt(tails, place)
@@ -457,23 +476,30 @@
     return mm_nt(jnp.ones((8, lanes), F32), total, precision=lax.Precision.HIGHEST)
 
 
-def finish_kernel(x_ref, p_ref, r_ref, image_ref, sums_ref, out_x_ref, out_r_ref):
+def finish_kernel(x_ref, p_ref, r_ref, image_ref, sums_ref, out_x_hbm, out_r_hbm, new_x_ref, new_r_ref, sems):
     sums = jnp.sum(sums_ref[...], axis=0)
     row = sums[0:1, :] / sums[1:2, :]
     lanes = 128
     step = jnp.transpose(jnp.broadcast_to(row, (lanes, row.shape[1])))
-    for start in range(0, x_ref.shape[1], lanes):
-        span = slice(start, start + lanes)
-        out_x_ref[:, span] = x_ref[:, span] + step * p_ref[:, span]
-        out_r_ref[:, span] = r_ref[:, span] - step * image_ref[:, span]
-
-
-def call(kernel, out, in_specs, scratch=()):
+    copies = []
+    for chunk in range(x_ref.shape[1] // lanes):
+        span = slice(chunk * lanes, (chunk + 1) * lanes)
+        new_x_ref[:, span] = x_ref[:, span] + step * p_ref[:, span]
+        new_r_ref[:, span] = r_ref[:, span] - step * image_ref[:, span]
+        for n, (source, target) in enumerate(((new_x_ref, out_x_hbm), (new_r_ref, out_r_hbm))):
+            copy = pltpu.make_async_copy(source.at[:, span], target.at[:, span], sems.at[n, chunk])
+            copy.start()
+            copies.append(copy)
+    for copy in copies:
+        copy.wait()
+
+
+def call(kernel, out, in_specs, scratch=(), out_spec=VMEM):
     return pl.pallas_call(
         kernel,
         out_shape=out,
         in_specs=in_specs,
-        out_specs=[VMEM] * len(out),
+        out_specs=[out_spec] * len(out),
         scratch_shapes=list(scratch),
         compiler_params=pltpu.CompilerParams(vmem_limit_bytes=16 * 2**20),
     )
@@ -505,12 +531,13 @@
     halo = struct((cases, margin), BF16)
     full = struct((cases, rows), F32)
     semaphores = pltpu.SemaphoreType.DMA
-    to_pair, to_other, basis_other, start, send_rows, basis, loads, diag, operator = call(
+    to_pair, to_other, basis_pair, basis_other, start, send_rows, basis, loads, diag, operator = call(
         load_kernel,
         [
-            struct((cases + 3 * modes, margin), BF16),
+            struct((cases + modes, margin), BF16),
             halo,
-            struct((2 * modes, margin), BF16),
+            struct((modes, 2 * margin), BF16),
+            struct((modes, 2 * margin), BF16),
             full,
             struct(send_rows.shape, send_rows.dtype),
             struct(basis.shape, BF16),
@@ -530,9 +557,9 @@
     ))
     first_pair = lax.ppermute(to_pair, AXES, pairs)
     (partial,) = call(own_kernel, [full], [VMEM] * 4)(start, loads, diag, operator)
-    known, message = call(
-        offer_kernel, [full, struct((3 * cases + margin + 2 * modes, margin), BF16)], [VMEM] * 6
-    )(partial, operator, send_rows, first_pair, to_other, basis_other)
+    known, message = call(offer_kernel, [full, struct((3 * cases + margin, margin), BF16)], [VMEM] * 5)(
+        partial, operator, send_rows, first_pair, to_other
+    )
     first_other = lax.ppermute(message, AXES, others)
     inverse, factor, plain = call(
         inverse_kernel,
@@ -548,10 +575,11 @@
         rounded, inverse, basis, other_halo
     )
     chips = members // 2
-    returned = struct((cases, 2 * margin), BF16)
-    local, message, to_pair, to_other = call(
-        local_kernel, [struct((cases, extended), F32), struct((modes, width), F32), returned, returned], [VMEM] * 8
-    )(local, coarse, inverse, basis, factor, plain, pair_halo, send_rows)
+    local, message = call(
+        local_kernel, [struct((cases, extended), F32), struct((modes, width), F32)], [VMEM] * 7
+    )(local, coarse, inverse, basis, factor, plain, pair_halo)
+    returned = struct((cases + modes, 2 * margin), BF16)
+    to_pair, to_other = call(return_kernel, [returned, returned], [VMEM] * 4)(local, basis_pair, basis_other, send_rows)
     from_other = lax.ppermute(to_other, AXES, others)
     from_pair = lax.ppermute(to_pair, AXES, pairs)
 
@@ -569,21 +597,26 @@
         [block],
     )(*same, *opposite)
     reduced = partners(reduced, members, groups)
+    (maps,) = call(
+        compose_kernel,
+        [struct((3, modes, width), F32)],
+        [VMEM],
+        [pltpu.VMEM((members + 1, modes, width), F32)],
+    )(solved)
     direction, image, sums = call(
         solve_kernel,
         [full, full, struct((total, 2, cases), F32)],
-        [VMEM] * (groups + 11),
-        [
-            pltpu.VMEM((groups, 3 * modes, width), F32),
-            pltpu.VMEM((groups + 1, modes, width), F32),
-            pltpu.VMEM((members + 1, modes, width), F32),
-        ],
-    )(
-        *reduced, solved, local, basis, send_rows, first_pair, first_other, from_pair, from_other,
-        residual, diag, operator
-    )
+        [VMEM] * (groups + 9),
+        [pltpu.VMEM((groups, 3 * modes, width), F32), pltpu.VMEM((groups + 1, modes, width), F32)],
+    )(*reduced, maps, local, basis, send_rows, from_pair, from_other, residual, diag, operator)
     sums = lax.all_to_all(sums, AXES, 0, 0, tiled=True)
-    iterate, residual = call(finish_kernel, [full, full], [VMEM] * 5)(start, direction, residual, image, sums)
+    iterate, residual = call(
+        finish_kernel,
+        [full, full],
+        [VMEM] * 5,
+        [pltpu.VMEM((cases, rows), F32), pltpu.VMEM((cases, rows), F32), semaphores((2, rows // margin))],
+        HBM,
+    )(start, direction, residual, image, sums)
     return iterate.T, residual.T
 
 

time: 60.9 us -> 58 us (0.952)
  blocking collectives: 15 us -> 10.5 us
  starting transfers between devices: 19.2 us -> 22.8 us
  waiting for transfers between devices: 10.1 us -> 8.01 us
    all_to_all x1, blocking collectives: 15 us -> 10.5 us  [shards(): sums = lax.all_to_all(sums, AXES, 0, 0, tiled=True)]
    ppermute x6, starting transfers between devices: 11.1 us -> 14.7 us  [partners(): return [value] + [lax.ppermute(value, AXES, swap) for swap in swaps]]
    pallas_call x3 -> x5, Pallas kernels: 3.47 us -> 4.42 us  [the longest x1 1.65 us: shards(): call(load_kernel, [struct((cases + modes, margin), BF16), halo, struct((m...]
    ppermute x4, waiting for transfers between devices: 0.86 us -> 0.01 us  [shards(): opposite = [lax.ppermute(value, AXES, pairs) for value in same]]
    pallas_call x1, Pallas kernels: 5.52 us -> 4.85 us  [shards(): call(solve_kernel, [full, full, struct((total, 2, cases), F32)], [VMEM] *...]
    ppermute x1, waiting for transfers between devices: 0.61 us -> 0.01 us  [shards(): from_pair = lax.ppermute(to_pair, AXES, pairs)]
  transfers between devices with their start and end apart: 15 -> 15, of which waited for: 10 -> 7; matrix products, arithmetic and copies ran while one was open for 0% -> 0% of each run, Pallas kernels for 5% -> 11%
where the time goes in v9:
time: 58 us; the launch traced here: 57.8 us
  starting transfers between devices  22.8 us (39%)
  Pallas kernels  15.7 us (27%)
  blocking collectives  10.5 us (18%)
  waiting for transfers between devices  8.01 us (14%)
  between operations  0.79 us (1%)
    ppermute x6, starting transfers between devices, partners(): return [value] + [lax.ppermute(value, AXES, swap) for swap in swaps]  14.7 us
    all_to_all x1, blocking collectives, shards(): sums = lax.all_to_all(sums, AXES, 0, 0, tiled=True)  10.5 us
    ppermute x6, waiting for transfers between devices, partners(): return [value] + [lax.ppermute(value, AXES, swap) for swap in swaps]  7.37 us
    ppermute x1, starting transfers between devices, shards(): pair_halo = lax.ppermute(to_pair, AXES, pairs)  5.55 us
    pallas_call x1, Pallas kernels, shards(): call(solve_kernel, [full, full, struct((total, 2, cases), F32)], [VMEM] *...  4.85 us
    pallas_call x1, Pallas kernels, shards(): call(group_kernel, [struct((members, modes, width), F32), struct((3 * mod...  2.77 us
    pallas_call x1, Pallas kernels, shards(): call(inverse_kernel, [struct(local_inverse.shape, BF16), struct((modes, 4...  1.66 us
    pallas_call x1, Pallas kernels, shards(): call(load_kernel, [struct((cases + modes, margin), BF16), halo, struct((m...  1.65 us
  transfers between devices with their start and end apart: 15, of which 7 were waited for; matrix products, arithmetic and copies ran while one was open for 0% of the time, Pallas kernels for 11%

profile of v9, /device:TPU:0, one launch (start us, length us, event | category | flops | bytes accessed | tf_op | source)
XLA Modules:
  0.0 57.8 jit_solution(6707797021838055187)
XLA Ops:
  0.6 1.6 %shard_map.131 = (bf16[192,128]{1,0:T(8,128)(2,1)S(1)}, bf16[160,128]{1,0:T(8,128)(2,1)S(1)}, bf16[32,256]{1,0:T(8,128)(2,1)S(1)}, bf16[32,256]{1,0:T(8,128)(2,1...) custom-call(f32[160,768]{1,0:T(8,128)} %bitcast.6, ...), custom_call_target="tpu_custom_call" | custom-call | tf_op jit(solution)/shard_map/pallas_call | solution.py:534
  2.3 0.6 collective-permute-start
  2.8 0.6 shard_map.132.partial_ref
  3.4 0.3 collective-permute-done.pair_ref.first_pair_ref
  3.7 0.5 shard_map.133
  4.3 0.7 %collective-permute-start.1 = (bf16[608,128]{1,0:T(8,128)(2,1)S(1)}, bf16[608,128]{1,0:T(8,128)(2,1)S(1)}, u32[]{:S(2)}, u32[]{:S(2)}) collective-permute-start(bf16[608,128]{1,0:T(8,128)(2,1)S(1)} %get-tuple-element.42), channel_id=1, source_target_pairs={{1,2},{2,1},{3,4},{4,3},{5,6},{6,5},{7,8},{8,7},{9,10},{10,9},{11,... | collective-permute-start | bytes 466952 | tf_op jit(solution)/shard_map/ppermute | solution.py:563
  4.9 1.7 %shard_map.134 = (bf16[1,1024,1024]{2,1,0:T(8,128)(2,1)S(1)}, f32[32,128]{1,0:T(8,128)S(1)}, f32[32,128]{1,0:T(8,128)S(1)}) custom-call(bf16[192,128]{1,0:T(8,128)(2,1)S(1)} %collective-permute-done.pair_ref.first_pair_ref, bf16[1,1024,1024]{2,1,0:T(8,128)(2,1)} %inverse_hbm.1, f32[1,32,32]{2,1,0:T(8,128)} %diag_hbm.3, f32[1,32,32]{2,1,0:T(8,128)} %up_hbm.3), custom_call_target="tpu_custom_call" | custom-call | tf_op jit(solution)/shard_map/pallas_call | solution.py:564
  6.6 0.0 collective-permute-done.1.other_ref
  6.6 0.4 shard_map.135
  7.0 5.5 %collective-permute-start.2 = (bf16[160,128]{1,0:T(8,128)(2,1)S(1)}, bf16[160,128]{1,0:T(8,128)(2,1)S(1)}, u32[]{:S(2)}, u32[]{:S(2)}) collective-permute-start(bf16[160,128]{1,0:T(8,128)(2,1)S(1)} %get-tuple-element.51), channel_id=1, source_target_pairs={{0,1},{1,0},{2,3},{3,2},{4,5},{5,4},{6,7},{7,6},{8,9},{9,8},{10,11... | collective-permute-start | bytes 122888 | tf_op jit(solution)/shard_map/ppermute | solution.py:573
  12.6 0.6 shard_map.136
  13.2 0.3 collective-permute-done.2.pair_ref
  13.5 0.4 shard_map.137
  13.9 6.6 %collective-permute-start.5 = (f32[32,256]{1,0:T(8,128)S(1)}, f32[32,256]{1,0:T(8,128)S(1)}, u32[]{:S(2)}, u32[]{:S(2)}) collective-permute-start(f32[32,256]{1,0:T(8,128)S(1)} %get-tuple-element.52.refs_0_), channel_id=1, source_target_pairs={{0,6},{1,7},{2,4},{3,5},{4,2},{5,3},{6,0},{7,1},{8,14},{9,15},{10,... | collective-permute-start | bytes 98312 | tf_op jit(solution)/shard_map/ppermute | solution.py:588
  20.5 0.0 collective-permute-start.4
  20.5 0.6 %collective-permute-start.3 = (f32[32,256]{1,0:T(8,128)S(1)}, f32[32,256]{1,0:T(8,128)S(1)}, u32[]{:S(2)}, u32[]{:S(2)}) collective-permute-start(f32[32,256]{1,0:T(8,128)S(1)} %get-tuple-element.52.refs_0_), channel_id=1, source_target_pairs={{0,2},{1,3},{2,0},{3,1},{4,6},{5,7},{6,4},{7,5},{8,10},{9,11},{10,... | collective-permute-start | bytes 98312 | tf_op jit(solution)/shard_map/ppermute | solution.py:588
  21.1 0.0 collective-permute-start.6
  21.1 1.6 %collective-permute-done.5.refs_3_ = f32[32,256]{1,0:T(8,128)S(1)} collective-permute-done((f32[32,256]{1,0:T(8,128)S(1)}, f32[32,256]{1,0:T(8,128)S(1)}, u32[]{:S(2)}, u32[]{:S(2)}) %collective-permute-start.5) | collective-permute-done | bytes 32800 | tf_op jit(solution)/shard_map/ppermute | solution.py:588
  22.7 0.0 collective-permute-start.9
  22.7 2.6 %collective-permute-done.4.refs_2_ = f32[32,256]{1,0:T(8,128)S(1)} collective-permute-done((f32[32,256]{1,0:T(8,128)S(1)}, f32[32,256]{1,0:T(8,128)S(1)}, u32[]{:S(2)}, u32[]{:S(2)}) %collective-permute-start.4) | collective-permute-done | bytes 32800 | tf_op jit(solution)/shard_map/ppermute | solution.py:588
  25.3 0.0 collective-permute-start.8
  25.3 0.0 collective-permute-done.3.refs_1_
  25.3 0.5 collective-permute-start.7
  25.8 0.3 shard_map.140
  26.2 0.1 collective-permute-start.13
  26.2 0.0 collective-permute-done.6.refs_4_
  26.2 0.7 %collective-permute-start.14 = (bf16[192,256]{1,0:T(8,128)(2,1)S(1)}, bf16[192,256]{1,0:T(8,128)(2,1)S(1)}, u32[]{:S(2)}, u32[]{:S(2)}) collective-permute-start(bf16[192,256]{1,0:T(8,128)(2,1)S(1)} %get-tuple-element.59), channel_id=1, source_target_pairs={{1,2},{2,1},{3,4},{4,3},{5,6},{6,5},{7,8},{8,7},{9,10},{10,9},{11,... | collective-permute-start | bytes 294920 | tf_op jit(solution)/shard_map/ppermute | solution.py:583
  26.9 0.0 collective-permute-done.9.refs_7_
  26.9 0.0 collective-permute-done.8.refs_6_
  26.9 0.0 collective-permute-done.7.refs_5_
  26.9 2.8 %shard_map.138 = (f32[8,32,256]{2,1,0:T(8,128)S(1)}, f32[96,256]{1,0:T(8,128)S(1)}) custom-call(f32[32,256]{1,0:T(8,128)S(1)} %get-tuple-element.52.refs_0_, f32[32,256]{1,0:T(8,128)S(1)} %collective-permute-done.3.refs_1_, f32[32,256]{1,0:T(8,128)S(1)} %collective-permute-done.4.refs_2_, f32[32,256]{1,0:T(8,128)S(1)} %collective-permute-done.5.refs_3_, ...), custom_call_target="tpu_custom_call" | custom-call | tf_op jit(solution)/shard_map/pallas_call | solution.py:593
  29.7 6.4 %collective-permute-start.12 = (f32[96,256]{1,0:T(8,128)S(1)}, f32[96,256]{1,0:T(8,128)S(1)}, u32[]{:S(2)}, u32[]{:S(2)}) collective-permute-start(f32[96,256]{1,0:T(8,128)S(1)} %get-tuple-element.53.refs_0_), channel_id=1, source_target_pairs={{0,24},{1,25},{2,26},{3,27},{4,28},{5,29},{6,30},{7,31},{8,16},{9,... | collective-permute-start | bytes 294920 | tf_op jit(solution)/shard_map/ppermute | solution.py:588
  36.1 0.0 collective-permute-start.11
  36.1 1.1 %collective-permute-start.10 = (f32[96,256]{1,0:T(8,128)S(1)}, f32[96,256]{1,0:T(8,128)S(1)}, u32[]{:S(2)}, u32[]{:S(2)}) collective-permute-start(f32[96,256]{1,0:T(8,128)S(1)} %get-tuple-element.53.refs_0_), channel_id=1, source_target_pairs={{0,8},{1,9},{2,10},{3,11},{4,12},{5,13},{6,14},{7,15},{8,0},{9,1},... | collective-permute-start | bytes 294920 | tf_op jit(solution)/shard_map/ppermute | solution.py:588
  37.2 0.6 %shard_map.139.refs_4_ = f32[3,32,256]{2,1,0:T(8,128)S(1)} custom-call(f32[8,32,256]{2,1,0:T(8,128)S(1)} %get-tuple-element.54.solved_ref), custom_call_target="tpu_custom_call" | custom-call | tf_op jit(solution)/shard_map/pallas_call | solution.py:600
  37.9 0.0 collective-permute-done.13.refs_8_
  37.9 0.0 collective-permute-done.14.refs_9_
  37.9 1.1 %collective-permute-done.12.refs_3_ = f32[96,256]{1,0:T(8,128)S(1)} collective-permute-done((f32[96,256]{1,0:T(8,128)S(1)}, f32[96,256]{1,0:T(8,128)S(1)}, u32[]{:S(2)}, u32[]{:S(2)}) %collective-permute-start.12) | collective-permute-done | bytes 98336 | tf_op jit(solution)/shard_map/ppermute | solution.py:588
  39.0 1.7 %collective-permute-done.11.refs_2_ = f32[96,256]{1,0:T(8,128)S(1)} collective-permute-done((f32[96,256]{1,0:T(8,128)S(1)}, f32[96,256]{1,0:T(8,128)S(1)}, u32[]{:S(2)}, u32[]{:S(2)}) %collective-permute-start.11) | collective-permute-done | bytes 98336 | tf_op jit(solution)/shard_map/ppermute | solution.py:588
  40.7 0.4 collective-permute-done.10.refs_1_
  41.1 4.8 %shard_map.141 = (f32[160,768]{1,0:T(8,128)S(1)}, f32[160,768]{1,0:T(8,128)S(1)}, f32[32,2,160]{2,1,0:T(2,128)S(1)}) custom-call(f32[96,256]{1,0:T(8,128)S(1)} %get-tuple-element.53.refs_0_, f32[96,256]{1,0:T(8,128)S(1)} %collective-permute-done.10.refs_1_, f32[96,256]{1,0:T(8,128)S(1)} %collective-permute-done.11.refs_2_, ...), custom_call_target="tpu_custom_call" | custom-call | tf_op jit(solution)/shard_map/pallas_call | solution.py:606
  46.0 10.5 %all_to_all.5.sums_ref = f32[32,2,160]{2,1,0:T(2,128)S(1)} all-to-all(f32[32,2,160]{2,1,0:T(2,128)S(1)} %get-tuple-element.63), channel_id=1, replica_groups=mesh['grp'=4,'sub'=8] {'grp','sub'}, dimensions={0} | all-to-all | bytes 81920 | tf_op jit(solution)/shard_map/all_to_all | solution.py:612
  56.5 1.2 %shard_map.142 = (f32[160,768]{1,0:T(8,128)}, f32[160,768]{1,0:T(8,128)}) custom-call(f32[160,768]{1,0:T(8,128)S(1)} %get-tuple-element.34.x_ref, f32[160,768]{1,0:T(8,128)S(1)} %get-tuple-element.61.p_ref, f32[160,768]{1,0:T(8,128)S(1)} %get-tuple-element.60.refs_10_.r_ref, f32[160,768]{1,0:T(8,128)S(1)} %get-tuple-element.62.image_ref, ...), custom_call_target="tpu_custom_call" | custom-call | tf_op jit(solution)/shard_map/pallas_call | solution.py:613
Async XLA Ops:
  2.3 1.4 %collective-permute-start = (bf16[192,128]{1,0:T(8,128)(2,1)S(1)}, bf16[192,128]{1,0:T(8,128)(2,1)S(1)}, u32[]{:S(2)}, u32[]{:S(2)}) collective-permute-start(bf16[192,128]{1,0:T(8,128)(2,1)S(1)} %get-tuple-element.39), channel_id=1, source_target_pairs={{0,1},{1,0},{2,3},{3,2},{4,5},{5,4},{6,7},{7,6},{8,9},{9,8},{10,11... | collective-permute-start | bytes 147464 | tf_op jit(solution)/shard_map/ppermute | solution.py:558
  4.3 2.3 %collective-permute-start.1 = (bf16[608,128]{1,0:T(8,128)(2,1)S(1)}, bf16[608,128]{1,0:T(8,128)(2,1)S(1)}, u32[]{:S(2)}, u32[]{:S(2)}) collective-permute-start(bf16[608,128]{1,0:T(8,128)(2,1)S(1)} %get-tuple-element.42), channel_id=1, source_target_pairs={{1,2},{2,1},{3,4},{4,3},{5,6},{6,5},{7,8},{8,7},{9,10},{10,9},{11,... | collective-permute-start | bytes 466952 | tf_op jit(solution)/shard_map/ppermute | solution.py:563
  7.0 6.4 %collective-permute-start.2 = (bf16[160,128]{1,0:T(8,128)(2,1)S(1)}, bf16[160,128]{1,0:T(8,128)(2,1)S(1)}, u32[]{:S(2)}, u32[]{:S(2)}) collective-permute-start(bf16[160,128]{1,0:T(8,128)(2,1)S(1)} %get-tuple-element.51), channel_id=1, source_target_pairs={{0,1},{1,0},{2,3},{3,2},{4,5},{5,4},{6,7},{7,6},{8,9},{9,8},{10,11... | collective-permute-start | bytes 122888 | tf_op jit(solution)/shard_map/ppermute | solution.py:573
  13.9 8.8 %collective-permute-start.5 = (f32[32,256]{1,0:T(8,128)S(1)}, f32[32,256]{1,0:T(8,128)S(1)}, u32[]{:S(2)}, u32[]{:S(2)}) collective-permute-start(f32[32,256]{1,0:T(8,128)S(1)} %get-tuple-element.52.refs_0_), channel_id=1, source_target_pairs={{0,6},{1,7},{2,4},{3,5},{4,2},{5,3},{6,0},{7,1},{8,14},{9,15},{10,... | collective-permute-start | bytes 98312 | tf_op jit(solution)/shard_map/ppermute | solution.py:588
  20.5 4.8 %collective-permute-start.4 = (f32[32,256]{1,0:T(8,128)S(1)}, f32[32,256]{1,0:T(8,128)S(1)}, u32[]{:S(2)}, u32[]{:S(2)}) collective-permute-start(f32[32,256]{1,0:T(8,128)S(1)} %get-tuple-element.52.refs_0_), channel_id=1, source_target_pairs={{0,4},{1,5},{2,6},{3,7},{4,0},{5,1},{6,2},{7,3},{8,12},{9,13},{10,... | collective-permute-start | bytes 98312 | tf_op jit(solution)/shard_map/ppermute | solution.py:588
  20.5 4.8 %collective-permute-start.3 = (f32[32,256]{1,0:T(8,128)S(1)}, f32[32,256]{1,0:T(8,128)S(1)}, u32[]{:S(2)}, u32[]{:S(2)}) collective-permute-start(f32[32,256]{1,0:T(8,128)S(1)} %get-tuple-element.52.refs_0_), channel_id=1, source_target_pairs={{0,2},{1,3},{2,0},{3,1},{4,6},{5,7},{6,4},{7,5},{8,10},{9,11},{10,... | collective-permute-start | bytes 98312 | tf_op jit(solution)/shard_map/ppermute | solution.py:588
  21.1 5.1 %collective-permute-start.6 = (f32[32,256]{1,0:T(8,128)S(1)}, f32[32,256]{1,0:T(8,128)S(1)}, u32[]{:S(2)}, u32[]{:S(2)}) collective-permute-start(f32[32,256]{1,0:T(8,128)S(1)} %get-tuple-element.52.refs_0_), channel_id=1, source_target_pairs={{0,1},{1,0},{2,3},{3,2},{4,5},{5,4},{6,7},{7,6},{8,9},{9,8},{10,11... | collective-permute-start | bytes 98312 | tf_op jit(solution)/shard_map/ppermute | solution.py:591
  22.7 4.2 %collective-permute-start.9 = (f32[32,256]{1,0:T(8,128)S(1)}, f32[32,256]{1,0:T(8,128)S(1)}, u32[]{:S(2)}, u32[]{:S(2)}) collective-permute-start(f32[32,256]{1,0:T(8,128)S(1)} %collective-permute-done.5.refs_3_), channel_id=1, source_target_pairs={{0,1},{1,0},{2,3},{3,2},{4,5},{5,4},{6,7},{7,6},{8,9},{9,8},{10,11... | collective-permute-start | bytes 98312 | tf_op jit(solution)/shard_map/ppermute | solution.py:591
  25.3 1.6 %collective-permute-start.8 = (f32[32,256]{1,0:T(8,128)S(1)}, f32[32,256]{1,0:T(8,128)S(1)}, u32[]{:S(2)}, u32[]{:S(2)}) collective-permute-start(f32[32,256]{1,0:T(8,128)S(1)} %collective-permute-done.4.refs_2_), channel_id=1, source_target_pairs={{0,1},{1,0},{2,3},{3,2},{4,5},{5,4},{6,7},{7,6},{8,9},{9,8},{10,11... | collective-permute-start | bytes 98312 | tf_op jit(solution)/shard_map/ppermute | solution.py:591
  25.3 1.6 %collective-permute-start.7 = (f32[32,256]{1,0:T(8,128)S(1)}, f32[32,256]{1,0:T(8,128)S(1)}, u32[]{:S(2)}, u32[]{:S(2)}) collective-permute-start(f32[32,256]{1,0:T(8,128)S(1)} %collective-permute-done.3.refs_1_), channel_id=1, source_target_pairs={{0,1},{1,0},{2,3},{3,2},{4,5},{5,4},{6,7},{7,6},{8,9},{9,8},{10,11... | collective-permute-start | bytes 98312 | tf_op jit(solution)/shard_map/ppermute | solution.py:591
  26.2 11.8 %collective-permute-start.13 = (bf16[192,256]{1,0:T(8,128)(2,1)S(1)}, bf16[192,256]{1,0:T(8,128)(2,1)S(1)}, u32[]{:S(2)}, u32[]{:S(2)}) collective-permute-start(bf16[192,256]{1,0:T(8,128)(2,1)S(1)} %get-tuple-element.58), channel_id=1, source_target_pairs={{0,1},{1,0},{2,3},{3,2},{4,5},{5,4},{6,7},{7,6},{8,9},{9,8},{10,11... | collective-permute-start | bytes 294920 | tf_op jit(solution)/shard_map/ppermute | solution.py:584
  26.2 11.7 %collective-permute-start.14 = (bf16[192,256]{1,0:T(8,128)(2,1)S(1)}, bf16[192,256]{1,0:T(8,128)(2,1)S(1)}, u32[]{:S(2)}, u32[]{:S(2)}) collective-permute-start(bf16[192,256]{1,0:T(8,128)(2,1)S(1)} %get-tuple-element.59), channel_id=1, source_target_pairs={{1,2},{2,1},{3,4},{4,3},{5,6},{6,5},{7,8},{8,7},{9,10},{10,9},{11,... | collective-permute-start | bytes 294920 | tf_op jit(solution)/shard_map/ppermute | solution.py:583
  29.7 9.3 %collective-permute-start.12 = (f32[96,256]{1,0:T(8,128)S(1)}, f32[96,256]{1,0:T(8,128)S(1)}, u32[]{:S(2)}, u32[]{:S(2)}) collective-permute-start(f32[96,256]{1,0:T(8,128)S(1)} %get-tuple-element.53.refs_0_), channel_id=1, source_target_pairs={{0,24},{1,25},{2,26},{3,27},{4,28},{5,29},{6,30},{7,31},{8,16},{9,... | collective-permute-start | bytes 294920 | tf_op jit(solution)/shard_map/ppermute | solution.py:588
  36.1 4.6 %collective-permute-start.11 = (f32[96,256]{1,0:T(8,128)S(1)}, f32[96,256]{1,0:T(8,128)S(1)}, u32[]{:S(2)}, u32[]{:S(2)}) collective-permute-start(f32[96,256]{1,0:T(8,128)S(1)} %get-tuple-element.53.refs_0_), channel_id=1, source_target_pairs={{0,16},{1,17},{2,18},{3,19},{4,20},{5,21},{6,22},{7,23},{8,24},{9,... | collective-permute-start | bytes 294920 | tf_op jit(solution)/shard_map/ppermute | solution.py:588
  36.1 5.0 %collective-permute-start.10 = (f32[96,256]{1,0:T(8,128)S(1)}, f32[96,256]{1,0:T(8,128)S(1)}, u32[]{:S(2)}, u32[]{:S(2)}) collective-permute-start(f32[96,256]{1,0:T(8,128)S(1)} %get-tuple-element.53.refs_0_), channel_id=1, source_target_pairs={{0,8},{1,9},{2,10},{3,11},{4,12},{5,13},{6,14},{7,15},{8,0},{9,1},... | collective-permute-start | bytes 294920 | tf_op jit(solution)/shard_map/ppermute | solution.py:588

commit v10 on v9

--- a/solution.py
+++ b/solution.py
@@ -476,30 +476,23 @@
     return mm_nt(jnp.ones((8, lanes), F32), total, precision=lax.Precision.HIGHEST)
 
 
-def finish_kernel(x_ref, p_ref, r_ref, image_ref, sums_ref, out_x_hbm, out_r_hbm, new_x_ref, new_r_ref, sems):
+def finish_kernel(x_ref, p_ref, r_ref, image_ref, sums_ref, out_x_ref, out_r_ref):
     sums = jnp.sum(sums_ref[...], axis=0)
     row = sums[0:1, :] / sums[1:2, :]
     lanes = 128
     step = jnp.transpose(jnp.broadcast_to(row, (lanes, row.shape[1])))
-    copies = []
-    for chunk in range(x_ref.shape[1] // lanes):
-        span = slice(chunk * lanes, (chunk + 1) * lanes)
-        new_x_ref[:, span] = x_ref[:, span] + step * p_ref[:, span]
-        new_r_ref[:, span] = r_ref[:, span] - step * image_ref[:, span]
-        for n, (source, target) in enumerate(((new_x_ref, out_x_hbm), (new_r_ref, out_r_hbm))):
-            copy = pltpu.make_async_copy(source.at[:, span], target.at[:, span], sems.at[n, chunk])
-            copy.start()
-            copies.append(copy)
-    for copy in copies:
-        copy.wait()
-
-
-def call(kernel, out, in_specs, scratch=(), out_spec=VMEM):
+    for start in range(0, x_ref.shape[1], lanes):
+        span = slice(start, start + lanes)
+        out_x_ref[:, span] = x_ref[:, span] + step * p_ref[:, span]
+        out_r_ref[:, span] = r_ref[:, span] - step * image_ref[:, span]
+
+
+def call(kernel, out, in_specs, scratch=()):
     return pl.pallas_call(
         kernel,
         out_shape=out,
         in_specs=in_specs,
-        out_specs=[out_spec] * len(out),
+        out_specs=[VMEM] * len(out),
         scratch_shapes=list(scratch),
         compiler_params=pltpu.CompilerParams(vmem_limit_bytes=16 * 2**20),
     )
@@ -588,7 +581,8 @@
         return [value] + [lax.ppermute(value, AXES, swap) for swap in swaps]
 
     same = partners(message, 2, chips)
-    opposite = [lax.ppermute(value, AXES, pairs) for value in same]
+    opposite = [lax.ppermute(same[0], AXES, pairs)]
+    opposite += [lax.ppermute(value, AXES, pairs) for value in same[1:]]
     block = pltpu.VMEM((members, modes, width), F32)
     solved, reduced = call(
         group_kernel,
@@ -610,13 +604,7 @@
         [pltpu.VMEM((groups, 3 * modes, width), F32), pltpu.VMEM((groups + 1, modes, width), F32)],
     )(*reduced, maps, local, basis, send_rows, from_pair, from_other, residual, diag, operator)
     sums = lax.all_to_all(sums, AXES, 0, 0, tiled=True)
-    iterate, residual = call(
-        finish_kernel,
-        [full, full],
-        [VMEM] * 5,
-        [pltpu.VMEM((cases, rows), F32), pltpu.VMEM((cases, rows), F32), semaphores((2, rows // margin))],
-        HBM,
-    )(start, direction, residual, image, sums)
+    iterate, residual = call(finish_kernel, [full, full], [VMEM] * 5)(start, direction, residual, image, sums)
     return iterate.T, residual.T
 
 

time: 58 us -> 57.9 us (level)
  no operation moved by 1% of the time
where the time goes in v10:
time: 57.9 us; the launch traced here: 57.7 us
  starting transfers between devices  22.8 us (39%)
  Pallas kernels  15.6 us (27%)
  blocking collectives  10.5 us (18%)
  waiting for transfers between devices  8.01 us (14%)
  between operations  0.79 us (1%)
    ppermute x6, starting transfers between devices, partners(): return [value] + [lax.ppermute(value, AXES, swap) for swap in swaps]  14.7 us
    all_to_all x1, blocking collectives, shards(): sums = lax.all_to_all(sums, AXES, 0, 0, tiled=True)  10.5 us
    ppermute x6, waiting for transfers between devices, partners(): return [value] + [lax.ppermute(value, AXES, swap) for swap in swaps]  7.37 us
    ppermute x1, starting transfers between devices, shards(): pair_halo = lax.ppermute(to_pair, AXES, pairs)  5.55 us
    pallas_call x1, Pallas kernels, shards(): call(solve_kernel, [full, full, struct((total, 2, cases), F32)], [VMEM] *...  4.85 us
    pallas_call x1, Pallas kernels, shards(): call(group_kernel, [struct((members, modes, width), F32), struct((3 * mod...  2.77 us
    pallas_call x1, Pallas kernels, shards(): call(inverse_kernel, [struct(local_inverse.shape, BF16), struct((modes, 4...  1.66 us
    pallas_call x1, Pallas kernels, shards(): call(load_kernel, [struct((cases + modes, margin), BF16), halo, struct((m...  1.65 us
  transfers between devices with their start and end apart: 15, of which 7 were waited for; matrix products, arithmetic and copies ran while one was open for 0% of the time, Pallas kernels for 11%

profile of v10, /device:TPU:0, one launch (start us, length us, event | category | flops | bytes accessed | tf_op | source)
XLA Modules:
  0.0 57.7 jit_solution(4494322104947386130)
XLA Ops:
  0.6 1.6 %shard_map.131 = (bf16[192,128]{1,0:T(8,128)(2,1)S(1)}, bf16[160,128]{1,0:T(8,128)(2,1)S(1)}, bf16[32,256]{1,0:T(8,128)(2,1)S(1)}, bf16[32,256]{1,0:T(8,128)(2,1...) custom-call(f32[160,768]{1,0:T(8,128)} %bitcast.6, ...), custom_call_target="tpu_custom_call" | custom-call | tf_op jit(solution)/shard_map/pallas_call | solution.py:527
  2.3 0.6 collective-permute-start
  2.8 0.6 shard_map.132.partial_ref
  3.4 0.3 collective-permute-done.pair_ref.first_pair_ref
  3.7 0.5 shard_map.133
  4.3 0.7 %collective-permute-start.1 = (bf16[608,128]{1,0:T(8,128)(2,1)S(1)}, bf16[608,128]{1,0:T(8,128)(2,1)S(1)}, u32[]{:S(2)}, u32[]{:S(2)}) collective-permute-start(bf16[608,128]{1,0:T(8,128)(2,1)S(1)} %get-tuple-element.42), channel_id=1, source_target_pairs={{1,2},{2,1},{3,4},{4,3},{5,6},{6,5},{7,8},{8,7},{9,10},{10,9},{11,... | collective-permute-start | bytes 466952 | tf_op jit(solution)/shard_map/ppermute | solution.py:556
  4.9 1.7 %shard_map.134 = (bf16[1,1024,1024]{2,1,0:T(8,128)(2,1)S(1)}, f32[32,128]{1,0:T(8,128)S(1)}, f32[32,128]{1,0:T(8,128)S(1)}) custom-call(bf16[192,128]{1,0:T(8,128)(2,1)S(1)} %collective-permute-done.pair_ref.first_pair_ref, bf16[1,1024,1024]{2,1,0:T(8,128)(2,1)} %inverse_hbm.1, f32[1,32,32]{2,1,0:T(8,128)} %diag_hbm.3, f32[1,32,32]{2,1,0:T(8,128)} %up_hbm.3), custom_call_target="tpu_custom_call" | custom-call | tf_op jit(solution)/shard_map/pallas_call | solution.py:557
  6.6 0.0 collective-permute-done.1.other_ref
  6.6 0.4 shard_map.135
  7.0 5.5 %collective-permute-start.2 = (bf16[160,128]{1,0:T(8,128)(2,1)S(1)}, bf16[160,128]{1,0:T(8,128)(2,1)S(1)}, u32[]{:S(2)}, u32[]{:S(2)}) collective-permute-start(bf16[160,128]{1,0:T(8,128)(2,1)S(1)} %get-tuple-element.51), channel_id=1, source_target_pairs={{0,1},{1,0},{2,3},{3,2},{4,5},{5,4},{6,7},{7,6},{8,9},{9,8},{10,11... | collective-permute-start | bytes 122888 | tf_op jit(solution)/shard_map/ppermute | solution.py:566
  12.6 0.6 shard_map.136
  13.2 0.3 collective-permute-done.2.pair_ref
  13.5 0.4 shard_map.137
  13.9 6.6 %collective-permute-start.5 = (f32[32,256]{1,0:T(8,128)S(1)}, f32[32,256]{1,0:T(8,128)S(1)}, u32[]{:S(2)}, u32[]{:S(2)}) collective-permute-start(f32[32,256]{1,0:T(8,128)S(1)} %get-tuple-element.52.refs_0_), channel_id=1, source_target_pairs={{0,6},{1,7},{2,4},{3,5},{4,2},{5,3},{6,0},{7,1},{8,14},{9,15},{10,... | collective-permute-start | bytes 98312 | tf_op jit(solution)/shard_map/ppermute | solution.py:581
  20.5 0.0 collective-permute-start.4
  20.5 0.6 %collective-permute-start.3 = (f32[32,256]{1,0:T(8,128)S(1)}, f32[32,256]{1,0:T(8,128)S(1)}, u32[]{:S(2)}, u32[]{:S(2)}) collective-permute-start(f32[32,256]{1,0:T(8,128)S(1)} %get-tuple-element.52.refs_0_), channel_id=1, source_target_pairs={{0,2},{1,3},{2,0},{3,1},{4,6},{5,7},{6,4},{7,5},{8,10},{9,11},{10,... | collective-permute-start | bytes 98312 | tf_op jit(solution)/shard_map/ppermute | solution.py:581
  21.1 0.0 collective-permute-start.6
  21.1 1.6 %collective-permute-done.5.refs_3_ = f32[32,256]{1,0:T(8,128)S(1)} collective-permute-done((f32[32,256]{1,0:T(8,128)S(1)}, f32[32,256]{1,0:T(8,128)S(1)}, u32[]{:S(2)}, u32[]{:S(2)}) %collective-permute-start.5) | collective-permute-done | bytes 32800 | tf_op jit(solution)/shard_map/ppermute | solution.py:581
  22.7 0.0 collective-permute-start.9
  22.7 2.6 %collective-permute-done.4.refs_2_ = f32[32,256]{1,0:T(8,128)S(1)} collective-permute-done((f32[32,256]{1,0:T(8,128)S(1)}, f32[32,256]{1,0:T(8,128)S(1)}, u32[]{:S(2)}, u32[]{:S(2)}) %collective-permute-start.4) | collective-permute-done | bytes 32800 | tf_op jit(solution)/shard_map/ppermute | solution.py:581
  25.3 0.0 collective-permute-start.8
  25.3 0.0 collective-permute-done.3.refs_1_
  25.3 0.5 collective-permute-start.7
  25.8 0.3 shard_map.140
  26.2 0.1 collective-permute-start.13
  26.2 0.0 collective-permute-done.6.refs_4_
  26.2 0.7 %collective-permute-start.14 = (bf16[192,256]{1,0:T(8,128)(2,1)S(1)}, bf16[192,256]{1,0:T(8,128)(2,1)S(1)}, u32[]{:S(2)}, u32[]{:S(2)}) collective-permute-start(bf16[192,256]{1,0:T(8,128)(2,1)S(1)} %get-tuple-element.59), channel_id=1, source_target_pairs={{1,2},{2,1},{3,4},{4,3},{5,6},{6,5},{7,8},{8,7},{9,10},{10,9},{11,... | collective-permute-start | bytes 294920 | tf_op jit(solution)/shard_map/ppermute | solution.py:576
  26.9 0.0 collective-permute-done.9.refs_7_
  26.9 0.0 collective-permute-done.8.refs_6_
  26.9 0.0 collective-permute-done.7.refs_5_
  26.9 2.8 %shard_map.138 = (f32[8,32,256]{2,1,0:T(8,128)S(1)}, f32[96,256]{1,0:T(8,128)S(1)}) custom-call(f32[32,256]{1,0:T(8,128)S(1)} %get-tuple-element.52.refs_0_, f32[32,256]{1,0:T(8,128)S(1)} %collective-permute-done.3.refs_1_, f32[32,256]{1,0:T(8,128)S(1)} %collective-permute-done.4.refs_2_, f32[32,256]{1,0:T(8,128)S(1)} %collective-permute-done.5.refs_3_, ...), custom_call_target="tpu_custom_call" | custom-call | tf_op jit(solution)/shard_map/pallas_call | solution.py:587
  29.7 6.4 %collective-permute-start.12 = (f32[96,256]{1,0:T(8,128)S(1)}, f32[96,256]{1,0:T(8,128)S(1)}, u32[]{:S(2)}, u32[]{:S(2)}) collective-permute-start(f32[96,256]{1,0:T(8,128)S(1)} %get-tuple-element.53.refs_0_), channel_id=1, source_target_pairs={{0,24},{1,25},{2,26},{3,27},{4,28},{5,29},{6,30},{7,31},{8,16},{9,... | collective-permute-start | bytes 294920 | tf_op jit(solution)/shard_map/ppermute | solution.py:581
  36.1 0.0 collective-permute-start.11
  36.1 1.1 %collective-permute-start.10 = (f32[96,256]{1,0:T(8,128)S(1)}, f32[96,256]{1,0:T(8,128)S(1)}, u32[]{:S(2)}, u32[]{:S(2)}) collective-permute-start(f32[96,256]{1,0:T(8,128)S(1)} %get-tuple-element.53.refs_0_), channel_id=1, source_target_pairs={{0,8},{1,9},{2,10},{3,11},{4,12},{5,13},{6,14},{7,15},{8,0},{9,1},... | collective-permute-start | bytes 294920 | tf_op jit(solution)/shard_map/ppermute | solution.py:581
  37.2 0.6 %shard_map.139.refs_4_ = f32[3,32,256]{2,1,0:T(8,128)S(1)} custom-call(f32[8,32,256]{2,1,0:T(8,128)S(1)} %get-tuple-element.54.solved_ref), custom_call_target="tpu_custom_call" | custom-call | tf_op jit(solution)/shard_map/pallas_call | solution.py:594
  37.9 0.0 collective-permute-done.13.refs_8_
  37.9 0.0 collective-permute-done.14.refs_9_
  37.9 1.1 %collective-permute-done.12.refs_3_ = f32[96,256]{1,0:T(8,128)S(1)} collective-permute-done((f32[96,256]{1,0:T(8,128)S(1)}, f32[96,256]{1,0:T(8,128)S(1)}, u32[]{:S(2)}, u32[]{:S(2)}) %collective-permute-start.12) | collective-permute-done | bytes 98336 | tf_op jit(solution)/shard_map/ppermute | solution.py:581
  39.0 1.7 %collective-permute-done.11.refs_2_ = f32[96,256]{1,0:T(8,128)S(1)} collective-permute-done((f32[96,256]{1,0:T(8,128)S(1)}, f32[96,256]{1,0:T(8,128)S(1)}, u32[]{:S(2)}, u32[]{:S(2)}) %collective-permute-start.11) | collective-permute-done | bytes 98336 | tf_op jit(solution)/shard_map/ppermute | solution.py:581
  40.7 0.4 collective-permute-done.10.refs_1_
  41.1 4.8 %shard_map.141 = (f32[160,768]{1,0:T(8,128)S(1)}, f32[160,768]{1,0:T(8,128)S(1)}, f32[32,2,160]{2,1,0:T(2,128)S(1)}) custom-call(f32[96,256]{1,0:T(8,128)S(1)} %get-tuple-element.53.refs_0_, f32[96,256]{1,0:T(8,128)S(1)} %collective-permute-done.10.refs_1_, f32[96,256]{1,0:T(8,128)S(1)} %collective-permute-done.11.refs_2_, ...), custom_call_target="tpu_custom_call" | custom-call | tf_op jit(solution)/shard_map/pallas_call | solution.py:600
  46.0 10.5 %all_to_all.5.sums_ref = f32[32,2,160]{2,1,0:T(2,128)S(1)} all-to-all(f32[32,2,160]{2,1,0:T(2,128)S(1)} %get-tuple-element.63), channel_id=1, replica_groups=mesh['grp'=4,'sub'=8] {'grp','sub'}, dimensions={0} | all-to-all | bytes 81920 | tf_op jit(solution)/shard_map/all_to_all | solution.py:606
  56.5 1.1 %shard_map.142 = (f32[160,768]{1,0:T(8,128)}, f32[160,768]{1,0:T(8,128)}) custom-call(f32[160,768]{1,0:T(8,128)S(1)} %get-tuple-element.34.x_ref, f32[160,768]{1,0:T(8,128)S(1)} %get-tuple-element.61.p_ref, f32[160,768]{1,0:T(8,128)S(1)} %get-tuple-element.60.refs_10_.r_ref, f32[160,768]{1,0:T(8,128)S(1)} %get-tuple-element.62.image_ref, ...), custom_call_target="tpu_custom_call" | custom-call | tf_op jit(solution)/shard_map/pallas_call | solution.py:607
Async XLA Ops:
  2.3 1.4 %collective-permute-start = (bf16[192,128]{1,0:T(8,128)(2,1)S(1)}, bf16[192,128]{1,0:T(8,128)(2,1)S(1)}, u32[]{:S(2)}, u32[]{:S(2)}) collective-permute-start(bf16[192,128]{1,0:T(8,128)(2,1)S(1)} %get-tuple-element.39), channel_id=1, source_target_pairs={{0,1},{1,0},{2,3},{3,2},{4,5},{5,4},{6,7},{7,6},{8,9},{9,8},{10,11... | collective-permute-start | bytes 147464 | tf_op jit(solution)/shard_map/ppermute | solution.py:551
  4.3 2.3 %collective-permute-start.1 = (bf16[608,128]{1,0:T(8,128)(2,1)S(1)}, bf16[608,128]{1,0:T(8,128)(2,1)S(1)}, u32[]{:S(2)}, u32[]{:S(2)}) collective-permute-start(bf16[608,128]{1,0:T(8,128)(2,1)S(1)} %get-tuple-element.42), channel_id=1, source_target_pairs={{1,2},{2,1},{3,4},{4,3},{5,6},{6,5},{7,8},{8,7},{9,10},{10,9},{11,... | collective-permute-start | bytes 466952 | tf_op jit(solution)/shard_map/ppermute | solution.py:556
  7.0 6.4 %collective-permute-start.2 = (bf16[160,128]{1,0:T(8,128)(2,1)S(1)}, bf16[160,128]{1,0:T(8,128)(2,1)S(1)}, u32[]{:S(2)}, u32[]{:S(2)}) collective-permute-start(bf16[160,128]{1,0:T(8,128)(2,1)S(1)} %get-tuple-element.51), channel_id=1, source_target_pairs={{0,1},{1,0},{2,3},{3,2},{4,5},{5,4},{6,7},{7,6},{8,9},{9,8},{10,11... | collective-permute-start | bytes 122888 | tf_op jit(solution)/shard_map/ppermute | solution.py:566
  13.9 8.8 %collective-permute-start.5 = (f32[32,256]{1,0:T(8,128)S(1)}, f32[32,256]{1,0:T(8,128)S(1)}, u32[]{:S(2)}, u32[]{:S(2)}) collective-permute-start(f32[32,256]{1,0:T(8,128)S(1)} %get-tuple-element.52.refs_0_), channel_id=1, source_target_pairs={{0,6},{1,7},{2,4},{3,5},{4,2},{5,3},{6,0},{7,1},{8,14},{9,15},{10,... | collective-permute-start | bytes 98312 | tf_op jit(solution)/shard_map/ppermute | solution.py:581
  20.5 4.8 %collective-permute-start.4 = (f32[32,256]{1,0:T(8,128)S(1)}, f32[32,256]{1,0:T(8,128)S(1)}, u32[]{:S(2)}, u32[]{:S(2)}) collective-permute-start(f32[32,256]{1,0:T(8,128)S(1)} %get-tuple-element.52.refs_0_), channel_id=1, source_target_pairs={{0,4},{1,5},{2,6},{3,7},{4,0},{5,1},{6,2},{7,3},{8,12},{9,13},{10,... | collective-permute-start | bytes 98312 | tf_op jit(solution)/shard_map/ppermute | solution.py:581
  20.5 4.8 %collective-permute-start.3 = (f32[32,256]{1,0:T(8,128)S(1)}, f32[32,256]{1,0:T(8,128)S(1)}, u32[]{:S(2)}, u32[]{:S(2)}) collective-permute-start(f32[32,256]{1,0:T(8,128)S(1)} %get-tuple-element.52.refs_0_), channel_id=1, source_target_pairs={{0,2},{1,3},{2,0},{3,1},{4,6},{5,7},{6,4},{7,5},{8,10},{9,11},{10,... | collective-permute-start | bytes 98312 | tf_op jit(solution)/shard_map/ppermute | solution.py:581
  21.1 5.1 %collective-permute-start.6 = (f32[32,256]{1,0:T(8,128)S(1)}, f32[32,256]{1,0:T(8,128)S(1)}, u32[]{:S(2)}, u32[]{:S(2)}) collective-permute-start(f32[32,256]{1,0:T(8,128)S(1)} %get-tuple-element.52.refs_0_), channel_id=1, source_target_pairs={{0,1},{1,0},{2,3},{3,2},{4,5},{5,4},{6,7},{7,6},{8,9},{9,8},{10,11... | collective-permute-start | bytes 98312 | tf_op jit(solution)/shard_map/ppermute | solution.py:584
  22.7 4.2 %collective-permute-start.9 = (f32[32,256]{1,0:T(8,128)S(1)}, f32[32,256]{1,0:T(8,128)S(1)}, u32[]{:S(2)}, u32[]{:S(2)}) collective-permute-start(f32[32,256]{1,0:T(8,128)S(1)} %collective-permute-done.5.refs_3_), channel_id=1, source_target_pairs={{0,1},{1,0},{2,3},{3,2},{4,5},{5,4},{6,7},{7,6},{8,9},{9,8},{10,11... | collective-permute-start | bytes 98312 | tf_op jit(solution)/shard_map/ppermute | solution.py:585
  25.3 1.6 %collective-permute-start.8 = (f32[32,256]{1,0:T(8,128)S(1)}, f32[32,256]{1,0:T(8,128)S(1)}, u32[]{:S(2)}, u32[]{:S(2)}) collective-permute-start(f32[32,256]{1,0:T(8,128)S(1)} %collective-permute-done.4.refs_2_), channel_id=1, source_target_pairs={{0,1},{1,0},{2,3},{3,2},{4,5},{5,4},{6,7},{7,6},{8,9},{9,8},{10,11... | collective-permute-start | bytes 98312 | tf_op jit(solution)/shard_map/ppermute | solution.py:585
  25.3 1.6 %collective-permute-start.7 = (f32[32,256]{1,0:T(8,128)S(1)}, f32[32,256]{1,0:T(8,128)S(1)}, u32[]{:S(2)}, u32[]{:S(2)}) collective-permute-start(f32[32,256]{1,0:T(8,128)S(1)} %collective-permute-done.3.refs_1_), channel_id=1, source_target_pairs={{0,1},{1,0},{2,3},{3,2},{4,5},{5,4},{6,7},{7,6},{8,9},{9,8},{10,11... | collective-permute-start | bytes 98312 | tf_op jit(solution)/shard_map/ppermute | solution.py:585
  26.2 11.8 %collective-permute-start.13 = (bf16[192,256]{1,0:T(8,128)(2,1)S(1)}, bf16[192,256]{1,0:T(8,128)(2,1)S(1)}, u32[]{:S(2)}, u32[]{:S(2)}) collective-permute-start(bf16[192,256]{1,0:T(8,128)(2,1)S(1)} %get-tuple-element.58), channel_id=1, source_target_pairs={{0,1},{1,0},{2,3},{3,2},{4,5},{5,4},{6,7},{7,6},{8,9},{9,8},{10,11... | collective-permute-start | bytes 294920 | tf_op jit(solution)/shard_map/ppermute | solution.py:577
  26.2 11.7 %collective-permute-start.14 = (bf16[192,256]{1,0:T(8,128)(2,1)S(1)}, bf16[192,256]{1,0:T(8,128)(2,1)S(1)}, u32[]{:S(2)}, u32[]{:S(2)}) collective-permute-start(bf16[192,256]{1,0:T(8,128)(2,1)S(1)} %get-tuple-element.59), channel_id=1, source_target_pairs={{1,2},{2,1},{3,4},{4,3},{5,6},{6,5},{7,8},{8,7},{9,10},{10,9},{11,... | collective-permute-start | bytes 294920 | tf_op jit(solution)/shard_map/ppermute | solution.py:576
  29.7 9.3 %collective-permute-start.12 = (f32[96,256]{1,0:T(8,128)S(1)}, f32[96,256]{1,0:T(8,128)S(1)}, u32[]{:S(2)}, u32[]{:S(2)}) collective-permute-start(f32[96,256]{1,0:T(8,128)S(1)} %get-tuple-element.53.refs_0_), channel_id=1, source_target_pairs={{0,24},{1,25},{2,26},{3,27},{4,28},{5,29},{6,30},{7,31},{8,16},{9,... | collective-permute-start | bytes 294920 | tf_op jit(solution)/shard_map/ppermute | solution.py:581
  36.1 4.6 %collective-permute-start.11 = (f32[96,256]{1,0:T(8,128)S(1)}, f32[96,256]{1,0:T(8,128)S(1)}, u32[]{:S(2)}, u32[]{:S(2)}) collective-permute-start(f32[96,256]{1,0:T(8,128)S(1)} %get-tuple-element.53.refs_0_), channel_id=1, source_target_pairs={{0,16},{1,17},{2,18},{3,19},{4,20},{5,21},{6,22},{7,23},{8,24},{9,... | collective-permute-start | bytes 294920 | tf_op jit(solution)/shard_map/ppermute | solution.py:581
  36.1 5.0 %collective-permute-start.10 = (f32[96,256]{1,0:T(8,128)S(1)}, f32[96,256]{1,0:T(8,128)S(1)}, u32[]{:S(2)}, u32[]{:S(2)}) collective-permute-start(f32[96,256]{1,0:T(8,128)S(1)} %get-tuple-element.53.refs_0_), channel_id=1, source_target_pairs={{0,8},{1,9},{2,10},{3,11},{4,12},{5,13},{6,14},{7,15},{8,0},{9,1},... | collective-permute-start | bytes 294920 | tf_op jit(solution)/shard_map/ppermute | solution.py:581

commit v11 on v10

--- a/solution.py
+++ b/solution.py
@@ -377,7 +377,9 @@
     message_ref[2 * size:, :] = whole
 
 
-def compose_kernel(solved_ref, maps_ref, all_ref):
+def compose_kernel(solved_ref, rows_ref, maps_ref, place_ref, all_ref):
+    rows = jnp.concatenate([rows_ref[0, 0:1, :], rows_ref[0, 1:2, :]], axis=1)
+    place_ref[...] = place_matrix(rows, place_ref.shape[0])
     members, size, width = solved_ref.shape
     lane = lax.broadcasted_iota(jnp.int32, (size, width), 1)
     row = lax.broadcasted_iota(jnp.int32, (size, width), 0)
@@ -397,7 +399,7 @@
 
 
 def solve_kernel(*refs):
-    (*received, maps_ref, local_ref, basis_ref, rows_ref, pair_ref, other_ref, r_ref, diag_ref, operator_ref,
+    (*received, maps_ref, local_ref, basis_ref, place_ref, pair_ref, other_ref, r_ref, diag_ref, operator_ref,
      p_ref, image_ref, sums_ref, messages_ref, sep_ref) = refs
     groups = len(received)
     size, width = received[0].shape
@@ -442,7 +444,7 @@
         return mm_t(solution.astype(BF16), basis)[3 * size:]
 
     cases = local_ref.shape[0]
-    margin = rows_ref.shape[2]
+    margin = place_ref.shape[1] // 2
     owned = p_ref.shape[1]
     even = is_even()
     pair, other = pair_ref[...], other_ref[...]
@@ -450,9 +452,8 @@
     left = left[:cases].astype(F32) + lifted(left_solution, left[cases:])
     right = right[:cases].astype(F32) + lifted(right_solution, right[cases:])
     correction = local_ref[...] + lifted(own_solution, basis_ref[0])
-    place = place_matrix(jnp.concatenate([rows_ref[0, 0:1, :], rows_ref[0, 1:2, :]], axis=1), owned)
     tails = jnp.concatenate([left[:, :margin], right[:, :margin]], axis=1).astype(BF16)
-    p = correction[:, margin:margin + owned] + mm_nt(tails, place)
+    p = correction[:, margin:margin + owned] + mm_nt(tails, place_ref[...])
     p_ref[...] = p
     me = position()
     last = lax.axis_size("grp") * lax.axis_size("sub") - 1
@@ -591,18 +592,18 @@
         [block],
     )(*same, *opposite)
     reduced = partners(reduced, members, groups)
-    (maps,) = call(
+    maps, place = call(
         compose_kernel,
-        [struct((3, modes, width), F32)],
-        [VMEM],
+        [struct((3, modes, width), F32), struct((rows, 2 * margin), BF16)],
+        [VMEM] * 2,
         [pltpu.VMEM((members + 1, modes, width), F32)],
-    )(solved)
+    )(solved, send_rows)
     direction, image, sums = call(
         solve_kernel,
         [full, full, struct((total, 2, cases), F32)],
         [VMEM] * (groups + 9),
         [pltpu.VMEM((groups, 3 * modes, width), F32), pltpu.VMEM((groups + 1, modes, width), F32)],
-    )(*reduced, maps, local, basis, send_rows, from_pair, from_other, residual, diag, operator)
+    )(*reduced, maps, local, basis, place, from_pair, from_other, residual, diag, operator)
     sums = lax.all_to_all(sums, AXES, 0, 0, tiled=True)
     iterate, residual = call(finish_kernel, [full, full], [VMEM] * 5)(start, direction, residual, image, sums)
     return iterate.T, residual.T

time: 57.9 us -> 57.9 us (level)
  transfers between devices with their start and end apart: 15 -> 15, of which waited for: 7 -> 7; matrix products, arithmetic and copies ran while one was open for 0% -> 0% of each run, Pallas kernels for 11% -> 12%
where the time goes in v11:
time: 57.9 us; the launch traced here: 57.6 us
  starting transfers between devices  22.8 us (39%)
  Pallas kernels  15.7 us (27%)
  blocking collectives  10.5 us (18%)
  waiting for transfers between devices  7.85 us (14%)
  between operations  0.79 us (1%)
    ppermute x6, starting transfers between devices, partners(): return [value] + [lax.ppermute(value, AXES, swap) for swap in swaps]  14.7 us
    all_to_all x1, blocking collectives, shards(): sums = lax.all_to_all(sums, AXES, 0, 0, tiled=True)  10.5 us
    ppermute x6, waiting for transfers between devices, partners(): return [value] + [lax.ppermute(value, AXES, swap) for swap in swaps]  7.22 us
    ppermute x1, starting transfers between devices, shards(): pair_halo = lax.ppermute(to_pair, AXES, pairs)  5.55 us
    pallas_call x1, Pallas kernels, shards(): call(solve_kernel, [full, full, struct((total, 2, cases), F32)], [VMEM] *...  4.84 us
    pallas_call x1, Pallas kernels, shards(): call(group_kernel, [struct((members, modes, width), F32), struct((3 * mod...  2.77 us
    pallas_call x1, Pallas kernels, shards(): call(inverse_kernel, [struct(local_inverse.shape, BF16), struct((modes, 4...  1.66 us
    pallas_call x1, Pallas kernels, shards(): call(load_kernel, [struct((cases + modes, margin), BF16), halo, struct((m...  1.65 us
  transfers between devices with their start and end apart: 15, of which 7 were waited for; matrix products, arithmetic and copies ran while one was open for 0% of the time, Pallas kernels for 12%

profile of v11, /device:TPU:0, one launch (start us, length us, event | category | flops | bytes accessed | tf_op | source)
XLA Modules:
  0.0 57.6 jit_solution(9658307058290064204)
XLA Ops:
  0.6 1.6 %shard_map.131 = (bf16[192,128]{1,0:T(8,128)(2,1)S(1)}, bf16[160,128]{1,0:T(8,128)(2,1)S(1)}, bf16[32,256]{1,0:T(8,128)(2,1)S(1)}, bf16[32,256]{1,0:T(8,128)(2,1...) custom-call(f32[160,768]{1,0:T(8,128)} %bitcast.6, ...), custom_call_target="tpu_custom_call" | custom-call | tf_op jit(solution)/shard_map/pallas_call | solution.py:528
  2.3 0.6 collective-permute-start
  2.8 0.6 shard_map.132.partial_ref
  3.4 0.3 collective-permute-done.pair_ref.first_pair_ref
  3.7 0.5 shard_map.133
  4.3 0.7 %collective-permute-start.1 = (bf16[608,128]{1,0:T(8,128)(2,1)S(1)}, bf16[608,128]{1,0:T(8,128)(2,1)S(1)}, u32[]{:S(2)}, u32[]{:S(2)}) collective-permute-start(bf16[608,128]{1,0:T(8,128)(2,1)S(1)} %get-tuple-element.44), channel_id=1, source_target_pairs={{1,2},{2,1},{3,4},{4,3},{5,6},{6,5},{7,8},{8,7},{9,10},{10,9},{11,... | collective-permute-start | bytes 466952 | tf_op jit(solution)/shard_map/ppermute | solution.py:557
  4.9 1.7 %shard_map.134 = (bf16[1,1024,1024]{2,1,0:T(8,128)(2,1)S(1)}, f32[32,128]{1,0:T(8,128)S(1)}, f32[32,128]{1,0:T(8,128)S(1)}) custom-call(bf16[192,128]{1,0:T(8,128)(2,1)S(1)} %collective-permute-done.pair_ref.first_pair_ref, bf16[1,1024,1024]{2,1,0:T(8,128)(2,1)} %inverse_hbm.1, f32[1,32,32]{2,1,0:T(8,128)} %diag_hbm.3, f32[1,32,32]{2,1,0:T(8,128)} %up_hbm.3), custom_call_target="tpu_custom_call" | custom-call | tf_op jit(solution)/shard_map/pallas_call | solution.py:558
  6.6 0.0 collective-permute-done.1.other_ref
  6.6 0.4 shard_map.135
  7.0 5.5 %collective-permute-start.2 = (bf16[160,128]{1,0:T(8,128)(2,1)S(1)}, bf16[160,128]{1,0:T(8,128)(2,1)S(1)}, u32[]{:S(2)}, u32[]{:S(2)}) collective-permute-start(bf16[160,128]{1,0:T(8,128)(2,1)S(1)} %get-tuple-element.53), channel_id=1, source_target_pairs={{0,1},{1,0},{2,3},{3,2},{4,5},{5,4},{6,7},{7,6},{8,9},{9,8},{10,11... | collective-permute-start | bytes 122888 | tf_op jit(solution)/shard_map/ppermute | solution.py:567
  12.6 0.6 shard_map.136
  13.2 0.3 collective-permute-done.2.pair_ref
  13.5 0.4 shard_map.137
  13.9 6.6 %collective-permute-start.5 = (f32[32,256]{1,0:T(8,128)S(1)}, f32[32,256]{1,0:T(8,128)S(1)}, u32[]{:S(2)}, u32[]{:S(2)}) collective-permute-start(f32[32,256]{1,0:T(8,128)S(1)} %get-tuple-element.54.refs_0_), channel_id=1, source_target_pairs={{0,6},{1,7},{2,4},{3,5},{4,2},{5,3},{6,0},{7,1},{8,14},{9,15},{10,... | collective-permute-start | bytes 98312 | tf_op jit(solution)/shard_map/ppermute | solution.py:582
  20.5 0.0 collective-permute-start.4
  20.5 0.6 %collective-permute-start.3 = (f32[32,256]{1,0:T(8,128)S(1)}, f32[32,256]{1,0:T(8,128)S(1)}, u32[]{:S(2)}, u32[]{:S(2)}) collective-permute-start(f32[32,256]{1,0:T(8,128)S(1)} %get-tuple-element.54.refs_0_), channel_id=1, source_target_pairs={{0,2},{1,3},{2,0},{3,1},{4,6},{5,7},{6,4},{7,5},{8,10},{9,11},{10,... | collective-permute-start | bytes 98312 | tf_op jit(solution)/shard_map/ppermute | solution.py:582
  21.1 0.0 collective-permute-start.6
  21.1 1.6 %collective-permute-done.5.refs_3_ = f32[32,256]{1,0:T(8,128)S(1)} collective-permute-done((f32[32,256]{1,0:T(8,128)S(1)}, f32[32,256]{1,0:T(8,128)S(1)}, u32[]{:S(2)}, u32[]{:S(2)}) %collective-permute-start.5) | collective-permute-done | bytes 32800 | tf_op jit(solution)/shard_map/ppermute | solution.py:582
  22.7 0.0 collective-permute-start.9
  22.7 2.6 %collective-permute-done.4.refs_2_ = f32[32,256]{1,0:T(8,128)S(1)} collective-permute-done((f32[32,256]{1,0:T(8,128)S(1)}, f32[32,256]{1,0:T(8,128)S(1)}, u32[]{:S(2)}, u32[]{:S(2)}) %collective-permute-start.4) | collective-permute-done | bytes 32800 | tf_op jit(solution)/shard_map/ppermute | solution.py:582
  25.3 0.0 collective-permute-start.8
  25.3 0.0 collective-permute-done.3.refs_1_
  25.3 0.5 collective-permute-start.7
  25.8 0.3 shard_map.140
  26.2 0.1 collective-permute-start.13
  26.2 0.0 collective-permute-done.6.refs_4_
  26.2 0.7 %collective-permute-start.14 = (bf16[192,256]{1,0:T(8,128)(2,1)S(1)}, bf16[192,256]{1,0:T(8,128)(2,1)S(1)}, u32[]{:S(2)}, u32[]{:S(2)}) collective-permute-start(bf16[192,256]{1,0:T(8,128)(2,1)S(1)} %get-tuple-element.63), channel_id=1, source_target_pairs={{1,2},{2,1},{3,4},{4,3},{5,6},{6,5},{7,8},{8,7},{9,10},{10,9},{11,... | collective-permute-start | bytes 294920 | tf_op jit(solution)/shard_map/ppermute | solution.py:577
  26.9 0.0 collective-permute-done.9.refs_7_
  26.9 0.0 collective-permute-done.8.refs_6_
  26.9 0.0 collective-permute-done.7.refs_5_
  26.9 2.8 %shard_map.138 = (f32[8,32,256]{2,1,0:T(8,128)S(1)}, f32[96,256]{1,0:T(8,128)S(1)}) custom-call(f32[32,256]{1,0:T(8,128)S(1)} %get-tuple-element.54.refs_0_, f32[32,256]{1,0:T(8,128)S(1)} %collective-permute-done.3.refs_1_, f32[32,256]{1,0:T(8,128)S(1)} %collective-permute-done.4.refs_2_, f32[32,256]{1,0:T(8,128)S(1)} %collective-permute-done.5.refs_3_, ...), custom_call_target="tpu_custom_call" | custom-call | tf_op jit(solution)/shard_map/pallas_call | solution.py:588
  29.7 6.4 %collective-permute-start.12 = (f32[96,256]{1,0:T(8,128)S(1)}, f32[96,256]{1,0:T(8,128)S(1)}, u32[]{:S(2)}, u32[]{:S(2)}) collective-permute-start(f32[96,256]{1,0:T(8,128)S(1)} %get-tuple-element.55.refs_0_), channel_id=1, source_target_pairs={{0,24},{1,25},{2,26},{3,27},{4,28},{5,29},{6,30},{7,31},{8,16},{9,... | collective-permute-start | bytes 294920 | tf_op jit(solution)/shard_map/ppermute | solution.py:582
  36.1 0.0 collective-permute-start.11
  36.1 1.1 %collective-permute-start.10 = (f32[96,256]{1,0:T(8,128)S(1)}, f32[96,256]{1,0:T(8,128)S(1)}, u32[]{:S(2)}, u32[]{:S(2)}) collective-permute-start(f32[96,256]{1,0:T(8,128)S(1)} %get-tuple-element.55.refs_0_), channel_id=1, source_target_pairs={{0,8},{1,9},{2,10},{3,11},{4,12},{5,13},{6,14},{7,15},{8,0},{9,1},... | collective-permute-start | bytes 294920 | tf_op jit(solution)/shard_map/ppermute | solution.py:582
  37.3 0.8 %shard_map.139 = (f32[3,32,256]{2,1,0:T(8,128)S(1)}, bf16[768,256]{1,0:T(8,128)(2,1)S(1)}) custom-call(f32[8,32,256]{2,1,0:T(8,128)S(1)} %get-tuple-element.56.solved_ref, s32[1,2,128]{2,1,0:T(2,128)S(1)} %get-tuple-element.40.rows_ref), custom_call_target="tpu_custom_call" | custom-call | tf_op jit(solution)/shard_map/pallas_call | solution.py:595
  38.0 0.0 collective-permute-done.13.refs_8_
  38.1 0.0 collective-permute-done.14.refs_9_
  38.1 1.0 %collective-permute-done.12.refs_3_ = f32[96,256]{1,0:T(8,128)S(1)} collective-permute-done((f32[96,256]{1,0:T(8,128)S(1)}, f32[96,256]{1,0:T(8,128)S(1)}, u32[]{:S(2)}, u32[]{:S(2)}) %collective-permute-start.12) | collective-permute-done | bytes 98336 | tf_op jit(solution)/shard_map/ppermute | solution.py:582
  39.0 1.7 %collective-permute-done.11.refs_2_ = f32[96,256]{1,0:T(8,128)S(1)} collective-permute-done((f32[96,256]{1,0:T(8,128)S(1)}, f32[96,256]{1,0:T(8,128)S(1)}, u32[]{:S(2)}, u32[]{:S(2)}) %collective-permute-start.11) | collective-permute-done | bytes 98336 | tf_op jit(solution)/shard_map/ppermute | solution.py:582
  40.7 0.4 collective-permute-done.10.refs_1_
  41.1 4.8 %shard_map.141 = (f32[160,768]{1,0:T(8,128)S(1)}, f32[160,768]{1,0:T(8,128)S(1)}, f32[32,2,160]{2,1,0:T(2,128)S(1)}) custom-call(f32[96,256]{1,0:T(8,128)S(1)} %get-tuple-element.55.refs_0_, f32[96,256]{1,0:T(8,128)S(1)} %collective-permute-done.10.refs_1_, f32[96,256]{1,0:T(8,128)S(1)} %collective-permute-done.11.refs_2_, ...), custom_call_target="tpu_custom_call" | custom-call | tf_op jit(solution)/shard_map/pallas_call | solution.py:601
  46.0 10.5 %all_to_all.5.sums_ref = f32[32,2,160]{2,1,0:T(2,128)S(1)} all-to-all(f32[32,2,160]{2,1,0:T(2,128)S(1)} %get-tuple-element.67), channel_id=1, replica_groups=mesh['grp'=4,'sub'=8] {'grp','sub'}, dimensions={0} | all-to-all | bytes 81920 | tf_op jit(solution)/shard_map/all_to_all | solution.py:607
  56.5 1.1 %shard_map.142 = (f32[160,768]{1,0:T(8,128)}, f32[160,768]{1,0:T(8,128)}) custom-call(f32[160,768]{1,0:T(8,128)S(1)} %get-tuple-element.36.x_ref, f32[160,768]{1,0:T(8,128)S(1)} %get-tuple-element.65.p_ref, f32[160,768]{1,0:T(8,128)S(1)} %get-tuple-element.64.refs_10_.r_ref, f32[160,768]{1,0:T(8,128)S(1)} %get-tuple-element.66.image_ref, ...), custom_call_target="tpu_custom_call" | custom-call | tf_op jit(solution)/shard_map/pallas_call | solution.py:608
Async XLA Ops:
  2.3 1.4 %collective-permute-start = (bf16[192,128]{1,0:T(8,128)(2,1)S(1)}, bf16[192,128]{1,0:T(8,128)(2,1)S(1)}, u32[]{:S(2)}, u32[]{:S(2)}) collective-permute-start(bf16[192,128]{1,0:T(8,128)(2,1)S(1)} %get-tuple-element.41), channel_id=1, source_target_pairs={{0,1},{1,0},{2,3},{3,2},{4,5},{5,4},{6,7},{7,6},{8,9},{9,8},{10,11... | collective-permute-start | bytes 147464 | tf_op jit(solution)/shard_map/ppermute | solution.py:552
  4.3 2.3 %collective-permute-start.1 = (bf16[608,128]{1,0:T(8,128)(2,1)S(1)}, bf16[608,128]{1,0:T(8,128)(2,1)S(1)}, u32[]{:S(2)}, u32[]{:S(2)}) collective-permute-start(bf16[608,128]{1,0:T(8,128)(2,1)S(1)} %get-tuple-element.44), channel_id=1, source_target_pairs={{1,2},{2,1},{3,4},{4,3},{5,6},{6,5},{7,8},{8,7},{9,10},{10,9},{11,... | collective-permute-start | bytes 466952 | tf_op jit(solution)/shard_map/ppermute | solution.py:557
  7.0 6.4 %collective-permute-start.2 = (bf16[160,128]{1,0:T(8,128)(2,1)S(1)}, bf16[160,128]{1,0:T(8,128)(2,1)S(1)}, u32[]{:S(2)}, u32[]{:S(2)}) collective-permute-start(bf16[160,128]{1,0:T(8,128)(2,1)S(1)} %get-tuple-element.53), channel_id=1, source_target_pairs={{0,1},{1,0},{2,3},{3,2},{4,5},{5,4},{6,7},{7,6},{8,9},{9,8},{10,11... | collective-permute-start | bytes 122888 | tf_op jit(solution)/shard_map/ppermute | solution.py:567
  13.9 8.8 %collective-permute-start.5 = (f32[32,256]{1,0:T(8,128)S(1)}, f32[32,256]{1,0:T(8,128)S(1)}, u32[]{:S(2)}, u32[]{:S(2)}) collective-permute-start(f32[32,256]{1,0:T(8,128)S(1)} %get-tuple-element.54.refs_0_), channel_id=1, source_target_pairs={{0,6},{1,7},{2,4},{3,5},{4,2},{5,3},{6,0},{7,1},{8,14},{9,15},{10,... | collective-permute-start | bytes 98312 | tf_op jit(solution)/shard_map/ppermute | solution.py:582
  20.5 4.8 %collective-permute-start.4 = (f32[32,256]{1,0:T(8,128)S(1)}, f32[32,256]{1,0:T(8,128)S(1)}, u32[]{:S(2)}, u32[]{:S(2)}) collective-permute-start(f32[32,256]{1,0:T(8,128)S(1)} %get-tuple-element.54.refs_0_), channel_id=1, source_target_pairs={{0,4},{1,5},{2,6},{3,7},{4,0},{5,1},{6,2},{7,3},{8,12},{9,13},{10,... | collective-permute-start | bytes 98312 | tf_op jit(solution)/shard_map/ppermute | solution.py:582
  20.5 4.8 %collective-permute-start.3 = (f32[32,256]{1,0:T(8,128)S(1)}, f32[32,256]{1,0:T(8,128)S(1)}, u32[]{:S(2)}, u32[]{:S(2)}) collective-permute-start(f32[32,256]{1,0:T(8,128)S(1)} %get-tuple-element.54.refs_0_), channel_id=1, source_target_pairs={{0,2},{1,3},{2,0},{3,1},{4,6},{5,7},{6,4},{7,5},{8,10},{9,11},{10,... | collective-permute-start | bytes 98312 | tf_op jit(solution)/shard_map/ppermute | solution.py:582
  21.1 5.1 %collective-permute-start.6 = (f32[32,256]{1,0:T(8,128)S(1)}, f32[32,256]{1,0:T(8,128)S(1)}, u32[]{:S(2)}, u32[]{:S(2)}) collective-permute-start(f32[32,256]{1,0:T(8,128)S(1)} %get-tuple-element.54.refs_0_), channel_id=1, source_target_pairs={{0,1},{1,0},{2,3},{3,2},{4,5},{5,4},{6,7},{7,6},{8,9},{9,8},{10,11... | collective-permute-start | bytes 98312 | tf_op jit(solution)/shard_map/ppermute | solution.py:585
  22.7 4.2 %collective-permute-start.9 = (f32[32,256]{1,0:T(8,128)S(1)}, f32[32,256]{1,0:T(8,128)S(1)}, u32[]{:S(2)}, u32[]{:S(2)}) collective-permute-start(f32[32,256]{1,0:T(8,128)S(1)} %collective-permute-done.5.refs_3_), channel_id=1, source_target_pairs={{0,1},{1,0},{2,3},{3,2},{4,5},{5,4},{6,7},{7,6},{8,9},{9,8},{10,11... | collective-permute-start | bytes 98312 | tf_op jit(solution)/shard_map/ppermute | solution.py:586
  25.3 1.6 %collective-permute-start.8 = (f32[32,256]{1,0:T(8,128)S(1)}, f32[32,256]{1,0:T(8,128)S(1)}, u32[]{:S(2)}, u32[]{:S(2)}) collective-permute-start(f32[32,256]{1,0:T(8,128)S(1)} %collective-permute-done.4.refs_2_), channel_id=1, source_target_pairs={{0,1},{1,0},{2,3},{3,2},{4,5},{5,4},{6,7},{7,6},{8,9},{9,8},{10,11... | collective-permute-start | bytes 98312 | tf_op jit(solution)/shard_map/ppermute | solution.py:586
  25.3 1.7 %collective-permute-start.7 = (f32[32,256]{1,0:T(8,128)S(1)}, f32[32,256]{1,0:T(8,128)S(1)}, u32[]{:S(2)}, u32[]{:S(2)}) collective-permute-start(f32[32,256]{1,0:T(8,128)S(1)} %collective-permute-done.3.refs_1_), channel_id=1, source_target_pairs={{0,1},{1,0},{2,3},{3,2},{4,5},{5,4},{6,7},{7,6},{8,9},{9,8},{10,11... | collective-permute-start | bytes 98312 | tf_op jit(solution)/shard_map/ppermute | solution.py:586
  26.2 11.9 %collective-permute-start.13 = (bf16[192,256]{1,0:T(8,128)(2,1)S(1)}, bf16[192,256]{1,0:T(8,128)(2,1)S(1)}, u32[]{:S(2)}, u32[]{:S(2)}) collective-permute-start(bf16[192,256]{1,0:T(8,128)(2,1)S(1)} %get-tuple-element.62), channel_id=1, source_target_pairs={{0,1},{1,0},{2,3},{3,2},{4,5},{5,4},{6,7},{7,6},{8,9},{9,8},{10,11... | collective-permute-start | bytes 294920 | tf_op jit(solution)/shard_map/ppermute | solution.py:578
  26.2 11.8 %collective-permute-start.14 = (bf16[192,256]{1,0:T(8,128)(2,1)S(1)}, bf16[192,256]{1,0:T(8,128)(2,1)S(1)}, u32[]{:S(2)}, u32[]{:S(2)}) collective-permute-start(bf16[192,256]{1,0:T(8,128)(2,1)S(1)} %get-tuple-element.63), channel_id=1, source_target_pairs={{1,2},{2,1},{3,4},{4,3},{5,6},{6,5},{7,8},{8,7},{9,10},{10,9},{11,... | collective-permute-start | bytes 294920 | tf_op jit(solution)/shard_map/ppermute | solution.py:577
  29.7 9.3 %collective-permute-start.12 = (f32[96,256]{1,0:T(8,128)S(1)}, f32[96,256]{1,0:T(8,128)S(1)}, u32[]{:S(2)}, u32[]{:S(2)}) collective-permute-start(f32[96,256]{1,0:T(8,128)S(1)} %get-tuple-element.55.refs_0_), channel_id=1, source_target_pairs={{0,24},{1,25},{2,26},{3,27},{4,28},{5,29},{6,30},{7,31},{8,16},{9,... | collective-permute-start | bytes 294920 | tf_op jit(solution)/shard_map/ppermute | solution.py:582
  36.1 4.6 %collective-permute-start.11 = (f32[96,256]{1,0:T(8,128)S(1)}, f32[96,256]{1,0:T(8,128)S(1)}, u32[]{:S(2)}, u32[]{:S(2)}) collective-permute-start(f32[96,256]{1,0:T(8,128)S(1)} %get-tuple-element.55.refs_0_), channel_id=1, source_target_pairs={{0,16},{1,17},{2,18},{3,19},{4,20},{5,21},{6,22},{7,23},{8,24},{9,... | collective-permute-start | bytes 294920 | tf_op jit(solution)/shard_map/ppermute | solution.py:582
  36.1 5.0 %collective-permute-start.10 = (f32[96,256]{1,0:T(8,128)S(1)}, f32[96,256]{1,0:T(8,128)S(1)}, u32[]{:S(2)}, u32[]{:S(2)}) collective-permute-start(f32[96,256]{1,0:T(8,128)S(1)} %get-tuple-element.55.refs_0_), channel_id=1, source_target_pairs={{0,8},{1,9},{2,10},{3,11},{4,12},{5,13},{6,14},{7,15},{8,0},{9,1},... | collective-permute-start | bytes 294920 | tf_op jit(solution)/shard_map/ppermute | solution.py:582
